TPU v7x, 256 devices: a whole 4x4x8 slice. The times are simulated.
256 devices in a mesh: tok: 64 (over x, z, y_hi), head: 4 (over y_lo, core).
Axes of the slice: x: 4, y: 4 (y_hi: 2, y_lo: 2; y = y_hi * 2 + y_lo), z: 8, core: 2. Of those that a mesh axis runs over, the one named last changes fastest.
Arguments:
- queries: bfloat16 [16384, 3072], P('tok', 'head'), may hold values from -96 to 96
- key_rows: bfloat16 [16384, 512], P('tok', 'head'), may hold values from -6 to 6
- value_rows: bfloat16 [16384, 512], P('tok', 'head'), may hold values from -12 to 12
- tile_mask: int32 [128, 128], P('tok'), may hold values from 0 to 1, as said below
- out_weight: bfloat16 [3072, 6144], P('head'), may hold values from -0.109375 to 0.109375
Outputs:
- mixed: bfloat16 [16384, 6144], P('tok', 'head')
Inputs may be any that keep to these rules, and one draw needn't show every extreme that they name: `tile_mask`: row r keeps key tile r; every row keeps between 1 and 64 tiles, and some row keeps exactly 64.
All inputs are finite; a program needn't handle non-finite values.
Results may differ from a plain program's by a relative error of at most 0.012.
Values may be sent and summed in bfloat16 or wider, within the bound.
No kernel may reach another device: no remote copies, remote signals or barrier semaphores. Data moves between devices by JAX's collectives and lax.ppermute only.
A program may use at most 128 MiB of HBM per device.

v0:
```python
import math

import jax
import jax.numpy as jnp
from jax import lax
from jax.sharding import PartitionSpec as P

HD = 128
TILE = 128


NEGATIVE = -1e30
tiles_per_turn = 16


def sent_together(arrays, axis, dim, along):
    ends, at = ([], 0)
    for a in arrays[:-1]:
        at += a.shape[along]
        ends.append(at)
    both = jnp.concatenate(arrays, axis=along)
    return tuple(jnp.split(lax.all_gather(both, axis, axis=dim, tiled=True), ends, axis=along))


def copy_for_each(x, axis):
    copies = jnp.broadcast_to(x, (lax.axis_size(axis), *x.shape))
    return lax.all_to_all(copies, axis, split_axis=0, concat_axis=0, tiled=True)


def joined_along(blocks, dim):
    blocks = jnp.moveaxis(blocks, 0, dim)
    shape = blocks.shape
    return blocks.reshape(*shape[:dim], shape[dim] * shape[dim + 1], *shape[dim + 2 :])


def collect(x, axis, dim):
    blocks = copy_for_each(x, axis)
    return joined_along(blocks, dim)


def tile_block(query_tile, key_chosen, value_chosen, shown_tiles, state, score_scale):
    scores = (
        jnp.einsum("qgjd,ckgd->gjqck", query_tile, key_chosen, preferred_element_type=jnp.float32)
        * score_scale
    )
    shown = shown_tiles[None, None, None, :]
    tile_max = jnp.where(shown, jnp.max(scores, axis=-1), NEGATIVE)
    prob_bf = jnp.where(shown[..., None], jnp.exp(scores - tile_max[..., None]), 0.0).astype(
        jnp.bfloat16
    )
    tile_sums = jnp.sum(prob_bf.astype(jnp.float32), axis=-1)
    tile_parts = jnp.einsum(
        "gjqck,ckgd->gjqcd", prob_bf, value_chosen, preferred_element_type=jnp.float32
    )
    running_max, denominator, numerator = state
    new_max = jnp.maximum(running_max, jnp.max(tile_max, axis=-1))
    rescale = jnp.exp(running_max - new_max)
    tile_weight = jnp.where(shown, jnp.exp(tile_max - new_max[..., None]), 0.0)
    denominator = denominator * rescale + jnp.sum(tile_weight * tile_sums, axis=-1)
    numerator = numerator * rescale[..., None] + jnp.sum(
        tile_weight[..., None] * tile_parts, axis=3
    )
    return (new_max, denominator, numerator)


def sweep_piece(state, query_tile, living, key_tiles, value_tiles, score_scale):
    tile_count = living.shape[0]
    block_tiles = min(tiles_per_turn, tile_count)
    ordering = jnp.argsort(1 - living, stable=True)
    live_total = jnp.sum(living)
    turn_count = (live_total + block_tiles - 1) // block_tiles

    def one_turn(turn_index, inner):
        offset = turn_index * block_tiles
        picked = lax.dynamic_slice_in_dim(ordering, offset, block_tiles)
        shown_tiles = offset + jnp.arange(block_tiles, dtype=jnp.int32) < live_total
        return tile_block(
            query_tile,
            jnp.take(key_tiles, picked, axis=0),
            jnp.take(value_tiles, picked, axis=0),
            shown_tiles,
            inner,
            score_scale,
        )

    return lax.fori_loop(0, turn_count, one_turn, state)


def per_device(queries, key_rows, value_rows, tile_mask, out_weight):
    own_rows = queries.shape[0]
    local_heads = queries.shape[1]
    slot_total = own_rows // TILE
    kv_local = key_rows.shape[1] // HD
    group_size = local_heads // HD // kv_local
    score_scale = 1.0 / math.sqrt(HD)
    query_tiles = queries.reshape(slot_total, TILE, kv_local, group_size, HD)
    slot_rows = [tile_mask[number] for number in range(slot_total)]
    slot_queries = [query_tiles[number] for number in range(slot_total)]
    slot_active = [jnp.int32(1) for number in range(slot_total)]
    empty_max = jnp.full((kv_local, group_size, TILE), NEGATIVE, jnp.float32)
    empty_sum = jnp.zeros((kv_local, group_size, TILE), jnp.float32)
    empty_out = jnp.zeros((kv_local, group_size, TILE, HD), jnp.float32)
    initial = tuple(((empty_max, empty_sum, empty_out) for number in range(len(slot_rows))))
    every_key, every_value = sent_together((key_rows, value_rows), "tok", 0, 1)
    tile_count = every_key.shape[0] // TILE
    key_tiles = every_key.reshape(tile_count, TILE, kv_local, HD)
    value_tiles = every_value.reshape(tile_count, TILE, kv_local, HD)
    result = []
    for absorb_number in range(len(slot_rows)):
        living = slot_rows[absorb_number] * slot_active[absorb_number]
        result.append(
            sweep_piece(
                initial[absorb_number],
                slot_queries[absorb_number],
                living,
                key_tiles,
                value_tiles,
                score_scale,
            )
        )
    carries = tuple(result)
    finished = []
    for number in range(len(slot_rows)):
        running_max, denominator, numerator = carries[number]
        safe_sum = jnp.where(denominator > 0, denominator, 1.0)
        attended = numerator / safe_sum[..., None]
        finished.append(
            attended.transpose(2, 0, 1, 3).reshape(TILE, local_heads).astype(jnp.bfloat16)
        )
    own_stack = jnp.stack(finished[:slot_total])
    attention = own_stack.reshape(own_rows, local_heads)
    columns = lax.all_to_all(out_weight, "head", split_axis=1, concat_axis=0, tiled=True)
    mixed = jnp.dot(collect(attention, "head", 1), columns, preferred_element_type=jnp.float32)
    return mixed.astype(jnp.bfloat16)


def solution(mesh):
    return jax.shard_map(
        per_device,
        mesh=mesh,
        in_specs=(
            P("tok", "head"),
            P("tok", "head"),
            P("tok", "head"),
            P("tok", None),
            P("head", None),
        ),
        out_specs=P("tok", "head"),
        check_vma=False,
    )
```

profile of v0, /device:TPU:1, one launch (start us, length us, event | category | flops | bytes accessed | tf_op | source)
XLA Modules:
  0.0 331.1 jit_solution(4789561493704052197)
XLA Ops:
  8.1 12.7 %copy.44 = bf16[768,6144]{0,1:T(8,128)(2,1)} copy(bf16[768,6144]{1,0:T(8,128)(2,1)} %param.15) | data formatting | bytes 18874368 | tf_op args[4]
  20.8 12.7 %copy.45 = bf16[768,4,1536]{2,0,1:T(8,128)(2,1)} copy(bf16[768,4,1536]{0,2,1:T(8,128)(2,1)} %bitcast.242) | data formatting | bytes 18874368 | tf_op jit(solution)/shard_map/all_to_all | solution.py:132
  33.5 9.1 %all-to-all-start.1 = ((bf16[768,4,1536]{2,0,1:T(8,128)(2,1)}), bf16[768,4,1536]{2,0,1:T(8,128)(2,1)}, u32[]{:S(2)}, u32[]{:S(2)}) async-start(bf16[768,4,1536]{2,0,1:T(8,128)(2,1)} %copy.45), calls=%async_computation.1 | async-start | bytes 18874368 | tf_op jit(solution)/shard_map/all_to_all | solution.py:132
  50.4 141.8 %all-gather.2.cloned.1.call-done = bf16[16384,256]{1,0:T(8,128)(2,1)} async-done(((bf16[256,256]{1,0:T(8,128)(2,1)}), bf16[16384,256]{1,0:T(8,128)(2,1)}) %all-gather.2.cloned.1.call-update) | async-done | bytes 8388624 | tf_op jit(solution)/shard_map/all_gather | solution.py:22
  192.2 5.8 %fusion.57 = (bf16[16384,128]{1,0:T(8,128)(2,1)}, bf16[16384,128]{1,0:T(8,128)(2,1)}) fusion(bf16[16384,256]{1,0:T(8,128)(2,1)} %all-gather.2.cloned.1.call-done), kind=kLoop, calls=%fused_computation.95 | loop fusion | bytes 16777216 | tf_op jit(solution)/shard_map/split | solution.py:22
  198.0 47.1 %while.28 = (s32[]{:T(128)}, f32[1,6,128]{2,1,0:T(8,128)S(1)}, f32[1,6,128]{2,1,0:T(8,128)S(1)}, f32[1,6,128,128]{2,3,1,0:T(8,128)S(1)}, s32[]{:T(128)}, /*index...) while((s32[]{:T(128)}, f32[1,6,128]{2,1,0:T(8,128)S(1)}, ...), condition=%wide.region_8.10_spmd, body=%wide.region_2.9_spmd.sunk | while | flops 828001664 | bytes 24331904 | solution.py:86
  198.7 2.8 gather_fusion.1
  201.6 2.8 gather_fusion
  210.5 2.8 gather_fusion.1
  213.3 2.8 gather_fusion
  222.3 2.8 gather_fusion.1
  225.1 2.8 gather_fusion
  234.1 2.8 gather_fusion.1
  236.9 2.8 gather_fusion
  245.2 47.0 %while.29 = (s32[]{:T(128)}, f32[1,6,128]{2,1,0:T(8,128)S(1)}, f32[1,6,128]{2,1,0:T(8,128)S(1)}, f32[1,6,128,128]{2,3,1,0:T(8,128)S(1)}, s32[]{:T(128)}, /*index...) while((s32[]{:T(128)}, f32[1,6,128]{2,1,0:T(8,128)S(1)}, ...), condition=%wide.region_17.19_spmd, body=%wide.region_11.18_spmd.sunk | while | flops 828001664 | bytes 24331904 | solution.py:86
  245.9 2.8 gather_fusion.3
  248.7 2.8 gather_fusion.2
  257.6 2.8 gather_fusion.3
  260.5 2.8 gather_fusion.2
  269.4 2.8 gather_fusion.3
  272.2 2.8 gather_fusion.2
  281.1 2.8 gather_fusion.3
  292.6 24.5 %all_to_all.21 = bf16[4,256,768]{2,1,0:T(8,128)(2,1)S(1)} all-to-all(bf16[4,256,768]{2,1,0:T(8,128)(2,1)S(1)} %broadcast_in_dim.92), channel_id=1, replica_groups=mesh['tok'=64,'head'=4] {'head'}, dimensions={0} | all-to-all | bytes 3145728 | tf_op jit(solution)/shard_map/all_to_all | solution.py:27
  317.1 7.2 %fusion.49 = bf16[256,1536]{1,0:T(8,128)(2,1)} fusion(bf16[768,4,1536]{2,0,1:T(8,128)(2,1)} %all-to-all-done.1, bf16[4,256,768]{2,1,0:T(8,128)(2,1)S(1)} %all_to_all.21), kind=kOutput, calls=%fused_computation.79 | convolution fusion | flops 2416312320 | bytes 11796480 | tf_op jit(solution)/shard_map/dot_general | solution.py:133
  (120 shorter events, 59.3 us)
Async XLA Ops:
  6.5 185.6 %all-gather.2.cloned.1.call-start = ((), (), s32[]{:S(2)}) async-start(), calls=%async_computation.2 | async-start | bytes 8519680 | tf_op jit(solution)/shard_map/all_gather | solution.py:22
  33.5 9.1 %copy-start.1 = (s32[2,128]{1,0:T(2,128)S(1)}, s32[2,128]{1,0:T(2,128)}, u32[]{:S(2)}) copy-start(s32[2,128]{1,0:T(2,128)} %param.14) | copy-start | bytes 3076
  33.5 11.1 %copy-start = (bf16[256,768]{1,0:T(8,128)(2,1)S(1)}, bf16[256,768]{1,0:T(8,128)(2,1)}, u32[]{:S(2)}) copy-start(bf16[256,768]{1,0:T(8,128)(2,1)} %param.11) | copy-start | bytes 1179652
  33.5 259.0 %all-to-all-start.1 = ((bf16[768,4,1536]{2,0,1:T(8,128)(2,1)}), bf16[768,4,1536]{2,0,1:T(8,128)(2,1)}, u32[]{:S(2)}, u32[]{:S(2)}) async-start(bf16[768,4,1536]{2,0,1:T(8,128)(2,1)} %copy.45), calls=%async_computation.1 | async-start | bytes 18874368 | tf_op jit(solution)/shard_map/all_to_all | solution.py:132
Sparse Core Ops, SparseCore 0:
  11.0 181.1 all-gather.1
where the time goes:
time: 333 us; the launch traced here: 331 us
  waiting for transfers between devices  142 us (43%)
  local copies, waits for them, and re-layouts  77.7 us (23%)
  matrix products  32.3 us (10%)
  other arithmetic  30.2 us (9%)
  blocking collectives  24.5 us (7%)
  between operations  14.8 us (4%)
  starting transfers between devices  9.14 us (3%)
    all_gather x1, waiting for transfers between devices, sent_together(): lax.all_gather(both, axis, axis=dim, tiled=True)  142 us
    all_to_all x1, blocking collectives, copy_for_each(): return lax.all_to_all(copies, axis, split_axis=0, concat_axis=0, tiled=True)  24.5 us
    gather x8, local copies, waits for them, and re-layouts, one_turn(): jnp.take(key_tiles, picked, axis=0)  22.7 us
    gather x8, local copies, waits for them, and re-layouts, one_turn(): jnp.take(value_tiles, picked, axis=0)  22.7 us
    dot_general x8, matrix products, tile_block(): jnp.einsum('gjqck,ckgd->gjqcd', prob_bf, value_chosen, preferred_element_...  16.9 us
    reduce_sum x8, other arithmetic, tile_block(): tile_sums = jnp.sum(prob_bf.astype(jnp.float32), axis=-1)  14.5 us
    unnamed x7, local copies, waits for them, and re-layouts  13 us
    all_to_all x1, local copies, waits for them, and re-layouts, per_device(): lax.all_to_all(out_weight, 'head', split_axis=1, concat_axis=0, tiled=True)  12.7 us
  transfers between devices with their start and end apart: 2, of which 1 were waited for; matrix products, arithmetic and copies ran while one was open for 40% of the time, Pallas kernels for 0%

commit v1 on v0

v1 whole, which is shorter than its diff:
```python
import math

import jax
import jax.numpy as jnp
from jax import lax
from jax.experimental import pallas as pl
from jax.experimental.pallas import tpu as pltpu
from jax.sharding import Mesh, PartitionSpec as P

HD = 128
TILE = 128
NX, NZ = 4, 8
HEADS = 6
WIDE = HEADS * TILE
SUM_ROW = HD
MAX_ROW = HD + 16
ROWS = HD + 24
NEGATIVE = -1e30
EXP2_SCALE = math.log2(math.e) / math.sqrt(HD)
Z_ORDER = (0, -1, 1, -2, 2, -3, 3, 4)


def vmem():
    return pl.BlockSpec(memory_space=pltpu.VMEM)


def smem():
    return pl.BlockSpec(memory_space=pltpu.SMEM)


def call(kernel, out_shape, args, in_specs, scratch=(), aliases=None, name=None):
    return pl.pallas_call(
        kernel,
        out_shape=out_shape,
        in_specs=in_specs,
        out_specs=jax.tree.map(lambda s: vmem(), out_shape),
        scratch_shapes=list(scratch),
        input_output_aliases=aliases or {},
        compiler_params=pltpu.CompilerParams(vmem_limit_bytes=48 * 1024 * 1024),
        name=name,
    )(*args)


def pack_kernel(key_ref, value_ref, out_ref):
    for t in range(2):
        rows = pl.ds(t * TILE, TILE)
        out_ref[t] = key_ref[rows, :]
        out_ref[2 + t] = value_ref[rows, :].astype(jnp.float32).T.astype(jnp.bfloat16)


def join_kernel(*refs):
    out_ref = refs[-1]
    at = 0
    for ref in refs[:-1]:
        out_ref[pl.ds(at, ref.shape[0])] = ref[...]
        at += ref.shape[0]


def join(parts):
    total = sum(p.shape[0] for p in parts)
    shape = jax.ShapeDtypeStruct((total, *parts[0].shape[1:]), parts[0].dtype)
    return call(join_kernel, shape, parts, [vmem()] * len(parts), name="join")


def stage_kernel(columns, count, first, place_ref, mask_ref, mine_ref, theirs_ref, *refs):
    parts, refs = refs[:count], refs[count:]
    if not first:
        refs = refs[2:]
    keep_ref, send_ref, tiles_ref, query_ref, list_ref = refs
    x, z, core = place_ref[0], place_ref[1], place_ref[2]
    at = 0
    for part in parts:
        tiles_ref[pl.ds(at, part.shape[0])] = part[...]
        at += part.shape[0]
    for number in range(4):
        source = mine_ref if number < 2 else theirs_ref
        rows = pl.ds(number % 2 * TILE, TILE)
        for h in range(HEADS):
            query_ref[number, pl.ds(h * TILE, TILE), :] = source[rows, pl.ds(h * HD, HD)]
    if first:
        for ref in (keep_ref, send_ref):
            ref[:, :MAX_ROW, :] = jnp.zeros((2, MAX_ROW, WIDE), jnp.float32)
            ref[:, MAX_ROW:, :] = jnp.full((2, ROWS - MAX_ROW, WIDE), NEGATIVE, jnp.float32)

    counts = [jnp.int32(0)] * 4
    slot = 0
    for dx, order in columns:
        for dz in order:
            block = lax.rem(x + dx + NX, NX) * NZ + lax.rem(z + dz + NZ, NZ)
            for r in range(2):
                tile = (block * 2 + core) * 2 + r
                for number in range(4):
                    list_ref[number, counts[number]] = slot // 2 * 4 + slot % 2
                    counts[number] = counts[number] + mask_ref[number, tile]
                slot += 1

    for number in range(4):
        state_ref = keep_ref if number < 2 else send_ref
        row = number % 2
        total = counts[number]

        def one_pair(turn, carry, number=number, state_ref=state_ref, row=row, total=total):
            first_at = list_ref[number, 2 * turn]
            both = 2 * turn + 1 < total
            second_at = jnp.where(both, list_ref[number, 2 * turn + 1], first_at)
            keys = jnp.concatenate([tiles_ref[first_at], tiles_ref[second_at]], axis=0)
            shown = jnp.where(both, 1.0, 0.0).astype(jnp.float32)
            lane = lax.broadcasted_iota(jnp.int32, (HD + 16, 2 * TILE), 1)
            shown_lanes = jnp.where(lane < TILE, 1.0, shown).astype(jnp.bfloat16)
            values = jnp.concatenate([tiles_ref[first_at + 2], tiles_ref[second_at + 2]], axis=1)
            values = jnp.concatenate(
                [values, jnp.ones((16, 2 * TILE), jnp.bfloat16)], axis=0
            ) * shown_lanes
            for chunk in range(3):
                lanes = pl.ds(chunk * 256, 256)
                scores = lax.dot_general(
                    keys,
                    query_ref[number, lanes, :],
                    (((1,), (1,)), ((), ())),
                    preferred_element_type=jnp.float32,
                )
                old_max = state_ref[row, pl.ds(MAX_ROW, 1), lanes]
                new_max = jnp.maximum(old_max, jnp.max(scores, axis=0, keepdims=True))
                prob = jnp.exp2((scores - new_max) * EXP2_SCALE).astype(jnp.bfloat16)
                fade = jnp.exp2((old_max - new_max) * EXP2_SCALE)
                part = lax.dot_general(
                    values, prob, (((1,), (0,)), ((), ())), preferred_element_type=jnp.float32
                )
                state_ref[row, pl.ds(0, MAX_ROW), lanes] = (
                    state_ref[row, pl.ds(0, MAX_ROW), lanes] * fade + part
                )
                state_ref[row, pl.ds(MAX_ROW, 8), lanes] = jnp.broadcast_to(new_max, (8, 256))
            return carry

        lax.fori_loop(0, (total + 1) // 2, one_pair, 0)


def stage(columns, place, mask, mine, theirs, parts, state, name):
    shape = jax.ShapeDtypeStruct((2, ROWS, WIDE), jnp.float32)
    slots = sum(2 * len(order) for _, order in columns)
    args = [place, mask, mine, theirs, *parts]
    aliases = {}
    if state is not None:
        aliases = {len(args): 0, len(args) + 1: 1}
        args += list(state)
    kernel = lambda *refs: stage_kernel(columns, len(parts), state is None, *refs)
    return call(
        kernel,
        (shape, shape),
        args,
        [smem(), smem()] + [vmem()] * (len(args) - 2),
        scratch=(
            pltpu.VMEM((2 * slots, TILE, TILE), jnp.bfloat16),
            pltpu.VMEM((4, WIDE, HD), jnp.bfloat16),
            pltpu.SMEM((4, slots + 1), jnp.int32),
        ),
        aliases=aliases,
        name=name,
    )


def merge_kernel(own_ref, other_ref, out_ref):
    for t in range(2):
        own_max = own_ref[t, pl.ds(MAX_ROW, 1), :]
        other_max = other_ref[t, pl.ds(MAX_ROW, 1), :]
        row_max = jnp.maximum(own_max, other_max)
        own_weight = jnp.exp2((own_max - row_max) * EXP2_SCALE)
        other_weight = jnp.exp2((other_max - row_max) * EXP2_SCALE)
        total = (
            own_ref[t, pl.ds(SUM_ROW, 1), :] * own_weight
            + other_ref[t, pl.ds(SUM_ROW, 1), :] * other_weight
        )
        own_weight = own_weight / total
        other_weight = other_weight / total
        for h in range(HEADS):
            lanes = slice(h * TILE, (h + 1) * TILE)
            attended = (
                own_ref[t, pl.ds(0, HD), lanes] * own_weight[:, lanes]
                + other_ref[t, pl.ds(0, HD), lanes] * other_weight[:, lanes]
            )
            out_ref[pl.ds(t * TILE, TILE), pl.ds(h * HD, HD)] = attended.T.astype(jnp.bfloat16)


def ring(size, step):
    return [(i, (i + step) % size) for i in range(size)]


def along_y(move):
    pairs = []
    for i in range(8):
        yh, yl, core = move(i // 4, i // 2 % 2, i % 2)
        pairs.append((i, yh % 2 * 4 + yl % 2 * 2 + core % 2))
    return pairs


def next_y(yh, yl, step):
    y = (yh * 2 + yl + step) % 4
    return y // 2, y % 2


Y = ("yh", "yl", "core")
YZ = ("z", "yh", "yl", "core")


def turned(shift):
    turn = along_y(lambda yh, yl, core: (core, yl, yh))
    return [(z * 8 + a, (z + shift) % NZ * 8 + b) for z in range(NZ) for a, b in turn]


def per_device(queries, key_rows, value_rows, tile_mask, out_weight):
    x, z = lax.axis_index("x"), lax.axis_index("z")
    yh, yl, core = lax.axis_index("yh"), lax.axis_index("yl"), lax.axis_index("core")
    turn = along_y(lambda yh, yl, core: (core, yl, yh))
    f32 = jnp.float32

    unit_shape = jax.ShapeDtypeStruct((4, TILE, TILE), jnp.bfloat16)
    unit = call(pack_kernel, unit_shape, (key_rows, value_rows), [vmem()] * 2, name="pack")
    up, down = ring(NZ, 1), ring(NZ, -1)
    own = lax.ppermute(unit, YZ, turned(0))
    units = {0: own}
    units[-1] = lax.ppermute(unit, YZ, turned(1))
    units[1] = lax.ppermute(unit, YZ, turned(-1))
    mine = lax.ppermute(queries, Y, turn)
    other_mask = lax.ppermute(tile_mask, "yh", [(0, 1), (1, 0)])
    for step in (2, 3):
        units[-step] = lax.ppermute(units[1 - step], "z", up)
        units[step] = lax.ppermute(units[step - 1], "z", down)
    far = (
        lax.ppermute(units[-3][:2], "z", up),
        lax.ppermute(units[3][2:], "z", down),
    )
    theirs = lax.ppermute(mine, "core", [(0, 1), (1, 0)])
    same = yh == core
    mask = jnp.concatenate(
        [jnp.where(same, tile_mask, other_mask), jnp.where(same, other_mask, tile_mask)]
    )
    place = jnp.stack([x, z, core]).astype(jnp.int32)

    column = join([units[d] for d in Z_ORDER[:-1]] + list(far))
    before = lax.ppermute(column, "x", ring(NX, 1))
    after = lax.ppermute(column, "x", ring(NX, -1))
    half = column.shape[0] // 2
    first_half = lax.ppermute(before[:half], "x", ring(NX, 1))
    second_half = lax.ppermute(after[half:], "x", ring(NX, -1))

    block = out_weight.shape[1] // 4
    column_block = lambda yl, core: lax.dynamic_slice_in_dim(
        out_weight, (yl * 2 + core) * block, block, 1
    )
    weight_own = column_block(yl, core)
    weight_core = lax.ppermute(column_block(yl, 1 - core), "core", [(0, 1), (1, 0)])
    weight_up = lax.ppermute(
        column_block(1 - yl, core), Y, along_y(lambda yh, yl, core: (*next_y(yh, yl, 1), core))
    )
    weight_down = lax.ppermute(
        column_block(1 - yl, 1 - core),
        Y,
        along_y(lambda yh, yl, core: (*next_y(yh, yl, -1), 1 - core)),
    )

    near = (place, mask, mine, theirs)
    state = stage(((0, Z_ORDER),), *near, [column], None, "stage_a")
    state = stage(((-1, Z_ORDER), (1, Z_ORDER)), *near, [before, after], state, "stage_b")
    state = stage(((2, Z_ORDER),), *near, [first_half, second_half], state, "stage_c")
    keep, send = state
    received = lax.ppermute(send, "core", [(0, 1), (1, 0)])
    shape = jax.ShapeDtypeStruct((2 * TILE, WIDE), jnp.bfloat16)
    attended = call(merge_kernel, shape, (keep, received), [vmem()] * 2, name="merge")

    near_part = lax.ppermute(attended, Y, turn)
    far_part = lax.ppermute(attended, Y, along_y(lambda yh, yl, core: (core, 1 - yl, yh)))
    swap = [(0, 1), (1, 0)]
    near_other = lax.ppermute(near_part, "core", swap)
    far_other = lax.ppermute(far_part, "core", swap)
    dot = lambda a, b: jnp.dot(a, b, preferred_element_type=f32)
    mixed = dot(near_part, weight_own) + dot(far_part, weight_up)
    mixed = mixed + dot(near_other, weight_core) + dot(far_other, weight_down)
    return mixed.astype(jnp.bfloat16)


def solution(mesh):
    fine = Mesh(mesh.devices.reshape(NX, NZ, 2, 2, 2), ("x", "z", "yh", "yl", "core"))
    tok, head = ("x", "z", "yh"), ("yl", "core")
    return jax.shard_map(
        per_device,
        mesh=fine,
        in_specs=(P(tok, head), P(tok, head), P(tok, head), P(tok, None), P(head, None)),
        out_specs=P(tok, head),
        check_vma=False,
    )
```

time: 333 us -> 187 us (0.56)
  the two profiles are of different devices: /device:TPU:1 before, /device:TPU:101 now
where the time goes in v1:
time: 187 us
  waiting for transfers between devices  65.8 us (35%)
  Pallas kernels  56.9 us (30%)
  starting transfers between devices  42.4 us (23%)
  matrix products  10.7 us (6%)
  local copies, waits for them, and re-layouts  10.6 us (6%)
    pallas_call x6, Pallas kernels, call(): pl.pallas_call(kernel, out_shape=out_shape, in_specs=in_specs, out_specs=...  56.9 us
    ppermute x1, waiting for transfers between devices, per_device(): mine = lax.ppermute(queries, Y, turn)  36.6 us
    dot_general x4, matrix products, per_device(): dot = lambda a, b: jnp.dot(a, b, preferred_element_type=f32)  10.7 us
    ppermute x1, waiting for transfers between devices, per_device(): before = lax.ppermute(column, 'x', ring(NX, 1))  8.16 us
    ppermute x1, waiting for transfers between devices, per_device(): lax.ppermute(attended, Y, along_y(lambda yh, yl, core: (core, 1 - yl, yh)))  7.01 us
    ppermute x2, starting transfers between devices, per_device(): units[-step] = lax.ppermute(units[1 - step], 'z', up)  6.81 us
    dynamic_slice x1, local copies, waits for them, and re-layouts, per_device(): lax.dynamic_slice_in_dim(out_weight, (yl * 2 + core) * block, block, 1)  6.15 us
    ppermute x1, starting transfers between devices, per_device(): units[-1] = lax.ppermute(unit, YZ, turned(1))  6.12 us
  transfers between devices with their start and end apart: 24, of which 11 were waited for; matrix products, arithmetic and copies ran while one was open for 9% of the time, Pallas kernels for 30%

profile of v1, /device:TPU:101, one launch (start us, length us, event | category | flops | bytes accessed | tf_op | source)
XLA Modules:
  0.0 186.6 jit_solution(15151521998186104463)
XLA Ops:
  1.8 6.1 %collective-permute-start.4 = (bf16[4,128,128]{2,1,0:T(8,128)(2,1)S(1)}, bf16[4,128,128]{2,1,0:T(8,128)(2,1)S(1)}, u32[]{:S(2)}, u32[]{:S(2)}) collective-permute-start(bf16[4,128,128]{2,1,0:T(8,128)(2,1)S(1)} %pack.1), channel_id=1, source_target_pairs={{0,8},{1,12},{2,10},{3,14},{4,9},{5,13},{6,11},{7,15},{8,16},{9,20... | collective-permute-start | bytes 393224 | tf_op jit(solution)/shard_map/ppermute | solution.py:221
  9.8 3.9 %collective-permute-start.6 = (bf16[4,128,128]{2,1,0:T(8,128)(2,1)S(1)}, bf16[4,128,128]{2,1,0:T(8,128)(2,1)S(1)}, u32[]{:S(2)}, u32[]{:S(2)}) collective-permute-start(bf16[4,128,128]{2,1,0:T(8,128)(2,1)S(1)} %collective-permute-done.4.refs_1_), channel_id=1, source_target_pairs={{0,8},{8,16},{16,24},{24,32},{32,40},{40,48},{48,56},{56,0},{1,9},... | collective-permute-start | bytes 393224 | tf_op jit(solution)/shard_map/ppermute | solution.py:226
  13.8 2.1 %collective-permute-done.5.refs_2_ = bf16[4,128,128]{2,1,0:T(8,128)(2,1)S(1)} collective-permute-done((bf16[4,128,128]{2,1,0:T(8,128)(2,1)S(1)}, bf16[4,128,128]{2,1,0:T(8,128)(2,1)S(1)}, u32[]{:S(2)}, u32[]{:S(2)}) %collective-permute-start.5) | collective-permute-done | bytes 131104 | tf_op jit(solution)/shard_map/ppermute | solution.py:222
  15.9 2.9 %collective-permute-start.8 = (bf16[4,128,128]{2,1,0:T(8,128)(2,1)S(1)}, bf16[4,128,128]{2,1,0:T(8,128)(2,1)S(1)}, u32[]{:S(2)}, u32[]{:S(2)}) collective-permute-start(bf16[4,128,128]{2,1,0:T(8,128)(2,1)S(1)} %collective-permute-done.6.refs_3_), channel_id=1, source_target_pairs={{0,8},{8,16},{16,24},{24,32},{32,40},{40,48},{48,56},{56,0},{1,9},... | collective-permute-start | bytes 393224 | tf_op jit(solution)/shard_map/ppermute | solution.py:226
  18.8 2.1 %collective-permute-done.7.refs_4_ = bf16[4,128,128]{2,1,0:T(8,128)(2,1)S(1)} collective-permute-done((bf16[4,128,128]{2,1,0:T(8,128)(2,1)S(1)}, bf16[4,128,128]{2,1,0:T(8,128)(2,1)S(1)}, u32[]{:S(2)}, u32[]{:S(2)}) %collective-permute-start.7) | collective-permute-done | bytes 131104 | tf_op jit(solution)/shard_map/ppermute | solution.py:227
  20.9 4.2 %collective-permute-start.3 = (bf16[4,128,128]{2,1,0:T(8,128)(2,1)S(1)}, bf16[4,128,128]{2,1,0:T(8,128)(2,1)S(1)}, u32[]{:S(2)}, u32[]{:S(2)}) collective-permute-start(bf16[4,128,128]{2,1,0:T(8,128)(2,1)S(1)} %pack.1), channel_id=1, source_target_pairs={{0,0},{1,4},{2,2},{3,6},{4,1},{5,5},{6,3},{7,7},{8,8},{9,12},{10,1... | collective-permute-start | bytes 393224 | tf_op jit(solution)/shard_map/ppermute | solution.py:219
  25.1 3.0 %collective-permute-start.10 = (bf16[2,128,128]{2,1,0:T(8,128)(2,1)S(1)}, bf16[2,128,128]{2,1,0:T(8,128)(2,1)S(1)}, u32[]{:S(2)}, u32[]{:S(2)}) collective-permute-start(bf16[2,128,128]{2,1,0:T(8,128)(2,1)S(1)} %slice.16), channel_id=1, source_target_pairs={{0,8},{8,16},{16,24},{24,32},{32,40},{40,48},{48,56},{56,0},{1,9},... | collective-permute-start | bytes 196616 | tf_op jit(solution)/shard_map/ppermute | solution.py:229
  29.5 3.1 %collective-permute-done.11.refs_8_ = bf16[2,128,128]{2,1,0:T(8,128)(2,1)S(1)} collective-permute-done((bf16[2,128,128]{2,1,0:T(8,128)(2,1)S(1)}, bf16[2,128,128]{2,1,0:T(8,128)(2,1)S(1)}, u32[]{:S(2)}, u32[]{:S(2)}) %collective-permute-start.11) | collective-permute-done | bytes 65568 | tf_op jit(solution)/shard_map/ppermute | solution.py:230
  34.2 6.2 %constant_dynamic-slice_fusion.1 = (bf16[768,1536]{1,0:T(8,128)(2,1)}, bf16[768,1536]{1,0:T(8,128)(2,1)}, bf16[768,1536]{1,0:T(8,128)(2,1)}) fusion(bf16[768,6144]{1,0:T(8,128)(2,1)} %param.9, s32[]{:T(128)S(6)} %select_n.29, s32[]{:T(128)S(6)} %select_n.28, s32[]{:T(128)S(6)} %select_n.30), kind=kLoop, calls=%fused_computation.7 | loop fusion | bytes 14155788 | tf_op jit(solution)/shard_map/dynamic_slice | solution.py:247
  40.4 2.3 %collective-permute-start.19 = (bf16[768,1536]{1,0:T(8,128)(2,1)}, bf16[768,1536]{1,0:T(8,128)(2,1)}, u32[]{:S(2)}, u32[]{:S(2)}) collective-permute-start(bf16[768,1536]{1,0:T(8,128)(2,1)} %get-tuple-element.18), channel_id=1, source_target_pairs={{0,2},{1,3},{2,4},{3,5},{4,6},{5,7},{6,0},{7,1},{8,10},{9,11},{10,... | collective-permute-start | bytes 7077896 | tf_op jit(solution)/shard_map/ppermute | solution.py:252
  42.7 5.7 %collective-permute-start.1 = (bf16[256,768]{1,0:T(8,128)(2,1)S(1)}, bf16[256,768]{1,0:T(8,128)(2,1)S(1)}, u32[]{:S(2)}, u32[]{:S(2)}) collective-permute-start(bf16[256,768]{1,0:T(8,128)(2,1)S(1)} %copy-done.3), channel_id=1, source_target_pairs={{0,0},{1,4},{2,2},{3,6},{4,1},{5,5},{6,3},{7,7},{8,8},{9,12},{10,1... | collective-permute-start | bytes 1179656 | tf_op jit(solution)/shard_map/ppermute | solution.py:223
  48.4 8.2 %collective-permute-done.12.refs_4_ = bf16[32,128,128]{2,1,0:T(8,128)(2,1)S(1)} collective-permute-done((bf16[32,128,128]{2,1,0:T(8,128)(2,1)S(1)}, bf16[32,128,128]{2,1,0:T(8,128)(2,1)S(1)}, u32[]{:S(2)}, u32[]{:S(2)}) %collective-permute-start.12) | collective-permute-done | bytes 1048608 | tf_op jit(solution)/shard_map/ppermute | solution.py:240
  60.7 36.6 %collective-permute-done.1.refs_2_ = bf16[256,768]{1,0:T(8,128)(2,1)S(1)} collective-permute-done((bf16[256,768]{1,0:T(8,128)(2,1)S(1)}, bf16[256,768]{1,0:T(8,128)(2,1)S(1)}, u32[]{:S(2)}, u32[]{:S(2)}) %collective-permute-start.1) | collective-permute-done | bytes 393248 | tf_op jit(solution)/shard_map/ppermute | solution.py:223
  97.3 4.1 %collective-permute-start = (s32[2,128]{1,0:T(2,128)S(1)}, s32[2,128]{1,0:T(2,128)S(1)}, u32[]{:S(2)}, u32[]{:S(2)}) collective-permute-start(s32[2,128]{1,0:T(2,128)S(1)} %copy-done.2), channel_id=1, source_target_pairs={{0,4},{4,0},{1,5},{5,1},{2,6},{6,2},{3,7},{7,3},{8,12},{12,8},{9,1... | collective-permute-start | bytes 3080 | tf_op jit(solution)/shard_map/ppermute | solution.py:224
  103.4 16.8 %stage_a.1 = (f32[2,152,768]{2,1,0:T(8,128)S(1)}, f32[2,152,768]{2,1,0:T(8,128)S(1)}) custom-call(s32[3]{0:T(128)S(1)} %pad_add_fusion.1.refs_0_, s32[4,128]{1,0:T(4,128)S(1)} %pad_add_fusion.refs_1_, bf16[256,768]{1,0:T(8,128)(2,1)S(1)} %collective-permute-done.1.refs_2_, bf16[256,768]{1,0:T(8,128)(2,1)S(1)} %collective-permute-done.2.refs_3_, ...), custom_call_target="tpu_custom_call" | custom-call | tf_op jit(solution)/shard_map/stage_a/pallas_call | solution.py:32
  120.2 29.4 %stage_b.1 = (f32[2,152,768]{2,1,0:T(8,128)S(1)}, f32[2,152,768]{2,1,0:T(8,128)S(1)}) custom-call(s32[3]{0:T(128)S(1)} %pad_add_fusion.1.refs_0_, s32[4,128]{1,0:T(4,128)S(1)} %pad_add_fusion.refs_1_, bf16[256,768]{1,0:T(8,128)(2,1)S(1)} %collective-permute-done.1.refs_2_, ...), custom_call_target="tpu_custom_call", output_to_operand_aliasing={{0}: (6, {}), {1}: (7, {})} | custom-call | tf_op jit(solution)/shard_map/stage_b/pallas_call | solution.py:32
  149.7 10.3 %stage_c.1 = (f32[2,152,768]{2,1,0:T(8,128)S(1)}, f32[2,152,768]{2,1,0:T(8,128)S(1)}) custom-call(s32[3]{0:T(128)S(1)} %pad_add_fusion.1.refs_0_, s32[4,128]{1,0:T(4,128)S(1)} %pad_add_fusion.refs_1_, bf16[256,768]{1,0:T(8,128)(2,1)S(1)} %collective-permute-done.1.refs_2_, ...), custom_call_target="tpu_custom_call", output_to_operand_aliasing={{0}: (6, {}), {1}: (7, {})} | custom-call | tf_op jit(solution)/shard_map/stage_c/pallas_call | solution.py:32
  160.1 2.5 %collective-permute-done.16.other_ref = f32[2,152,768]{2,1,0:T(8,128)S(1)} collective-permute-done((f32[2,152,768]{2,1,0:T(8,128)S(1)}, f32[2,152,768]{2,1,0:T(8,128)S(1)}, u32[]{:S(2)}, u32[]{:S(2)}) %collective-permute-start.16) | collective-permute-done | bytes 933920 | tf_op jit(solution)/shard_map/ppermute | solution.py:266
  162.8 3.5 %collective-permute-start.18 = (bf16[256,768]{1,0:T(8,128)(2,1)S(1)}, bf16[256,768]{1,0:T(8,128)(2,1)S(1)}, u32[]{:S(2)}, u32[]{:S(2)}) collective-permute-start(bf16[256,768]{1,0:T(8,128)(2,1)S(1)} %merge.1), channel_id=1, source_target_pairs={{0,2},{1,6},{2,0},{3,4},{4,3},{5,7},{6,1},{7,5},{8,10},{9,14},{10,... | collective-permute-start | bytes 1179656 | tf_op jit(solution)/shard_map/ppermute | solution.py:271
  168.2 7.0 %collective-permute-done.18 = bf16[256,768]{1,0:T(8,128)(2,1)S(1)} collective-permute-done((bf16[256,768]{1,0:T(8,128)(2,1)S(1)}, bf16[256,768]{1,0:T(8,128)(2,1)S(1)}, u32[]{:S(2)}, u32[]{:S(2)}) %collective-permute-start.18) | collective-permute-done | bytes 393248 | tf_op jit(solution)/shard_map/ppermute | solution.py:271
  175.3 2.4 %fusion.4 = f32[256,1536]{1,0:T(8,128)S(1)} fusion(bf16[256,768]{1,0:T(8,128)(2,1)S(1)} %collective-permute-done.18, bf16[768,1536]{1,0:T(8,128)(2,1)} %collective-permute-done.19), kind=kOutput, calls=%fused_computation.13 | convolution fusion | flops 603979776 | bytes 4325376 | tf_op jit(solution)/shard_map/dot_general | solution.py:275
  178.3 2.5 %convolution_add_fusion.1 = f32[256,1536]{1,0:T(8,128)S(1)} fusion(f32[256,1536]{1,0:T(8,128)S(1)} %fusion.4, bf16[256,768]{1,0:T(8,128)(2,1)S(1)} %collective-permute-done.17, bf16[768,6144]{1,0:T(8,128)(2,1)} %param.9, s32[]{:T(128)S(6)} %select_n.27), kind=kOutput, calls=%fused_computation.2 | convolution fusion | flops 604372992 | bytes 5898244 | tf_op jit(solution)/shard_map/dot_general | solution.py:275
  180.8 2.4 %fusion.5 = f32[256,1536]{1,0:T(8,128)S(1)} fusion(bf16[256,768]{1,0:T(8,128)(2,1)S(1)} %collective-permute-done.22, bf16[768,1536]{1,0:T(8,128)(2,1)} %collective-permute-done.23), kind=kOutput, calls=%fused_computation.14 | convolution fusion | flops 603979776 | bytes 4325376 | tf_op jit(solution)/shard_map/dot_general | solution.py:275
  183.3 3.4 %fusion.1 = bf16[256,1536]{1,0:T(8,128)(2,1)} fusion(f32[256,1536]{1,0:T(8,128)S(1)} %fusion.5, f32[256,1536]{1,0:T(8,128)S(1)} %convolution_add_fusion.1, bf16[256,768]{1,0:T(8,128)(2,1)S(1)} %collective-permute-done.20, bf16[768,1536]{1,0:T(8,128)(2,1)} %collective-permute-done.21), kind=kOutput, calls=%fused_computation.3 | convolution fusion | flops 605159424 | bytes 6684672 | tf_op jit(solution)/shard_map/dot_general | solution.py:275
  (50 shorter events, 15.7 us)
Async XLA Ops:
  1.8 8.1 %collective-permute-start.4 = (bf16[4,128,128]{2,1,0:T(8,128)(2,1)S(1)}, bf16[4,128,128]{2,1,0:T(8,128)(2,1)S(1)}, u32[]{:S(2)}, u32[]{:S(2)}) collective-permute-start(bf16[4,128,128]{2,1,0:T(8,128)(2,1)S(1)} %pack.1), channel_id=1, source_target_pairs={{0,8},{1,12},{2,10},{3,14},{4,9},{5,13},{6,11},{7,15},{8,16},{9,20... | collective-permute-start | bytes 393224 | tf_op jit(solution)/shard_map/ppermute | solution.py:221
  7.9 8.0 %collective-permute-start.5 = (bf16[4,128,128]{2,1,0:T(8,128)(2,1)S(1)}, bf16[4,128,128]{2,1,0:T(8,128)(2,1)S(1)}, u32[]{:S(2)}, u32[]{:S(2)}) collective-permute-start(bf16[4,128,128]{2,1,0:T(8,128)(2,1)S(1)} %pack.1), channel_id=1, source_target_pairs={{0,56},{1,60},{2,58},{3,62},{4,57},{5,61},{6,59},{7,63},{8,0},{9,4... | collective-permute-start | bytes 393224 | tf_op jit(solution)/shard_map/ppermute | solution.py:222
  9.8 6.1 %collective-permute-start.6 = (bf16[4,128,128]{2,1,0:T(8,128)(2,1)S(1)}, bf16[4,128,128]{2,1,0:T(8,128)(2,1)S(1)}, u32[]{:S(2)}, u32[]{:S(2)}) collective-permute-start(bf16[4,128,128]{2,1,0:T(8,128)(2,1)S(1)} %collective-permute-done.4.refs_1_), channel_id=1, source_target_pairs={{0,8},{8,16},{16,24},{24,32},{32,40},{40,48},{48,56},{56,0},{1,9},... | collective-permute-start | bytes 393224 | tf_op jit(solution)/shard_map/ppermute | solution.py:226
  15.9 5.0 %collective-permute-start.7 = (bf16[4,128,128]{2,1,0:T(8,128)(2,1)S(1)}, bf16[4,128,128]{2,1,0:T(8,128)(2,1)S(1)}, u32[]{:S(2)}, u32[]{:S(2)}) collective-permute-start(bf16[4,128,128]{2,1,0:T(8,128)(2,1)S(1)} %collective-permute-done.5.refs_2_), channel_id=1, source_target_pairs={{0,56},{8,0},{16,8},{24,16},{32,24},{40,32},{48,40},{56,48},{1,57}... | collective-permute-start | bytes 393224 | tf_op jit(solution)/shard_map/ppermute | solution.py:227
  15.9 9.2 %collective-permute-start.8 = (bf16[4,128,128]{2,1,0:T(8,128)(2,1)S(1)}, bf16[4,128,128]{2,1,0:T(8,128)(2,1)S(1)}, u32[]{:S(2)}, u32[]{:S(2)}) collective-permute-start(bf16[4,128,128]{2,1,0:T(8,128)(2,1)S(1)} %collective-permute-done.6.refs_3_), channel_id=1, source_target_pairs={{0,8},{8,16},{16,24},{24,32},{32,40},{40,48},{48,56},{56,0},{1,9},... | collective-permute-start | bytes 393224 | tf_op jit(solution)/shard_map/ppermute | solution.py:226
  20.9 7.2 %collective-permute-start.9 = (bf16[4,128,128]{2,1,0:T(8,128)(2,1)S(1)}, bf16[4,128,128]{2,1,0:T(8,128)(2,1)S(1)}, u32[]{:S(2)}, u32[]{:S(2)}) collective-permute-start(bf16[4,128,128]{2,1,0:T(8,128)(2,1)S(1)} %collective-permute-done.7.refs_4_), channel_id=1, source_target_pairs={{0,56},{8,0},{16,8},{24,16},{32,24},{40,32},{48,40},{56,48},{1,57}... | collective-permute-start | bytes 393224 | tf_op jit(solution)/shard_map/ppermute | solution.py:227
  20.9 7.8 %collective-permute-start.3 = (bf16[4,128,128]{2,1,0:T(8,128)(2,1)S(1)}, bf16[4,128,128]{2,1,0:T(8,128)(2,1)S(1)}, u32[]{:S(2)}, u32[]{:S(2)}) collective-permute-start(bf16[4,128,128]{2,1,0:T(8,128)(2,1)S(1)} %pack.1), channel_id=1, source_target_pairs={{0,0},{1,4},{2,2},{3,6},{4,1},{5,5},{6,3},{7,7},{8,8},{9,12},{10,1... | collective-permute-start | bytes 393224 | tf_op jit(solution)/shard_map/ppermute | solution.py:219
  25.1 4.4 %collective-permute-start.10 = (bf16[2,128,128]{2,1,0:T(8,128)(2,1)S(1)}, bf16[2,128,128]{2,1,0:T(8,128)(2,1)S(1)}, u32[]{:S(2)}, u32[]{:S(2)}) collective-permute-start(bf16[2,128,128]{2,1,0:T(8,128)(2,1)S(1)} %slice.16), channel_id=1, source_target_pairs={{0,8},{8,16},{16,24},{24,32},{32,40},{40,48},{48,56},{56,0},{1,9},... | collective-permute-start | bytes 196616 | tf_op jit(solution)/shard_map/ppermute | solution.py:229
  28.2 4.4 %collective-permute-start.11 = (bf16[2,128,128]{2,1,0:T(8,128)(2,1)S(1)}, bf16[2,128,128]{2,1,0:T(8,128)(2,1)S(1)}, u32[]{:S(2)}, u32[]{:S(2)}) collective-permute-start(bf16[2,128,128]{2,1,0:T(8,128)(2,1)S(1)} %slice.17), channel_id=1, source_target_pairs={{0,56},{8,0},{16,8},{24,16},{32,24},{40,32},{48,40},{56,48},{1,57}... | collective-permute-start | bytes 196616 | tf_op jit(solution)/shard_map/ppermute | solution.py:230
  32.7 23.9 %collective-permute-start.12 = (bf16[32,128,128]{2,1,0:T(8,128)(2,1)S(1)}, bf16[32,128,128]{2,1,0:T(8,128)(2,1)S(1)}, u32[]{:S(2)}, u32[]{:S(2)}) collective-permute-start(bf16[32,128,128]{2,1,0:T(8,128)(2,1)S(1)} %join.1.refs_4_), channel_id=1, source_target_pairs={{0,64},{64,128},{128,192},{192,0},{1,65},{65,129},{129,193},{193,1... | collective-permute-start | bytes 3145736 | tf_op jit(solution)/shard_map/ppermute | solution.py:240
  33.7 24.6 %collective-permute-start.14 = (bf16[32,128,128]{2,1,0:T(8,128)(2,1)S(1)}, bf16[32,128,128]{2,1,0:T(8,128)(2,1)}, u32[]{:S(2)}, u32[]{:S(2)}) collective-permute-start(bf16[32,128,128]{2,1,0:T(8,128)(2,1)S(1)} %join.1.refs_4_), channel_id=1, source_target_pairs={{0,192},{64,0},{128,64},{192,128},{1,193},{65,1},{129,65},{193,129... | collective-permute-start | bytes 3145736 | tf_op jit(solution)/shard_map/ppermute | solution.py:241
  40.4 134.9 %collective-permute-start.19 = (bf16[768,1536]{1,0:T(8,128)(2,1)}, bf16[768,1536]{1,0:T(8,128)(2,1)}, u32[]{:S(2)}, u32[]{:S(2)}) collective-permute-start(bf16[768,1536]{1,0:T(8,128)(2,1)} %get-tuple-element.18), channel_id=1, source_target_pairs={{0,2},{1,3},{2,4},{3,5},{4,6},{5,7},{6,0},{7,1},{8,10},{9,11},{10,... | collective-permute-start | bytes 7077896 | tf_op jit(solution)/shard_map/ppermute | solution.py:252
  42.7 54.6 %collective-permute-start.1 = (bf16[256,768]{1,0:T(8,128)(2,1)S(1)}, bf16[256,768]{1,0:T(8,128)(2,1)S(1)}, u32[]{:S(2)}, u32[]{:S(2)}) collective-permute-start(bf16[256,768]{1,0:T(8,128)(2,1)S(1)} %copy-done.3), channel_id=1, source_target_pairs={{0,0},{1,4},{2,2},{3,6},{4,1},{5,5},{6,3},{7,7},{8,8},{9,12},{10,1... | collective-permute-start | bytes 1179656 | tf_op jit(solution)/shard_map/ppermute | solution.py:223
  57.4 92.3 %collective-permute-start.13 = (bf16[16,128,128]{2,1,0:T(8,128)(2,1)}, bf16[16,128,128]{2,1,0:T(8,128)(2,1)S(1)}, u32[]{:S(2)}, u32[]{:S(2)}) collective-permute-start(bf16[16,128,128]{2,1,0:T(8,128)(2,1)} %slice.18), channel_id=1, source_target_pairs={{0,64},{64,128},{128,192},{192,0},{1,65},{65,129},{129,193},{193,1... | collective-permute-start | bytes 1572872 | tf_op jit(solution)/shard_map/ppermute | solution.py:243
  60.2 89.5 %collective-permute-start.15 = (bf16[16,128,128]{2,1,0:T(8,128)(2,1)}, bf16[16,128,128]{2,1,0:T(8,128)(2,1)}, u32[]{:S(2)}, u32[]{:S(2)}) collective-permute-start(bf16[16,128,128]{2,1,0:T(8,128)(2,1)} %slice.19), channel_id=1, source_target_pairs={{0,192},{64,0},{128,64},{192,128},{1,193},{65,1},{129,65},{193,129... | collective-permute-start | bytes 1572872 | tf_op jit(solution)/shard_map/ppermute | solution.py:244
  97.3 5.1 %collective-permute-start.2 = (bf16[256,768]{1,0:T(8,128)(2,1)S(1)}, bf16[256,768]{1,0:T(8,128)(2,1)S(1)}, u32[]{:S(2)}, u32[]{:S(2)}) collective-permute-start(bf16[256,768]{1,0:T(8,128)(2,1)S(1)} %collective-permute-done.1.refs_2_), channel_id=1, source_target_pairs={{0,1},{1,0},{2,3},{3,2},{4,5},{5,4},{6,7},{7,6},{8,9},{9,8},{10,11... | collective-permute-start | bytes 1179656 | tf_op jit(solution)/shard_map/ppermute | solution.py:232
  97.3 5.1 %collective-permute-start = (s32[2,128]{1,0:T(2,128)S(1)}, s32[2,128]{1,0:T(2,128)S(1)}, u32[]{:S(2)}, u32[]{:S(2)}) collective-permute-start(s32[2,128]{1,0:T(2,128)S(1)} %copy-done.2), channel_id=1, source_target_pairs={{0,4},{4,0},{1,5},{5,1},{2,6},{6,2},{3,7},{7,3},{8,12},{12,8},{9,1... | collective-permute-start | bytes 3080 | tf_op jit(solution)/shard_map/ppermute | solution.py:224
  102.4 78.4 %collective-permute-start.23 = (bf16[768,1536]{1,0:T(8,128)(2,1)}, bf16[768,1536]{1,0:T(8,128)(2,1)}, u32[]{:S(2)}, u32[]{:S(2)}) collective-permute-start(bf16[768,1536]{1,0:T(8,128)(2,1)} %get-tuple-element.19), channel_id=1, source_target_pairs={{0,7},{1,6},{2,1},{3,0},{4,3},{5,2},{6,5},{7,4},{8,15},{9,14},{10,... | collective-permute-start | bytes 7077896 | tf_op jit(solution)/shard_map/ppermute | solution.py:255
  102.4 80.8 %collective-permute-start.21 = (bf16[768,1536]{1,0:T(8,128)(2,1)}, bf16[768,1536]{1,0:T(8,128)(2,1)}, u32[]{:S(2)}, u32[]{:S(2)}) collective-permute-start(bf16[768,1536]{1,0:T(8,128)(2,1)} %get-tuple-element.17), channel_id=1, source_target_pairs={{0,1},{1,0},{2,3},{3,2},{4,5},{5,4},{6,7},{7,6},{8,9},{9,8},{10,11... | collective-permute-start | bytes 7077896 | tf_op jit(solution)/shard_map/ppermute | solution.py:251
  160.0 2.6 %collective-permute-start.16 = (f32[2,152,768]{2,1,0:T(8,128)S(1)}, f32[2,152,768]{2,1,0:T(8,128)S(1)}, u32[]{:S(2)}, u32[]{:S(2)}) collective-permute-start(f32[2,152,768]{2,1,0:T(8,128)S(1)} %get-tuple-element.16), channel_id=1, source_target_pairs={{0,1},{1,0},{2,3},{3,2},{4,5},{5,4},{6,7},{7,6},{8,9},{9,8},{10,11... | collective-permute-start | bytes 2801672 | tf_op jit(solution)/shard_map/ppermute | solution.py:266
  162.8 12.5 %collective-permute-start.18 = (bf16[256,768]{1,0:T(8,128)(2,1)S(1)}, bf16[256,768]{1,0:T(8,128)(2,1)S(1)}, u32[]{:S(2)}, u32[]{:S(2)}) collective-permute-start(bf16[256,768]{1,0:T(8,128)(2,1)S(1)} %merge.1), channel_id=1, source_target_pairs={{0,2},{1,6},{2,0},{3,4},{4,3},{5,7},{6,1},{7,5},{8,10},{9,14},{10,... | collective-permute-start | bytes 1179656 | tf_op jit(solution)/shard_map/ppermute | solution.py:271
  166.3 11.4 %collective-permute-start.17 = (bf16[256,768]{1,0:T(8,128)(2,1)S(1)}, bf16[256,768]{1,0:T(8,128)(2,1)S(1)}, u32[]{:S(2)}, u32[]{:S(2)}) collective-permute-start(bf16[256,768]{1,0:T(8,128)(2,1)S(1)} %merge.1), channel_id=1, source_target_pairs={{0,0},{1,4},{2,2},{3,6},{4,1},{5,5},{6,3},{7,7},{8,8},{9,12},{10,1... | collective-permute-start | bytes 1179656 | tf_op jit(solution)/shard_map/ppermute | solution.py:270
  175.2 5.5 %collective-permute-start.22 = (bf16[256,768]{1,0:T(8,128)(2,1)S(1)}, bf16[256,768]{1,0:T(8,128)(2,1)S(1)}, u32[]{:S(2)}, u32[]{:S(2)}) collective-permute-start(bf16[256,768]{1,0:T(8,128)(2,1)S(1)} %collective-permute-done.18), channel_id=1, source_target_pairs={{0,1},{1,0},{2,3},{3,2},{4,5},{5,4},{6,7},{7,6},{8,9},{9,8},{10,11... | collective-permute-start | bytes 1179656 | tf_op jit(solution)/shard_map/ppermute | solution.py:274
  177.7 5.6 %collective-permute-start.20 = (bf16[256,768]{1,0:T(8,128)(2,1)S(1)}, bf16[256,768]{1,0:T(8,128)(2,1)S(1)}, u32[]{:S(2)}, u32[]{:S(2)}) collective-permute-start(bf16[256,768]{1,0:T(8,128)(2,1)S(1)} %collective-permute-done.17), channel_id=1, source_target_pairs={{0,1},{1,0},{2,3},{3,2},{4,5},{5,4},{6,7},{7,6},{8,9},{9,8},{10,11... | collective-permute-start | bytes 1179656 | tf_op jit(solution)/shard_map/ppermute | solution.py:273
  (4 other events, 73.2 us)

commit v2 on v1

v2 whole, which is shorter than its diff:
```python
import math

import jax
import jax.numpy as jnp
from jax import lax
from jax.experimental import pallas as pl
from jax.experimental.pallas import tpu as pltpu
from jax.sharding import Mesh, PartitionSpec as P

HD = 128
TILE = 128
NX, NZ = 4, 8
HEADS = 6
WIDE = HEADS * TILE
SUM_ROW = HD
MAX_ROW = HD + 16
ROWS = HD + 24
NEGATIVE = -1e30
BLOCK = 4
EXP2_SCALE = math.log2(math.e) / math.sqrt(HD)
Z_ORDER = (0, -1, 1, -2, 2, -3, 3, 4)


def vmem():
    return pl.BlockSpec(memory_space=pltpu.VMEM)


def smem():
    return pl.BlockSpec(memory_space=pltpu.SMEM)


def call(kernel, out_shape, args, in_specs, scratch=(), aliases=None, name=None, flops=0):
    return pl.pallas_call(
        kernel,
        out_shape=out_shape,
        in_specs=in_specs,
        out_specs=jax.tree.map(lambda s: vmem(), out_shape),
        scratch_shapes=list(scratch),
        input_output_aliases=aliases or {},
        compiler_params=pltpu.CompilerParams(vmem_limit_bytes=48 * 1024 * 1024),
        cost_estimate=pl.CostEstimate(flops=flops, transcendentals=0, bytes_accessed=0),
        name=name,
    )(*args)


def pack_kernel(key_ref, value_ref, out_ref):
    for t in range(2):
        rows = pl.ds(t * TILE, TILE)
        out_ref[t] = key_ref[rows, :]
        out_ref[2 + t] = value_ref[rows, :].astype(jnp.float32).T.astype(jnp.bfloat16)


def join_kernel(*refs):
    out_ref = refs[-1]
    at = 0
    for ref in refs[:-1]:
        out_ref[pl.ds(at, ref.shape[0])] = ref[...]
        at += ref.shape[0]


def join(parts):
    total = sum(p.shape[0] for p in parts)
    shape = jax.ShapeDtypeStruct((total, *parts[0].shape[1:]), parts[0].dtype)
    return call(join_kernel, shape, parts, [vmem()] * len(parts), name="join")


def stage_kernel(columns, count, numbers, first, table_ref, mine_ref, theirs_ref, *refs):
    parts, refs = refs[:count], refs[count:]
    targets = sorted({number // 2 for number in numbers})
    if not first:
        refs = refs[len(targets) :]
    states, (tiles_ref, query_ref, list_ref) = refs[: len(targets)], refs[len(targets) :]
    x, z, core = table_ref[4, 0], table_ref[4, 1], table_ref[4, 2]
    at = 0
    for part in parts:
        tiles_ref[pl.ds(at, part.shape[0])] = part[...]
        at += part.shape[0]
    for number in numbers:
        source = mine_ref if number < 2 else theirs_ref
        rows = pl.ds(number % 2 * TILE, TILE)
        for h in range(HEADS):
            query_ref[number, pl.ds(h * TILE, TILE), :] = source[rows, pl.ds(h * HD, HD)]
    if first:
        for ref in states:
            ref[:, :MAX_ROW, :] = jnp.zeros((2, MAX_ROW, WIDE), jnp.float32)
            ref[:, MAX_ROW:, :] = jnp.full((2, ROWS - MAX_ROW, WIDE), NEGATIVE, jnp.float32)

    counts = [jnp.int32(0)] * 4
    slot = 0
    for dx, order in columns:
        for dz in order:
            block = lax.rem(x + dx + NX, NX) * NZ + lax.rem(z + dz + NZ, NZ)
            for r in range(2):
                tile = (block * 2 + core) * 2 + r
                for number in numbers:
                    list_ref[number, counts[number]] = slot // 2 * 4 + slot % 2
                    counts[number] = counts[number] + table_ref[number, tile]
                slot += 1

    for number in numbers:
        state_ref = states[targets.index(number // 2)]
        row = number % 2
        total = counts[number]

        def one_block(turn, carry, number=number, state_ref=state_ref, row=row, total=total):
            base = turn * BLOCK
            first_at = list_ref[number, base]
            at, values = [first_at], []
            ones = jnp.ones((16, TILE), jnp.bfloat16)
            for j in range(BLOCK):
                if j:
                    live = base + j < total
                    at.append(jnp.where(live, list_ref[number, base + j], first_at))
                value = jnp.concatenate([tiles_ref[at[j] + 2], ones], axis=0)
                if j:
                    value = value * jnp.where(live, 1.0, 0.0).astype(jnp.bfloat16)
                values.append(value)
            values = jnp.concatenate(values, axis=1)
            keys = jnp.concatenate([tiles_ref[i] for i in at], axis=0)
            chunks = [pl.ds(c * TILE, TILE) for c in range(HEADS)]
            scores = [
                lax.dot_general(
                    keys,
                    query_ref[number, lanes, :],
                    (((1,), (1,)), ((), ())),
                    preferred_element_type=jnp.float32,
                )
                for lanes in chunks
            ]
            probs = []
            for lanes, score in zip(chunks, scores):
                old_max = state_ref[row, pl.ds(MAX_ROW, 1), lanes]
                new_max = jnp.maximum(old_max, jnp.max(score, axis=0, keepdims=True))
                prob = jnp.exp2((score - new_max) * EXP2_SCALE).astype(jnp.bfloat16)
                probs.append((prob, jnp.exp2((old_max - new_max) * EXP2_SCALE)))
                state_ref[row, pl.ds(MAX_ROW, 8), lanes] = jnp.broadcast_to(new_max, (8, TILE))
            for lanes, (prob, fade) in zip(chunks, probs):
                part = lax.dot_general(
                    values, prob, (((1,), (0,)), ((), ())), preferred_element_type=jnp.float32
                )
                state_ref[row, pl.ds(0, MAX_ROW), lanes] = (
                    state_ref[row, pl.ds(0, MAX_ROW), lanes] * fade + part
                )
            return carry

        lax.fori_loop(0, (total + BLOCK - 1) // BLOCK, one_block, 0)


def stage(columns, near, parts, state, numbers, name):
    shape = jax.ShapeDtypeStruct((2, ROWS, WIDE), jnp.float32)
    slots = sum(2 * len(order) for _, order in columns)
    args = [*near, *parts]
    outs = len({number // 2 for number in numbers})
    aliases = {}
    if state is not None:
        aliases = {len(args) + i: i for i in range(outs)}
        args += list(state)
    kernel = lambda *refs: stage_kernel(columns, len(parts), numbers, state is None, *refs)
    return call(
        kernel,
        (shape,) * outs,
        args,
        [smem()] + [vmem()] * (len(args) - 1),
        scratch=(
            pltpu.VMEM((2 * slots, TILE, TILE), jnp.bfloat16),
            pltpu.VMEM((4, WIDE, HD), jnp.bfloat16),
            pltpu.SMEM((4, slots + BLOCK), jnp.int32),
        ),
        aliases=aliases,
        name=name,
    )


def merge_kernel(own_ref, other_ref, out_ref):
    for t in range(2):
        own_max = own_ref[t, pl.ds(MAX_ROW, 1), :]
        other_max = other_ref[t, pl.ds(MAX_ROW, 1), :]
        row_max = jnp.maximum(own_max, other_max)
        own_weight = jnp.exp2((own_max - row_max) * EXP2_SCALE)
        other_weight = jnp.exp2((other_max - row_max) * EXP2_SCALE)
        total = (
            own_ref[t, pl.ds(SUM_ROW, 1), :] * own_weight
            + other_ref[t, pl.ds(SUM_ROW, 1), :] * other_weight
        )
        own_weight = own_weight / total
        other_weight = other_weight / total
        for h in range(HEADS):
            lanes = slice(h * TILE, (h + 1) * TILE)
            attended = (
                own_ref[t, pl.ds(0, HD), lanes] * own_weight[:, lanes]
                + other_ref[t, pl.ds(0, HD), lanes] * other_weight[:, lanes]
            )
            out_ref[pl.ds(t * TILE, TILE), pl.ds(h * HD, HD)] = attended.T.astype(jnp.bfloat16)


def ring(size, step):
    return [(i, (i + step) % size) for i in range(size)]


def along_y(move):
    pairs = []
    for i in range(8):
        yh, yl, core = move(i // 4, i // 2 % 2, i % 2)
        pairs.append((i, yh % 2 * 4 + yl % 2 * 2 + core % 2))
    return pairs


def next_y(yh, yl, step):
    y = (yh * 2 + yl + step) % 4
    return y // 2, y % 2


Y = ("yh", "yl", "core")
YZ = ("z", "yh", "yl", "core")


def turned(shift):
    turn = along_y(lambda yh, yl, core: (core, yl, yh))
    return [(z * 8 + a, (z + shift) % NZ * 8 + b) for z in range(NZ) for a, b in turn]


def project_kernel(count, *refs):
    out_ref = refs[-1]
    before = refs[-2] if count < len(refs) - 1 else None
    pairs, at = [], 0
    while at < count:
        left, depth, used = refs[at], refs[at].shape[1], 0
        at += 1
        while used < depth:
            pairs.append((left, used, refs[at]))
            used += refs[at].shape[0]
            at += 1
    for n in range(out_ref.shape[1] // 256):
        lanes = pl.ds(n * 256, 256)
        total = None if before is None else before[:, lanes]
        for left, used, right in pairs:
            part = jnp.dot(
                left[:, pl.ds(used, right.shape[0])],
                right[:, lanes],
                preferred_element_type=jnp.float32,
            )
            total = part if total is None else total + part
        out_ref[:, lanes] = total.astype(out_ref.dtype)


def project(args, before, dtype, name):
    count = len(args)
    shape = jax.ShapeDtypeStruct((args[0].shape[0], args[1].shape[1]), dtype)
    args = args + ([] if before is None else [before])
    kernel = lambda *refs: project_kernel(count, *refs)
    return call(kernel, shape, args, [vmem()] * len(args), name=name, flops=args[0].size * args[1].shape[1] * 4)


def per_device(queries, key_rows, value_rows, tile_mask, out_weight):
    x, z = lax.axis_index("x"), lax.axis_index("z")
    yh, yl, core = lax.axis_index("yh"), lax.axis_index("yl"), lax.axis_index("core")
    turn = along_y(lambda yh, yl, core: (core, yl, yh))
    swap = [(0, 1), (1, 0)]
    together = lax.optimization_barrier

    block = out_weight.shape[1] // 4
    depth = out_weight.shape[0]

    def columns_of(source, yl, core, start=0, rows=depth):
        return lax.dynamic_slice(source, (jnp.int32(start), (yl * 2 + core) * block), (rows, block))

    unit_shape = jax.ShapeDtypeStruct((4, TILE, TILE), jnp.bfloat16)
    unit = call(pack_kernel, unit_shape, (key_rows, value_rows), [vmem()] * 2, name="pack")
    up, down = ring(NZ, 1), ring(NZ, -1)
    units = {0: lax.ppermute(unit, YZ, turned(0))}
    units[-1] = lax.ppermute(unit, YZ, turned(1))
    units[1] = lax.ppermute(unit, YZ, turned(-1))
    queries, tile_mask, _ = together((queries, tile_mask, units[-1]))
    mine = lax.ppermute(queries, Y, turn)
    other_mask = lax.ppermute(tile_mask, "yh", swap)
    units[-2] = lax.ppermute(units[-1], "z", up)
    units[2] = lax.ppermute(units[1], "z", down)
    weight_own = columns_of(out_weight, yl, core)
    weight_core = lax.ppermute(columns_of(out_weight, yl, 1 - core), "core", swap)
    units[-2], units[2], weight_core = together((units[-2], units[2], weight_core))
    units[-3] = lax.ppermute(units[-2], "z", up)
    units[3] = lax.ppermute(units[2], "z", down)
    units[-3], units[3], mine, other_mask = together((units[-3], units[3], mine, other_mask))
    far = [
        lax.ppermute(units[-3][:2], "z", up),
        lax.ppermute(units[3][2:], "z", down),
    ]
    theirs = lax.ppermute(mine, "core", swap)
    *far, theirs = together((*far, theirs))
    same = yh == core
    place = jnp.pad(jnp.stack([x, z, core]).astype(jnp.int32), (0, 125))[None]
    table = jnp.concatenate(
        [
            jnp.where(same, tile_mask, other_mask),
            jnp.where(same, other_mask, tile_mask),
            place,
            jnp.zeros((3, 128), jnp.int32),
        ]
    )

    same_core = along_y(lambda yh, yl, core: (*next_y(yh, yl, 1 - 2 * core), core))
    other_core = along_y(lambda yh, yl, core: (*next_y(yh, yl, 1 - 2 * core), 1 - core))
    source, _ = together((out_weight, mine))
    weight_far = lax.ppermute(columns_of(source, 1 - yl, core), Y, same_core)

    def send_half(number, after):
        source, _ = together((out_weight, after))
        piece = columns_of(source, 1 - yl, 1 - core, number * depth // 2, depth // 2)
        return lax.ppermute(piece, Y, other_core)

    low = join([units[d] for d in Z_ORDER[:4]])
    high = join([units[d] for d in Z_ORDER[4:7]] + far)
    forth, back = ring(NX, 1), ring(NX, -1)
    before_low = lax.ppermute(low, "x", forth)
    after_high = lax.ppermute(high, "x", back)
    before_high = lax.ppermute(high, "x", forth)
    after_low = lax.ppermute(low, "x", back)

    near = (table, mine, theirs)
    every = (0, 1, 2, 3)
    state = stage(((0, Z_ORDER),), near, [low, high], None, every, "stage_a")
    before_low, after_high, weight_far, *state = together(
        (before_low, after_high, weight_far, *state)
    )
    weight_cross = [send_half(0, weight_far)]
    far_low = lax.ppermute(before_low, "x", forth)
    far_high = lax.ppermute(after_high, "x", back)
    before_high, after_low, weight_cross[0] = together((before_high, after_low, weight_cross[0]))
    weight_cross.append(send_half(1, weight_cross[0]))
    low_order, high_order = Z_ORDER[:4], Z_ORDER[4:]
    keep, send = stage(
        ((-1, low_order), (1, high_order), (-1, high_order), (1, low_order)),
        near,
        [before_low, after_high, before_high, after_low],
        state,
        every,
        "stage_b",
    )
    far_low, far_high, keep, send = together((far_low, far_high, keep, send))
    last = (((2, Z_ORDER),), near, [far_low, far_high])
    (send,) = stage(*last, (send,), (2, 3), "stage_c")
    received = lax.ppermute(send, "core", swap)
    (keep,) = stage(*last, (keep,), (0, 1), "stage_d")
    keep, received, weight_cross[1] = together((keep, received, weight_cross[1]))
    shape = jax.ShapeDtypeStruct((2 * TILE, WIDE), jnp.bfloat16)
    attended = call(merge_kernel, shape, (keep, received), [vmem()] * 2, name="merge")

    near_part = lax.ppermute(attended, Y, turn)
    far_part = lax.ppermute(attended, Y, along_y(lambda yh, yl, core: (core, 1 - yl, yh)))
    near_other = lax.ppermute(near_part, "core", swap)
    far_other = lax.ppermute(far_part, "core", swap)
    half = project([near_part, weight_own, far_part, weight_far], None, jnp.float32, "project_a")
    return project(
        [near_other, weight_core, far_other, *weight_cross], half, jnp.bfloat16, "project_b"
    )


def solution(mesh):
    fine = Mesh(mesh.devices.reshape(NX, NZ, 2, 2, 2), ("x", "z", "yh", "yl", "core"))
    tok, head = ("x", "z", "yh"), ("yl", "core")
    return jax.shard_map(
        per_device,
        mesh=fine,
        in_specs=(P(tok, head), P(tok, head), P(tok, head), P(tok, None), P(head, None)),
        out_specs=P(tok, head),
        check_vma=False,
    )
```

time: 187 us -> 150 us (0.80)
  the two profiles are of different devices: /device:TPU:101 before, /device:TPU:1 now
where the time goes in v2:
time: 150 us; the launch traced here: 149 us
  waiting for transfers between devices  61.1 us (41%)
  starting transfers between devices  45.8 us (31%)
  Pallas kernels  28.5 us (19%)
  local copies, waits for them, and re-layouts  12.9 us (9%)
    pallas_call x10, Pallas kernels, call(): pl.pallas_call(kernel, out_shape=out_shape, in_specs=in_specs, out_specs=...  28.5 us
    ppermute x1, waiting for transfers between devices, per_device(): units = {0: lax.ppermute(unit, YZ, turned(0))}  24.5 us
    ppermute x1, waiting for transfers between devices, per_device(): after_low = lax.ppermute(low, 'x', back)  9.09 us
    ppermute x1, waiting for transfers between devices, per_device(): near_part = lax.ppermute(attended, Y, turn)  8.8 us
    dynamic_slice x4, local copies, waits for them, and re-layouts, columns_of(): lax.dynamic_slice(source, (jnp.int32(start), (yl * 2 + core) * block), (r...  8.66 us
    ppermute x1, starting transfers between devices, per_device(): near_part = lax.ppermute(attended, Y, turn)  8.36 us
    ppermute x1, starting transfers between devices, per_device(): units = {0: lax.ppermute(unit, YZ, turned(0))}  5.64 us
    unnamed x20, local copies, waits for them, and re-layouts  4.17 us
  transfers between devices with their start and end apart: 27, of which 11 were waited for; matrix products, arithmetic and copies ran while one was open for 1% of the time, Pallas kernels for 16%

profile of v2, /device:TPU:1, one launch (start us, length us, event | category | flops | bytes accessed | tf_op | source)
XLA Modules:
  0.0 148.8 jit_solution(17294833351522638068)
XLA Ops:
  0.0 2.7 %constant_dynamic-slice_fusion = (bf16[768,1536]{1,0:T(8,128)(2,1)S(1)}, bf16[768,1536]{1,0:T(8,128)(2,1)S(1)}) fusion(bf16[768,6144]{1,0:T(8,128)(2,1)} %param.9, s32[]{:T(128)S(6)} %select_n.31, s32[]{:T(128)S(6)} %select_n.26), kind=kLoop, calls=%fused_computation.1 | loop fusion | bytes 9437192 | tf_op jit(solution)/shard_map/dynamic_slice | solution.py:265
  2.7 3.3 %collective-permute-start.4 = (bf16[768,1536]{1,0:T(8,128)(2,1)S(1)}, bf16[768,1536]{1,0:T(8,128)(2,1)S(1)}, u32[]{:S(2)}, u32[]{:S(2)}) collective-permute-start(bf16[768,1536]{1,0:T(8,128)(2,1)S(1)} %get-tuple-element.74), channel_id=1, source_target_pairs={{0,1},{1,0},{2,3},{3,2},{4,5},{5,4},{6,7},{7,6},{8,9},{9,8},{10,11... | collective-permute-start | bytes 7077896 | tf_op jit(solution)/shard_map/ppermute | solution.py:279
  6.2 2.5 %collective-permute-start = (bf16[4,128,128]{2,1,0:T(8,128)(2,1)S(1)}, bf16[4,128,128]{2,1,0:T(8,128)(2,1)S(1)}, u32[]{:S(2)}, u32[]{:S(2)}) collective-permute-start(bf16[4,128,128]{2,1,0:T(8,128)(2,1)S(1)} %pack.1), channel_id=1, source_target_pairs={{0,8},{1,12},{2,10},{3,14},{4,9},{5,13},{6,11},{7,15},{8,16},{9,20... | collective-permute-start | bytes 393224 | tf_op jit(solution)/shard_map/ppermute | solution.py:271
  8.7 4.0 %collective-permute-start.2 = (bf16[4,128,128]{2,1,0:T(8,128)(2,1)S(1)}, bf16[4,128,128]{2,1,0:T(8,128)(2,1)S(1)}, u32[]{:S(2)}, u32[]{:S(2)}) collective-permute-start(bf16[4,128,128]{2,1,0:T(8,128)(2,1)S(1)} %pack.1), channel_id=1, source_target_pairs={{0,56},{1,60},{2,58},{3,62},{4,57},{5,61},{6,59},{7,63},{8,0},{9,4... | collective-permute-start | bytes 393224 | tf_op jit(solution)/shard_map/ppermute | solution.py:272
  12.7 4.1 %collective-permute-done.refs_1_ = bf16[4,128,128]{2,1,0:T(8,128)(2,1)S(1)} collective-permute-done((bf16[4,128,128]{2,1,0:T(8,128)(2,1)S(1)}, bf16[4,128,128]{2,1,0:T(8,128)(2,1)S(1)}, u32[]{:S(2)}, u32[]{:S(2)}) %collective-permute-start) | collective-permute-done | bytes 131104 | tf_op jit(solution)/shard_map/ppermute | solution.py:271
  19.2 2.8 %collective-permute-start.3 = (bf16[4,128,128]{2,1,0:T(8,128)(2,1)S(1)}, bf16[4,128,128]{2,1,0:T(8,128)(2,1)S(1)}, u32[]{:S(2)}, u32[]{:S(2)}) collective-permute-start(bf16[4,128,128]{2,1,0:T(8,128)(2,1)S(1)} %collective-permute-done.2.refs_2_), channel_id=1, source_target_pairs={{0,56},{8,0},{16,8},{24,16},{32,24},{40,32},{48,40},{56,48},{1,57}... | collective-permute-start | bytes 393224 | tf_op jit(solution)/shard_map/ppermute | solution.py:277
  25.7 2.7 %collective-permute-start.6 = (bf16[4,128,128]{2,1,0:T(8,128)(2,1)S(1)}, bf16[4,128,128]{2,1,0:T(8,128)(2,1)S(1)}, u32[]{:S(2)}, u32[]{:S(2)}) collective-permute-start(bf16[4,128,128]{2,1,0:T(8,128)(2,1)S(1)} %collective-permute-done.3.refs_0_), channel_id=1, source_target_pairs={{0,56},{8,0},{16,8},{24,16},{32,24},{40,32},{48,40},{56,48},{1,57}... | collective-permute-start | bytes 393224 | tf_op jit(solution)/shard_map/ppermute | solution.py:282
  28.4 3.9 %collective-permute-done.8 = s32[2,128]{1,0:T(2,128)S(1)} collective-permute-done((s32[2,128]{1,0:T(2,128)S(1)}, s32[2,128]{1,0:T(2,128)S(1)}, u32[]{:S(2)}, u32[]{:S(2)}) %collective-permute-start.8) | collective-permute-done | bytes 1056 | tf_op jit(solution)/shard_map/ppermute | solution.py:275
  32.6 3.2 %constant_dynamic-slice_fusion.2 = bf16[768,1536]{1,0:T(8,128)(2,1)} fusion(bf16[768,6144]{1,0:T(8,128)(2,1)} %param.9, s32[]{:T(128)S(6)} %select_n.29), kind=kLoop, calls=%fused_computation.3 | loop fusion | bytes 4718596 | tf_op jit(solution)/shard_map/dynamic_slice | solution.py:265
  36.4 2.6 %collective-permute-start.11 = (bf16[256,768]{1,0:T(8,128)(2,1)S(1)}, bf16[256,768]{1,0:T(8,128)(2,1)S(1)}, u32[]{:S(2)}, u32[]{:S(2)}) collective-permute-start(bf16[256,768]{1,0:T(8,128)(2,1)S(1)} %collective-permute-done.7.refs_1_), channel_id=1, source_target_pairs={{0,1},{1,0},{2,3},{3,2},{4,5},{5,4},{6,7},{7,6},{8,9},{9,8},{10,11... | collective-permute-start | bytes 1179656 | tf_op jit(solution)/shard_map/ppermute | solution.py:288
  39.0 5.6 %collective-permute-start.12 = (bf16[4,128,128]{2,1,0:T(8,128)(2,1)S(1)}, bf16[4,128,128]{2,1,0:T(8,128)(2,1)}, u32[]{:S(2)}, u32[]{:S(2)}) collective-permute-start(bf16[4,128,128]{2,1,0:T(8,128)(2,1)S(1)} %pack.1), channel_id=1, source_target_pairs={{0,0},{1,4},{2,2},{3,6},{4,1},{5,5},{6,3},{7,7},{8,8},{9,12},{10,1... | collective-permute-start | bytes 393224 | tf_op jit(solution)/shard_map/ppermute | solution.py:270
  46.5 24.5 %collective-permute-done.12.refs_0_ = bf16[4,128,128]{2,1,0:T(8,128)(2,1)} collective-permute-done((bf16[4,128,128]{2,1,0:T(8,128)(2,1)S(1)}, bf16[4,128,128]{2,1,0:T(8,128)(2,1)}, u32[]{:S(2)}, u32[]{:S(2)}) %collective-permute-start.12) | collective-permute-done | bytes 131104 | tf_op jit(solution)/shard_map/ppermute | solution.py:270
  77.7 6.3 %stage_a.1 = (f32[2,152,768]{2,1,0:T(8,128)S(1)}, f32[2,152,768]{2,1,0:T(8,128)S(1)}) custom-call(s32[8,128]{1,0:T(8,128)S(1)} %add_add_fusion.refs_0_, bf16[256,768]{1,0:T(8,128)(2,1)S(1)} %collective-permute-done.7.refs_1_, bf16[256,768]{1,0:T(8,128)(2,1)S(1)} %collective-permute-done.11.refs_2_, bf16[16,128,128]{2,1,0:T(8,128)(2,1)S(1)} %join.2.refs_3_, ...), custom_call_target="tpu_custom_call" | custom-call | tf_op jit(solution)/shard_map/stage_a/pallas_call | solution.py:33
  85.6 2.8 %collective-permute-start.19 = (bf16[16,128,128]{2,1,0:T(8,128)(2,1)S(1)}, bf16[16,128,128]{2,1,0:T(8,128)(2,1)S(1)}, u32[]{:S(2)}, u32[]{:S(2)}) collective-permute-start(bf16[16,128,128]{2,1,0:T(8,128)(2,1)S(1)} %join.2.refs_3_), channel_id=1, source_target_pairs={{0,192},{64,0},{128,64},{192,128},{1,193},{65,1},{129,65},{193,129... | collective-permute-start | bytes 1572872 | tf_op jit(solution)/shard_map/ppermute | solution.py:317
  88.4 2.7 %collective-permute-start.17 = (bf16[16,128,128]{2,1,0:T(8,128)(2,1)S(1)}, bf16[16,128,128]{2,1,0:T(8,128)(2,1)S(1)}, u32[]{:S(2)}, u32[]{:S(2)}) collective-permute-start(bf16[16,128,128]{2,1,0:T(8,128)(2,1)S(1)} %collective-permute-done.14.refs_4_), channel_id=1, source_target_pairs={{0,192},{64,0},{128,64},{192,128},{1,193},{65,1},{129,65},{193,129... | collective-permute-start | bytes 1572872 | tf_op jit(solution)/shard_map/ppermute | solution.py:327
  91.1 9.1 %collective-permute-done.19.refs_6_ = bf16[16,128,128]{2,1,0:T(8,128)(2,1)S(1)} collective-permute-done((bf16[16,128,128]{2,1,0:T(8,128)(2,1)S(1)}, bf16[16,128,128]{2,1,0:T(8,128)(2,1)S(1)}, u32[]{:S(2)}, u32[]{:S(2)}) %collective-permute-start.19) | collective-permute-done | bytes 524320 | tf_op jit(solution)/shard_map/ppermute | solution.py:317
  100.2 3.4 %collective-permute-done.18.refs_5_ = bf16[16,128,128]{2,1,0:T(8,128)(2,1)S(1)} collective-permute-done((bf16[16,128,128]{2,1,0:T(8,128)(2,1)S(1)}, bf16[16,128,128]{2,1,0:T(8,128)(2,1)S(1)}, u32[]{:S(2)}, u32[]{:S(2)}) %collective-permute-start.18) | collective-permute-done | bytes 524320 | tf_op jit(solution)/shard_map/ppermute | solution.py:316
  105.6 7.7 %stage_b.1 = (f32[2,152,768]{2,1,0:T(8,128)S(1)}, f32[2,152,768]{2,1,0:T(8,128)S(1)}) custom-call(s32[8,128]{1,0:T(8,128)S(1)} %add_add_fusion.refs_0_, bf16[256,768]{1,0:T(8,128)(2,1)S(1)} %collective-permute-done.7.refs_1_, bf16[256,768]{1,0:T(8,128)(2,1)S(1)} %collective-permute-done.11.refs_2_, ...), custom_call_target="tpu_custom_call", output_to_operand_aliasing={{0}: (7, {}), {1}: (8, {})} | custom-call | tf_op jit(solution)/shard_map/stage_b/pallas_call | solution.py:33
  113.3 3.0 %stage_c.1 = f32[2,152,768]{2,1,0:T(8,128)S(1)} custom-call(s32[8,128]{1,0:T(8,128)S(1)} %add_add_fusion.refs_0_, bf16[256,768]{1,0:T(8,128)(2,1)S(1)} %collective-permute-done.7.refs_1_, bf16[256,768]{1,0:T(8,128)(2,1)S(1)} %collective-permute-done.11.refs_2_, ...), custom_call_target="tpu_custom_call", output_to_operand_aliasing={{}: (5, {})} | custom-call | tf_op jit(solution)/shard_map/stage_c/pallas_call | solution.py:33
  116.6 3.0 %stage_d.1.own_ref = f32[2,152,768]{2,1,0:T(8,128)S(1)} custom-call(s32[8,128]{1,0:T(8,128)S(1)} %add_add_fusion.refs_0_, bf16[256,768]{1,0:T(8,128)(2,1)S(1)} %collective-permute-done.7.refs_1_, bf16[256,768]{1,0:T(8,128)(2,1)S(1)} %collective-permute-done.11.refs_2_, ...), custom_call_target="tpu_custom_call", output_to_operand_aliasing={{}: (5, {})} | custom-call | tf_op jit(solution)/shard_map/stage_d/pallas_call | solution.py:33
  122.1 8.4 %collective-permute-start.23 = (bf16[256,768]{1,0:T(8,128)(2,1)S(1)}, bf16[256,768]{1,0:T(8,128)(2,1)S(1)}, u32[]{:S(2)}, u32[]{:S(2)}) collective-permute-start(bf16[256,768]{1,0:T(8,128)(2,1)S(1)} %merge.1), channel_id=1, source_target_pairs={{0,0},{1,4},{2,2},{3,6},{4,1},{5,5},{6,3},{7,7},{8,8},{9,12},{10,1... | collective-permute-start | bytes 1179656 | tf_op jit(solution)/shard_map/ppermute | solution.py:348
  130.6 8.8 %collective-permute-done.23.refs_0_ = bf16[256,768]{1,0:T(8,128)(2,1)S(1)} collective-permute-done((bf16[256,768]{1,0:T(8,128)(2,1)S(1)}, bf16[256,768]{1,0:T(8,128)(2,1)S(1)}, u32[]{:S(2)}, u32[]{:S(2)}) %collective-permute-start.23) | collective-permute-done | bytes 393248 | tf_op jit(solution)/shard_map/ppermute | solution.py:348
  141.6 3.0 %project_a.1.refs_5_ = f32[256,1536]{1,0:T(8,128)S(1)} custom-call(bf16[256,768]{1,0:T(8,128)(2,1)S(1)} %collective-permute-done.23.refs_0_, bf16[768,1536]{1,0:T(8,128)(2,1)S(1)} %get-tuple-element.73.refs_1_, bf16[256,768]{1,0:T(8,128)(2,1)S(1)} %collective-permute-done.25.refs_2_, bf16[768,1536]{1,0:T(8,128)(2,1)} %collective-permute-done.15.refs_3_), custom_call_target="tpu_custom_call" | custom-call | flops 1207959552 | tf_op jit(solution)/shard_map/project_a/pallas_call | solution.py:33
  144.7 4.1 %project_b.1 = bf16[256,1536]{1,0:T(8,128)(2,1)} custom-call(bf16[256,768]{1,0:T(8,128)(2,1)S(1)} %collective-permute-done.24.refs_0_, bf16[768,1536]{1,0:T(8,128)(2,1)} %copy-done.8, bf16[256,768]{1,0:T(8,128)(2,1)S(1)} %collective-permute-done.26.refs_2_, bf16[384,1536]{1,0:T(8,128)(2,1)S(1)} %collective-permute-done.20.refs_3_, ...), custom_call_target="tpu_custom_call" | custom-call | flops 1207959552 | tf_op jit(solution)/shard_map/project_b/pallas_call | solution.py:33
  (72 shorter events, 24.3 us)
Async XLA Ops:
  2.7 21.5 %collective-permute-start.4 = (bf16[768,1536]{1,0:T(8,128)(2,1)S(1)}, bf16[768,1536]{1,0:T(8,128)(2,1)S(1)}, u32[]{:S(2)}, u32[]{:S(2)}) collective-permute-start(bf16[768,1536]{1,0:T(8,128)(2,1)S(1)} %get-tuple-element.74), channel_id=1, source_target_pairs={{0,1},{1,0},{2,3},{3,2},{4,5},{5,4},{6,7},{7,6},{8,9},{9,8},{10,11... | collective-permute-start | bytes 7077896 | tf_op jit(solution)/shard_map/ppermute | solution.py:279
  6.2 10.6 %collective-permute-start = (bf16[4,128,128]{2,1,0:T(8,128)(2,1)S(1)}, bf16[4,128,128]{2,1,0:T(8,128)(2,1)S(1)}, u32[]{:S(2)}, u32[]{:S(2)}) collective-permute-start(bf16[4,128,128]{2,1,0:T(8,128)(2,1)S(1)} %pack.1), channel_id=1, source_target_pairs={{0,8},{1,12},{2,10},{3,14},{4,9},{5,13},{6,11},{7,15},{8,16},{9,20... | collective-permute-start | bytes 393224 | tf_op jit(solution)/shard_map/ppermute | solution.py:271
  8.7 10.4 %collective-permute-start.2 = (bf16[4,128,128]{2,1,0:T(8,128)(2,1)S(1)}, bf16[4,128,128]{2,1,0:T(8,128)(2,1)S(1)}, u32[]{:S(2)}, u32[]{:S(2)}) collective-permute-start(bf16[4,128,128]{2,1,0:T(8,128)(2,1)S(1)} %pack.1), channel_id=1, source_target_pairs={{0,56},{1,60},{2,58},{3,62},{4,57},{5,61},{6,59},{7,63},{8,0},{9,4... | collective-permute-start | bytes 393224 | tf_op jit(solution)/shard_map/ppermute | solution.py:272
  16.8 15.5 %collective-permute-start.7 = (bf16[256,768]{1,0:T(8,128)(2,1)}, bf16[256,768]{1,0:T(8,128)(2,1)S(1)}, u32[]{:S(2)}, u32[]{:S(2)}) collective-permute-start(bf16[256,768]{1,0:T(8,128)(2,1)} %param.5), channel_id=1, source_target_pairs={{0,0},{1,4},{2,2},{3,6},{4,1},{5,5},{6,3},{7,7},{8,8},{9,12},{10,1... | collective-permute-start | bytes 1179656 | tf_op jit(solution)/shard_map/ppermute | solution.py:274
  19.0 5.2 %collective-permute-start.1 = (bf16[4,128,128]{2,1,0:T(8,128)(2,1)S(1)}, bf16[4,128,128]{2,1,0:T(8,128)(2,1)}, u32[]{:S(2)}, u32[]{:S(2)}) collective-permute-start(bf16[4,128,128]{2,1,0:T(8,128)(2,1)S(1)} %collective-permute-done.refs_1_), channel_id=1, source_target_pairs={{0,8},{8,16},{16,24},{24,32},{32,40},{40,48},{48,56},{56,0},{1,9},... | collective-permute-start | bytes 393224 | tf_op jit(solution)/shard_map/ppermute | solution.py:276
  19.2 5.1 %collective-permute-start.3 = (bf16[4,128,128]{2,1,0:T(8,128)(2,1)S(1)}, bf16[4,128,128]{2,1,0:T(8,128)(2,1)S(1)}, u32[]{:S(2)}, u32[]{:S(2)}) collective-permute-start(bf16[4,128,128]{2,1,0:T(8,128)(2,1)S(1)} %collective-permute-done.2.refs_2_), channel_id=1, source_target_pairs={{0,56},{8,0},{16,8},{24,16},{32,24},{40,32},{48,40},{56,48},{1,57}... | collective-permute-start | bytes 393224 | tf_op jit(solution)/shard_map/ppermute | solution.py:277
  25.7 6.6 %collective-permute-start.5 = (bf16[4,128,128]{2,1,0:T(8,128)(2,1)}, bf16[4,128,128]{2,1,0:T(8,128)(2,1)S(1)}, u32[]{:S(2)}, u32[]{:S(2)}) collective-permute-start(bf16[4,128,128]{2,1,0:T(8,128)(2,1)} %collective-permute-done.1.refs_3_), channel_id=1, source_target_pairs={{0,8},{8,16},{16,24},{24,32},{32,40},{40,48},{48,56},{56,0},{1,9},... | collective-permute-start | bytes 393224 | tf_op jit(solution)/shard_map/ppermute | solution.py:281
  25.7 6.9 %collective-permute-start.6 = (bf16[4,128,128]{2,1,0:T(8,128)(2,1)S(1)}, bf16[4,128,128]{2,1,0:T(8,128)(2,1)S(1)}, u32[]{:S(2)}, u32[]{:S(2)}) collective-permute-start(bf16[4,128,128]{2,1,0:T(8,128)(2,1)S(1)} %collective-permute-done.3.refs_0_), channel_id=1, source_target_pairs={{0,56},{8,0},{16,8},{24,16},{32,24},{40,32},{48,40},{56,48},{1,57}... | collective-permute-start | bytes 393224 | tf_op jit(solution)/shard_map/ppermute | solution.py:282
  35.9 48.2 %collective-permute-start.15 = (bf16[768,1536]{1,0:T(8,128)(2,1)}, bf16[768,1536]{1,0:T(8,128)(2,1)}, u32[]{:S(2)}, u32[]{:S(2)}) collective-permute-start(bf16[768,1536]{1,0:T(8,128)(2,1)} %constant_dynamic-slice_fusion.2), channel_id=1, source_target_pairs={{0,2},{1,7},{2,4},{3,1},{4,6},{5,3},{6,0},{7,5},{8,10},{9,15},{10,... | collective-permute-start | bytes 7077896 | tf_op jit(solution)/shard_map/ppermute | solution.py:304
  36.4 38.7 %collective-permute-start.11 = (bf16[256,768]{1,0:T(8,128)(2,1)S(1)}, bf16[256,768]{1,0:T(8,128)(2,1)S(1)}, u32[]{:S(2)}, u32[]{:S(2)}) collective-permute-start(bf16[256,768]{1,0:T(8,128)(2,1)S(1)} %collective-permute-done.7.refs_1_), channel_id=1, source_target_pairs={{0,1},{1,0},{2,3},{3,2},{4,5},{5,4},{6,7},{7,6},{8,9},{9,8},{10,11... | collective-permute-start | bytes 1179656 | tf_op jit(solution)/shard_map/ppermute | solution.py:288
  39.0 32.0 %collective-permute-start.12 = (bf16[4,128,128]{2,1,0:T(8,128)(2,1)S(1)}, bf16[4,128,128]{2,1,0:T(8,128)(2,1)}, u32[]{:S(2)}, u32[]{:S(2)}) collective-permute-start(bf16[4,128,128]{2,1,0:T(8,128)(2,1)S(1)} %pack.1), channel_id=1, source_target_pairs={{0,0},{1,4},{2,2},{3,6},{4,1},{5,5},{6,3},{7,7},{8,8},{9,12},{10,1... | collective-permute-start | bytes 393224 | tf_op jit(solution)/shard_map/ppermute | solution.py:270
  44.7 30.3 %collective-permute-start.10 = (bf16[2,128,128]{2,1,0:T(8,128)(2,1)S(1)}, bf16[2,128,128]{2,1,0:T(8,128)(2,1)S(1)}, u32[]{:S(2)}, u32[]{:S(2)}) collective-permute-start(bf16[2,128,128]{2,1,0:T(8,128)(2,1)S(1)} %slice.7), channel_id=1, source_target_pairs={{0,56},{8,0},{16,8},{24,16},{32,24},{40,32},{48,40},{56,48},{1,57}... | collective-permute-start | bytes 196616 | tf_op jit(solution)/shard_map/ppermute | solution.py:286
  46.4 28.7 %collective-permute-start.9 = (bf16[2,128,128]{2,1,0:T(8,128)(2,1)S(1)}, bf16[2,128,128]{2,1,0:T(8,128)(2,1)S(1)}, u32[]{:S(2)}, u32[]{:S(2)}) collective-permute-start(bf16[2,128,128]{2,1,0:T(8,128)(2,1)S(1)} %slice.6), channel_id=1, source_target_pairs={{0,8},{8,16},{16,24},{24,32},{32,40},{40,48},{48,56},{56,0},{1,9},... | collective-permute-start | bytes 196616 | tf_op jit(solution)/shard_map/ppermute | solution.py:285
  73.8 10.2 %collective-permute-start.13 = (bf16[16,128,128]{2,1,0:T(8,128)(2,1)S(1)}, bf16[16,128,128]{2,1,0:T(8,128)(2,1)S(1)}, u32[]{:S(2)}, u32[]{:S(2)}) collective-permute-start(bf16[16,128,128]{2,1,0:T(8,128)(2,1)S(1)} %join.2.refs_3_), channel_id=1, source_target_pairs={{0,64},{64,128},{128,192},{192,0},{1,65},{65,129},{129,193},{193,1... | collective-permute-start | bytes 1572872 | tf_op jit(solution)/shard_map/ppermute | solution.py:314
  76.0 8.1 %collective-permute-start.14 = (bf16[16,128,128]{2,1,0:T(8,128)(2,1)S(1)}, bf16[16,128,128]{2,1,0:T(8,128)(2,1)S(1)}, u32[]{:S(2)}, u32[]{:S(2)}) collective-permute-start(bf16[16,128,128]{2,1,0:T(8,128)(2,1)S(1)} %join.3.refs_4_), channel_id=1, source_target_pairs={{0,192},{64,0},{128,64},{192,128},{1,193},{65,1},{129,65},{193,129... | collective-permute-start | bytes 1572872 | tf_op jit(solution)/shard_map/ppermute | solution.py:315
  85.5 18.1 %collective-permute-start.20 = (bf16[384,1536]{1,0:T(8,128)(2,1)S(1)}, bf16[384,1536]{1,0:T(8,128)(2,1)S(1)}, u32[]{:S(2)}, u32[]{:S(2)}) collective-permute-start(bf16[384,1536]{1,0:T(8,128)(2,1)S(1)} %constant_dynamic-slice_fusion.1), channel_id=1, source_target_pairs={{0,3},{1,6},{2,5},{3,0},{4,7},{5,2},{6,1},{7,4},{8,11},{9,14},{10,... | collective-permute-start | bytes 3538952 | tf_op jit(solution)/shard_map/ppermute | solution.py:309
  85.6 14.6 %collective-permute-start.19 = (bf16[16,128,128]{2,1,0:T(8,128)(2,1)S(1)}, bf16[16,128,128]{2,1,0:T(8,128)(2,1)S(1)}, u32[]{:S(2)}, u32[]{:S(2)}) collective-permute-start(bf16[16,128,128]{2,1,0:T(8,128)(2,1)S(1)} %join.2.refs_3_), channel_id=1, source_target_pairs={{0,192},{64,0},{128,64},{192,128},{1,193},{65,1},{129,65},{193,129... | collective-permute-start | bytes 1572872 | tf_op jit(solution)/shard_map/ppermute | solution.py:317
  88.3 15.2 %collective-permute-start.18 = (bf16[16,128,128]{2,1,0:T(8,128)(2,1)S(1)}, bf16[16,128,128]{2,1,0:T(8,128)(2,1)S(1)}, u32[]{:S(2)}, u32[]{:S(2)}) collective-permute-start(bf16[16,128,128]{2,1,0:T(8,128)(2,1)S(1)} %join.3.refs_4_), channel_id=1, source_target_pairs={{0,64},{64,128},{128,192},{192,0},{1,65},{65,129},{129,193},{193,1... | collective-permute-start | bytes 1572872 | tf_op jit(solution)/shard_map/ppermute | solution.py:316
  88.4 24.9 %collective-permute-start.16 = (bf16[16,128,128]{2,1,0:T(8,128)(2,1)S(1)}, bf16[16,128,128]{2,1,0:T(8,128)(2,1)S(1)}, u32[]{:S(2)}, u32[]{:S(2)}) collective-permute-start(bf16[16,128,128]{2,1,0:T(8,128)(2,1)S(1)} %collective-permute-done.13.refs_3_), channel_id=1, source_target_pairs={{0,64},{64,128},{128,192},{192,0},{1,65},{65,129},{129,193},{193,1... | collective-permute-start | bytes 1572872 | tf_op jit(solution)/shard_map/ppermute | solution.py:326
  88.4 24.9 %collective-permute-start.17 = (bf16[16,128,128]{2,1,0:T(8,128)(2,1)S(1)}, bf16[16,128,128]{2,1,0:T(8,128)(2,1)S(1)}, u32[]{:S(2)}, u32[]{:S(2)}) collective-permute-start(bf16[16,128,128]{2,1,0:T(8,128)(2,1)S(1)} %collective-permute-done.14.refs_4_), channel_id=1, source_target_pairs={{0,192},{64,0},{128,64},{192,128},{1,193},{65,1},{129,65},{193,129... | collective-permute-start | bytes 1572872 | tf_op jit(solution)/shard_map/ppermute | solution.py:327
  104.9 16.9 %collective-permute-start.22 = (bf16[384,1536]{1,0:T(8,128)(2,1)S(1)}, bf16[384,1536]{1,0:T(8,128)(2,1)S(1)}, u32[]{:S(2)}, u32[]{:S(2)}) collective-permute-start(bf16[384,1536]{1,0:T(8,128)(2,1)S(1)} %constant_dynamic-slice_fusion.4), channel_id=1, source_target_pairs={{0,3},{1,6},{2,5},{3,0},{4,7},{5,2},{6,1},{7,4},{8,11},{9,14},{10,... | collective-permute-start | bytes 3538952 | tf_op jit(solution)/shard_map/ppermute | solution.py:309
  122.1 17.3 %collective-permute-start.23 = (bf16[256,768]{1,0:T(8,128)(2,1)S(1)}, bf16[256,768]{1,0:T(8,128)(2,1)S(1)}, u32[]{:S(2)}, u32[]{:S(2)}) collective-permute-start(bf16[256,768]{1,0:T(8,128)(2,1)S(1)} %merge.1), channel_id=1, source_target_pairs={{0,0},{1,4},{2,2},{3,6},{4,1},{5,5},{6,3},{7,7},{8,8},{9,12},{10,1... | collective-permute-start | bytes 1179656 | tf_op jit(solution)/shard_map/ppermute | solution.py:348
  130.5 11.2 %collective-permute-start.25 = (bf16[256,768]{1,0:T(8,128)(2,1)S(1)}, bf16[256,768]{1,0:T(8,128)(2,1)S(1)}, u32[]{:S(2)}, u32[]{:S(2)}) collective-permute-start(bf16[256,768]{1,0:T(8,128)(2,1)S(1)} %merge.1), channel_id=1, source_target_pairs={{0,2},{1,6},{2,0},{3,4},{4,3},{5,7},{6,1},{7,5},{8,10},{9,14},{10,... | collective-permute-start | bytes 1179656 | tf_op jit(solution)/shard_map/ppermute | solution.py:349
  139.4 5.3 %collective-permute-start.24 = (bf16[256,768]{1,0:T(8,128)(2,1)S(1)}, bf16[256,768]{1,0:T(8,128)(2,1)S(1)}, u32[]{:S(2)}, u32[]{:S(2)}) collective-permute-start(bf16[256,768]{1,0:T(8,128)(2,1)S(1)} %collective-permute-done.23.refs_0_), channel_id=1, source_target_pairs={{0,1},{1,0},{2,3},{3,2},{4,5},{5,4},{6,7},{7,6},{8,9},{9,8},{10,11... | collective-permute-start | bytes 1179656 | tf_op jit(solution)/shard_map/ppermute | solution.py:350
  (13 other events, 102.4 us)

commit v3 on v2

v3 whole, which is shorter than its diff:
```python
import math

import jax
import jax.numpy as jnp
from jax import lax
from jax.experimental import pallas as pl
from jax.experimental.pallas import tpu as pltpu
from jax.sharding import Mesh, PartitionSpec as P

HD = 128
TILE = 128
NX, NZ = 4, 8
HEADS = 6
WIDE = HEADS * TILE
SUM_ROW = HD
MAX_ROW = HD + 16
ROWS = HD + 24
NEGATIVE = -1e30
BLOCK = 4
MASK_AT = 2 * HEADS
UNIT_AT = MASK_AT + 1
EXP2_SCALE = math.log2(math.e) / math.sqrt(HD)
Z_ORDER = (0, -1, 1, -2, 2, -3, 3, 4)


def vmem():
    return pl.BlockSpec(memory_space=pltpu.VMEM)


def smem():
    return pl.BlockSpec(memory_space=pltpu.SMEM)


def hbm():
    return pl.BlockSpec(memory_space=pl.ANY)


def call(kernel, out_shape, args, in_specs, scratch=(), aliases=None, name=None, flops=0):
    return pl.pallas_call(
        kernel,
        out_shape=out_shape,
        in_specs=in_specs,
        out_specs=jax.tree.map(lambda s: vmem(), out_shape),
        scratch_shapes=list(scratch),
        input_output_aliases=aliases or {},
        compiler_params=pltpu.CompilerParams(vmem_limit_bytes=24 * 1024 * 1024),
        cost_estimate=pl.CostEstimate(flops=flops, transcendentals=0, bytes_accessed=0),
        name=name,
    )(*args)


def pack_kernel(key_hbm, value_hbm, out_ref, key_ref, value_ref, sems):
    copies = [
        pltpu.make_async_copy(key_hbm, key_ref, sems.at[0]),
        pltpu.make_async_copy(value_hbm, value_ref, sems.at[1]),
    ]
    for copy in copies:
        copy.start()
    for copy in copies:
        copy.wait()
    for t in range(2):
        rows = pl.ds(t * TILE, TILE)
        out_ref[t] = key_ref[rows, :]
        out_ref[2 + t] = value_ref[rows, :].astype(jnp.float32).T.astype(jnp.bfloat16)


def pack(key_rows, value_rows):
    rows = pltpu.VMEM((2 * TILE, HD), jnp.bfloat16)
    return call(
        pack_kernel,
        jax.ShapeDtypeStruct((4, TILE, TILE), jnp.bfloat16),
        (key_rows, value_rows),
        [hbm()] * 2,
        scratch=(rows, rows, pltpu.SemaphoreType.DMA((2,))),
        name="pack",
    )


def bundle_kernel(query_ref, mask_ref, unit_ref, out_ref):
    for t in range(2):
        for h in range(HEADS):
            out_ref[t * HEADS + h] = query_ref[pl.ds(t * TILE, TILE), pl.ds(h * HD, HD)]
    out_ref[MASK_AT] = jnp.zeros((TILE, TILE), jnp.bfloat16)
    out_ref[MASK_AT, 0:2, :] = mask_ref[...].astype(jnp.float32).astype(jnp.bfloat16)
    out_ref[UNIT_AT:] = unit_ref[...]


def bundle(queries, tile_mask, unit):
    shape = jax.ShapeDtypeStruct((UNIT_AT + 4, TILE, TILE), jnp.bfloat16)
    return call(bundle_kernel, shape, (queries, tile_mask, unit), [vmem()] * 3, name="bundle")


def half_kernel(half_ref, source_ref, out_ref, sems):
    rows = out_ref.shape[0] // 8
    start = pl.multiple_of(half_ref[0] * out_ref.shape[1], out_ref.shape[1])
    copies = [
        pltpu.make_async_copy(
            source_ref.at[pl.ds(i * rows, rows), pl.ds(start, out_ref.shape[1])],
            out_ref.at[pl.ds(i * rows, rows), :],
            sems.at[i],
        )
        for i in range(8)
    ]
    for copy in copies:
        copy.start()
    for copy in copies:
        copy.wait()


def column_half(source, number):
    return pl.pallas_call(
        half_kernel,
        out_shape=jax.ShapeDtypeStruct((source.shape[0], source.shape[1] // 2), source.dtype),
        in_specs=[smem(), hbm()],
        out_specs=hbm(),
        scratch_shapes=[pltpu.SemaphoreType.DMA((8,))],
        name="column_half",
    )(number.reshape(1).astype(jnp.int32), source)


def join_kernel(*refs):
    out_ref = refs[-1]
    at = 0
    for ref in refs[:-1]:
        out_ref[pl.ds(at, ref.shape[0])] = ref[...]
        at += ref.shape[0]


def join(parts):
    total = sum(p.shape[0] for p in parts)
    shape = jax.ShapeDtypeStruct((total, *parts[0].shape[1:]), parts[0].dtype)
    return call(join_kernel, shape, parts, [vmem()] * len(parts), name="join")


def stage_kernel(columns, count, numbers, first, table_ref, mine_ref, theirs_ref, *refs):
    parts, refs = refs[:count], refs[count:]
    targets = sorted({number // 2 for number in numbers})
    if not first:
        refs = refs[len(targets) :]
    states, (tiles_ref, list_ref) = refs[: len(targets)], refs[len(targets) :]
    x, z, core = table_ref[4, 0], table_ref[4, 1], table_ref[4, 2]
    at = 0
    for part in parts:
        tiles_ref[pl.ds(at, part.shape[0])] = part[...]
        at += part.shape[0]
    if first:
        for ref in states:
            ref[:, :MAX_ROW, :] = jnp.zeros((2, MAX_ROW, WIDE), jnp.float32)
            ref[:, MAX_ROW:, :] = jnp.full((2, ROWS - MAX_ROW, WIDE), NEGATIVE, jnp.float32)

    counts = [jnp.int32(0)] * 4
    slot = 0
    for dx, order in columns:
        for dz in order:
            block = lax.rem(x + dx + NX, NX) * NZ + lax.rem(z + dz + NZ, NZ)
            for r in range(2):
                tile = (block * 2 + core) * 2 + r
                for number in numbers:
                    list_ref[number, counts[number]] = slot // 2 * 4 + slot % 2
                    counts[number] = counts[number] + table_ref[number, tile]
                slot += 1

    for number in numbers:
        state_ref = states[targets.index(number // 2)]
        total = counts[number]
        source = mine_ref if number < 2 else theirs_ref

        def one_block(turn, carry, number=number, state_ref=state_ref, total=total, source=source):
            row = number % 2
            base = turn * BLOCK
            first_at = list_ref[number, base]
            at, values = [first_at], []
            ones = jnp.ones((16, TILE), jnp.bfloat16)
            for j in range(BLOCK):
                if j:
                    live = base + j < total
                    at.append(jnp.where(live, list_ref[number, base + j], first_at))
                value = jnp.concatenate([tiles_ref[at[j] + 2], ones], axis=0)
                if j:
                    value = value * jnp.where(live, 1.0, 0.0).astype(jnp.bfloat16)
                values.append(value)
            values = jnp.concatenate(values, axis=1)
            keys = jnp.concatenate([tiles_ref[i] for i in at], axis=0)
            chunks = [pl.ds(c * TILE, TILE) for c in range(HEADS)]
            scores = [
                lax.dot_general(
                    keys,
                    source[row * HEADS + h],
                    (((1,), (1,)), ((), ())),
                    preferred_element_type=jnp.float32,
                )
                for h in range(HEADS)
            ]
            probs = []
            for lanes, score in zip(chunks, scores):
                old_max = state_ref[row, pl.ds(MAX_ROW, 1), lanes]
                new_max = jnp.maximum(old_max, jnp.max(score, axis=0, keepdims=True))
                prob = jnp.exp2((score - new_max) * EXP2_SCALE).astype(jnp.bfloat16)
                probs.append((prob, jnp.exp2((old_max - new_max) * EXP2_SCALE)))
                state_ref[row, pl.ds(MAX_ROW, 8), lanes] = jnp.broadcast_to(new_max, (8, TILE))
            for lanes, (prob, fade) in zip(chunks, probs):
                part = lax.dot_general(
                    values, prob, (((1,), (0,)), ((), ())), preferred_element_type=jnp.float32
                )
                state_ref[row, pl.ds(0, MAX_ROW), lanes] = (
                    state_ref[row, pl.ds(0, MAX_ROW), lanes] * fade + part
                )
            return carry

        lax.fori_loop(0, (total + BLOCK - 1) // BLOCK, one_block, 0)


def stage(columns, near, parts, state, numbers, name):
    shape = jax.ShapeDtypeStruct((2, ROWS, WIDE), jnp.float32)
    slots = sum(2 * len(order) for _, order in columns)
    args = [*near, *parts]
    outs = len({number // 2 for number in numbers})
    aliases = {}
    if state is not None:
        aliases = {len(args) + i: i for i in range(outs)}
        args += list(state)
    kernel = lambda *refs: stage_kernel(columns, len(parts), numbers, state is None, *refs)
    return call(
        kernel,
        (shape,) * outs,
        args,
        [smem()] + [vmem()] * (len(args) - 1),
        scratch=(
            pltpu.VMEM((2 * slots, TILE, TILE), jnp.bfloat16),
            pltpu.SMEM((4, slots + BLOCK), jnp.int32),
        ),
        aliases=aliases,
        name=name,
    )


def merge_kernel(own_ref, other_ref, out_ref):
    for t in range(2):
        own_max = own_ref[t, pl.ds(MAX_ROW, 1), :]
        other_max = other_ref[t, pl.ds(MAX_ROW, 1), :]
        row_max = jnp.maximum(own_max, other_max)
        own_weight = jnp.exp2((own_max - row_max) * EXP2_SCALE)
        other_weight = jnp.exp2((other_max - row_max) * EXP2_SCALE)
        total = (
            own_ref[t, pl.ds(SUM_ROW, 1), :] * own_weight
            + other_ref[t, pl.ds(SUM_ROW, 1), :] * other_weight
        )
        own_weight = own_weight / total
        other_weight = other_weight / total
        for h in range(HEADS):
            lanes = slice(h * TILE, (h + 1) * TILE)
            attended = (
                own_ref[t, pl.ds(0, HD), lanes] * own_weight[:, lanes]
                + other_ref[t, pl.ds(0, HD), lanes] * other_weight[:, lanes]
            )
            out_ref[pl.ds(t * TILE, TILE), pl.ds(h * HD, HD)] = attended.T.astype(jnp.bfloat16)


def ring(size, step):
    return [(i, (i + step) % size) for i in range(size)]


def along_y(move):
    pairs = []
    for i in range(8):
        yh, yl, core = move(i // 4, i // 2 % 2, i % 2)
        pairs.append((i, yh % 2 * 4 + yl % 2 * 2 + core % 2))
    return pairs


def next_y(yh, yl, step):
    y = (yh * 2 + yl + step) % 4
    return y // 2, y % 2


Y = ("yh", "yl", "core")
YZ = ("z", "yh", "yl", "core")


def turned(shift):
    turn = along_y(lambda yh, yl, core: (core, yl, yh))
    return [(z * 8 + a, (z + shift) % NZ * 8 + b) for z in range(NZ) for a, b in turn]


def project_kernel(flip, place_ref, near_ref, far_ref, weight_ref, far_weight_ref, out_ref, own_ref, sems):
    width = out_ref.shape[1]
    parts = width // 256
    which = place_ref[1] + flip - 2 * flip * place_ref[1]
    base = pl.multiple_of(place_ref[0] * (2 * width) + which * width, 256)
    copies = [
        pltpu.make_async_copy(
            weight_ref.at[:, pl.ds(base + n * 256, 256)], own_ref.at[n], sems.at[n]
        )
        for n in range(parts)
    ]
    for copy in copies:
        copy.start()
    for n in range(parts):
        at = pl.multiple_of(which * width + n * 256, 256)
        total = jnp.dot(
            far_ref[...], far_weight_ref[:, pl.ds(at, 256)], preferred_element_type=jnp.float32
        )
        copies[n].wait()
        total = total + jnp.dot(near_ref[...], own_ref[n], preferred_element_type=jnp.float32)
        out_ref[:, n * 256 : (n + 1) * 256] = total.astype(out_ref.dtype)


def project(flip, place, near, far, weight, far_weight, dtype, name):
    width = far_weight.shape[1] // 2
    shape = jax.ShapeDtypeStruct((near.shape[0], width), dtype)
    return call(
        lambda *refs: project_kernel(flip, *refs),
        shape,
        (place, near, far, weight, far_weight),
        [smem(), vmem(), vmem(), hbm(), vmem()],
        scratch=(
            pltpu.VMEM((width // 256, weight.shape[0], 256), jnp.bfloat16),
            pltpu.SemaphoreType.DMA((width // 256,)),
        ),
        name=name,
    )


def add_kernel(keep_ref, other_ref, out_ref):
    out_ref[...] = (keep_ref[...] + other_ref[...].astype(jnp.float32)).astype(out_ref.dtype)


def per_device(queries, key_rows, value_rows, tile_mask, out_weight):
    x, z = lax.axis_index("x"), lax.axis_index("z")
    yh, yl, core = lax.axis_index("yh"), lax.axis_index("yl"), lax.axis_index("core")
    turn = along_y(lambda yh, yl, core: (core, yl, yh))
    swap = [(0, 1), (1, 0)]
    together = lax.optimization_barrier

    unit = pack(key_rows, value_rows)
    up, down = ring(NZ, 1), ring(NZ, -1)
    units = {-1: lax.ppermute(unit, YZ, turned(1)), 1: lax.ppermute(unit, YZ, turned(-1))}
    mine = lax.ppermute(bundle(queries, tile_mask, unit), Y, turn)
    half_away = column_half(out_weight, 1 - yl)
    away = along_y(lambda yh, yl, core: (*next_y(yh, yl, 1 - 2 * core), core))
    units[-2] = lax.ppermute(units[-1], "z", up)
    units[2] = lax.ppermute(units[1], "z", down)
    units[-2], units[2], half_away = together((units[-2], units[2], half_away))
    far_weight = lax.ppermute(half_away, Y, away)
    units[-3] = lax.ppermute(units[-2], "z", up)
    units[3] = lax.ppermute(units[2], "z", down)
    units[-3], units[3], mine = together((units[-3], units[3], mine))
    far = [
        lax.ppermute(units[-3][:2], "z", up),
        lax.ppermute(units[3][2:], "z", down),
    ]
    theirs = lax.ppermute(mine, "core", swap)
    *far, theirs = together((*far, theirs))
    place = jnp.pad(jnp.stack([x, z, core]).astype(jnp.int32), (0, 125))[None]
    masks = jnp.concatenate([mine[MASK_AT, :2], theirs[MASK_AT, :2]]).astype(jnp.int32)
    table = jnp.concatenate([masks, place])

    units[0] = mine[UNIT_AT:]
    column = join([units[d] for d in Z_ORDER[:-1]] + far)
    forth, back = ring(NX, 1), ring(NX, -1)
    before = lax.ppermute(column, "x", forth)
    after = lax.ppermute(column, "x", back)
    near = (table, mine, theirs)
    every = (0, 1, 2, 3)
    state = stage(((0, Z_ORDER),), near, [column], None, every, "stage_a")
    before, after, *state = together((before, after, *state))
    half = column.shape[0] // 2
    far_low = lax.ppermute(before[:half], "x", forth)
    far_high = lax.ppermute(after[half:], "x", back)
    keep, send = stage(
        ((-1, Z_ORDER), (1, Z_ORDER)), near, [before, after], state, every, "stage_b"
    )
    far_low, far_high, keep, send = together((far_low, far_high, keep, send))
    last = (((2, Z_ORDER),), near, [far_low, far_high])
    (send,) = stage(*last, (send,), (2, 3), "stage_c")
    received = lax.ppermute(send, "core", swap)
    (keep,) = stage(*last, (keep,), (0, 1), "stage_d")
    keep, received, far_weight = together((keep, received, far_weight))
    shape = jax.ShapeDtypeStruct((2 * TILE, WIDE), jnp.bfloat16)
    attended = call(merge_kernel, shape, (keep, received), [vmem()] * 2, name="merge")

    near_part = lax.ppermute(attended, Y, turn)
    far_part = lax.ppermute(attended, Y, along_y(lambda yh, yl, core: (core, 1 - yl, yh)))
    where = jnp.stack([yl, core]).astype(jnp.int32)
    sides = (where, near_part, far_part, out_weight, far_weight)
    other = project(1, *sides, jnp.bfloat16, "project_send")
    other = lax.ppermute(other, "core", swap)
    own = project(0, *sides, jnp.float32, "project_keep")
    shape = jax.ShapeDtypeStruct(own.shape, jnp.bfloat16)
    return call(add_kernel, shape, (own, other), [vmem()] * 2, name="add")


def solution(mesh):
    fine = Mesh(mesh.devices.reshape(NX, NZ, 2, 2, 2), ("x", "z", "yh", "yl", "core"))
    tok, head = ("x", "z", "yh"), ("yl", "core")
    return jax.shard_map(
        per_device,
        mesh=fine,
        in_specs=(P(tok, head), P(tok, head), P(tok, head), P(tok, None), P(head, None)),
        out_specs=P(tok, head),
        check_vma=False,
    )
```

time: 150 us -> 309 us (2.06)
  Pallas kernels: 28.5 us -> 183 us
  waiting for transfers between devices: 61.1 us -> 85.6 us
  local copies, waits for them, and re-layouts: 12.9 us -> 2.86 us
  starting transfers between devices: 45.8 us -> 36.4 us
    pallas_call x0 -> x1, Pallas kernels: none -> 144 us  [column_half(): pl.pallas_call(half_kernel, out_shape=jax.ShapeDtypeStruct((source.shape[...]
    ppermute x17 -> x9, waiting for transfers between devices: 47.4 us -> 70.3 us  [the longest x1 50.2 us: per_device(): mine = lax.ppermute(bundle(queries, tile_mask, unit), Y, turn)]
    pallas_call x10 -> x11, Pallas kernels: 28.5 us -> 39.3 us  [call(): pl.pallas_call(kernel, out_shape=out_shape, in_specs=in_specs, out_specs=...]
    dynamic_slice x4 -> x0, local copies, waits for them, and re-layouts: 8.66 us -> none  [columns_of(): lax.dynamic_slice(source, (jnp.int32(start), (yl * 2 + core) * block), (r...]
    ppermute x17 -> x9, starting transfers between devices: 27.3 us -> 20.3 us  [the longest x1 9.67 us: per_device(): lax.ppermute(unit, YZ, turned(-1))]
    ppermute x1, starting transfers between devices: 8.36 us -> 2.13 us  [per_device(): near_part = lax.ppermute(attended, Y, turn)]
    ppermute x1, waiting for transfers between devices: 8.8 us -> 4.05 us  [per_device(): near_part = lax.ppermute(attended, Y, turn)]
  transfers between devices with their start and end apart: 27 -> 19, of which waited for: 11 -> 10; matrix products, arithmetic and copies ran while one was open for 1% -> 0% of each run, Pallas kernels for 16% -> 57%
where the time goes in v3:
time: 309 us
  Pallas kernels  183 us (59%)
  waiting for transfers between devices  85.6 us (28%)
  starting transfers between devices  36.4 us (12%)
    pallas_call x1, Pallas kernels, column_half(): pl.pallas_call(half_kernel, out_shape=jax.ShapeDtypeStruct((source.shape[...  144 us
    ppermute x1, waiting for transfers between devices, per_device(): mine = lax.ppermute(bundle(queries, tile_mask, unit), Y, turn)  50.2 us
    pallas_call x11, Pallas kernels, call(): pl.pallas_call(kernel, out_shape=out_shape, in_specs=in_specs, out_specs=...  39.3 us
    ppermute x1, waiting for transfers between devices, per_device(): after = lax.ppermute(column, 'x', back)  12.7 us
    ppermute x1, starting transfers between devices, per_device(): lax.ppermute(unit, YZ, turned(-1))  9.67 us
  transfers between devices with their start and end apart: 19, of which 10 were waited for; matrix products, arithmetic and copies ran while one was open for 0% of the time, Pallas kernels for 57%

profile of v3, /device:TPU:1, one launch (start us, length us, event | category | flops | bytes accessed | tf_op | source)
XLA Modules:
  0.0 308.8 jit_solution(222182887762792209)
XLA Ops:
  2.0 9.7 %collective-permute-start.2 = (bf16[4,128,128]{2,1,0:T(8,128)(2,1)S(1)}, bf16[4,128,128]{2,1,0:T(8,128)(2,1)S(1)}, u32[]{:S(2)}, u32[]{:S(2)}) collective-permute-start(bf16[4,128,128]{2,1,0:T(8,128)(2,1)S(1)} %pack.1.unit_ref), channel_id=1, source_target_pairs={{0,56},{1,60},{2,58},{3,62},{4,57},{5,61},{6,59},{7,63},{8,0},{9,4... | collective-permute-start | bytes 393224 | tf_op jit(solution)/shard_map/ppermute | solution.py:337
  13.6 3.9 %collective-permute-start.3 = (bf16[4,128,128]{2,1,0:T(8,128)(2,1)S(1)}, bf16[4,128,128]{2,1,0:T(8,128)(2,1)S(1)}, u32[]{:S(2)}, u32[]{:S(2)}) collective-permute-start(bf16[4,128,128]{2,1,0:T(8,128)(2,1)S(1)} %collective-permute-done.2.refs_2_), channel_id=1, source_target_pairs={{0,56},{8,0},{16,8},{24,16},{32,24},{40,32},{48,40},{56,48},{1,57}... | collective-permute-start | bytes 393224 | tf_op jit(solution)/shard_map/ppermute | solution.py:342
  17.5 2.1 collective-permute-done.refs_1_
  19.6 144.1 %column_half.1 = bf16[768,3072]{1,0:T(8,128)(2,1)} custom-call(s32[1]{0:T(128)} %bitcast.2.half_ref, bf16[768,6144]{1,0:T(8,128)(2,1)} %refs_3_.3), custom_call_target="tpu_custom_call" | custom-call | tf_op jit(solution)/shard_map/column_half/pallas_call | solution.py:111
  164.0 5.1 %collective-permute-start.6 = (bf16[17,128,128]{2,1,0:T(8,128)(2,1)S(1)}, bf16[17,128,128]{2,1,0:T(8,128)(2,1)S(1)}, u32[]{:S(2)}, u32[]{:S(2)}) collective-permute-start(bf16[17,128,128]{2,1,0:T(8,128)(2,1)S(1)} %bundle.1), channel_id=1, source_target_pairs={{0,0},{1,4},{2,2},{3,6},{4,1},{5,5},{6,3},{7,7},{8,8},{9,12},{10,1... | collective-permute-start | bytes 1671176 | tf_op jit(solution)/shard_map/ppermute | solution.py:338
  169.2 3.0 collective-permute-start.5
  172.2 2.7 collective-permute-done.4.refs_5_
  174.9 50.2 %collective-permute-done.6.refs_1_ = bf16[17,128,128]{2,1,0:T(8,128)(2,1)S(1)} collective-permute-done((bf16[17,128,128]{2,1,0:T(8,128)(2,1)S(1)}, bf16[17,128,128]{2,1,0:T(8,128)(2,1)S(1)}, u32[]{:S(2)}, u32[]{:S(2)}) %collective-permute-start.6) | collective-permute-done | bytes 557088 | tf_op jit(solution)/shard_map/ppermute | solution.py:338
  225.1 3.0 collective-permute-start.8
  229.5 3.0 collective-permute-done.7.refs_7_
  232.5 2.6 collective-permute-start.11
  235.2 7.6 %stage_a.1 = (f32[2,152,768]{2,1,0:T(8,128)S(1)}, f32[2,152,768]{2,1,0:T(8,128)S(1)}) custom-call(s32[5,128]{1,0:T(8,128)S(1)} %pad_add_fusion.refs_0_, bf16[17,128,128]{2,1,0:T(8,128)(2,1)S(1)} %collective-permute-done.6.refs_1_, bf16[17,128,128]{2,1,0:T(8,128)(2,1)S(1)} %collective-permute-done.9.refs_2_, bf16[32,128,128]{2,1,0:T(8,128)(2,1)S(1)} %join.1.refs_3_), custom_call_target="tpu_custom_call" | custom-call | tf_op jit(solution)/shard_map/stage_a/pallas_call | solution.py:39
  242.9 12.7 %collective-permute-done.11.refs_4_ = bf16[32,128,128]{2,1,0:T(8,128)(2,1)S(1)} collective-permute-done((bf16[32,128,128]{2,1,0:T(8,128)(2,1)S(1)}, bf16[32,128,128]{2,1,0:T(8,128)(2,1)S(1)}, u32[]{:S(2)}, u32[]{:S(2)}) %collective-permute-start.11) | collective-permute-done | bytes 1048608 | tf_op jit(solution)/shard_map/ppermute | solution.py:362
  255.6 3.2 %collective-permute-done.10.refs_3_ = bf16[32,128,128]{2,1,0:T(8,128)(2,1)} collective-permute-done((bf16[32,128,128]{2,1,0:T(8,128)(2,1)S(1)}, bf16[32,128,128]{2,1,0:T(8,128)(2,1)}, u32[]{:S(2)}, u32[]{:S(2)}) %collective-permute-start.10) | collective-permute-done | bytes 1048608 | tf_op jit(solution)/shard_map/ppermute | solution.py:361
  260.1 2.7 collective-permute-start.13
  262.7 11.1 %stage_b.1 = (f32[2,152,768]{2,1,0:T(8,128)S(1)}, f32[2,152,768]{2,1,0:T(8,128)S(1)}) custom-call(s32[5,128]{1,0:T(8,128)S(1)} %pad_add_fusion.refs_0_, bf16[17,128,128]{2,1,0:T(8,128)(2,1)S(1)} %collective-permute-done.6.refs_1_, bf16[17,128,128]{2,1,0:T(8,128)(2,1)S(1)} %collective-permute-done.9.refs_2_, ...), custom_call_target="tpu_custom_call", output_to_operand_aliasing={{0}: (5, {}), {1}: (6, {})} | custom-call | tf_op jit(solution)/shard_map/stage_b/pallas_call | solution.py:39
  273.9 3.7 %stage_c.1 = f32[2,152,768]{2,1,0:T(8,128)S(1)} custom-call(s32[5,128]{1,0:T(8,128)S(1)} %pad_add_fusion.refs_0_, bf16[17,128,128]{2,1,0:T(8,128)(2,1)S(1)} %collective-permute-done.6.refs_1_, bf16[17,128,128]{2,1,0:T(8,128)(2,1)S(1)} %collective-permute-done.9.refs_2_, ...), custom_call_target="tpu_custom_call", output_to_operand_aliasing={{}: (5, {})} | custom-call | tf_op jit(solution)/shard_map/stage_c/pallas_call | solution.py:39
  278.4 2.2 stage_d.1.own_ref
  280.9 3.1 collective-permute-start.17
  284.0 2.1 collective-permute-start.16
  286.2 4.3 %collective-permute-done.17.refs_2_ = bf16[256,768]{1,0:T(8,128)(2,1)S(1)} collective-permute-done((bf16[256,768]{1,0:T(8,128)(2,1)S(1)}, bf16[256,768]{1,0:T(8,128)(2,1)S(1)}, u32[]{:S(2)}, u32[]{:S(2)}) %collective-permute-start.17) | collective-permute-done | bytes 393248 | tf_op jit(solution)/shard_map/ppermute | solution.py:383
  290.5 4.0 %collective-permute-done.16.refs_1_ = bf16[256,768]{1,0:T(8,128)(2,1)S(1)} collective-permute-done((bf16[256,768]{1,0:T(8,128)(2,1)S(1)}, bf16[256,768]{1,0:T(8,128)(2,1)S(1)}, u32[]{:S(2)}, u32[]{:S(2)}) %collective-permute-start.16) | collective-permute-done | bytes 393248 | tf_op jit(solution)/shard_map/ppermute | solution.py:382
  294.6 6.5 %project_send.1 = bf16[256,1536]{1,0:T(8,128)(2,1)S(1)} custom-call(s32[2]{0:T(128)S(1)} %pad_add_fusion.1.refs_0_, bf16[256,768]{1,0:T(8,128)(2,1)S(1)} %collective-permute-done.16.refs_1_, bf16[256,768]{1,0:T(8,128)(2,1)S(1)} %collective-permute-done.17.refs_2_, bf16[768,6144]{1,0:T(8,128)(2,1)S(1)} %bitcast.12, ...), custom_call_target="tpu_custom_call" | custom-call | tf_op jit(solution)/shard_map/project_send/pallas_call | solution.py:39
  301.2 6.5 %project_keep.1.keep_ref = f32[256,1536]{1,0:T(8,128)S(1)} custom-call(s32[2]{0:T(128)S(1)} %pad_add_fusion.1.refs_0_, bf16[256,768]{1,0:T(8,128)(2,1)S(1)} %collective-permute-done.16.refs_1_, bf16[256,768]{1,0:T(8,128)(2,1)S(1)} %collective-permute-done.17.refs_2_, bf16[768,6144]{1,0:T(8,128)(2,1)S(1)} %bitcast.12, ...), custom_call_target="tpu_custom_call" | custom-call | tf_op jit(solution)/shard_map/project_keep/pallas_call | solution.py:39
  (53 shorter events, 9.2 us)
Async XLA Ops:
  2.0 11.6 %collective-permute-start.2 = (bf16[4,128,128]{2,1,0:T(8,128)(2,1)S(1)}, bf16[4,128,128]{2,1,0:T(8,128)(2,1)S(1)}, u32[]{:S(2)}, u32[]{:S(2)}) collective-permute-start(bf16[4,128,128]{2,1,0:T(8,128)(2,1)S(1)} %pack.1.unit_ref), channel_id=1, source_target_pairs={{0,56},{1,60},{2,58},{3,62},{4,57},{5,61},{6,59},{7,63},{8,0},{9,4... | collective-permute-start | bytes 393224 | tf_op jit(solution)/shard_map/ppermute | solution.py:337
  11.6 8.0 %collective-permute-start = (bf16[4,128,128]{2,1,0:T(8,128)(2,1)S(1)}, bf16[4,128,128]{2,1,0:T(8,128)(2,1)S(1)}, u32[]{:S(2)}, u32[]{:S(2)}) collective-permute-start(bf16[4,128,128]{2,1,0:T(8,128)(2,1)S(1)} %pack.1.unit_ref), channel_id=1, source_target_pairs={{0,8},{1,12},{2,10},{3,14},{4,9},{5,13},{6,11},{7,15},{8,16},{9,20... | collective-permute-start | bytes 393224 | tf_op jit(solution)/shard_map/ppermute | solution.py:337
  13.6 150.2 %collective-permute-start.3 = (bf16[4,128,128]{2,1,0:T(8,128)(2,1)S(1)}, bf16[4,128,128]{2,1,0:T(8,128)(2,1)S(1)}, u32[]{:S(2)}, u32[]{:S(2)}) collective-permute-start(bf16[4,128,128]{2,1,0:T(8,128)(2,1)S(1)} %collective-permute-done.2.refs_2_), channel_id=1, source_target_pairs={{0,56},{8,0},{16,8},{24,16},{32,24},{40,32},{48,40},{56,48},{1,57}... | collective-permute-start | bytes 393224 | tf_op jit(solution)/shard_map/ppermute | solution.py:342
  19.6 144.1 %collective-permute-start.1 = (bf16[4,128,128]{2,1,0:T(8,128)(2,1)S(1)}, bf16[4,128,128]{2,1,0:T(8,128)(2,1)S(1)}, u32[]{:S(2)}, u32[]{:S(2)}) collective-permute-start(bf16[4,128,128]{2,1,0:T(8,128)(2,1)S(1)} %collective-permute-done.refs_1_), channel_id=1, source_target_pairs={{0,8},{8,16},{16,24},{24,32},{32,40},{40,48},{48,56},{56,0},{1,9},... | collective-permute-start | bytes 393224 | tf_op jit(solution)/shard_map/ppermute | solution.py:341
  19.6 144.2 %copy-start = (bf16[256,768]{1,0:T(8,128)(2,1)S(1)}, bf16[256,768]{1,0:T(8,128)(2,1)}, u32[]{:S(2)}) copy-start(bf16[256,768]{1,0:T(8,128)(2,1)} %query_ref.1) | copy-start | bytes 1179652
  19.6 144.2 %copy-start.3 = (s32[2,128]{1,0:T(2,128)S(1)}, s32[2,128]{1,0:T(2,128)}, u32[]{:S(2)}) copy-start(s32[2,128]{1,0:T(2,128)} %mask_ref.1) | copy-start | bytes 3076
  163.8 116.9 %collective-permute-start.15 = (bf16[768,3072]{1,0:T(8,128)(2,1)}, bf16[768,3072]{1,0:T(8,128)(2,1)}, u32[]{:S(2)}, u32[]{:S(2)}) collective-permute-start(bf16[768,3072]{1,0:T(8,128)(2,1)} %column_half.1), channel_id=1, source_target_pairs={{0,2},{1,7},{2,4},{3,1},{4,6},{5,3},{6,0},{7,5},{8,10},{9,15},{10,... | collective-permute-start | bytes 14155784 | tf_op jit(solution)/shard_map/ppermute | solution.py:344
  164.0 61.1 %collective-permute-start.6 = (bf16[17,128,128]{2,1,0:T(8,128)(2,1)S(1)}, bf16[17,128,128]{2,1,0:T(8,128)(2,1)S(1)}, u32[]{:S(2)}, u32[]{:S(2)}) collective-permute-start(bf16[17,128,128]{2,1,0:T(8,128)(2,1)S(1)} %bundle.1), channel_id=1, source_target_pairs={{0,0},{1,4},{2,2},{3,6},{4,1},{5,5},{6,3},{7,7},{8,8},{9,12},{10,1... | collective-permute-start | bytes 1671176 | tf_op jit(solution)/shard_map/ppermute | solution.py:338
  169.1 5.8 %collective-permute-start.4 = (bf16[4,128,128]{2,1,0:T(8,128)(2,1)S(1)}, bf16[4,128,128]{2,1,0:T(8,128)(2,1)S(1)}, u32[]{:S(2)}, u32[]{:S(2)}) collective-permute-start(bf16[4,128,128]{2,1,0:T(8,128)(2,1)S(1)} %collective-permute-done.1.refs_3_), channel_id=1, source_target_pairs={{0,8},{8,16},{16,24},{24,32},{32,40},{40,48},{48,56},{56,0},{1,9},... | collective-permute-start | bytes 393224 | tf_op jit(solution)/shard_map/ppermute | solution.py:345
  169.2 5.7 %collective-permute-start.5 = (bf16[4,128,128]{2,1,0:T(8,128)(2,1)S(1)}, bf16[4,128,128]{2,1,0:T(8,128)(2,1)S(1)}, u32[]{:S(2)}, u32[]{:S(2)}) collective-permute-start(bf16[4,128,128]{2,1,0:T(8,128)(2,1)S(1)} %collective-permute-done.3.refs_4_), channel_id=1, source_target_pairs={{0,56},{8,0},{16,8},{24,16},{32,24},{40,32},{48,40},{56,48},{1,57}... | collective-permute-start | bytes 393224 | tf_op jit(solution)/shard_map/ppermute | solution.py:346
  225.1 7.4 %collective-permute-start.9 = (bf16[17,128,128]{2,1,0:T(8,128)(2,1)S(1)}, bf16[17,128,128]{2,1,0:T(8,128)(2,1)S(1)}, u32[]{:S(2)}, u32[]{:S(2)}) collective-permute-start(bf16[17,128,128]{2,1,0:T(8,128)(2,1)S(1)} %collective-permute-done.6.refs_1_), channel_id=1, source_target_pairs={{0,1},{1,0},{2,3},{3,2},{4,5},{5,4},{6,7},{7,6},{8,9},{9,8},{10,11... | collective-permute-start | bytes 1671176 | tf_op jit(solution)/shard_map/ppermute | solution.py:352
  225.1 4.3 %collective-permute-start.8 = (bf16[2,128,128]{2,1,0:T(8,128)(2,1)S(1)}, bf16[2,128,128]{2,1,0:T(8,128)(2,1)S(1)}, u32[]{:S(2)}, u32[]{:S(2)}) collective-permute-start(bf16[2,128,128]{2,1,0:T(8,128)(2,1)S(1)} %slice.23), channel_id=1, source_target_pairs={{0,56},{8,0},{16,8},{24,16},{32,24},{40,32},{48,40},{56,48},{1,57}... | collective-permute-start | bytes 196616 | tf_op jit(solution)/shard_map/ppermute | solution.py:350
  228.1 4.3 %collective-permute-start.7 = (bf16[2,128,128]{2,1,0:T(8,128)(2,1)S(1)}, bf16[2,128,128]{2,1,0:T(8,128)(2,1)S(1)}, u32[]{:S(2)}, u32[]{:S(2)}) collective-permute-start(bf16[2,128,128]{2,1,0:T(8,128)(2,1)S(1)} %slice.22), channel_id=1, source_target_pairs={{0,8},{8,16},{16,24},{24,32},{32,40},{40,48},{48,56},{56,0},{1,9},... | collective-permute-start | bytes 196616 | tf_op jit(solution)/shard_map/ppermute | solution.py:349
  232.5 23.1 %collective-permute-start.11 = (bf16[32,128,128]{2,1,0:T(8,128)(2,1)S(1)}, bf16[32,128,128]{2,1,0:T(8,128)(2,1)S(1)}, u32[]{:S(2)}, u32[]{:S(2)}) collective-permute-start(bf16[32,128,128]{2,1,0:T(8,128)(2,1)S(1)} %join.1.refs_3_), channel_id=1, source_target_pairs={{0,192},{64,0},{128,64},{192,128},{1,193},{65,1},{129,65},{193,129... | collective-permute-start | bytes 3145736 | tf_op jit(solution)/shard_map/ppermute | solution.py:362
  235.1 23.8 %collective-permute-start.10 = (bf16[32,128,128]{2,1,0:T(8,128)(2,1)S(1)}, bf16[32,128,128]{2,1,0:T(8,128)(2,1)}, u32[]{:S(2)}, u32[]{:S(2)}) collective-permute-start(bf16[32,128,128]{2,1,0:T(8,128)(2,1)S(1)} %join.1.refs_3_), channel_id=1, source_target_pairs={{0,64},{64,128},{128,192},{192,0},{1,65},{65,129},{129,193},{193,1... | collective-permute-start | bytes 3145736 | tf_op jit(solution)/shard_map/ppermute | solution.py:361
  235.2 59.4 %slice-start = ((s8[9437184]{0:T(1024)(128)(4,1)}), s8[4194304]{0:T(1024)(128)(4,1)S(1)}, s32[]{:S(2)}) async-start(s8[9437184]{0:T(1024)(128)(4,1)} %bitcast.11), calls=%async_computation | async-start | bytes 8388608
  260.0 34.6 %slice-start.1 = ((s8[9437184]{0:T(1024)(128)(4,1)}), s8[4194304]{0:T(1024)(128)(4,1)S(1)}, s32[]{:S(2)}) async-start(s8[9437184]{0:T(1024)(128)(4,1)} %bitcast.11), calls=%async_computation.1 | async-start | bytes 8388608
  260.0 13.9 %collective-permute-start.12 = (bf16[16,128,128]{2,1,0:T(8,128)(2,1)S(1)}, bf16[16,128,128]{2,1,0:T(8,128)(2,1)S(1)}, u32[]{:S(2)}, u32[]{:S(2)}) collective-permute-start(bf16[16,128,128]{2,1,0:T(8,128)(2,1)S(1)} %slice.26), channel_id=1, source_target_pairs={{0,64},{64,128},{128,192},{192,0},{1,65},{65,129},{129,193},{193,1... | collective-permute-start | bytes 1572872 | tf_op jit(solution)/shard_map/ppermute | solution.py:368
  260.1 13.8 %collective-permute-start.13 = (bf16[16,128,128]{2,1,0:T(8,128)(2,1)S(1)}, bf16[16,128,128]{2,1,0:T(8,128)(2,1)S(1)}, u32[]{:S(2)}, u32[]{:S(2)}) collective-permute-start(bf16[16,128,128]{2,1,0:T(8,128)(2,1)S(1)} %slice.27), channel_id=1, source_target_pairs={{0,192},{64,0},{128,64},{192,128},{1,193},{65,1},{129,65},{193,129... | collective-permute-start | bytes 1572872 | tf_op jit(solution)/shard_map/ppermute | solution.py:369
  273.9 20.7 %slice-start.2 = ((s8[9437184]{0:T(1024)(128)(4,1)}), s8[1048576]{0:T(1024)(128)(4,1)S(1)}, s32[]{:S(2)}) async-start(s8[9437184]{0:T(1024)(128)(4,1)} %bitcast.11), calls=%async_computation.2 | async-start | bytes 2097152
  277.6 3.1 %collective-permute-start.14 = (f32[2,152,768]{2,1,0:T(8,128)S(1)}, f32[2,152,768]{2,1,0:T(8,128)S(1)}, u32[]{:S(2)}, u32[]{:S(2)}) collective-permute-start(f32[2,152,768]{2,1,0:T(8,128)S(1)} %stage_c.1), channel_id=1, source_target_pairs={{0,1},{1,0},{2,3},{3,2},{4,5},{5,4},{6,7},{7,6},{8,9},{9,8},{10,11... | collective-permute-start | bytes 2801672 | tf_op jit(solution)/shard_map/ppermute | solution.py:376
  280.9 9.6 %collective-permute-start.17 = (bf16[256,768]{1,0:T(8,128)(2,1)S(1)}, bf16[256,768]{1,0:T(8,128)(2,1)S(1)}, u32[]{:S(2)}, u32[]{:S(2)}) collective-permute-start(bf16[256,768]{1,0:T(8,128)(2,1)S(1)} %merge.1), channel_id=1, source_target_pairs={{0,2},{1,6},{2,0},{3,4},{4,3},{5,7},{6,1},{7,5},{8,10},{9,14},{10,... | collective-permute-start | bytes 1179656 | tf_op jit(solution)/shard_map/ppermute | solution.py:383
  284.0 10.6 %collective-permute-start.16 = (bf16[256,768]{1,0:T(8,128)(2,1)S(1)}, bf16[256,768]{1,0:T(8,128)(2,1)S(1)}, u32[]{:S(2)}, u32[]{:S(2)}) collective-permute-start(bf16[256,768]{1,0:T(8,128)(2,1)S(1)} %merge.1), channel_id=1, source_target_pairs={{0,0},{1,4},{2,2},{3,6},{4,1},{5,5},{6,3},{7,7},{8,8},{9,12},{10,1... | collective-permute-start | bytes 1179656 | tf_op jit(solution)/shard_map/ppermute | solution.py:382
  301.1 6.6 %collective-permute-start.18 = (bf16[256,1536]{1,0:T(8,128)(2,1)S(1)}, bf16[256,1536]{1,0:T(8,128)(2,1)S(1)}, u32[]{:S(2)}, u32[]{:S(2)}) collective-permute-start(bf16[256,1536]{1,0:T(8,128)(2,1)S(1)} %project_send.1), channel_id=1, source_target_pairs={{0,1},{1,0},{2,3},{3,2},{4,5},{5,4},{6,7},{7,6},{8,9},{9,8},{10,11... | collective-permute-start | bytes 2359304 | tf_op jit(solution)/shard_map/ppermute | solution.py:387
  (2 other events, 1.7 us)

commit v4 on v3

--- a/solution.py
+++ b/solution.py
@@ -108,14 +108,14 @@
 
 
 def column_half(source, number):
-    return pl.pallas_call(
+    return call(
         half_kernel,
-        out_shape=jax.ShapeDtypeStruct((source.shape[0], source.shape[1] // 2), source.dtype),
-        in_specs=[smem(), hbm()],
-        out_specs=hbm(),
-        scratch_shapes=[pltpu.SemaphoreType.DMA((8,))],
+        jax.ShapeDtypeStruct((source.shape[0], source.shape[1] // 2), source.dtype),
+        (number.reshape(1).astype(jnp.int32), source),
+        [smem(), hbm()],
+        scratch=(pltpu.SemaphoreType.DMA((8,)),),
         name="column_half",
-    )(number.reshape(1).astype(jnp.int32), source)
+    )
 
 
 def join_kernel(*refs):
@@ -282,41 +282,26 @@
     return [(z * 8 + a, (z + shift) % NZ * 8 + b) for z in range(NZ) for a, b in turn]
 
 
-def project_kernel(flip, place_ref, near_ref, far_ref, weight_ref, far_weight_ref, out_ref, own_ref, sems):
+def project_kernel(flip, place_ref, near_ref, far_ref, weight_ref, far_weight_ref, out_ref):
     width = out_ref.shape[1]
-    parts = width // 256
     which = place_ref[1] + flip - 2 * flip * place_ref[1]
-    base = pl.multiple_of(place_ref[0] * (2 * width) + which * width, 256)
-    copies = [
-        pltpu.make_async_copy(
-            weight_ref.at[:, pl.ds(base + n * 256, 256)], own_ref.at[n], sems.at[n]
-        )
-        for n in range(parts)
-    ]
-    for copy in copies:
-        copy.start()
-    for n in range(parts):
+    for n in range(width // 256):
         at = pl.multiple_of(which * width + n * 256, 256)
-        total = jnp.dot(
-            far_ref[...], far_weight_ref[:, pl.ds(at, 256)], preferred_element_type=jnp.float32
-        )
-        copies[n].wait()
-        total = total + jnp.dot(near_ref[...], own_ref[n], preferred_element_type=jnp.float32)
+        far = far_weight_ref[:, pl.ds(at, 256)]
+        total = jnp.dot(far_ref[...], far, preferred_element_type=jnp.float32)
+        at = pl.multiple_of(place_ref[0] * (2 * width) + which * width + n * 256, 256)
+        near = weight_ref[:, pl.ds(at, 256)]
+        total = total + jnp.dot(near_ref[...], near, preferred_element_type=jnp.float32)
         out_ref[:, n * 256 : (n + 1) * 256] = total.astype(out_ref.dtype)
 
 
 def project(flip, place, near, far, weight, far_weight, dtype, name):
-    width = far_weight.shape[1] // 2
-    shape = jax.ShapeDtypeStruct((near.shape[0], width), dtype)
+    shape = jax.ShapeDtypeStruct((near.shape[0], far_weight.shape[1] // 2), dtype)
     return call(
         lambda *refs: project_kernel(flip, *refs),
         shape,
         (place, near, far, weight, far_weight),
-        [smem(), vmem(), vmem(), hbm(), vmem()],
-        scratch=(
-            pltpu.VMEM((width // 256, weight.shape[0], 256), jnp.bfloat16),
-            pltpu.SemaphoreType.DMA((width // 256,)),
-        ),
+        [smem()] + [vmem()] * 4,
         name=name,
     )
 
@@ -335,16 +320,17 @@
     unit = pack(key_rows, value_rows)
     up, down = ring(NZ, 1), ring(NZ, -1)
     units = {-1: lax.ppermute(unit, YZ, turned(1)), 1: lax.ppermute(unit, YZ, turned(-1))}
+    queries, units[-1], units[1] = together((queries, units[-1], units[1]))
     mine = lax.ppermute(bundle(queries, tile_mask, unit), Y, turn)
     half_away = column_half(out_weight, 1 - yl)
     away = along_y(lambda yh, yl, core: (*next_y(yh, yl, 1 - 2 * core), core))
     units[-2] = lax.ppermute(units[-1], "z", up)
     units[2] = lax.ppermute(units[1], "z", down)
     units[-2], units[2], half_away = together((units[-2], units[2], half_away))
-    far_weight = lax.ppermute(half_away, Y, away)
     units[-3] = lax.ppermute(units[-2], "z", up)
     units[3] = lax.ppermute(units[2], "z", down)
-    units[-3], units[3], mine = together((units[-3], units[3], mine))
+    units[-3], units[3], mine, half_away = together((units[-3], units[3], mine, half_away))
+    far_weight = lax.ppermute(half_away, Y, away)
     far = [
         lax.ppermute(units[-3][:2], "z", up),
         lax.ppermute(units[3][2:], "z", down),

time: 309 us -> 121 us (0.39)
  Pallas kernels: 183 us -> 34.5 us
  waiting for transfers between devices: 85.6 us -> 40.3 us
  local copies, waits for them, and re-layouts: 2.86 us -> 8.2 us
    pallas_call x1 -> x0, Pallas kernels: 144 us -> none  [column_half(): pl.pallas_call(half_kernel, out_shape=jax.ShapeDtypeStruct((source.shape[...]
    ppermute x1, waiting for transfers between devices: 50.2 us -> 0.01 us  [per_device(): mine = lax.ppermute(bundle(queries, tile_mask, unit), Y, turn)]
    unnamed x14 -> x16, local copies, waits for them, and re-layouts: 1.71 us -> 7.05 us
    pallas_call x11 -> x12, Pallas kernels: 39.3 us -> 34.5 us  [call(): pl.pallas_call(kernel, out_shape=out_shape, in_specs=in_specs, out_specs=...]
    ppermute x1, waiting for transfers between devices: 2.13 us -> 6.06 us  [per_device(): lax.ppermute(unit, YZ, turned(1))]
    ppermute x1, waiting for transfers between devices: 4.32 us -> 0.96 us  [per_device(): lax.ppermute(attended, Y, along_y(lambda yh, yl, core: (core, 1 - yl, yh)))]
    ppermute x1, starting transfers between devices: 5.13 us -> 1.92 us  [per_device(): mine = lax.ppermute(bundle(queries, tile_mask, unit), Y, turn)]
  transfers between devices with their start and end apart: 19 -> 19, of which waited for: 10 -> 9; matrix products, arithmetic and copies ran while one was open for 0% -> 1% of each run, Pallas kernels for 57% -> 24%
where the time goes in v4:
time: 121 us; the launch traced here: 120 us
  waiting for transfers between devices  40.3 us (33%)
  starting transfers between devices  36.8 us (30%)
  Pallas kernels  34.5 us (29%)
  local copies, waits for them, and re-layouts  8.2 us (7%)
    pallas_call x12, Pallas kernels, call(): pl.pallas_call(kernel, out_shape=out_shape, in_specs=in_specs, out_specs=...  34.5 us
    ppermute x1, waiting for transfers between devices, per_device(): after = lax.ppermute(column, 'x', back)  15.3 us
    ppermute x1, starting transfers between devices, per_device(): lax.ppermute(unit, YZ, turned(-1))  9.67 us
    unnamed x16, local copies, waits for them, and re-layouts  7.05 us
    ppermute x1, waiting for transfers between devices, per_device(): lax.ppermute(unit, YZ, turned(1))  6.06 us
    ppermute x1, waiting for transfers between devices, per_device(): near_part = lax.ppermute(attended, Y, turn)  5.7 us
    ppermute x1, starting transfers between devices, per_device(): near_part = lax.ppermute(attended, Y, turn)  4.93 us
    ppermute x1, starting transfers between devices, per_device(): lax.ppermute(attended, Y, along_y(lambda yh, yl, core: (core, 1 - yl, yh)))  4 us
  transfers between devices with their start and end apart: 19, of which 9 were waited for; matrix products, arithmetic and copies ran while one was open for 1% of the time, Pallas kernels for 24%

profile of v4, /device:TPU:1, one launch (start us, length us, event | category | flops | bytes accessed | tf_op | source)
XLA Modules:
  0.0 120.2 jit_solution(2399076355824238223)
XLA Ops:
  2.0 9.7 %collective-permute-start.1 = (bf16[4,128,128]{2,1,0:T(8,128)(2,1)S(1)}, bf16[4,128,128]{2,1,0:T(8,128)(2,1)S(1)}, u32[]{:S(2)}, u32[]{:S(2)}) collective-permute-start(bf16[4,128,128]{2,1,0:T(8,128)(2,1)S(1)} %pack.1.unit_ref), channel_id=1, source_target_pairs={{0,56},{1,60},{2,58},{3,62},{4,57},{5,61},{6,59},{7,63},{8,0},{9,4... | collective-permute-start | bytes 393224 | tf_op jit(solution)/shard_map/ppermute | solution.py:322
  11.6 1.9 %collective-permute-done.1.refs_2_ = bf16[4,128,128]{2,1,0:T(8,128)(2,1)S(1)} collective-permute-done((bf16[4,128,128]{2,1,0:T(8,128)(2,1)S(1)}, bf16[4,128,128]{2,1,0:T(8,128)(2,1)S(1)}, u32[]{:S(2)}, u32[]{:S(2)}) %collective-permute-start.1) | collective-permute-done | bytes 131104 | tf_op jit(solution)/shard_map/ppermute | solution.py:322
  13.6 6.1 %collective-permute-done.refs_1_ = bf16[4,128,128]{2,1,0:T(8,128)(2,1)S(1)} collective-permute-done((bf16[4,128,128]{2,1,0:T(8,128)(2,1)S(1)}, bf16[4,128,128]{2,1,0:T(8,128)(2,1)S(1)}, u32[]{:S(2)}, u32[]{:S(2)}) %collective-permute-start) | collective-permute-done | bytes 131104 | tf_op jit(solution)/shard_map/ppermute | solution.py:322
  23.4 2.7 %collective-permute-start.3 = (bf16[4,128,128]{2,1,0:T(8,128)(2,1)S(1)}, bf16[4,128,128]{2,1,0:T(8,128)(2,1)S(1)}, u32[]{:S(2)}, u32[]{:S(2)}) collective-permute-start(bf16[4,128,128]{2,1,0:T(8,128)(2,1)S(1)} %collective-permute-done.1.refs_2_), channel_id=1, source_target_pairs={{0,56},{8,0},{16,8},{24,16},{32,24},{40,32},{48,40},{56,48},{1,57}... | collective-permute-start | bytes 393224 | tf_op jit(solution)/shard_map/ppermute | solution.py:328
  26.1 3.7 %copy-done = bf16[768,6144]{1,0:T(8,128)(2,1)S(1)} copy-done((bf16[768,6144]{1,0:T(8,128)(2,1)S(1)}, bf16[768,6144]{1,0:T(8,128)(2,1)}, u32[]{:S(2)}) %copy-start) | copy-done | bytes 9437208
  29.8 2.7 %column_half.1 = bf16[768,3072]{1,0:T(8,128)(2,1)} custom-call(s32[1]{0:T(128)} %bitcast.2.half_ref, bf16[768,6144]{1,0:T(8,128)(2,1)S(1)} %copy-done), custom_call_target="tpu_custom_call" | custom-call | tf_op jit(solution)/shard_map/column_half/pallas_call | solution.py:39
  32.6 2.7 %collective-permute-start.5 = (bf16[4,128,128]{2,1,0:T(8,128)(2,1)S(1)}, bf16[4,128,128]{2,1,0:T(8,128)(2,1)S(1)}, u32[]{:S(2)}, u32[]{:S(2)}) collective-permute-start(bf16[4,128,128]{2,1,0:T(8,128)(2,1)S(1)} %collective-permute-done.3.refs_4_), channel_id=1, source_target_pairs={{0,56},{8,0},{16,8},{24,16},{32,24},{40,32},{48,40},{56,48},{1,57}... | collective-permute-start | bytes 393224 | tf_op jit(solution)/shard_map/ppermute | solution.py:331
  35.2 2.4 %collective-permute-done.4.refs_5_ = bf16[4,128,128]{2,1,0:T(8,128)(2,1)S(1)} collective-permute-done((bf16[4,128,128]{2,1,0:T(8,128)(2,1)S(1)}, bf16[4,128,128]{2,1,0:T(8,128)(2,1)S(1)}, u32[]{:S(2)}, u32[]{:S(2)}) %collective-permute-start.4) | collective-permute-done | bytes 131104 | tf_op jit(solution)/shard_map/ppermute | solution.py:330
  37.7 2.7 %collective-permute-start.8 = (bf16[2,128,128]{2,1,0:T(8,128)(2,1)S(1)}, bf16[2,128,128]{2,1,0:T(8,128)(2,1)S(1)}, u32[]{:S(2)}, u32[]{:S(2)}) collective-permute-start(bf16[2,128,128]{2,1,0:T(8,128)(2,1)S(1)} %slice.23), channel_id=1, source_target_pairs={{0,56},{8,0},{16,8},{24,16},{32,24},{40,32},{48,40},{56,48},{1,57}... | collective-permute-start | bytes 196616 | tf_op jit(solution)/shard_map/ppermute | solution.py:336
  41.7 3.4 %collective-permute-done.7.refs_7_ = bf16[2,128,128]{2,1,0:T(8,128)(2,1)S(1)} collective-permute-done((bf16[2,128,128]{2,1,0:T(8,128)(2,1)S(1)}, bf16[2,128,128]{2,1,0:T(8,128)(2,1)S(1)}, u32[]{:S(2)}, u32[]{:S(2)}) %collective-permute-start.7) | collective-permute-done | bytes 65568 | tf_op jit(solution)/shard_map/ppermute | solution.py:335
  45.2 2.6 %collective-permute-start.11 = (bf16[32,128,128]{2,1,0:T(8,128)(2,1)S(1)}, bf16[32,128,128]{2,1,0:T(8,128)(2,1)S(1)}, u32[]{:S(2)}, u32[]{:S(2)}) collective-permute-start(bf16[32,128,128]{2,1,0:T(8,128)(2,1)S(1)} %join.1.refs_3_), channel_id=1, source_target_pairs={{0,192},{64,0},{128,64},{192,128},{1,193},{65,1},{129,65},{193,129... | collective-permute-start | bytes 3145736 | tf_op jit(solution)/shard_map/ppermute | solution.py:348
  47.9 5.5 %stage_a.1 = (f32[2,152,768]{2,1,0:T(8,128)S(1)}, f32[2,152,768]{2,1,0:T(8,128)S(1)}) custom-call(s32[5,128]{1,0:T(8,128)S(1)} %pad_add_fusion.refs_0_, bf16[17,128,128]{2,1,0:T(8,128)(2,1)S(1)} %collective-permute-done.6.refs_1_, bf16[17,128,128]{2,1,0:T(8,128)(2,1)S(1)} %collective-permute-done.9.refs_2_, bf16[32,128,128]{2,1,0:T(8,128)(2,1)S(1)} %join.1.refs_3_), custom_call_target="tpu_custom_call" | custom-call | tf_op jit(solution)/shard_map/stage_a/pallas_call | solution.py:39
  53.4 15.3 %collective-permute-done.11.refs_4_ = bf16[32,128,128]{2,1,0:T(8,128)(2,1)S(1)} collective-permute-done((bf16[32,128,128]{2,1,0:T(8,128)(2,1)S(1)}, bf16[32,128,128]{2,1,0:T(8,128)(2,1)S(1)}, u32[]{:S(2)}, u32[]{:S(2)}) %collective-permute-start.11) | collective-permute-done | bytes 1048608 | tf_op jit(solution)/shard_map/ppermute | solution.py:348
  68.7 3.2 %collective-permute-done.10.refs_3_ = bf16[32,128,128]{2,1,0:T(8,128)(2,1)} collective-permute-done((bf16[32,128,128]{2,1,0:T(8,128)(2,1)S(1)}, bf16[32,128,128]{2,1,0:T(8,128)(2,1)}, u32[]{:S(2)}, u32[]{:S(2)}) %collective-permute-start.10) | collective-permute-done | bytes 1048608 | tf_op jit(solution)/shard_map/ppermute | solution.py:347
  73.1 2.7 %collective-permute-start.13 = (bf16[16,128,128]{2,1,0:T(8,128)(2,1)S(1)}, bf16[16,128,128]{2,1,0:T(8,128)(2,1)S(1)}, u32[]{:S(2)}, u32[]{:S(2)}) collective-permute-start(bf16[16,128,128]{2,1,0:T(8,128)(2,1)S(1)} %slice.27), channel_id=1, source_target_pairs={{0,192},{64,0},{128,64},{192,128},{1,193},{65,1},{129,65},{193,129... | collective-permute-start | bytes 1572872 | tf_op jit(solution)/shard_map/ppermute | solution.py:355
  75.8 9.7 %stage_b.1 = (f32[2,152,768]{2,1,0:T(8,128)S(1)}, f32[2,152,768]{2,1,0:T(8,128)S(1)}) custom-call(s32[5,128]{1,0:T(8,128)S(1)} %pad_add_fusion.refs_0_, bf16[17,128,128]{2,1,0:T(8,128)(2,1)S(1)} %collective-permute-done.6.refs_1_, bf16[17,128,128]{2,1,0:T(8,128)(2,1)S(1)} %collective-permute-done.9.refs_2_, ...), custom_call_target="tpu_custom_call", output_to_operand_aliasing={{0}: (5, {}), {1}: (6, {})} | custom-call | tf_op jit(solution)/shard_map/stage_b/pallas_call | solution.py:39
  85.6 3.7 %stage_c.1 = f32[2,152,768]{2,1,0:T(8,128)S(1)} custom-call(s32[5,128]{1,0:T(8,128)S(1)} %pad_add_fusion.refs_0_, bf16[17,128,128]{2,1,0:T(8,128)(2,1)S(1)} %collective-permute-done.6.refs_1_, bf16[17,128,128]{2,1,0:T(8,128)(2,1)S(1)} %collective-permute-done.9.refs_2_, ...), custom_call_target="tpu_custom_call", output_to_operand_aliasing={{}: (5, {})} | custom-call | tf_op jit(solution)/shard_map/stage_c/pallas_call | solution.py:39
  89.3 2.6 %collective-permute-start.14 = (f32[2,152,768]{2,1,0:T(8,128)S(1)}, f32[2,152,768]{2,1,0:T(8,128)S(1)}, u32[]{:S(2)}, u32[]{:S(2)}) collective-permute-start(f32[2,152,768]{2,1,0:T(8,128)S(1)} %stage_c.1), channel_id=1, source_target_pairs={{0,1},{1,0},{2,3},{3,2},{4,5},{5,4},{6,7},{7,6},{8,9},{9,8},{10,11... | collective-permute-start | bytes 2801672 | tf_op jit(solution)/shard_map/ppermute | solution.py:362
  91.9 3.7 %stage_d.1.own_ref = f32[2,152,768]{2,1,0:T(8,128)S(1)} custom-call(s32[5,128]{1,0:T(8,128)S(1)} %pad_add_fusion.refs_0_, bf16[17,128,128]{2,1,0:T(8,128)(2,1)S(1)} %collective-permute-done.6.refs_1_, bf16[17,128,128]{2,1,0:T(8,128)(2,1)S(1)} %collective-permute-done.9.refs_2_, ...), custom_call_target="tpu_custom_call", output_to_operand_aliasing={{}: (5, {})} | custom-call | tf_op jit(solution)/shard_map/stage_d/pallas_call | solution.py:39
  95.8 4.0 %collective-permute-start.17 = (bf16[256,768]{1,0:T(8,128)(2,1)S(1)}, bf16[256,768]{1,0:T(8,128)(2,1)S(1)}, u32[]{:S(2)}, u32[]{:S(2)}) collective-permute-start(bf16[256,768]{1,0:T(8,128)(2,1)S(1)} %merge.1), channel_id=1, source_target_pairs={{0,2},{1,6},{2,0},{3,4},{4,3},{5,7},{6,1},{7,5},{8,10},{9,14},{10,... | collective-permute-start | bytes 1179656 | tf_op jit(solution)/shard_map/ppermute | solution.py:369
  99.8 4.9 %collective-permute-start.16 = (bf16[256,768]{1,0:T(8,128)(2,1)S(1)}, bf16[256,768]{1,0:T(8,128)(2,1)S(1)}, u32[]{:S(2)}, u32[]{:S(2)}) collective-permute-start(bf16[256,768]{1,0:T(8,128)(2,1)S(1)} %merge.1), channel_id=1, source_target_pairs={{0,0},{1,4},{2,2},{3,6},{4,1},{5,5},{6,3},{7,7},{8,8},{9,12},{10,1... | collective-permute-start | bytes 1179656 | tf_op jit(solution)/shard_map/ppermute | solution.py:368
  105.8 5.7 %collective-permute-done.16.refs_1_ = bf16[256,768]{1,0:T(8,128)(2,1)S(1)} collective-permute-done((bf16[256,768]{1,0:T(8,128)(2,1)S(1)}, bf16[256,768]{1,0:T(8,128)(2,1)S(1)}, u32[]{:S(2)}, u32[]{:S(2)}) %collective-permute-start.16) | collective-permute-done | bytes 393248 | tf_op jit(solution)/shard_map/ppermute | solution.py:368
  111.5 3.8 %project_send.1 = bf16[256,1536]{1,0:T(8,128)(2,1)S(1)} custom-call(s32[2]{0:T(128)S(1)} %pad_add_fusion.1.refs_0_, bf16[256,768]{1,0:T(8,128)(2,1)S(1)} %collective-permute-done.16.refs_1_, bf16[256,768]{1,0:T(8,128)(2,1)S(1)} %collective-permute-done.17.refs_2_, bf16[768,6144]{1,0:T(8,128)(2,1)S(1)} %bitcast.12, ...), custom_call_target="tpu_custom_call" | custom-call | tf_op jit(solution)/shard_map/project_send/pallas_call | solution.py:39
  115.4 3.8 %project_keep.1.keep_ref = f32[256,1536]{1,0:T(8,128)S(1)} custom-call(s32[2]{0:T(128)S(1)} %pad_add_fusion.1.refs_0_, bf16[256,768]{1,0:T(8,128)(2,1)S(1)} %collective-permute-done.16.refs_1_, bf16[256,768]{1,0:T(8,128)(2,1)S(1)} %collective-permute-done.17.refs_2_, bf16[768,6144]{1,0:T(8,128)(2,1)S(1)} %bitcast.12, ...), custom_call_target="tpu_custom_call" | custom-call | tf_op jit(solution)/shard_map/project_keep/pallas_call | solution.py:39
  (55 shorter events, 11.0 us)
Async XLA Ops:
  2.0 11.6 %collective-permute-start.1 = (bf16[4,128,128]{2,1,0:T(8,128)(2,1)S(1)}, bf16[4,128,128]{2,1,0:T(8,128)(2,1)S(1)}, u32[]{:S(2)}, u32[]{:S(2)}) collective-permute-start(bf16[4,128,128]{2,1,0:T(8,128)(2,1)S(1)} %pack.1.unit_ref), channel_id=1, source_target_pairs={{0,56},{1,60},{2,58},{3,62},{4,57},{5,61},{6,59},{7,63},{8,0},{9,4... | collective-permute-start | bytes 393224 | tf_op jit(solution)/shard_map/ppermute | solution.py:322
  11.6 8.0 %collective-permute-start = (bf16[4,128,128]{2,1,0:T(8,128)(2,1)S(1)}, bf16[4,128,128]{2,1,0:T(8,128)(2,1)S(1)}, u32[]{:S(2)}, u32[]{:S(2)}) collective-permute-start(bf16[4,128,128]{2,1,0:T(8,128)(2,1)S(1)} %pack.1.unit_ref), channel_id=1, source_target_pairs={{0,8},{1,12},{2,10},{3,14},{4,9},{5,13},{6,11},{7,15},{8,16},{9,20... | collective-permute-start | bytes 393224 | tf_op jit(solution)/shard_map/ppermute | solution.py:322
  19.6 1.0 copy-start.1
  21.4 16.2 %collective-permute-start.6 = (bf16[17,128,128]{2,1,0:T(8,128)(2,1)S(1)}, bf16[17,128,128]{2,1,0:T(8,128)(2,1)S(1)}, u32[]{:S(2)}, u32[]{:S(2)}) collective-permute-start(bf16[17,128,128]{2,1,0:T(8,128)(2,1)S(1)} %bundle.1), channel_id=1, source_target_pairs={{0,0},{1,4},{2,2},{3,6},{4,1},{5,5},{6,3},{7,7},{8,8},{9,12},{10,1... | collective-permute-start | bytes 1671176 | tf_op jit(solution)/shard_map/ppermute | solution.py:324
  23.3 9.1 %collective-permute-start.2 = (bf16[4,128,128]{2,1,0:T(8,128)(2,1)S(1)}, bf16[4,128,128]{2,1,0:T(8,128)(2,1)S(1)}, u32[]{:S(2)}, u32[]{:S(2)}) collective-permute-start(bf16[4,128,128]{2,1,0:T(8,128)(2,1)S(1)} %collective-permute-done.refs_1_), channel_id=1, source_target_pairs={{0,8},{8,16},{16,24},{24,32},{32,40},{40,48},{48,56},{56,0},{1,9},... | collective-permute-start | bytes 393224 | tf_op jit(solution)/shard_map/ppermute | solution.py:327
  23.4 9.1 %collective-permute-start.3 = (bf16[4,128,128]{2,1,0:T(8,128)(2,1)S(1)}, bf16[4,128,128]{2,1,0:T(8,128)(2,1)S(1)}, u32[]{:S(2)}, u32[]{:S(2)}) collective-permute-start(bf16[4,128,128]{2,1,0:T(8,128)(2,1)S(1)} %collective-permute-done.1.refs_2_), channel_id=1, source_target_pairs={{0,56},{8,0},{16,8},{24,16},{32,24},{40,32},{48,40},{56,48},{1,57}... | collective-permute-start | bytes 393224 | tf_op jit(solution)/shard_map/ppermute | solution.py:328
  26.1 3.7 %copy-start = (bf16[768,6144]{1,0:T(8,128)(2,1)S(1)}, bf16[768,6144]{1,0:T(8,128)(2,1)}, u32[]{:S(2)}) copy-start(bf16[768,6144]{1,0:T(8,128)(2,1)} %refs_3_.3) | copy-start | bytes 28311556
  32.5 5.1 %collective-permute-start.4 = (bf16[4,128,128]{2,1,0:T(8,128)(2,1)S(1)}, bf16[4,128,128]{2,1,0:T(8,128)(2,1)S(1)}, u32[]{:S(2)}, u32[]{:S(2)}) collective-permute-start(bf16[4,128,128]{2,1,0:T(8,128)(2,1)S(1)} %collective-permute-done.2.refs_3_), channel_id=1, source_target_pairs={{0,8},{8,16},{16,24},{24,32},{32,40},{40,48},{48,56},{56,0},{1,9},... | collective-permute-start | bytes 393224 | tf_op jit(solution)/shard_map/ppermute | solution.py:330
  32.6 5.0 %collective-permute-start.5 = (bf16[4,128,128]{2,1,0:T(8,128)(2,1)S(1)}, bf16[4,128,128]{2,1,0:T(8,128)(2,1)S(1)}, u32[]{:S(2)}, u32[]{:S(2)}) collective-permute-start(bf16[4,128,128]{2,1,0:T(8,128)(2,1)S(1)} %collective-permute-done.3.refs_4_), channel_id=1, source_target_pairs={{0,56},{8,0},{16,8},{24,16},{32,24},{40,32},{48,40},{56,48},{1,57}... | collective-permute-start | bytes 393224 | tf_op jit(solution)/shard_map/ppermute | solution.py:331
  37.6 58.0 %collective-permute-start.15 = (bf16[768,3072]{1,0:T(8,128)(2,1)}, bf16[768,3072]{1,0:T(8,128)(2,1)}, u32[]{:S(2)}, u32[]{:S(2)}) collective-permute-start(bf16[768,3072]{1,0:T(8,128)(2,1)} %column_half.1), channel_id=1, source_target_pairs={{0,2},{1,7},{2,4},{3,1},{4,6},{5,3},{6,0},{7,5},{8,10},{9,15},{10,... | collective-permute-start | bytes 14155784 | tf_op jit(solution)/shard_map/ppermute | solution.py:333
  37.6 7.5 %collective-permute-start.9 = (bf16[17,128,128]{2,1,0:T(8,128)(2,1)S(1)}, bf16[17,128,128]{2,1,0:T(8,128)(2,1)S(1)}, u32[]{:S(2)}, u32[]{:S(2)}) collective-permute-start(bf16[17,128,128]{2,1,0:T(8,128)(2,1)S(1)} %collective-permute-done.6.refs_1_), channel_id=1, source_target_pairs={{0,1},{1,0},{2,3},{3,2},{4,5},{5,4},{6,7},{7,6},{8,9},{9,8},{10,11... | collective-permute-start | bytes 1671176 | tf_op jit(solution)/shard_map/ppermute | solution.py:338
  37.7 4.0 %collective-permute-start.8 = (bf16[2,128,128]{2,1,0:T(8,128)(2,1)S(1)}, bf16[2,128,128]{2,1,0:T(8,128)(2,1)S(1)}, u32[]{:S(2)}, u32[]{:S(2)}) collective-permute-start(bf16[2,128,128]{2,1,0:T(8,128)(2,1)S(1)} %slice.23), channel_id=1, source_target_pairs={{0,56},{8,0},{16,8},{24,16},{32,24},{40,32},{48,40},{56,48},{1,57}... | collective-permute-start | bytes 196616 | tf_op jit(solution)/shard_map/ppermute | solution.py:336
  40.4 4.7 %collective-permute-start.7 = (bf16[2,128,128]{2,1,0:T(8,128)(2,1)S(1)}, bf16[2,128,128]{2,1,0:T(8,128)(2,1)S(1)}, u32[]{:S(2)}, u32[]{:S(2)}) collective-permute-start(bf16[2,128,128]{2,1,0:T(8,128)(2,1)S(1)} %slice.22), channel_id=1, source_target_pairs={{0,8},{8,16},{16,24},{24,32},{32,40},{40,48},{48,56},{56,0},{1,9},... | collective-permute-start | bytes 196616 | tf_op jit(solution)/shard_map/ppermute | solution.py:335
  45.2 23.5 %collective-permute-start.11 = (bf16[32,128,128]{2,1,0:T(8,128)(2,1)S(1)}, bf16[32,128,128]{2,1,0:T(8,128)(2,1)S(1)}, u32[]{:S(2)}, u32[]{:S(2)}) collective-permute-start(bf16[32,128,128]{2,1,0:T(8,128)(2,1)S(1)} %join.1.refs_3_), channel_id=1, source_target_pairs={{0,192},{64,0},{128,64},{192,128},{1,193},{65,1},{129,65},{193,129... | collective-permute-start | bytes 3145736 | tf_op jit(solution)/shard_map/ppermute | solution.py:348
  47.7 24.2 %collective-permute-start.10 = (bf16[32,128,128]{2,1,0:T(8,128)(2,1)S(1)}, bf16[32,128,128]{2,1,0:T(8,128)(2,1)}, u32[]{:S(2)}, u32[]{:S(2)}) collective-permute-start(bf16[32,128,128]{2,1,0:T(8,128)(2,1)S(1)} %join.1.refs_3_), channel_id=1, source_target_pairs={{0,64},{64,128},{128,192},{192,0},{1,65},{65,129},{129,193},{193,1... | collective-permute-start | bytes 3145736 | tf_op jit(solution)/shard_map/ppermute | solution.py:347
  47.9 63.6 %slice-start = ((s8[9437184]{0:T(1024)(128)(4,1)}), s8[4194304]{0:T(1024)(128)(4,1)S(1)}, s32[]{:S(2)}) async-start(s8[9437184]{0:T(1024)(128)(4,1)} %bitcast.11), calls=%async_computation | async-start | bytes 8388608
  73.0 38.5 %slice-start.1 = ((s8[9437184]{0:T(1024)(128)(4,1)}), s8[4194304]{0:T(1024)(128)(4,1)S(1)}, s32[]{:S(2)}) async-start(s8[9437184]{0:T(1024)(128)(4,1)} %bitcast.11), calls=%async_computation.1 | async-start | bytes 8388608
  73.1 12.5 %collective-permute-start.12 = (bf16[16,128,128]{2,1,0:T(8,128)(2,1)S(1)}, bf16[16,128,128]{2,1,0:T(8,128)(2,1)S(1)}, u32[]{:S(2)}, u32[]{:S(2)}) collective-permute-start(bf16[16,128,128]{2,1,0:T(8,128)(2,1)S(1)} %slice.26), channel_id=1, source_target_pairs={{0,64},{64,128},{128,192},{192,0},{1,65},{65,129},{129,193},{193,1... | collective-permute-start | bytes 1572872 | tf_op jit(solution)/shard_map/ppermute | solution.py:354
  73.1 12.4 %collective-permute-start.13 = (bf16[16,128,128]{2,1,0:T(8,128)(2,1)S(1)}, bf16[16,128,128]{2,1,0:T(8,128)(2,1)S(1)}, u32[]{:S(2)}, u32[]{:S(2)}) collective-permute-start(bf16[16,128,128]{2,1,0:T(8,128)(2,1)S(1)} %slice.27), channel_id=1, source_target_pairs={{0,192},{64,0},{128,64},{192,128},{1,193},{65,1},{129,65},{193,129... | collective-permute-start | bytes 1572872 | tf_op jit(solution)/shard_map/ppermute | solution.py:355
  85.6 25.9 %slice-start.2 = ((s8[9437184]{0:T(1024)(128)(4,1)}), s8[1048576]{0:T(1024)(128)(4,1)S(1)}, s32[]{:S(2)}) async-start(s8[9437184]{0:T(1024)(128)(4,1)} %bitcast.11), calls=%async_computation.2 | async-start | bytes 2097152
  89.3 6.3 %collective-permute-start.14 = (f32[2,152,768]{2,1,0:T(8,128)S(1)}, f32[2,152,768]{2,1,0:T(8,128)S(1)}, u32[]{:S(2)}, u32[]{:S(2)}) collective-permute-start(f32[2,152,768]{2,1,0:T(8,128)S(1)} %stage_c.1), channel_id=1, source_target_pairs={{0,1},{1,0},{2,3},{3,2},{4,5},{5,4},{6,7},{7,6},{8,9},{9,8},{10,11... | collective-permute-start | bytes 2801672 | tf_op jit(solution)/shard_map/ppermute | solution.py:362
  95.8 10.0 %collective-permute-start.17 = (bf16[256,768]{1,0:T(8,128)(2,1)S(1)}, bf16[256,768]{1,0:T(8,128)(2,1)S(1)}, u32[]{:S(2)}, u32[]{:S(2)}) collective-permute-start(bf16[256,768]{1,0:T(8,128)(2,1)S(1)} %merge.1), channel_id=1, source_target_pairs={{0,2},{1,6},{2,0},{3,4},{4,3},{5,7},{6,1},{7,5},{8,10},{9,14},{10,... | collective-permute-start | bytes 1179656 | tf_op jit(solution)/shard_map/ppermute | solution.py:369
  99.8 11.7 %collective-permute-start.16 = (bf16[256,768]{1,0:T(8,128)(2,1)S(1)}, bf16[256,768]{1,0:T(8,128)(2,1)S(1)}, u32[]{:S(2)}, u32[]{:S(2)}) collective-permute-start(bf16[256,768]{1,0:T(8,128)(2,1)S(1)} %merge.1), channel_id=1, source_target_pairs={{0,0},{1,4},{2,2},{3,6},{4,1},{5,5},{6,3},{7,7},{8,8},{9,12},{10,1... | collective-permute-start | bytes 1179656 | tf_op jit(solution)/shard_map/ppermute | solution.py:368
  115.3 3.9 %collective-permute-start.18 = (bf16[256,1536]{1,0:T(8,128)(2,1)S(1)}, bf16[256,1536]{1,0:T(8,128)(2,1)S(1)}, u32[]{:S(2)}, u32[]{:S(2)}) collective-permute-start(bf16[256,1536]{1,0:T(8,128)(2,1)S(1)} %project_send.1), channel_id=1, source_target_pairs={{0,1},{1,0},{2,3},{3,2},{4,5},{5,4},{6,7},{7,6},{8,9},{9,8},{10,11... | collective-permute-start | bytes 2359304 | tf_op jit(solution)/shard_map/ppermute | solution.py:373
  (3 other events, 2.4 us)

commit v5 on v4

--- a/solution.py
+++ b/solution.py
@@ -16,11 +16,11 @@
 MAX_ROW = HD + 16
 ROWS = HD + 24
 NEGATIVE = -1e30
-BLOCK = 4
 MASK_AT = 2 * HEADS
 UNIT_AT = MASK_AT + 1
 EXP2_SCALE = math.log2(math.e) / math.sqrt(HD)
-Z_ORDER = (0, -1, 1, -2, 2, -3, 3, 4)
+EARLY = (-1, 1, -2, 2)
+LATE = (0, -3, 3, 4)
 
 
 def vmem():
@@ -161,53 +161,63 @@
                 slot += 1
 
     for number in numbers:
-        state_ref = states[targets.index(number // 2)]
-        total = counts[number]
-        source = mine_ref if number < 2 else theirs_ref
-
-        def one_block(turn, carry, number=number, state_ref=state_ref, total=total, source=source):
-            row = number % 2
-            base = turn * BLOCK
-            first_at = list_ref[number, base]
-            at, values = [first_at], []
-            ones = jnp.ones((16, TILE), jnp.bfloat16)
-            for j in range(BLOCK):
-                if j:
-                    live = base + j < total
-                    at.append(jnp.where(live, list_ref[number, base + j], first_at))
-                value = jnp.concatenate([tiles_ref[at[j] + 2], ones], axis=0)
-                if j:
-                    value = value * jnp.where(live, 1.0, 0.0).astype(jnp.bfloat16)
-                values.append(value)
-            values = jnp.concatenate(values, axis=1)
-            keys = jnp.concatenate([tiles_ref[i] for i in at], axis=0)
-            chunks = [pl.ds(c * TILE, TILE) for c in range(HEADS)]
-            scores = [
-                lax.dot_general(
-                    keys,
-                    source[row * HEADS + h],
-                    (((1,), (1,)), ((), ())),
-                    preferred_element_type=jnp.float32,
-                )
-                for h in range(HEADS)
-            ]
-            probs = []
-            for lanes, score in zip(chunks, scores):
-                old_max = state_ref[row, pl.ds(MAX_ROW, 1), lanes]
-                new_max = jnp.maximum(old_max, jnp.max(score, axis=0, keepdims=True))
-                prob = jnp.exp2((score - new_max) * EXP2_SCALE).astype(jnp.bfloat16)
-                probs.append((prob, jnp.exp2((old_max - new_max) * EXP2_SCALE)))
-                state_ref[row, pl.ds(MAX_ROW, 8), lanes] = jnp.broadcast_to(new_max, (8, TILE))
-            for lanes, (prob, fade) in zip(chunks, probs):
-                part = lax.dot_general(
-                    values, prob, (((1,), (0,)), ((), ())), preferred_element_type=jnp.float32
-                )
-                state_ref[row, pl.ds(0, MAX_ROW), lanes] = (
-                    state_ref[row, pl.ds(0, MAX_ROW), lanes] * fade + part
-                )
+        list_ref[number, slot] = counts[number]
+
+    def block(target, row, base, size):
+        state_ref = states[targets.index(target)]
+        source = theirs_ref if target else mine_ref
+        number = 2 * target + row
+        at = [list_ref[number, base + j] for j in range(size - 1)]
+        live = base + size - 1 < list_ref[number, slot]
+        at.append(jnp.where(live, list_ref[number, base + size - 1], at[0]))
+        ones = jnp.ones((16, TILE), jnp.bfloat16)
+        values = [jnp.concatenate([tiles_ref[i + 2], ones], axis=0) for i in at]
+        values[-1] = values[-1] * jnp.where(live, 1.0, 0.0).astype(jnp.bfloat16)
+        values = jnp.concatenate(values, axis=1)
+        keys = jnp.concatenate([tiles_ref[i] for i in at], axis=0)
+        chunks = [pl.ds(h * TILE, TILE) for h in range(HEADS)]
+        scores = [
+            lax.dot_general(
+                keys,
+                source[row * HEADS + h],
+                (((1,), (1,)), ((), ())),
+                preferred_element_type=jnp.float32,
+            )
+            for h in range(HEADS)
+        ]
+        probs = []
+        for lanes, score in zip(chunks, scores):
+            old_max = state_ref[row, pl.ds(MAX_ROW, 1), lanes]
+            new_max = jnp.maximum(old_max, jnp.max(score, axis=0, keepdims=True))
+            prob = jnp.exp2((score - new_max) * EXP2_SCALE).astype(jnp.bfloat16)
+            probs.append((prob, jnp.exp2((old_max - new_max) * EXP2_SCALE)))
+            state_ref[row, pl.ds(MAX_ROW, 8), lanes] = jnp.broadcast_to(new_max, (8, TILE))
+        for lanes, (prob, fade) in zip(chunks, probs):
+            part = lax.dot_general(
+                values, prob, (((1,), (0,)), ((), ())), preferred_element_type=jnp.float32
+            )
+            state_ref[row, pl.ds(0, MAX_ROW), lanes] = (
+                state_ref[row, pl.ds(0, MAX_ROW), lanes] * fade + part
+            )
+
+    def one_query_tile(target, row):
+        total = list_ref[2 * target + row, slot]
+        blocks = (total + 1) // 4
+        rest = total - 4 * blocks
+
+        def full(turn, carry):
+            block(target, row, 4 * turn, 4)
             return carry
 
-        lax.fori_loop(0, (total + BLOCK - 1) // BLOCK, one_block, 0)
+        lax.fori_loop(0, blocks, full, 0)
+
+        @pl.when(rest > 0)
+        def _():
+            block(target, row, 4 * blocks, 2)
+
+    for target in targets:
+        for row in range(2):
+            one_query_tile(target, row)
 
 
 def stage(columns, near, parts, state, numbers, name):
@@ -227,7 +237,7 @@
         [smem()] + [vmem()] * (len(args) - 1),
         scratch=(
             pltpu.VMEM((2 * slots, TILE, TILE), jnp.bfloat16),
-            pltpu.SMEM((4, slots + BLOCK), jnp.int32),
+            pltpu.SMEM((4, slots + 1), jnp.int32),
         ),
         aliases=aliases,
         name=name,
@@ -320,47 +330,52 @@
     unit = pack(key_rows, value_rows)
     up, down = ring(NZ, 1), ring(NZ, -1)
     units = {-1: lax.ppermute(unit, YZ, turned(1)), 1: lax.ppermute(unit, YZ, turned(-1))}
-    queries, units[-1], units[1] = together((queries, units[-1], units[1]))
+    half_away = column_half(out_weight, 1 - yl)
+    units[-1], units[1], unit, half_away = together((units[-1], units[1], unit, half_away))
     mine = lax.ppermute(bundle(queries, tile_mask, unit), Y, turn)
-    half_away = column_half(out_weight, 1 - yl)
-    away = along_y(lambda yh, yl, core: (*next_y(yh, yl, 1 - 2 * core), core))
     units[-2] = lax.ppermute(units[-1], "z", up)
     units[2] = lax.ppermute(units[1], "z", down)
-    units[-2], units[2], half_away = together((units[-2], units[2], half_away))
+    units[-2], units[2] = together((units[-2], units[2]))
+    early = join([units[d] for d in EARLY])
+    forth, back = ring(NX, 1), ring(NX, -1)
+    early_before = lax.ppermute(early, "x", forth)
+    early_after = lax.ppermute(early, "x", back)
     units[-3] = lax.ppermute(units[-2], "z", up)
     units[3] = lax.ppermute(units[2], "z", down)
-    units[-3], units[3], mine, half_away = together((units[-3], units[3], mine, half_away))
-    far_weight = lax.ppermute(half_away, Y, away)
+    units[-3], units[3], mine = together((units[-3], units[3], mine))
     far = [
         lax.ppermute(units[-3][:2], "z", up),
         lax.ppermute(units[3][2:], "z", down),
     ]
     theirs = lax.ppermute(mine, "core", swap)
-    *far, theirs = together((*far, theirs))
+    *far, theirs, early_before, early_after = together((*far, theirs, early_before, early_after))
+    late = join([mine[UNIT_AT:], units[-3], units[3], *far])
+    late_before = lax.ppermute(late, "x", forth)
+    late_after = lax.ppermute(late, "x", back)
+    away = along_y(lambda yh, yl, core: (*next_y(yh, yl, 1 - 2 * core), core))
+    half_away, theirs = together((half_away, theirs))
+    far_weight = lax.ppermute(half_away, Y, away)
     place = jnp.pad(jnp.stack([x, z, core]).astype(jnp.int32), (0, 125))[None]
     masks = jnp.concatenate([mine[MASK_AT, :2], theirs[MASK_AT, :2]]).astype(jnp.int32)
     table = jnp.concatenate([masks, place])
 
-    units[0] = mine[UNIT_AT:]
-    column = join([units[d] for d in Z_ORDER[:-1]] + far)
-    forth, back = ring(NX, 1), ring(NX, -1)
-    before = lax.ppermute(column, "x", forth)
-    after = lax.ppermute(column, "x", back)
     near = (table, mine, theirs)
     every = (0, 1, 2, 3)
-    state = stage(((0, Z_ORDER),), near, [column], None, every, "stage_a")
-    before, after, *state = together((before, after, *state))
-    half = column.shape[0] // 2
-    far_low = lax.ppermute(before[:half], "x", forth)
-    far_high = lax.ppermute(after[half:], "x", back)
+    state = stage(((0, EARLY), (0, LATE)), near, [early, late], None, every, "own_column")
+    early_far = lax.ppermute(early_before, "x", forth)
+    state = stage(
+        ((-1, EARLY), (1, EARLY)), near, [early_before, early_after], state, every, "early"
+    )
+    late_before, late_after, *state = together((late_before, late_after, *state))
+    late_far = lax.ppermute(late_after, "x", back)
     keep, send = stage(
-        ((-1, Z_ORDER), (1, Z_ORDER)), near, [before, after], state, every, "stage_b"
-    )
-    far_low, far_high, keep, send = together((far_low, far_high, keep, send))
-    last = (((2, Z_ORDER),), near, [far_low, far_high])
-    (send,) = stage(*last, (send,), (2, 3), "stage_c")
+        ((-1, LATE), (1, LATE)), near, [late_before, late_after], state, every, "late"
+    )
+    early_far, late_far, keep, send = together((early_far, late_far, keep, send))
+    last = (((2, EARLY), (2, LATE)), near, [early_far, late_far])
+    (send,) = stage(*last, (send,), (2, 3), "last_send")
     received = lax.ppermute(send, "core", swap)
-    (keep,) = stage(*last, (keep,), (0, 1), "stage_d")
+    (keep,) = stage(*last, (keep,), (0, 1), "last_keep")
     keep, received, far_weight = together((keep, received, far_weight))
     shape = jax.ShapeDtypeStruct((2 * TILE, WIDE), jnp.bfloat16)
     attended = call(merge_kernel, shape, (keep, received), [vmem()] * 2, name="merge")

time: 121 us -> 130 us (1.074)
  Pallas kernels: 34.5 us -> 39.1 us
  starting transfers between devices: 36.8 us -> 41 us
  waiting for transfers between devices: 40.3 us -> 43.1 us
  local copies, waits for them, and re-layouts: 8.2 us -> 5.41 us
    ppermute x1, waiting for transfers between devices: 0.01 us -> 15.9 us  [per_device(): far_weight = lax.ppermute(half_away, Y, away)]
    ppermute x4 -> x6, waiting for transfers between devices: 18.5 us -> 7.55 us  [the longest x1 4.47 us: per_device(): early_before = lax.ppermute(early, 'x', forth)]
    ppermute x1, waiting for transfers between devices: 6.06 us -> 0.01 us  [per_device(): lax.ppermute(unit, YZ, turned(1))]
    ppermute x1, starting transfers between devices: 0.01 us -> 5.73 us  [per_device(): lax.ppermute(unit, YZ, turned(1))]
    ppermute x1, starting transfers between devices: 9.67 us -> 4.03 us  [per_device(): lax.ppermute(unit, YZ, turned(-1))]
    ppermute x1, starting transfers between devices: 0.01 us -> 4.79 us  [per_device(): far_weight = lax.ppermute(half_away, Y, away)]
    pallas_call x12 -> x14, Pallas kernels: 34.5 us -> 39.1 us  [call(): pl.pallas_call(kernel, out_shape=out_shape, in_specs=in_specs, out_specs=...]
    ppermute x1, starting transfers between devices: 4 us -> 0.09 us  [per_device(): lax.ppermute(attended, Y, along_y(lambda yh, yl, core: (core, 1 - yl, yh)))]
  transfers between devices with their start and end apart: 19 -> 21, of which waited for: 9 -> 10; matrix products, arithmetic and copies ran while one was open for 1% -> 0% of each run, Pallas kernels for 24% -> 26%
where the time goes in v5:
time: 130 us; the launch traced here: 129 us
  waiting for transfers between devices  43.1 us (33%)
  starting transfers between devices  41 us (32%)
  Pallas kernels  39.1 us (30%)
  local copies, waits for them, and re-layouts  5.41 us (4%)
    pallas_call x14, Pallas kernels, call(): pl.pallas_call(kernel, out_shape=out_shape, in_specs=in_specs, out_specs=...  39.1 us
    ppermute x1, waiting for transfers between devices, per_device(): far_weight = lax.ppermute(half_away, Y, away)  15.9 us
    ppermute x1, waiting for transfers between devices, per_device(): near_part = lax.ppermute(attended, Y, turn)  8.55 us
    ppermute x1, starting transfers between devices, per_device(): near_part = lax.ppermute(attended, Y, turn)  5.82 us
    ppermute x1, starting transfers between devices, per_device(): lax.ppermute(unit, YZ, turned(1))  5.73 us
    unnamed x16, local copies, waits for them, and re-layouts  5.38 us
    ppermute x1, starting transfers between devices, per_device(): far_weight = lax.ppermute(half_away, Y, away)  4.79 us
    ppermute x1, waiting for transfers between devices, per_device(): early_before = lax.ppermute(early, 'x', forth)  4.47 us
  transfers between devices with their start and end apart: 21, of which 10 were waited for; matrix products, arithmetic and copies ran while one was open for 0% of the time, Pallas kernels for 26%

profile of v5, /device:TPU:1, one launch (start us, length us, event | category | flops | bytes accessed | tf_op | source)
XLA Modules:
  0.0 129.2 jit_solution(13799270565171369636)
XLA Ops:
  2.0 5.7 %collective-permute-start = (bf16[4,128,128]{2,1,0:T(8,128)(2,1)S(1)}, bf16[4,128,128]{2,1,0:T(8,128)(2,1)S(1)}, u32[]{:S(2)}, u32[]{:S(2)}) collective-permute-start(bf16[4,128,128]{2,1,0:T(8,128)(2,1)S(1)} %pack.1.unit_ref), channel_id=1, source_target_pairs={{0,8},{1,12},{2,10},{3,14},{4,9},{5,13},{6,11},{7,15},{8,16},{9,20... | collective-permute-start | bytes 393224 | tf_op jit(solution)/shard_map/ppermute | solution.py:332
  7.7 4.0 %collective-permute-start.1 = (bf16[4,128,128]{2,1,0:T(8,128)(2,1)S(1)}, bf16[4,128,128]{2,1,0:T(8,128)(2,1)S(1)}, u32[]{:S(2)}, u32[]{:S(2)}) collective-permute-start(bf16[4,128,128]{2,1,0:T(8,128)(2,1)S(1)} %pack.1.unit_ref), channel_id=1, source_target_pairs={{0,56},{1,60},{2,58},{3,62},{4,57},{5,61},{6,59},{7,63},{8,0},{9,4... | collective-permute-start | bytes 393224 | tf_op jit(solution)/shard_map/ppermute | solution.py:332
  11.7 3.7 %copy-done = bf16[768,6144]{1,0:T(8,128)(2,1)S(1)} copy-done((bf16[768,6144]{1,0:T(8,128)(2,1)S(1)}, bf16[768,6144]{1,0:T(8,128)(2,1)}, u32[]{:S(2)}) %copy-start) | copy-done | bytes 9437208
  15.4 2.7 %column_half.1 = bf16[768,3072]{1,0:T(8,128)(2,1)} custom-call(s32[1]{0:T(128)} %bitcast.2.half_ref, bf16[768,6144]{1,0:T(8,128)(2,1)S(1)} %copy-done), custom_call_target="tpu_custom_call" | custom-call | tf_op jit(solution)/shard_map/column_half/pallas_call | solution.py:39
  20.6 4.0 %collective-permute-start.3 = (bf16[4,128,128]{2,1,0:T(8,128)(2,1)S(1)}, bf16[4,128,128]{2,1,0:T(8,128)(2,1)S(1)}, u32[]{:S(2)}, u32[]{:S(2)}) collective-permute-start(bf16[4,128,128]{2,1,0:T(8,128)(2,1)S(1)} %collective-permute-done.1.refs_1_), channel_id=1, source_target_pairs={{0,56},{8,0},{16,8},{24,16},{32,24},{40,32},{48,40},{56,48},{1,57}... | collective-permute-start | bytes 393224 | tf_op jit(solution)/shard_map/ppermute | solution.py:337
  24.7 2.3 %collective-permute-done.2.refs_2_ = bf16[4,128,128]{2,1,0:T(8,128)(2,1)S(1)} collective-permute-done((bf16[4,128,128]{2,1,0:T(8,128)(2,1)S(1)}, bf16[4,128,128]{2,1,0:T(8,128)(2,1)S(1)}, u32[]{:S(2)}, u32[]{:S(2)}) %collective-permute-start.2) | collective-permute-done | bytes 131104 | tf_op jit(solution)/shard_map/ppermute | solution.py:336
  27.0 2.8 %collective-permute-start.5 = (bf16[4,128,128]{2,1,0:T(8,128)(2,1)S(1)}, bf16[4,128,128]{2,1,0:T(8,128)(2,1)S(1)}, u32[]{:S(2)}, u32[]{:S(2)}) collective-permute-start(bf16[4,128,128]{2,1,0:T(8,128)(2,1)S(1)} %collective-permute-done.3.refs_3_), channel_id=1, source_target_pairs={{0,56},{8,0},{16,8},{24,16},{32,24},{40,32},{48,40},{56,48},{1,57}... | collective-permute-start | bytes 393224 | tf_op jit(solution)/shard_map/ppermute | solution.py:344
  29.7 2.4 %collective-permute-done.4.refs_1_ = bf16[4,128,128]{2,1,0:T(8,128)(2,1)S(1)} collective-permute-done((bf16[4,128,128]{2,1,0:T(8,128)(2,1)S(1)}, bf16[4,128,128]{2,1,0:T(8,128)(2,1)S(1)}, u32[]{:S(2)}, u32[]{:S(2)}) %collective-permute-start.4) | collective-permute-done | bytes 131104 | tf_op jit(solution)/shard_map/ppermute | solution.py:343
  35.5 3.6 %collective-permute-start.7 = (bf16[2,128,128]{2,1,0:T(8,128)(2,1)S(1)}, bf16[2,128,128]{2,1,0:T(8,128)(2,1)S(1)}, u32[]{:S(2)}, u32[]{:S(2)}) collective-permute-start(bf16[2,128,128]{2,1,0:T(8,128)(2,1)S(1)} %slice.16), channel_id=1, source_target_pairs={{0,8},{8,16},{16,24},{24,32},{32,40},{40,48},{48,56},{56,0},{1,9},... | collective-permute-start | bytes 196616 | tf_op jit(solution)/shard_map/ppermute | solution.py:347
  40.5 2.1 %collective-permute-done.8.refs_4_ = bf16[2,128,128]{2,1,0:T(8,128)(2,1)S(1)} collective-permute-done((bf16[2,128,128]{2,1,0:T(8,128)(2,1)S(1)}, bf16[2,128,128]{2,1,0:T(8,128)(2,1)S(1)}, u32[]{:S(2)}, u32[]{:S(2)}) %collective-permute-start.8) | collective-permute-done | bytes 65568 | tf_op jit(solution)/shard_map/ppermute | solution.py:348
  42.5 4.5 %collective-permute-done.10.refs_3_ = bf16[16,128,128]{2,1,0:T(8,128)(2,1)S(1)} collective-permute-done((bf16[16,128,128]{2,1,0:T(8,128)(2,1)S(1)}, bf16[16,128,128]{2,1,0:T(8,128)(2,1)S(1)}, u32[]{:S(2)}, u32[]{:S(2)}) %collective-permute-start.10) | collective-permute-done | bytes 524320 | tf_op jit(solution)/shard_map/ppermute | solution.py:341
  47.0 4.8 %collective-permute-start.17 = (bf16[768,3072]{1,0:T(8,128)(2,1)}, bf16[768,3072]{1,0:T(8,128)(2,1)}, u32[]{:S(2)}, u32[]{:S(2)}) collective-permute-start(bf16[768,3072]{1,0:T(8,128)(2,1)} %column_half.1), channel_id=1, source_target_pairs={{0,2},{1,7},{2,4},{3,1},{4,6},{5,3},{6,0},{7,5},{8,10},{9,15},{10,... | collective-permute-start | bytes 14155784 | tf_op jit(solution)/shard_map/ppermute | solution.py:357
  54.7 7.4 %own_column.1 = (f32[2,152,768]{2,1,0:T(8,128)S(1)}, f32[2,152,768]{2,1,0:T(8,128)S(1)}) custom-call(s32[5,128]{1,0:T(8,128)S(1)} %pad_add_fusion.refs_0_, bf16[17,128,128]{2,1,0:T(8,128)(2,1)S(1)} %collective-permute-done.6.refs_1_, bf16[17,128,128]{2,1,0:T(8,128)(2,1)S(1)} %collective-permute-done.9.refs_2_, bf16[16,128,128]{2,1,0:T(8,128)(2,1)S(1)} %join.2.refs_3_, ...), custom_call_target="tpu_custom_call" | custom-call | tf_op jit(solution)/shard_map/own_column/pallas_call | solution.py:39
  62.3 5.6 %early.1 = (f32[2,152,768]{2,1,0:T(8,128)S(1)}, f32[2,152,768]{2,1,0:T(8,128)S(1)}) custom-call(s32[5,128]{1,0:T(8,128)S(1)} %pad_add_fusion.refs_0_, bf16[17,128,128]{2,1,0:T(8,128)(2,1)S(1)} %collective-permute-done.6.refs_1_, bf16[17,128,128]{2,1,0:T(8,128)(2,1)S(1)} %collective-permute-done.9.refs_2_, ...), custom_call_target="tpu_custom_call", output_to_operand_aliasing={{0}: (5, {}), {1}: (6, {})} | custom-call | tf_op jit(solution)/shard_map/early/pallas_call | solution.py:39
  69.9 7.9 %late.1 = (f32[2,152,768]{2,1,0:T(8,128)S(1)}, f32[2,152,768]{2,1,0:T(8,128)S(1)}) custom-call(s32[5,128]{1,0:T(8,128)S(1)} %pad_add_fusion.refs_0_, bf16[17,128,128]{2,1,0:T(8,128)(2,1)S(1)} %collective-permute-done.6.refs_1_, bf16[17,128,128]{2,1,0:T(8,128)(2,1)S(1)} %collective-permute-done.9.refs_2_, ...), custom_call_target="tpu_custom_call", output_to_operand_aliasing={{0}: (5, {}), {1}: (6, {})} | custom-call | tf_op jit(solution)/shard_map/late/pallas_call | solution.py:39
  77.8 3.1 %collective-permute-done.15.refs_4_ = bf16[16,128,128]{2,1,0:T(8,128)(2,1)S(1)} collective-permute-done((bf16[16,128,128]{2,1,0:T(8,128)(2,1)S(1)}, bf16[16,128,128]{2,1,0:T(8,128)(2,1)S(1)}, u32[]{:S(2)}, u32[]{:S(2)}) %collective-permute-start.15) | collective-permute-done | bytes 524320 | tf_op jit(solution)/shard_map/ppermute | solution.py:370
  80.9 3.5 %last_send.1 = f32[2,152,768]{2,1,0:T(8,128)S(1)} custom-call(s32[5,128]{1,0:T(8,128)S(1)} %pad_add_fusion.refs_0_, bf16[17,128,128]{2,1,0:T(8,128)(2,1)S(1)} %collective-permute-done.6.refs_1_, bf16[17,128,128]{2,1,0:T(8,128)(2,1)S(1)} %collective-permute-done.9.refs_2_, ...), custom_call_target="tpu_custom_call", output_to_operand_aliasing={{}: (5, {})} | custom-call | tf_op jit(solution)/shard_map/last_send/pallas_call | solution.py:39
  84.5 2.8 %last_keep.1.own_ref = f32[2,152,768]{2,1,0:T(8,128)S(1)} custom-call(s32[5,128]{1,0:T(8,128)S(1)} %pad_add_fusion.refs_0_, bf16[17,128,128]{2,1,0:T(8,128)(2,1)S(1)} %collective-permute-done.6.refs_1_, bf16[17,128,128]{2,1,0:T(8,128)(2,1)S(1)} %collective-permute-done.9.refs_2_, ...), custom_call_target="tpu_custom_call", output_to_operand_aliasing={{}: (5, {})} | custom-call | tf_op jit(solution)/shard_map/last_keep/pallas_call | solution.py:39
  87.3 15.9 %collective-permute-done.17.refs_4_ = bf16[768,3072]{1,0:T(8,128)(2,1)} collective-permute-done((bf16[768,3072]{1,0:T(8,128)(2,1)}, bf16[768,3072]{1,0:T(8,128)(2,1)}, u32[]{:S(2)}, u32[]{:S(2)}) %collective-permute-start.17) | collective-permute-done | bytes 4718624 | tf_op jit(solution)/shard_map/ppermute | solution.py:357
  103.4 5.8 %collective-permute-start.18 = (bf16[256,768]{1,0:T(8,128)(2,1)S(1)}, bf16[256,768]{1,0:T(8,128)(2,1)S(1)}, u32[]{:S(2)}, u32[]{:S(2)}) collective-permute-start(bf16[256,768]{1,0:T(8,128)(2,1)S(1)} %merge.1), channel_id=1, source_target_pairs={{0,0},{1,4},{2,2},{3,6},{4,1},{5,5},{6,3},{7,7},{8,8},{9,12},{10,1... | collective-permute-start | bytes 1179656 | tf_op jit(solution)/shard_map/ppermute | solution.py:383
  109.4 8.5 %collective-permute-done.18.refs_1_ = bf16[256,768]{1,0:T(8,128)(2,1)S(1)} collective-permute-done((bf16[256,768]{1,0:T(8,128)(2,1)S(1)}, bf16[256,768]{1,0:T(8,128)(2,1)S(1)}, u32[]{:S(2)}, u32[]{:S(2)}) %collective-permute-start.18) | collective-permute-done | bytes 393248 | tf_op jit(solution)/shard_map/ppermute | solution.py:383
  118.0 2.5 %collective-permute-done.19.refs_2_ = bf16[256,768]{1,0:T(8,128)(2,1)S(1)} collective-permute-done((bf16[256,768]{1,0:T(8,128)(2,1)S(1)}, bf16[256,768]{1,0:T(8,128)(2,1)S(1)}, u32[]{:S(2)}, u32[]{:S(2)}) %collective-permute-start.19) | collective-permute-done | bytes 393248 | tf_op jit(solution)/shard_map/ppermute | solution.py:384
  120.4 3.8 %project_send.1 = bf16[256,1536]{1,0:T(8,128)(2,1)S(1)} custom-call(s32[2]{0:T(128)S(1)} %pad_add_fusion.1.refs_0_, bf16[256,768]{1,0:T(8,128)(2,1)S(1)} %collective-permute-done.18.refs_1_, bf16[256,768]{1,0:T(8,128)(2,1)S(1)} %collective-permute-done.19.refs_2_, bf16[768,6144]{1,0:T(8,128)(2,1)S(1)} %bitcast.12, ...), custom_call_target="tpu_custom_call" | custom-call | tf_op jit(solution)/shard_map/project_send/pallas_call | solution.py:39
  124.3 3.8 %project_keep.1.keep_ref = f32[256,1536]{1,0:T(8,128)S(1)} custom-call(s32[2]{0:T(128)S(1)} %pad_add_fusion.1.refs_0_, bf16[256,768]{1,0:T(8,128)(2,1)S(1)} %collective-permute-done.18.refs_1_, bf16[256,768]{1,0:T(8,128)(2,1)S(1)} %collective-permute-done.19.refs_2_, bf16[768,6144]{1,0:T(8,128)(2,1)S(1)} %bitcast.12, ...), custom_call_target="tpu_custom_call" | custom-call | tf_op jit(solution)/shard_map/project_keep/pallas_call | solution.py:39
  (59 shorter events, 15.8 us)
Async XLA Ops:
  2.0 16.2 %collective-permute-start = (bf16[4,128,128]{2,1,0:T(8,128)(2,1)S(1)}, bf16[4,128,128]{2,1,0:T(8,128)(2,1)S(1)}, u32[]{:S(2)}, u32[]{:S(2)}) collective-permute-start(bf16[4,128,128]{2,1,0:T(8,128)(2,1)S(1)} %pack.1.unit_ref), channel_id=1, source_target_pairs={{0,8},{1,12},{2,10},{3,14},{4,9},{5,13},{6,11},{7,15},{8,16},{9,20... | collective-permute-start | bytes 393224 | tf_op jit(solution)/shard_map/ppermute | solution.py:332
  7.7 10.4 %collective-permute-start.1 = (bf16[4,128,128]{2,1,0:T(8,128)(2,1)S(1)}, bf16[4,128,128]{2,1,0:T(8,128)(2,1)S(1)}, u32[]{:S(2)}, u32[]{:S(2)}) collective-permute-start(bf16[4,128,128]{2,1,0:T(8,128)(2,1)S(1)} %pack.1.unit_ref), channel_id=1, source_target_pairs={{0,56},{1,60},{2,58},{3,62},{4,57},{5,61},{6,59},{7,63},{8,0},{9,4... | collective-permute-start | bytes 393224 | tf_op jit(solution)/shard_map/ppermute | solution.py:332
  18.3 14.4 %collective-permute-start.6 = (bf16[17,128,128]{2,1,0:T(8,128)(2,1)S(1)}, bf16[17,128,128]{2,1,0:T(8,128)(2,1)S(1)}, u32[]{:S(2)}, u32[]{:S(2)}) collective-permute-start(bf16[17,128,128]{2,1,0:T(8,128)(2,1)S(1)} %bundle.1), channel_id=1, source_target_pairs={{0,0},{1,4},{2,2},{3,6},{4,1},{5,5},{6,3},{7,7},{8,8},{9,12},{10,1... | collective-permute-start | bytes 1671176 | tf_op jit(solution)/shard_map/ppermute | solution.py:335
  20.2 6.8 %collective-permute-start.2 = (bf16[4,128,128]{2,1,0:T(8,128)(2,1)S(1)}, bf16[4,128,128]{2,1,0:T(8,128)(2,1)S(1)}, u32[]{:S(2)}, u32[]{:S(2)}) collective-permute-start(bf16[4,128,128]{2,1,0:T(8,128)(2,1)S(1)} %collective-permute-done.refs_0_), channel_id=1, source_target_pairs={{0,8},{8,16},{16,24},{24,32},{32,40},{40,48},{48,56},{56,0},{1,9},... | collective-permute-start | bytes 393224 | tf_op jit(solution)/shard_map/ppermute | solution.py:336
  20.6 6.3 %collective-permute-start.3 = (bf16[4,128,128]{2,1,0:T(8,128)(2,1)S(1)}, bf16[4,128,128]{2,1,0:T(8,128)(2,1)S(1)}, u32[]{:S(2)}, u32[]{:S(2)}) collective-permute-start(bf16[4,128,128]{2,1,0:T(8,128)(2,1)S(1)} %collective-permute-done.1.refs_1_), channel_id=1, source_target_pairs={{0,56},{8,0},{16,8},{24,16},{32,24},{40,32},{48,40},{56,48},{1,57}... | collective-permute-start | bytes 393224 | tf_op jit(solution)/shard_map/ppermute | solution.py:337
  26.9 5.1 %collective-permute-start.4 = (bf16[4,128,128]{2,1,0:T(8,128)(2,1)S(1)}, bf16[4,128,128]{2,1,0:T(8,128)(2,1)S(1)}, u32[]{:S(2)}, u32[]{:S(2)}) collective-permute-start(bf16[4,128,128]{2,1,0:T(8,128)(2,1)S(1)} %collective-permute-done.2.refs_2_), channel_id=1, source_target_pairs={{0,8},{8,16},{16,24},{24,32},{32,40},{40,48},{48,56},{56,0},{1,9},... | collective-permute-start | bytes 393224 | tf_op jit(solution)/shard_map/ppermute | solution.py:343
  27.0 5.7 %collective-permute-start.5 = (bf16[4,128,128]{2,1,0:T(8,128)(2,1)S(1)}, bf16[4,128,128]{2,1,0:T(8,128)(2,1)S(1)}, u32[]{:S(2)}, u32[]{:S(2)}) collective-permute-start(bf16[4,128,128]{2,1,0:T(8,128)(2,1)S(1)} %collective-permute-done.3.refs_3_), channel_id=1, source_target_pairs={{0,56},{8,0},{16,8},{24,16},{32,24},{40,32},{48,40},{56,48},{1,57}... | collective-permute-start | bytes 393224 | tf_op jit(solution)/shard_map/ppermute | solution.py:344
  32.7 14.3 %collective-permute-start.9 = (bf16[17,128,128]{2,1,0:T(8,128)(2,1)S(1)}, bf16[17,128,128]{2,1,0:T(8,128)(2,1)S(1)}, u32[]{:S(2)}, u32[]{:S(2)}) collective-permute-start(bf16[17,128,128]{2,1,0:T(8,128)(2,1)S(1)} %collective-permute-done.6.refs_1_), channel_id=1, source_target_pairs={{0,1},{1,0},{2,3},{3,2},{4,5},{5,4},{6,7},{7,6},{8,9},{9,8},{10,11... | collective-permute-start | bytes 1671176 | tf_op jit(solution)/shard_map/ppermute | solution.py:350
  32.7 14.3 %collective-permute-start.10 = (bf16[16,128,128]{2,1,0:T(8,128)(2,1)S(1)}, bf16[16,128,128]{2,1,0:T(8,128)(2,1)S(1)}, u32[]{:S(2)}, u32[]{:S(2)}) collective-permute-start(bf16[16,128,128]{2,1,0:T(8,128)(2,1)S(1)} %join.2.refs_3_), channel_id=1, source_target_pairs={{0,64},{64,128},{128,192},{192,0},{1,65},{65,129},{129,193},{193,1... | collective-permute-start | bytes 1572872 | tf_op jit(solution)/shard_map/ppermute | solution.py:341
  34.0 13.0 %collective-permute-start.11 = (bf16[16,128,128]{2,1,0:T(8,128)(2,1)S(1)}, bf16[16,128,128]{2,1,0:T(8,128)(2,1)S(1)}, u32[]{:S(2)}, u32[]{:S(2)}) collective-permute-start(bf16[16,128,128]{2,1,0:T(8,128)(2,1)S(1)} %join.2.refs_3_), channel_id=1, source_target_pairs={{0,192},{64,0},{128,64},{192,128},{1,193},{65,1},{129,65},{193,129... | collective-permute-start | bytes 1572872 | tf_op jit(solution)/shard_map/ppermute | solution.py:342
  35.5 4.9 %collective-permute-start.7 = (bf16[2,128,128]{2,1,0:T(8,128)(2,1)S(1)}, bf16[2,128,128]{2,1,0:T(8,128)(2,1)S(1)}, u32[]{:S(2)}, u32[]{:S(2)}) collective-permute-start(bf16[2,128,128]{2,1,0:T(8,128)(2,1)S(1)} %slice.16), channel_id=1, source_target_pairs={{0,8},{8,16},{16,24},{24,32},{32,40},{40,48},{48,56},{56,0},{1,9},... | collective-permute-start | bytes 196616 | tf_op jit(solution)/shard_map/ppermute | solution.py:347
  39.1 3.4 %collective-permute-start.8 = (bf16[2,128,128]{2,1,0:T(8,128)(2,1)S(1)}, bf16[2,128,128]{2,1,0:T(8,128)(2,1)S(1)}, u32[]{:S(2)}, u32[]{:S(2)}) collective-permute-start(bf16[2,128,128]{2,1,0:T(8,128)(2,1)S(1)} %slice.17), channel_id=1, source_target_pairs={{0,56},{8,0},{16,8},{24,16},{32,24},{40,32},{48,40},{56,48},{1,57}... | collective-permute-start | bytes 196616 | tf_op jit(solution)/shard_map/ppermute | solution.py:348
  47.0 56.2 %collective-permute-start.17 = (bf16[768,3072]{1,0:T(8,128)(2,1)}, bf16[768,3072]{1,0:T(8,128)(2,1)}, u32[]{:S(2)}, u32[]{:S(2)}) collective-permute-start(bf16[768,3072]{1,0:T(8,128)(2,1)} %column_half.1), channel_id=1, source_target_pairs={{0,2},{1,7},{2,4},{3,1},{4,6},{5,3},{6,0},{7,5},{8,10},{9,15},{10,... | collective-permute-start | bytes 14155784 | tf_op jit(solution)/shard_map/ppermute | solution.py:357
  51.9 68.5 %slice-start = ((s8[9437184]{0:T(1024)(128)(4,1)}), s8[4194304]{0:T(1024)(128)(4,1)S(1)}, s32[]{:S(2)}) async-start(s8[9437184]{0:T(1024)(128)(4,1)} %bitcast.11), calls=%async_computation | async-start | bytes 8388608
  52.0 16.0 %collective-permute-start.13 = (bf16[16,128,128]{2,1,0:T(8,128)(2,1)S(1)}, bf16[16,128,128]{2,1,0:T(8,128)(2,1)S(1)}, u32[]{:S(2)}, u32[]{:S(2)}) collective-permute-start(bf16[16,128,128]{2,1,0:T(8,128)(2,1)S(1)} %join.3.refs_4_), channel_id=1, source_target_pairs={{0,64},{64,128},{128,192},{192,0},{1,65},{65,129},{129,193},{193,1... | collective-permute-start | bytes 1572872 | tf_op jit(solution)/shard_map/ppermute | solution.py:353
  52.9 15.0 %collective-permute-start.14 = (bf16[16,128,128]{2,1,0:T(8,128)(2,1)S(1)}, bf16[16,128,128]{2,1,0:T(8,128)(2,1)S(1)}, u32[]{:S(2)}, u32[]{:S(2)}) collective-permute-start(bf16[16,128,128]{2,1,0:T(8,128)(2,1)S(1)} %join.3.refs_4_), channel_id=1, source_target_pairs={{0,192},{64,0},{128,64},{192,128},{1,193},{65,1},{129,65},{193,129... | collective-permute-start | bytes 1572872 | tf_op jit(solution)/shard_map/ppermute | solution.py:354
  62.2 15.6 %collective-permute-start.12 = (bf16[16,128,128]{2,1,0:T(8,128)(2,1)S(1)}, bf16[16,128,128]{2,1,0:T(8,128)(2,1)S(1)}, u32[]{:S(2)}, u32[]{:S(2)}) collective-permute-start(bf16[16,128,128]{2,1,0:T(8,128)(2,1)S(1)} %collective-permute-done.10.refs_3_), channel_id=1, source_target_pairs={{0,64},{64,128},{128,192},{192,0},{1,65},{65,129},{129,193},{193,1... | collective-permute-start | bytes 1572872 | tf_op jit(solution)/shard_map/ppermute | solution.py:365
  62.3 58.2 %slice-start.1 = ((s8[9437184]{0:T(1024)(128)(4,1)}), s8[4194304]{0:T(1024)(128)(4,1)S(1)}, s32[]{:S(2)}) async-start(s8[9437184]{0:T(1024)(128)(4,1)} %bitcast.11), calls=%async_computation.1 | async-start | bytes 8388608
  67.9 12.9 %collective-permute-start.15 = (bf16[16,128,128]{2,1,0:T(8,128)(2,1)S(1)}, bf16[16,128,128]{2,1,0:T(8,128)(2,1)S(1)}, u32[]{:S(2)}, u32[]{:S(2)}) collective-permute-start(bf16[16,128,128]{2,1,0:T(8,128)(2,1)S(1)} %collective-permute-done.14.refs_4_), channel_id=1, source_target_pairs={{0,192},{64,0},{128,64},{192,128},{1,193},{65,1},{129,65},{193,129... | collective-permute-start | bytes 1572872 | tf_op jit(solution)/shard_map/ppermute | solution.py:370
  80.9 39.6 %slice-start.2 = ((s8[9437184]{0:T(1024)(128)(4,1)}), s8[1048576]{0:T(1024)(128)(4,1)S(1)}, s32[]{:S(2)}) async-start(s8[9437184]{0:T(1024)(128)(4,1)} %bitcast.11), calls=%async_computation.2 | async-start | bytes 2097152
  84.4 2.9 %collective-permute-start.16 = (f32[2,152,768]{2,1,0:T(8,128)S(1)}, f32[2,152,768]{2,1,0:T(8,128)S(1)}, u32[]{:S(2)}, u32[]{:S(2)}) collective-permute-start(f32[2,152,768]{2,1,0:T(8,128)S(1)} %last_send.1), channel_id=1, source_target_pairs={{0,1},{1,0},{2,3},{3,2},{4,5},{5,4},{6,7},{7,6},{8,9},{9,8},{10,11... | collective-permute-start | bytes 2801672 | tf_op jit(solution)/shard_map/ppermute | solution.py:377
  103.4 14.6 %collective-permute-start.18 = (bf16[256,768]{1,0:T(8,128)(2,1)S(1)}, bf16[256,768]{1,0:T(8,128)(2,1)S(1)}, u32[]{:S(2)}, u32[]{:S(2)}) collective-permute-start(bf16[256,768]{1,0:T(8,128)(2,1)S(1)} %merge.1), channel_id=1, source_target_pairs={{0,0},{1,4},{2,2},{3,6},{4,1},{5,5},{6,3},{7,7},{8,8},{9,12},{10,1... | collective-permute-start | bytes 1179656 | tf_op jit(solution)/shard_map/ppermute | solution.py:383
  109.2 11.2 %collective-permute-start.19 = (bf16[256,768]{1,0:T(8,128)(2,1)S(1)}, bf16[256,768]{1,0:T(8,128)(2,1)S(1)}, u32[]{:S(2)}, u32[]{:S(2)}) collective-permute-start(bf16[256,768]{1,0:T(8,128)(2,1)S(1)} %merge.1), channel_id=1, source_target_pairs={{0,2},{1,6},{2,0},{3,4},{4,3},{5,7},{6,1},{7,5},{8,10},{9,14},{10,... | collective-permute-start | bytes 1179656 | tf_op jit(solution)/shard_map/ppermute | solution.py:384
  124.2 3.9 %collective-permute-start.20 = (bf16[256,1536]{1,0:T(8,128)(2,1)S(1)}, bf16[256,1536]{1,0:T(8,128)(2,1)S(1)}, u32[]{:S(2)}, u32[]{:S(2)}) collective-permute-start(bf16[256,1536]{1,0:T(8,128)(2,1)S(1)} %project_send.1), channel_id=1, source_target_pairs={{0,1},{1,0},{2,3},{3,2},{4,5},{5,4},{6,7},{7,6},{8,9},{9,8},{10,11... | collective-permute-start | bytes 2359304 | tf_op jit(solution)/shard_map/ppermute | solution.py:388
  (5 other events, 10.9 us)

commit v6 on v5

--- a/solution.py
+++ b/solution.py
@@ -35,6 +35,10 @@
     return pl.BlockSpec(memory_space=pl.ANY)
 
 
+def in_hbm(x):
+    return pltpu.with_memory_space_constraint(x, pltpu.HBM)
+
+
 def call(kernel, out_shape, args, in_specs, scratch=(), aliases=None, name=None, flops=0):
     return pl.pallas_call(
         kernel,
@@ -43,7 +47,7 @@
         out_specs=jax.tree.map(lambda s: vmem(), out_shape),
         scratch_shapes=list(scratch),
         input_output_aliases=aliases or {},
-        compiler_params=pltpu.CompilerParams(vmem_limit_bytes=24 * 1024 * 1024),
+        compiler_params=pltpu.CompilerParams(vmem_limit_bytes=14 * 1024 * 1024),
         cost_estimate=pl.CostEstimate(flops=flops, transcendentals=0, bytes_accessed=0),
         name=name,
     )(*args)
@@ -69,7 +73,7 @@
     return call(
         pack_kernel,
         jax.ShapeDtypeStruct((4, TILE, TILE), jnp.bfloat16),
-        (key_rows, value_rows),
+        (in_hbm(key_rows), in_hbm(value_rows)),
         [hbm()] * 2,
         scratch=(rows, rows, pltpu.SemaphoreType.DMA((2,))),
         name="pack",
@@ -111,7 +115,7 @@
     return call(
         half_kernel,
         jax.ShapeDtypeStruct((source.shape[0], source.shape[1] // 2), source.dtype),
-        (number.reshape(1).astype(jnp.int32), source),
+        (number.reshape(1).astype(jnp.int32), in_hbm(source)),
         [smem(), hbm()],
         scratch=(pltpu.SemaphoreType.DMA((8,)),),
         name="column_half",
@@ -335,26 +339,21 @@
     mine = lax.ppermute(bundle(queries, tile_mask, unit), Y, turn)
     units[-2] = lax.ppermute(units[-1], "z", up)
     units[2] = lax.ppermute(units[1], "z", down)
-    units[-2], units[2] = together((units[-2], units[2]))
+    units[-2], units[2], mine, half_away = together((units[-2], units[2], mine, half_away))
+    away = along_y(lambda yh, yl, core: (*next_y(yh, yl, 1 - 2 * core), core))
+    far_weight = lax.ppermute(half_away, Y, away)
     early = join([units[d] for d in EARLY])
     forth, back = ring(NX, 1), ring(NX, -1)
     early_before = lax.ppermute(early, "x", forth)
     early_after = lax.ppermute(early, "x", back)
     units[-3] = lax.ppermute(units[-2], "z", up)
     units[3] = lax.ppermute(units[2], "z", down)
-    units[-3], units[3], mine = together((units[-3], units[3], mine))
-    far = [
-        lax.ppermute(units[-3][:2], "z", up),
-        lax.ppermute(units[3][2:], "z", down),
-    ]
+    units[4] = lax.ppermute(units[-3], "z", up)
+    late = join([mine[UNIT_AT:]] + [units[d] for d in LATE[1:]])
+    late, mine, early_before, early_after = together((late, mine, early_before, early_after))
     theirs = lax.ppermute(mine, "core", swap)
-    *far, theirs, early_before, early_after = together((*far, theirs, early_before, early_after))
-    late = join([mine[UNIT_AT:], units[-3], units[3], *far])
     late_before = lax.ppermute(late, "x", forth)
     late_after = lax.ppermute(late, "x", back)
-    away = along_y(lambda yh, yl, core: (*next_y(yh, yl, 1 - 2 * core), core))
-    half_away, theirs = together((half_away, theirs))
-    far_weight = lax.ppermute(half_away, Y, away)
     place = jnp.pad(jnp.stack([x, z, core]).astype(jnp.int32), (0, 125))[None]
     masks = jnp.concatenate([mine[MASK_AT, :2], theirs[MASK_AT, :2]]).astype(jnp.int32)
     table = jnp.concatenate([masks, place])
@@ -367,12 +366,16 @@
         ((-1, EARLY), (1, EARLY)), near, [early_before, early_after], state, every, "early"
     )
     late_before, late_after, *state = together((late_before, late_after, *state))
-    late_far = lax.ppermute(late_after, "x", back)
+    half = late.shape[0] // 2
+    late_far = [
+        lax.ppermute(late_before[:half], "x", forth),
+        lax.ppermute(late_after[half:], "x", back),
+    ]
     keep, send = stage(
         ((-1, LATE), (1, LATE)), near, [late_before, late_after], state, every, "late"
     )
-    early_far, late_far, keep, send = together((early_far, late_far, keep, send))
-    last = (((2, EARLY), (2, LATE)), near, [early_far, late_far])
+    early_far, *late_far, keep, send = together((early_far, *late_far, keep, send))
+    last = (((2, EARLY), (2, LATE)), near, [early_far, *late_far])
     (send,) = stage(*last, (send,), (2, 3), "last_send")
     received = lax.ppermute(send, "core", swap)
     (keep,) = stage(*last, (keep,), (0, 1), "last_keep")

time: 130 us -> 114 us (0.88)
  waiting for transfers between devices: 43.1 us -> 36 us
  starting transfers between devices: 41 us -> 37 us
  local copies, waits for them, and re-layouts: 5.41 us -> 1.91 us
    ppermute x1, waiting for transfers between devices: 15.9 us -> 3.82 us  [per_device(): far_weight = lax.ppermute(half_away, Y, away)]
    ppermute x1, starting transfers between devices: 4.79 us -> 0.01 us  [per_device(): far_weight = lax.ppermute(half_away, Y, away)]
    ppermute x3, waiting for transfers between devices: 6.47 us -> 11 us  [the longest x1 5.62 us: per_device(): lax.ppermute(late_before[:half], 'x', forth)]
    ppermute x1, waiting for transfers between devices: 4.47 us -> 0.01 us  [per_device(): early_before = lax.ppermute(early, 'x', forth)]
    ppermute x1, waiting for transfers between devices: 0.01 us -> 3.66 us  [per_device(): mine = lax.ppermute(bundle(queries, tile_mask, unit), Y, turn)]
    unnamed x16 -> x14, local copies, waits for them, and re-layouts: 5.38 us -> 1.85 us
    ppermute x3, starting transfers between devices: 5.6 us -> 2.82 us  [the longest x1 2.73 us: per_device(): lax.ppermute(late_after[half:], 'x', back)]
    ppermute x1, starting transfers between devices: 5.82 us -> 7.98 us  [per_device(): near_part = lax.ppermute(attended, Y, turn)]
  transfers between devices with their start and end apart: 21 -> 21, of which waited for: 10 -> 9; matrix products, arithmetic and copies ran while one was open for 0% -> 0% of each run, Pallas kernels for 26% -> 28%
where the time goes in v6:
time: 114 us
  Pallas kernels  38.5 us (34%)
  starting transfers between devices  37 us (32%)
  waiting for transfers between devices  36 us (32%)
  local copies, waits for them, and re-layouts  1.91 us (2%)
    pallas_call x14, Pallas kernels, call(): pl.pallas_call(kernel, out_shape=out_shape, in_specs=in_specs, out_specs=...  38.5 us
    ppermute x1, waiting for transfers between devices, per_device(): near_part = lax.ppermute(attended, Y, turn)  8.26 us
    ppermute x1, starting transfers between devices, per_device(): near_part = lax.ppermute(attended, Y, turn)  7.98 us
    ppermute x1, starting transfers between devices, per_device(): lax.ppermute(unit, YZ, turned(1))  5.73 us
    ppermute x1, waiting for transfers between devices, per_device(): lax.ppermute(late_before[:half], 'x', forth)  5.62 us
    ppermute x1, waiting for transfers between devices, per_device(): units[4] = lax.ppermute(units[-3], 'z', up)  5.4 us
    ppermute x1, starting transfers between devices, per_device(): lax.ppermute(unit, YZ, turned(-1))  4.03 us
    ppermute x1, starting transfers between devices, per_device(): units[2] = lax.ppermute(units[1], 'z', down)  4.03 us
  transfers between devices with their start and end apart: 21, of which 9 were waited for; matrix products, arithmetic and copies ran while one was open for 0% of the time, Pallas kernels for 28%

profile of v6, /device:TPU:1, one launch (start us, length us, event | category | flops | bytes accessed | tf_op | source)
XLA Modules:
  0.0 113.9 jit_solution(10434823019490919395)
XLA Ops:
  1.0 5.7 %collective-permute-start = (bf16[4,128,128]{2,1,0:T(8,128)(2,1)S(1)}, bf16[4,128,128]{2,1,0:T(8,128)(2,1)S(1)}, u32[]{:S(2)}, u32[]{:S(2)}) collective-permute-start(bf16[4,128,128]{2,1,0:T(8,128)(2,1)S(1)} %pack.1.unit_ref), channel_id=1, source_target_pairs={{0,8},{1,12},{2,10},{3,14},{4,9},{5,13},{6,11},{7,15},{8,16},{9,20... | collective-permute-start | bytes 393224 | tf_op jit(solution)/shard_map/ppermute | solution.py:336
  6.7 4.0 %collective-permute-start.1 = (bf16[4,128,128]{2,1,0:T(8,128)(2,1)S(1)}, bf16[4,128,128]{2,1,0:T(8,128)(2,1)S(1)}, u32[]{:S(2)}, u32[]{:S(2)}) collective-permute-start(bf16[4,128,128]{2,1,0:T(8,128)(2,1)S(1)} %pack.1.unit_ref), channel_id=1, source_target_pairs={{0,56},{1,60},{2,58},{3,62},{4,57},{5,61},{6,59},{7,63},{8,0},{9,4... | collective-permute-start | bytes 393224 | tf_op jit(solution)/shard_map/ppermute | solution.py:336
  10.8 4.6 %column_half.1 = bf16[768,3072]{1,0:T(8,128)(2,1)} custom-call(s32[1]{0:T(128)} %bitcast.2.half_ref, bf16[768,6144]{1,0:T(8,128)(2,1)} %refs_3_.3), custom_call_target="tpu_custom_call" | custom-call | tf_op jit(solution)/shard_map/column_half/pallas_call | solution.py:43
  15.5 1.9 %collective-permute-start.4 = (bf16[17,128,128]{2,1,0:T(8,128)(2,1)S(1)}, bf16[17,128,128]{2,1,0:T(8,128)(2,1)S(1)}, u32[]{:S(2)}, u32[]{:S(2)}) collective-permute-start(bf16[17,128,128]{2,1,0:T(8,128)(2,1)S(1)} %bundle.1), channel_id=1, source_target_pairs={{0,0},{1,4},{2,2},{3,6},{4,1},{5,5},{6,3},{7,7},{8,8},{9,12},{10,1... | collective-permute-start | bytes 1671176 | tf_op jit(solution)/shard_map/ppermute | solution.py:339
  17.9 4.0 %collective-permute-start.3 = (bf16[4,128,128]{2,1,0:T(8,128)(2,1)S(1)}, bf16[4,128,128]{2,1,0:T(8,128)(2,1)S(1)}, u32[]{:S(2)}, u32[]{:S(2)}) collective-permute-start(bf16[4,128,128]{2,1,0:T(8,128)(2,1)S(1)} %collective-permute-done.1.refs_1_), channel_id=1, source_target_pairs={{0,56},{8,0},{16,8},{24,16},{32,24},{40,32},{48,40},{56,48},{1,57}... | collective-permute-start | bytes 393224 | tf_op jit(solution)/shard_map/ppermute | solution.py:341
  21.9 2.3 %collective-permute-done.2.refs_2_ = bf16[4,128,128]{2,1,0:T(8,128)(2,1)S(1)} collective-permute-done((bf16[4,128,128]{2,1,0:T(8,128)(2,1)S(1)}, bf16[4,128,128]{2,1,0:T(8,128)(2,1)S(1)}, u32[]{:S(2)}, u32[]{:S(2)}) %collective-permute-start.2) | collective-permute-done | bytes 131104 | tf_op jit(solution)/shard_map/ppermute | solution.py:340
  24.2 3.7 %collective-permute-done.4.refs_1_ = bf16[17,128,128]{2,1,0:T(8,128)(2,1)S(1)} collective-permute-done((bf16[17,128,128]{2,1,0:T(8,128)(2,1)S(1)}, bf16[17,128,128]{2,1,0:T(8,128)(2,1)S(1)}, u32[]{:S(2)}, u32[]{:S(2)}) %collective-permute-start.4) | collective-permute-done | bytes 557088 | tf_op jit(solution)/shard_map/ppermute | solution.py:339
  30.7 2.8 %collective-permute-start.6 = (bf16[4,128,128]{2,1,0:T(8,128)(2,1)S(1)}, bf16[4,128,128]{2,1,0:T(8,128)(2,1)S(1)}, u32[]{:S(2)}, u32[]{:S(2)}) collective-permute-start(bf16[4,128,128]{2,1,0:T(8,128)(2,1)S(1)} %collective-permute-done.3.refs_3_), channel_id=1, source_target_pairs={{0,56},{8,0},{16,8},{24,16},{32,24},{40,32},{48,40},{56,48},{1,57}... | collective-permute-start | bytes 393224 | tf_op jit(solution)/shard_map/ppermute | solution.py:350
  33.5 3.2 %collective-permute-done.5.refs_1_ = bf16[4,128,128]{2,1,0:T(8,128)(2,1)S(1)} collective-permute-done((bf16[4,128,128]{2,1,0:T(8,128)(2,1)S(1)}, bf16[4,128,128]{2,1,0:T(8,128)(2,1)S(1)}, u32[]{:S(2)}, u32[]{:S(2)}) %collective-permute-start.5) | collective-permute-done | bytes 131104 | tf_op jit(solution)/shard_map/ppermute | solution.py:349
  36.7 5.4 %collective-permute-done.7.refs_3_ = bf16[4,128,128]{2,1,0:T(8,128)(2,1)S(1)} collective-permute-done((bf16[4,128,128]{2,1,0:T(8,128)(2,1)S(1)}, bf16[4,128,128]{2,1,0:T(8,128)(2,1)S(1)}, u32[]{:S(2)}, u32[]{:S(2)}) %collective-permute-start.7) | collective-permute-done | bytes 131104 | tf_op jit(solution)/shard_map/ppermute | solution.py:351
  43.1 2.7 %collective-permute-start.13 = (bf16[16,128,128]{2,1,0:T(8,128)(2,1)S(1)}, bf16[16,128,128]{2,1,0:T(8,128)(2,1)S(1)}, u32[]{:S(2)}, u32[]{:S(2)}) collective-permute-start(bf16[16,128,128]{2,1,0:T(8,128)(2,1)S(1)} %join.2.refs_4_), channel_id=1, source_target_pairs={{0,192},{64,0},{128,64},{192,128},{1,193},{65,1},{129,65},{193,129... | collective-permute-start | bytes 1572872 | tf_op jit(solution)/shard_map/ppermute | solution.py:356
  45.8 5.9 %own_column.1 = (f32[2,152,768]{2,1,0:T(8,128)S(1)}, f32[2,152,768]{2,1,0:T(8,128)S(1)}) custom-call(s32[5,128]{1,0:T(8,128)S(1)} %pad_add_fusion.refs_0_, bf16[17,128,128]{2,1,0:T(8,128)(2,1)S(1)} %collective-permute-done.4.refs_1_, bf16[17,128,128]{2,1,0:T(8,128)(2,1)S(1)} %collective-permute-done.10.refs_2_, bf16[16,128,128]{2,1,0:T(8,128)(2,1)S(1)} %join.3.refs_3_, ...), custom_call_target="tpu_custom_call" | custom-call | tf_op jit(solution)/shard_map/own_column/pallas_call | solution.py:43
  52.8 6.1 %early.1 = (f32[2,152,768]{2,1,0:T(8,128)S(1)}, f32[2,152,768]{2,1,0:T(8,128)S(1)}) custom-call(s32[5,128]{1,0:T(8,128)S(1)} %pad_add_fusion.refs_0_, bf16[17,128,128]{2,1,0:T(8,128)(2,1)S(1)} %collective-permute-done.4.refs_1_, bf16[17,128,128]{2,1,0:T(8,128)(2,1)S(1)} %collective-permute-done.10.refs_2_, ...), custom_call_target="tpu_custom_call", output_to_operand_aliasing={{0}: (5, {}), {1}: (6, {})} | custom-call | tf_op jit(solution)/shard_map/early/pallas_call | solution.py:43
  59.1 2.7 %collective-permute-start.15 = (bf16[8,128,128]{2,1,0:T(8,128)(2,1)S(1)}, bf16[8,128,128]{2,1,0:T(8,128)(2,1)S(1)}, u32[]{:S(2)}, u32[]{:S(2)}) collective-permute-start(bf16[8,128,128]{2,1,0:T(8,128)(2,1)S(1)} %slice.19), channel_id=1, source_target_pairs={{0,192},{64,0},{128,64},{192,128},{1,193},{65,1},{129,65},{193,129... | collective-permute-start | bytes 786440 | tf_op jit(solution)/shard_map/ppermute | solution.py:372
  61.8 5.9 %late.1 = (f32[2,152,768]{2,1,0:T(8,128)S(1)}, f32[2,152,768]{2,1,0:T(8,128)S(1)}) custom-call(s32[5,128]{1,0:T(8,128)S(1)} %pad_add_fusion.refs_0_, bf16[17,128,128]{2,1,0:T(8,128)(2,1)S(1)} %collective-permute-done.4.refs_1_, bf16[17,128,128]{2,1,0:T(8,128)(2,1)S(1)} %collective-permute-done.10.refs_2_, ...), custom_call_target="tpu_custom_call", output_to_operand_aliasing={{0}: (5, {}), {1}: (6, {})} | custom-call | tf_op jit(solution)/shard_map/late/pallas_call | solution.py:43
  68.6 5.6 %collective-permute-done.14.refs_4_ = bf16[8,128,128]{2,1,0:T(8,128)(2,1)S(1)} collective-permute-done((bf16[8,128,128]{2,1,0:T(8,128)(2,1)S(1)}, bf16[8,128,128]{2,1,0:T(8,128)(2,1)S(1)}, u32[]{:S(2)}, u32[]{:S(2)}) %collective-permute-start.14) | collective-permute-done | bytes 262176 | tf_op jit(solution)/shard_map/ppermute | solution.py:371
  74.2 3.3 %last_send.1 = f32[2,152,768]{2,1,0:T(8,128)S(1)} custom-call(s32[5,128]{1,0:T(8,128)S(1)} %pad_add_fusion.refs_0_, bf16[17,128,128]{2,1,0:T(8,128)(2,1)S(1)} %collective-permute-done.4.refs_1_, bf16[17,128,128]{2,1,0:T(8,128)(2,1)S(1)} %collective-permute-done.10.refs_2_, ...), custom_call_target="tpu_custom_call", output_to_operand_aliasing={{}: (6, {})} | custom-call | tf_op jit(solution)/shard_map/last_send/pallas_call | solution.py:43
  79.1 2.8 %last_keep.1.own_ref = f32[2,152,768]{2,1,0:T(8,128)S(1)} custom-call(s32[5,128]{1,0:T(8,128)S(1)} %pad_add_fusion.refs_0_, bf16[17,128,128]{2,1,0:T(8,128)(2,1)S(1)} %collective-permute-done.4.refs_1_, bf16[17,128,128]{2,1,0:T(8,128)(2,1)S(1)} %collective-permute-done.10.refs_2_, ...), custom_call_target="tpu_custom_call", output_to_operand_aliasing={{}: (6, {})} | custom-call | tf_op jit(solution)/shard_map/last_keep/pallas_call | solution.py:43
  81.9 3.8 %collective-permute-done.17.refs_4_ = bf16[768,3072]{1,0:T(8,128)(2,1)} collective-permute-done((bf16[768,3072]{1,0:T(8,128)(2,1)}, bf16[768,3072]{1,0:T(8,128)(2,1)}, u32[]{:S(2)}, u32[]{:S(2)}) %collective-permute-start.17) | collective-permute-done | bytes 4718624 | tf_op jit(solution)/shard_map/ppermute | solution.py:344
  85.9 8.0 %collective-permute-start.18 = (bf16[256,768]{1,0:T(8,128)(2,1)S(1)}, bf16[256,768]{1,0:T(8,128)(2,1)S(1)}, u32[]{:S(2)}, u32[]{:S(2)}) collective-permute-start(bf16[256,768]{1,0:T(8,128)(2,1)S(1)} %merge.1), channel_id=1, source_target_pairs={{0,0},{1,4},{2,2},{3,6},{4,1},{5,5},{6,3},{7,7},{8,8},{9,12},{10,1... | collective-permute-start | bytes 1179656 | tf_op jit(solution)/shard_map/ppermute | solution.py:386
  94.1 8.3 %collective-permute-done.18.refs_1_ = bf16[256,768]{1,0:T(8,128)(2,1)S(1)} collective-permute-done((bf16[256,768]{1,0:T(8,128)(2,1)S(1)}, bf16[256,768]{1,0:T(8,128)(2,1)S(1)}, u32[]{:S(2)}, u32[]{:S(2)}) %collective-permute-start.18) | collective-permute-done | bytes 393248 | tf_op jit(solution)/shard_map/ppermute | solution.py:386
  102.4 2.8 %collective-permute-done.19.refs_2_ = bf16[256,768]{1,0:T(8,128)(2,1)S(1)} collective-permute-done((bf16[256,768]{1,0:T(8,128)(2,1)S(1)}, bf16[256,768]{1,0:T(8,128)(2,1)S(1)}, u32[]{:S(2)}, u32[]{:S(2)}) %collective-permute-start.19) | collective-permute-done | bytes 393248 | tf_op jit(solution)/shard_map/ppermute | solution.py:387
  105.2 3.8 %project_send.1 = bf16[256,1536]{1,0:T(8,128)(2,1)S(1)} custom-call(s32[2]{0:T(128)S(1)} %pad_add_fusion.1.refs_0_, bf16[256,768]{1,0:T(8,128)(2,1)S(1)} %collective-permute-done.18.refs_1_, bf16[256,768]{1,0:T(8,128)(2,1)S(1)} %collective-permute-done.19.refs_2_, bf16[768,6144]{1,0:T(8,128)(2,1)S(1)} %bitcast.12, ...), custom_call_target="tpu_custom_call" | custom-call | tf_op jit(solution)/shard_map/project_send/pallas_call | solution.py:43
  109.0 3.8 %project_keep.1.keep_ref = f32[256,1536]{1,0:T(8,128)S(1)} custom-call(s32[2]{0:T(128)S(1)} %pad_add_fusion.1.refs_0_, bf16[256,768]{1,0:T(8,128)(2,1)S(1)} %collective-permute-done.18.refs_1_, bf16[256,768]{1,0:T(8,128)(2,1)S(1)} %collective-permute-done.19.refs_2_, bf16[768,6144]{1,0:T(8,128)(2,1)S(1)} %bitcast.12, ...), custom_call_target="tpu_custom_call" | custom-call | tf_op jit(solution)/shard_map/project_keep/pallas_call | solution.py:43
  (57 shorter events, 10.5 us)
Async XLA Ops:
  1.0 14.4 %collective-permute-start = (bf16[4,128,128]{2,1,0:T(8,128)(2,1)S(1)}, bf16[4,128,128]{2,1,0:T(8,128)(2,1)S(1)}, u32[]{:S(2)}, u32[]{:S(2)}) collective-permute-start(bf16[4,128,128]{2,1,0:T(8,128)(2,1)S(1)} %pack.1.unit_ref), channel_id=1, source_target_pairs={{0,8},{1,12},{2,10},{3,14},{4,9},{5,13},{6,11},{7,15},{8,16},{9,20... | collective-permute-start | bytes 393224 | tf_op jit(solution)/shard_map/ppermute | solution.py:336
  6.7 8.7 %collective-permute-start.1 = (bf16[4,128,128]{2,1,0:T(8,128)(2,1)S(1)}, bf16[4,128,128]{2,1,0:T(8,128)(2,1)S(1)}, u32[]{:S(2)}, u32[]{:S(2)}) collective-permute-start(bf16[4,128,128]{2,1,0:T(8,128)(2,1)S(1)} %pack.1.unit_ref), channel_id=1, source_target_pairs={{0,56},{1,60},{2,58},{3,62},{4,57},{5,61},{6,59},{7,63},{8,0},{9,4... | collective-permute-start | bytes 393224 | tf_op jit(solution)/shard_map/ppermute | solution.py:336
  15.5 12.4 %collective-permute-start.4 = (bf16[17,128,128]{2,1,0:T(8,128)(2,1)S(1)}, bf16[17,128,128]{2,1,0:T(8,128)(2,1)S(1)}, u32[]{:S(2)}, u32[]{:S(2)}) collective-permute-start(bf16[17,128,128]{2,1,0:T(8,128)(2,1)S(1)} %bundle.1), channel_id=1, source_target_pairs={{0,0},{1,4},{2,2},{3,6},{4,1},{5,5},{6,3},{7,7},{8,8},{9,12},{10,1... | collective-permute-start | bytes 1671176 | tf_op jit(solution)/shard_map/ppermute | solution.py:339
  17.4 6.8 %collective-permute-start.2 = (bf16[4,128,128]{2,1,0:T(8,128)(2,1)S(1)}, bf16[4,128,128]{2,1,0:T(8,128)(2,1)S(1)}, u32[]{:S(2)}, u32[]{:S(2)}) collective-permute-start(bf16[4,128,128]{2,1,0:T(8,128)(2,1)S(1)} %collective-permute-done.refs_0_), channel_id=1, source_target_pairs={{0,8},{8,16},{16,24},{24,32},{32,40},{40,48},{48,56},{56,0},{1,9},... | collective-permute-start | bytes 393224 | tf_op jit(solution)/shard_map/ppermute | solution.py:340
  17.9 6.3 %collective-permute-start.3 = (bf16[4,128,128]{2,1,0:T(8,128)(2,1)S(1)}, bf16[4,128,128]{2,1,0:T(8,128)(2,1)S(1)}, u32[]{:S(2)}, u32[]{:S(2)}) collective-permute-start(bf16[4,128,128]{2,1,0:T(8,128)(2,1)S(1)} %collective-permute-done.1.refs_1_), channel_id=1, source_target_pairs={{0,56},{8,0},{16,8},{24,16},{32,24},{40,32},{48,40},{56,48},{1,57}... | collective-permute-start | bytes 393224 | tf_op jit(solution)/shard_map/ppermute | solution.py:341
  27.9 57.8 %collective-permute-start.17 = (bf16[768,3072]{1,0:T(8,128)(2,1)}, bf16[768,3072]{1,0:T(8,128)(2,1)}, u32[]{:S(2)}, u32[]{:S(2)}) collective-permute-start(bf16[768,3072]{1,0:T(8,128)(2,1)} %column_half.1), channel_id=1, source_target_pairs={{0,2},{1,7},{2,4},{3,1},{4,6},{5,3},{6,0},{7,5},{8,10},{9,15},{10,... | collective-permute-start | bytes 14155784 | tf_op jit(solution)/shard_map/ppermute | solution.py:344
  27.9 14.3 %collective-permute-start.8 = (bf16[16,128,128]{2,1,0:T(8,128)(2,1)S(1)}, bf16[16,128,128]{2,1,0:T(8,128)(2,1)}, u32[]{:S(2)}, u32[]{:S(2)}) collective-permute-start(bf16[16,128,128]{2,1,0:T(8,128)(2,1)S(1)} %join.3.refs_3_), channel_id=1, source_target_pairs={{0,64},{64,128},{128,192},{192,0},{1,65},{65,129},{129,193},{193,1... | collective-permute-start | bytes 1572872 | tf_op jit(solution)/shard_map/ppermute | solution.py:347
  29.2 13.0 %collective-permute-start.9 = (bf16[16,128,128]{2,1,0:T(8,128)(2,1)S(1)}, bf16[16,128,128]{2,1,0:T(8,128)(2,1)S(1)}, u32[]{:S(2)}, u32[]{:S(2)}) collective-permute-start(bf16[16,128,128]{2,1,0:T(8,128)(2,1)S(1)} %join.3.refs_3_), channel_id=1, source_target_pairs={{0,192},{64,0},{128,64},{192,128},{1,193},{65,1},{129,65},{193,129... | collective-permute-start | bytes 1572872 | tf_op jit(solution)/shard_map/ppermute | solution.py:348
  30.7 6.0 %collective-permute-start.5 = (bf16[4,128,128]{2,1,0:T(8,128)(2,1)S(1)}, bf16[4,128,128]{2,1,0:T(8,128)(2,1)S(1)}, u32[]{:S(2)}, u32[]{:S(2)}) collective-permute-start(bf16[4,128,128]{2,1,0:T(8,128)(2,1)S(1)} %collective-permute-done.2.refs_2_), channel_id=1, source_target_pairs={{0,8},{8,16},{16,24},{24,32},{32,40},{40,48},{48,56},{56,0},{1,9},... | collective-permute-start | bytes 393224 | tf_op jit(solution)/shard_map/ppermute | solution.py:349
  30.7 6.0 %collective-permute-start.6 = (bf16[4,128,128]{2,1,0:T(8,128)(2,1)S(1)}, bf16[4,128,128]{2,1,0:T(8,128)(2,1)S(1)}, u32[]{:S(2)}, u32[]{:S(2)}) collective-permute-start(bf16[4,128,128]{2,1,0:T(8,128)(2,1)S(1)} %collective-permute-done.3.refs_3_), channel_id=1, source_target_pairs={{0,56},{8,0},{16,8},{24,16},{32,24},{40,32},{48,40},{56,48},{1,57}... | collective-permute-start | bytes 393224 | tf_op jit(solution)/shard_map/ppermute | solution.py:350
  36.7 5.4 %collective-permute-start.7 = (bf16[4,128,128]{2,1,0:T(8,128)(2,1)S(1)}, bf16[4,128,128]{2,1,0:T(8,128)(2,1)S(1)}, u32[]{:S(2)}, u32[]{:S(2)}) collective-permute-start(bf16[4,128,128]{2,1,0:T(8,128)(2,1)S(1)} %collective-permute-done.5.refs_1_), channel_id=1, source_target_pairs={{0,8},{8,16},{16,24},{24,32},{32,40},{40,48},{48,56},{56,0},{1,9},... | collective-permute-start | bytes 393224 | tf_op jit(solution)/shard_map/ppermute | solution.py:351
  42.1 63.0 %slice-start = ((s8[9437184]{0:T(1024)(128)(4,1)}), s8[1048576]{0:T(1024)(128)(4,1)S(1)}, s32[]{:S(2)}) async-start(s8[9437184]{0:T(1024)(128)(4,1)} %bitcast.11), calls=%async_computation | async-start | bytes 2097152
  43.0 2.8 %collective-permute-start.10 = (bf16[17,128,128]{2,1,0:T(8,128)(2,1)S(1)}, bf16[17,128,128]{2,1,0:T(8,128)(2,1)S(1)}, u32[]{:S(2)}, u32[]{:S(2)}) collective-permute-start(bf16[17,128,128]{2,1,0:T(8,128)(2,1)S(1)} %collective-permute-done.4.refs_1_), channel_id=1, source_target_pairs={{0,1},{1,0},{2,3},{3,2},{4,5},{5,4},{6,7},{7,6},{8,9},{9,8},{10,11... | collective-permute-start | bytes 1671176 | tf_op jit(solution)/shard_map/ppermute | solution.py:354
  43.1 15.8 %collective-permute-start.12 = (bf16[16,128,128]{2,1,0:T(8,128)(2,1)S(1)}, bf16[16,128,128]{2,1,0:T(8,128)(2,1)S(1)}, u32[]{:S(2)}, u32[]{:S(2)}) collective-permute-start(bf16[16,128,128]{2,1,0:T(8,128)(2,1)S(1)} %join.2.refs_4_), channel_id=1, source_target_pairs={{0,64},{64,128},{128,192},{192,0},{1,65},{65,129},{129,193},{193,1... | collective-permute-start | bytes 1572872 | tf_op jit(solution)/shard_map/ppermute | solution.py:355
  43.1 15.8 %collective-permute-start.13 = (bf16[16,128,128]{2,1,0:T(8,128)(2,1)S(1)}, bf16[16,128,128]{2,1,0:T(8,128)(2,1)S(1)}, u32[]{:S(2)}, u32[]{:S(2)}) collective-permute-start(bf16[16,128,128]{2,1,0:T(8,128)(2,1)S(1)} %join.2.refs_4_), channel_id=1, source_target_pairs={{0,192},{64,0},{128,64},{192,128},{1,193},{65,1},{129,65},{193,129... | collective-permute-start | bytes 1572872 | tf_op jit(solution)/shard_map/ppermute | solution.py:356
  45.8 22.9 %collective-permute-start.11 = (bf16[16,128,128]{2,1,0:T(8,128)(2,1)}, bf16[16,128,128]{2,1,0:T(8,128)(2,1)S(1)}, u32[]{:S(2)}, u32[]{:S(2)}) collective-permute-start(bf16[16,128,128]{2,1,0:T(8,128)(2,1)} %collective-permute-done.8.refs_3_), channel_id=1, source_target_pairs={{0,64},{64,128},{128,192},{192,0},{1,65},{65,129},{129,193},{193,1... | collective-permute-start | bytes 1572872 | tf_op jit(solution)/shard_map/ppermute | solution.py:364
  58.9 46.2 %slice-start.1 = ((s8[9437184]{0:T(1024)(128)(4,1)}), s8[4194304]{0:T(1024)(128)(4,1)S(1)}, s32[]{:S(2)}) async-start(s8[9437184]{0:T(1024)(128)(4,1)} %bitcast.11), calls=%async_computation.1 | async-start | bytes 8388608
  59.0 15.3 %collective-permute-start.14 = (bf16[8,128,128]{2,1,0:T(8,128)(2,1)S(1)}, bf16[8,128,128]{2,1,0:T(8,128)(2,1)S(1)}, u32[]{:S(2)}, u32[]{:S(2)}) collective-permute-start(bf16[8,128,128]{2,1,0:T(8,128)(2,1)S(1)} %slice.18), channel_id=1, source_target_pairs={{0,64},{64,128},{128,192},{192,0},{1,65},{65,129},{129,193},{193,1... | collective-permute-start | bytes 786440 | tf_op jit(solution)/shard_map/ppermute | solution.py:371
  59.1 15.2 %collective-permute-start.15 = (bf16[8,128,128]{2,1,0:T(8,128)(2,1)S(1)}, bf16[8,128,128]{2,1,0:T(8,128)(2,1)S(1)}, u32[]{:S(2)}, u32[]{:S(2)}) collective-permute-start(bf16[8,128,128]{2,1,0:T(8,128)(2,1)S(1)} %slice.19), channel_id=1, source_target_pairs={{0,192},{64,0},{128,64},{192,128},{1,193},{65,1},{129,65},{193,129... | collective-permute-start | bytes 786440 | tf_op jit(solution)/shard_map/ppermute | solution.py:372
  74.2 30.9 %slice-start.2 = ((s8[9437184]{0:T(1024)(128)(4,1)}), s8[4194304]{0:T(1024)(128)(4,1)S(1)}, s32[]{:S(2)}) async-start(s8[9437184]{0:T(1024)(128)(4,1)} %bitcast.11), calls=%async_computation.2 | async-start | bytes 8388608
  77.6 4.3 %collective-permute-start.16 = (f32[2,152,768]{2,1,0:T(8,128)S(1)}, f32[2,152,768]{2,1,0:T(8,128)S(1)}, u32[]{:S(2)}, u32[]{:S(2)}) collective-permute-start(f32[2,152,768]{2,1,0:T(8,128)S(1)} %last_send.1), channel_id=1, source_target_pairs={{0,1},{1,0},{2,3},{3,2},{4,5},{5,4},{6,7},{7,6},{8,9},{9,8},{10,11... | collective-permute-start | bytes 2801672 | tf_op jit(solution)/shard_map/ppermute | solution.py:380
  85.9 16.4 %collective-permute-start.18 = (bf16[256,768]{1,0:T(8,128)(2,1)S(1)}, bf16[256,768]{1,0:T(8,128)(2,1)S(1)}, u32[]{:S(2)}, u32[]{:S(2)}) collective-permute-start(bf16[256,768]{1,0:T(8,128)(2,1)S(1)} %merge.1), channel_id=1, source_target_pairs={{0,0},{1,4},{2,2},{3,6},{4,1},{5,5},{6,3},{7,7},{8,8},{9,12},{10,1... | collective-permute-start | bytes 1179656 | tf_op jit(solution)/shard_map/ppermute | solution.py:386
  93.9 11.2 %collective-permute-start.19 = (bf16[256,768]{1,0:T(8,128)(2,1)S(1)}, bf16[256,768]{1,0:T(8,128)(2,1)S(1)}, u32[]{:S(2)}, u32[]{:S(2)}) collective-permute-start(bf16[256,768]{1,0:T(8,128)(2,1)S(1)} %merge.1), channel_id=1, source_target_pairs={{0,2},{1,6},{2,0},{3,4},{4,3},{5,7},{6,1},{7,5},{8,10},{9,14},{10,... | collective-permute-start | bytes 1179656 | tf_op jit(solution)/shard_map/ppermute | solution.py:387
  108.9 3.9 %collective-permute-start.20 = (bf16[256,1536]{1,0:T(8,128)(2,1)S(1)}, bf16[256,1536]{1,0:T(8,128)(2,1)S(1)}, u32[]{:S(2)}, u32[]{:S(2)}) collective-permute-start(bf16[256,1536]{1,0:T(8,128)(2,1)S(1)} %project_send.1), channel_id=1, source_target_pairs={{0,1},{1,0},{2,3},{3,2},{4,5},{5,4},{6,7},{7,6},{8,9},{9,8},{10,11... | collective-permute-start | bytes 2359304 | tf_op jit(solution)/shard_map/ppermute | solution.py:391
  (4 other events, 11.1 us)

commit v7 on v6

--- a/solution.py
+++ b/solution.py
@@ -53,10 +53,14 @@
     )(*args)
 
 
-def pack_kernel(key_hbm, value_hbm, out_ref, key_ref, value_ref, sems):
+def pack_kernel(key_hbm, value_hbm, query_hbm, mask_hbm, unit_ref, out_ref, *scratch):
+    *buffers, sems = scratch
+    key_ref, value_ref, query_ref, mask_ref = buffers
     copies = [
-        pltpu.make_async_copy(key_hbm, key_ref, sems.at[0]),
-        pltpu.make_async_copy(value_hbm, value_ref, sems.at[1]),
+        pltpu.make_async_copy(source, target, sems.at[i])
+        for i, (source, target) in enumerate(
+            zip((key_hbm, value_hbm, query_hbm, mask_hbm), buffers)
+        )
     ]
     for copy in copies:
         copy.start()
@@ -64,34 +68,27 @@
         copy.wait()
     for t in range(2):
         rows = pl.ds(t * TILE, TILE)
-        out_ref[t] = key_ref[rows, :]
-        out_ref[2 + t] = value_ref[rows, :].astype(jnp.float32).T.astype(jnp.bfloat16)
-
-
-def pack(key_rows, value_rows):
-    rows = pltpu.VMEM((2 * TILE, HD), jnp.bfloat16)
+        values = value_ref[rows, :].astype(jnp.float32).T.astype(jnp.bfloat16)
+        for ref, at in ((unit_ref, 0), (out_ref, UNIT_AT)):
+            ref[at + t] = key_ref[rows, :]
+            ref[at + 2 + t] = values
+        for h in range(HEADS):
+            out_ref[t * HEADS + h] = query_ref[rows, pl.ds(h * HD, HD)]
+    out_ref[MASK_AT] = jnp.zeros((TILE, TILE), jnp.bfloat16)
+    out_ref[MASK_AT, 0:2, :] = mask_ref[...].astype(jnp.float32).astype(jnp.bfloat16)
+
+
+def pack(*arrays):
     return call(
         pack_kernel,
-        jax.ShapeDtypeStruct((4, TILE, TILE), jnp.bfloat16),
-        (in_hbm(key_rows), in_hbm(value_rows)),
-        [hbm()] * 2,
-        scratch=(rows, rows, pltpu.SemaphoreType.DMA((2,))),
+        tuple(
+            jax.ShapeDtypeStruct((size, TILE, TILE), jnp.bfloat16) for size in (4, UNIT_AT + 4)
+        ),
+        tuple(in_hbm(a) for a in arrays),
+        [hbm()] * 4,
+        scratch=[pltpu.VMEM(a.shape, a.dtype) for a in arrays] + [pltpu.SemaphoreType.DMA((4,))],
         name="pack",
     )
-
-
-def bundle_kernel(query_ref, mask_ref, unit_ref, out_ref):
-    for t in range(2):
-        for h in range(HEADS):
-            out_ref[t * HEADS + h] = query_ref[pl.ds(t * TILE, TILE), pl.ds(h * HD, HD)]
-    out_ref[MASK_AT] = jnp.zeros((TILE, TILE), jnp.bfloat16)
-    out_ref[MASK_AT, 0:2, :] = mask_ref[...].astype(jnp.float32).astype(jnp.bfloat16)
-    out_ref[UNIT_AT:] = unit_ref[...]
-
-
-def bundle(queries, tile_mask, unit):
-    shape = jax.ShapeDtypeStruct((UNIT_AT + 4, TILE, TILE), jnp.bfloat16)
-    return call(bundle_kernel, shape, (queries, tile_mask, unit), [vmem()] * 3, name="bundle")
 
 
 def half_kernel(half_ref, source_ref, out_ref, sems):
@@ -120,6 +117,26 @@
         scratch=(pltpu.SemaphoreType.DMA((8,)),),
         name="column_half",
     )
+
+
+def fetch_kernel(source_ref, out_ref, sems):
+    rows = out_ref.shape[0] // 4
+    copies = [
+        pltpu.make_async_copy(
+            source_ref.at[pl.ds(i * rows, rows), :], out_ref.at[pl.ds(i * rows, rows), :], sems.at[i]
+        )
+        for i in range(4)
+    ]
+    for copy in copies:
+        copy.start()
+    for copy in copies:
+        copy.wait()
+
+
+def fetch(source):
+    shape = jax.ShapeDtypeStruct(source.shape, source.dtype)
+    scratch = (pltpu.SemaphoreType.DMA((4,)),)
+    return call(fetch_kernel, shape, (in_hbm(source),), [hbm()], scratch=scratch, name="fetch")
 
 
 def join_kernel(*refs):
@@ -331,17 +348,17 @@
     swap = [(0, 1), (1, 0)]
     together = lax.optimization_barrier
 
-    unit = pack(key_rows, value_rows)
+    unit, bundle = pack(key_rows, value_rows, queries, tile_mask)
     up, down = ring(NZ, 1), ring(NZ, -1)
     units = {-1: lax.ppermute(unit, YZ, turned(1)), 1: lax.ppermute(unit, YZ, turned(-1))}
+    mine = lax.ppermute(bundle, Y, turn)
     half_away = column_half(out_weight, 1 - yl)
-    units[-1], units[1], unit, half_away = together((units[-1], units[1], unit, half_away))
-    mine = lax.ppermute(bundle(queries, tile_mask, unit), Y, turn)
+    units[-1], units[1], mine, half_away = together((units[-1], units[1], mine, half_away))
+    away = along_y(lambda yh, yl, core: (*next_y(yh, yl, 1 - 2 * core), core))
+    far_weight = lax.ppermute(half_away, Y, away)
     units[-2] = lax.ppermute(units[-1], "z", up)
     units[2] = lax.ppermute(units[1], "z", down)
-    units[-2], units[2], mine, half_away = together((units[-2], units[2], mine, half_away))
-    away = along_y(lambda yh, yl, core: (*next_y(yh, yl, 1 - 2 * core), core))
-    far_weight = lax.ppermute(half_away, Y, away)
+    units[-2], units[2] = together((units[-2], units[2]))
     early = join([units[d] for d in EARLY])
     forth, back = ring(NX, 1), ring(NX, -1)
     early_before = lax.ppermute(early, "x", forth)
@@ -350,8 +367,8 @@
     units[3] = lax.ppermute(units[2], "z", down)
     units[4] = lax.ppermute(units[-3], "z", up)
     late = join([mine[UNIT_AT:]] + [units[d] for d in LATE[1:]])
-    late, mine, early_before, early_after = together((late, mine, early_before, early_after))
     theirs = lax.ppermute(mine, "core", swap)
+    late, theirs, early_before, early_after = together((late, theirs, early_before, early_after))
     late_before = lax.ppermute(late, "x", forth)
     late_after = lax.ppermute(late, "x", back)
     place = jnp.pad(jnp.stack([x, z, core]).astype(jnp.int32), (0, 125))[None]
@@ -361,12 +378,15 @@
     near = (table, mine, theirs)
     every = (0, 1, 2, 3)
     state = stage(((0, EARLY), (0, LATE)), near, [early, late], None, every, "own_column")
-    early_far = lax.ppermute(early_before, "x", forth)
+    half = early.shape[0] // 2
+    early_far = [
+        lax.ppermute(early_before[:half], "x", forth),
+        lax.ppermute(early_after[half:], "x", back),
+    ]
     state = stage(
         ((-1, EARLY), (1, EARLY)), near, [early_before, early_after], state, every, "early"
     )
     late_before, late_after, *state = together((late_before, late_after, *state))
-    half = late.shape[0] // 2
     late_far = [
         lax.ppermute(late_before[:half], "x", forth),
         lax.ppermute(late_after[half:], "x", back),
@@ -374,8 +394,8 @@
     keep, send = stage(
         ((-1, LATE), (1, LATE)), near, [late_before, late_after], state, every, "late"
     )
-    early_far, *late_far, keep, send = together((early_far, *late_far, keep, send))
-    last = (((2, EARLY), (2, LATE)), near, [early_far, *late_far])
+    *far, keep, send = together((*early_far, *late_far, keep, send))
+    last = (((2, EARLY), (2, LATE)), near, far)
     (send,) = stage(*last, (send,), (2, 3), "last_send")
     received = lax.ppermute(send, "core", swap)
     (keep,) = stage(*last, (keep,), (0, 1), "last_keep")
@@ -386,7 +406,7 @@
     near_part = lax.ppermute(attended, Y, turn)
     far_part = lax.ppermute(attended, Y, along_y(lambda yh, yl, core: (core, 1 - yl, yh)))
     where = jnp.stack([yl, core]).astype(jnp.int32)
-    sides = (where, near_part, far_part, out_weight, far_weight)
+    sides = (where, near_part, far_part, out_weight, fetch(far_weight))
     other = project(1, *sides, jnp.bfloat16, "project_send")
     other = lax.ppermute(other, "core", swap)
     own = project(0, *sides, jnp.float32, "project_keep")

time: 114 us -> 108 us (0.947); the launches traced: 114 us -> 109 us
  waiting for transfers between devices: 36 us -> 25 us
  starting transfers between devices: 37 us -> 42.8 us
  Pallas kernels: 38.5 us -> 40.6 us
  local copies, waits for them, and re-layouts: 1.91 us -> 0.11 us
    ppermute x2 -> x3, starting transfers between devices: 1.92 us -> 9.03 us  [the longest x1 6.21 us: per_device(): mine = lax.ppermute(bundle, Y, turn)]
    ppermute x1, waiting for transfers between devices: 5.62 us -> 0.01 us  [per_device(): lax.ppermute(late_before[:half], 'x', forth)]
    ppermute x1, waiting for transfers between devices: 8.26 us -> 3.5 us  [per_device(): near_part = lax.ppermute(attended, Y, turn)]
    ppermute x2 -> x3, waiting for transfers between devices: 4.61 us -> 0.01 us  [the longest x1 0.01 us: per_device(): mine = lax.ppermute(bundle, Y, turn)]
    ppermute x1, starting transfers between devices: 5.73 us -> 1.44 us  [per_device(): lax.ppermute(unit, YZ, turned(1))]
    ppermute x1, waiting for transfers between devices: 3.82 us -> 0.01 us  [per_device(): far_weight = lax.ppermute(half_away, Y, away)]
    ppermute x1, waiting for transfers between devices: 0.01 us -> 3.41 us  [per_device(): units[3] = lax.ppermute(units[2], 'z', down)]
    ppermute x1, starting transfers between devices: 0.47 us -> 3.11 us  [per_device(): units[-2] = lax.ppermute(units[-1], 'z', up)]
  transfers between devices with their start and end apart: 21 -> 22, of which waited for: 9 -> 7; matrix products, arithmetic and copies ran while one was open for 0% -> 0% of each run, Pallas kernels for 28% -> 33%
where the time goes in v7:
time: 108 us; the launch traced here: 109 us
  starting transfers between devices  42.8 us (40%)
  Pallas kernels  40.6 us (38%)
  waiting for transfers between devices  25 us (23%)
    pallas_call x14, Pallas kernels, call(): pl.pallas_call(kernel, out_shape=out_shape, in_specs=in_specs, out_specs=...  40.6 us
    ppermute x1, starting transfers between devices, per_device(): near_part = lax.ppermute(attended, Y, turn)  6.9 us
    ppermute x1, waiting for transfers between devices, per_device(): units[4] = lax.ppermute(units[-3], 'z', up)  6.69 us
    ppermute x1, starting transfers between devices, per_device(): mine = lax.ppermute(bundle, Y, turn)  6.21 us
    ppermute x1, starting transfers between devices, per_device(): units[2] = lax.ppermute(units[1], 'z', down)  5.54 us
    ppermute x1, waiting for transfers between devices, per_device(): units[-3] = lax.ppermute(units[-2], 'z', up)  5.43 us
    ppermute x1, starting transfers between devices, per_device(): lax.ppermute(unit, YZ, turned(-1))  4.03 us
    ppermute x1, waiting for transfers between devices, per_device(): near_part = lax.ppermute(attended, Y, turn)  3.5 us
  transfers between devices with their start and end apart: 22, of which 7 were waited for; matrix products, arithmetic and copies ran while one was open for 0% of the time, Pallas kernels for 33%

profile of v7, /device:TPU:1, one launch (start us, length us, event | category | flops | bytes accessed | tf_op | source)
XLA Modules:
  0.0 109.0 jit_solution(14199344306426514111)
XLA Ops:
  1.3 6.2 %collective-permute-start.2 = (bf16[17,128,128]{2,1,0:T(8,128)(2,1)S(1)}, bf16[17,128,128]{2,1,0:T(8,128)(2,1)S(1)}, u32[]{:S(2)}, u32[]{:S(2)}) collective-permute-start(bf16[17,128,128]{2,1,0:T(8,128)(2,1)S(1)} %get-tuple-element.37), channel_id=1, source_target_pairs={{0,0},{1,4},{2,2},{3,6},{4,1},{5,5},{6,3},{7,7},{8,8},{9,12},{10,1... | collective-permute-start | bytes 1671176 | tf_op jit(solution)/shard_map/ppermute | solution.py:354
  9.0 4.0 %collective-permute-start.1 = (bf16[4,128,128]{2,1,0:T(8,128)(2,1)S(1)}, bf16[4,128,128]{2,1,0:T(8,128)(2,1)S(1)}, u32[]{:S(2)}, u32[]{:S(2)}) collective-permute-start(bf16[4,128,128]{2,1,0:T(8,128)(2,1)S(1)} %get-tuple-element.36), channel_id=1, source_target_pairs={{0,56},{1,60},{2,58},{3,62},{4,57},{5,61},{6,59},{7,63},{8,0},{9,4... | collective-permute-start | bytes 393224 | tf_op jit(solution)/shard_map/ppermute | solution.py:353
  13.0 4.6 %column_half.1 = bf16[768,3072]{1,0:T(8,128)(2,1)} custom-call(s32[1]{0:T(128)} %bitcast.2.half_ref, bf16[768,6144]{1,0:T(8,128)(2,1)} %refs_3_.3), custom_call_target="tpu_custom_call" | custom-call | tf_op jit(solution)/shard_map/column_half/pallas_call | solution.py:43
  17.7 3.1 %collective-permute-start.3 = (bf16[4,128,128]{2,1,0:T(8,128)(2,1)S(1)}, bf16[4,128,128]{2,1,0:T(8,128)(2,1)S(1)}, u32[]{:S(2)}, u32[]{:S(2)}) collective-permute-start(bf16[4,128,128]{2,1,0:T(8,128)(2,1)S(1)} %collective-permute-done.refs_0_), channel_id=1, source_target_pairs={{0,8},{8,16},{16,24},{24,32},{32,40},{40,48},{48,56},{56,0},{1,9},... | collective-permute-start | bytes 393224 | tf_op jit(solution)/shard_map/ppermute | solution.py:359
  20.8 5.5 %collective-permute-start.4 = (bf16[4,128,128]{2,1,0:T(8,128)(2,1)S(1)}, bf16[4,128,128]{2,1,0:T(8,128)(2,1)S(1)}, u32[]{:S(2)}, u32[]{:S(2)}) collective-permute-start(bf16[4,128,128]{2,1,0:T(8,128)(2,1)S(1)} %collective-permute-done.1.refs_1_), channel_id=1, source_target_pairs={{0,56},{8,0},{16,8},{24,16},{32,24},{40,32},{48,40},{56,48},{1,57}... | collective-permute-start | bytes 393224 | tf_op jit(solution)/shard_map/ppermute | solution.py:360
  26.3 2.7 %collective-permute-done.3.refs_2_ = bf16[4,128,128]{2,1,0:T(8,128)(2,1)S(1)} collective-permute-done((bf16[4,128,128]{2,1,0:T(8,128)(2,1)S(1)}, bf16[4,128,128]{2,1,0:T(8,128)(2,1)S(1)}, u32[]{:S(2)}, u32[]{:S(2)}) %collective-permute-start.3) | collective-permute-done | bytes 131104 | tf_op jit(solution)/shard_map/ppermute | solution.py:359
  29.1 2.6 %collective-permute-start.10 = (bf16[16,128,128]{2,1,0:T(8,128)(2,1)S(1)}, bf16[16,128,128]{2,1,0:T(8,128)(2,1)S(1)}, u32[]{:S(2)}, u32[]{:S(2)}) collective-permute-start(bf16[16,128,128]{2,1,0:T(8,128)(2,1)S(1)} %join.3.refs_3_), channel_id=1, source_target_pairs={{0,192},{64,0},{128,64},{192,128},{1,193},{65,1},{129,65},{193,129... | collective-permute-start | bytes 1572872 | tf_op jit(solution)/shard_map/ppermute | solution.py:365
  31.7 5.4 %collective-permute-done.5.refs_1_ = bf16[4,128,128]{2,1,0:T(8,128)(2,1)S(1)} collective-permute-done((bf16[4,128,128]{2,1,0:T(8,128)(2,1)S(1)}, bf16[4,128,128]{2,1,0:T(8,128)(2,1)S(1)}, u32[]{:S(2)}, u32[]{:S(2)}) %collective-permute-start.5) | collective-permute-done | bytes 131104 | tf_op jit(solution)/shard_map/ppermute | solution.py:366
  38.6 3.4 %collective-permute-done.6.refs_2_ = bf16[4,128,128]{2,1,0:T(8,128)(2,1)S(1)} collective-permute-done((bf16[4,128,128]{2,1,0:T(8,128)(2,1)S(1)}, bf16[4,128,128]{2,1,0:T(8,128)(2,1)S(1)}, u32[]{:S(2)}, u32[]{:S(2)}) %collective-permute-start.6) | collective-permute-done | bytes 131104 | tf_op jit(solution)/shard_map/ppermute | solution.py:367
  42.1 6.7 %collective-permute-done.7.refs_3_ = bf16[4,128,128]{2,1,0:T(8,128)(2,1)S(1)} collective-permute-done((bf16[4,128,128]{2,1,0:T(8,128)(2,1)S(1)}, bf16[4,128,128]{2,1,0:T(8,128)(2,1)S(1)}, u32[]{:S(2)}, u32[]{:S(2)}) %collective-permute-start.7) | collective-permute-done | bytes 131104 | tf_op jit(solution)/shard_map/ppermute | solution.py:368
  49.3 2.6 %collective-permute-start.14 = (bf16[16,128,128]{2,1,0:T(8,128)(2,1)S(1)}, bf16[16,128,128]{2,1,0:T(8,128)(2,1)S(1)}, u32[]{:S(2)}, u32[]{:S(2)}) collective-permute-start(bf16[16,128,128]{2,1,0:T(8,128)(2,1)S(1)} %join.2.refs_4_), channel_id=1, source_target_pairs={{0,192},{64,0},{128,64},{192,128},{1,193},{65,1},{129,65},{193,129... | collective-permute-start | bytes 1572872 | tf_op jit(solution)/shard_map/ppermute | solution.py:373
  51.9 7.2 %own_column.1 = (f32[2,152,768]{2,1,0:T(8,128)S(1)}, f32[2,152,768]{2,1,0:T(8,128)S(1)}) custom-call(s32[5,128]{1,0:T(8,128)S(1)} %pad_add_fusion.refs_0_, bf16[17,128,128]{2,1,0:T(8,128)(2,1)S(1)} %collective-permute-done.2.refs_1_, bf16[17,128,128]{2,1,0:T(8,128)(2,1)S(1)} %collective-permute-done.8.refs_2_, bf16[16,128,128]{2,1,0:T(8,128)(2,1)S(1)} %join.3.refs_3_, ...), custom_call_target="tpu_custom_call" | custom-call | tf_op jit(solution)/shard_map/own_column/pallas_call | solution.py:43
  59.2 2.7 %collective-permute-start.12 = (bf16[8,128,128]{2,1,0:T(8,128)(2,1)S(1)}, bf16[8,128,128]{2,1,0:T(8,128)(2,1)S(1)}, u32[]{:S(2)}, u32[]{:S(2)}) collective-permute-start(bf16[8,128,128]{2,1,0:T(8,128)(2,1)S(1)} %slice.25), channel_id=1, source_target_pairs={{0,192},{64,0},{128,64},{192,128},{1,193},{65,1},{129,65},{193,129... | collective-permute-start | bytes 786440 | tf_op jit(solution)/shard_map/ppermute | solution.py:384
  62.0 6.9 %early.1 = (f32[2,152,768]{2,1,0:T(8,128)S(1)}, f32[2,152,768]{2,1,0:T(8,128)S(1)}) custom-call(s32[5,128]{1,0:T(8,128)S(1)} %pad_add_fusion.refs_0_, bf16[17,128,128]{2,1,0:T(8,128)(2,1)S(1)} %collective-permute-done.2.refs_1_, bf16[17,128,128]{2,1,0:T(8,128)(2,1)S(1)} %collective-permute-done.8.refs_2_, ...), custom_call_target="tpu_custom_call", output_to_operand_aliasing={{0}: (5, {}), {1}: (6, {})} | custom-call | tf_op jit(solution)/shard_map/early/pallas_call | solution.py:43
  69.0 2.7 %collective-permute-start.16 = (bf16[8,128,128]{2,1,0:T(8,128)(2,1)S(1)}, bf16[8,128,128]{2,1,0:T(8,128)(2,1)S(1)}, u32[]{:S(2)}, u32[]{:S(2)}) collective-permute-start(bf16[8,128,128]{2,1,0:T(8,128)(2,1)S(1)} %slice.27), channel_id=1, source_target_pairs={{0,192},{64,0},{128,64},{192,128},{1,193},{65,1},{129,65},{193,129... | collective-permute-start | bytes 786440 | tf_op jit(solution)/shard_map/ppermute | solution.py:392
  71.8 6.4 %late.1 = (f32[2,152,768]{2,1,0:T(8,128)S(1)}, f32[2,152,768]{2,1,0:T(8,128)S(1)}) custom-call(s32[5,128]{1,0:T(8,128)S(1)} %pad_add_fusion.refs_0_, bf16[17,128,128]{2,1,0:T(8,128)(2,1)S(1)} %collective-permute-done.2.refs_1_, bf16[17,128,128]{2,1,0:T(8,128)(2,1)S(1)} %collective-permute-done.8.refs_2_, ...), custom_call_target="tpu_custom_call", output_to_operand_aliasing={{0}: (5, {}), {1}: (6, {})} | custom-call | tf_op jit(solution)/shard_map/late/pallas_call | solution.py:43
  78.2 3.5 %last_send.1 = f32[2,152,768]{2,1,0:T(8,128)S(1)} custom-call(s32[5,128]{1,0:T(8,128)S(1)} %pad_add_fusion.refs_0_, bf16[17,128,128]{2,1,0:T(8,128)(2,1)S(1)} %collective-permute-done.2.refs_1_, bf16[17,128,128]{2,1,0:T(8,128)(2,1)S(1)} %collective-permute-done.8.refs_2_, ...), custom_call_target="tpu_custom_call", output_to_operand_aliasing={{}: (7, {})} | custom-call | tf_op jit(solution)/shard_map/last_send/pallas_call | solution.py:43
  82.2 3.0 %last_keep.1.own_ref = f32[2,152,768]{2,1,0:T(8,128)S(1)} custom-call(s32[5,128]{1,0:T(8,128)S(1)} %pad_add_fusion.refs_0_, bf16[17,128,128]{2,1,0:T(8,128)(2,1)S(1)} %collective-permute-done.2.refs_1_, bf16[17,128,128]{2,1,0:T(8,128)(2,1)S(1)} %collective-permute-done.8.refs_2_, ...), custom_call_target="tpu_custom_call", output_to_operand_aliasing={{}: (7, {})} | custom-call | tf_op jit(solution)/shard_map/last_keep/pallas_call | solution.py:43
  85.5 6.9 %collective-permute-start.19 = (bf16[256,768]{1,0:T(8,128)(2,1)S(1)}, bf16[256,768]{1,0:T(8,128)(2,1)S(1)}, u32[]{:S(2)}, u32[]{:S(2)}) collective-permute-start(bf16[256,768]{1,0:T(8,128)(2,1)S(1)} %merge.1), channel_id=1, source_target_pairs={{0,0},{1,4},{2,2},{3,6},{4,1},{5,5},{6,3},{7,7},{8,8},{9,12},{10,1... | collective-permute-start | bytes 1179656 | tf_op jit(solution)/shard_map/ppermute | solution.py:406
  92.4 2.3 %collective-permute-start.20 = (bf16[256,768]{1,0:T(8,128)(2,1)S(1)}, bf16[256,768]{1,0:T(8,128)(2,1)S(1)}, u32[]{:S(2)}, u32[]{:S(2)}) collective-permute-start(bf16[256,768]{1,0:T(8,128)(2,1)S(1)} %merge.1), channel_id=1, source_target_pairs={{0,2},{1,6},{2,0},{3,4},{4,3},{5,7},{6,1},{7,5},{8,10},{9,14},{10,... | collective-permute-start | bytes 1179656 | tf_op jit(solution)/shard_map/ppermute | solution.py:407
  94.7 2.5 %fetch.1.refs_4_ = bf16[768,3072]{1,0:T(8,128)(2,1)S(1)} custom-call(bf16[768,3072]{1,0:T(8,128)(2,1)} %collective-permute-done.18.source_ref), custom_call_target="tpu_custom_call" | custom-call | tf_op jit(solution)/shard_map/fetch/pallas_call | solution.py:43
  97.2 3.5 %collective-permute-done.19.refs_1_ = bf16[256,768]{1,0:T(8,128)(2,1)S(1)} collective-permute-done((bf16[256,768]{1,0:T(8,128)(2,1)S(1)}, bf16[256,768]{1,0:T(8,128)(2,1)S(1)}, u32[]{:S(2)}, u32[]{:S(2)}) %collective-permute-start.19) | collective-permute-done | bytes 393248 | tf_op jit(solution)/shard_map/ppermute | solution.py:406
  100.7 2.9 %collective-permute-done.20.refs_2_ = bf16[256,768]{1,0:T(8,128)(2,1)S(1)} collective-permute-done((bf16[256,768]{1,0:T(8,128)(2,1)S(1)}, bf16[256,768]{1,0:T(8,128)(2,1)S(1)}, u32[]{:S(2)}, u32[]{:S(2)}) %collective-permute-start.20) | collective-permute-done | bytes 393248 | tf_op jit(solution)/shard_map/ppermute | solution.py:407
  103.6 2.0 %project_send.1 = bf16[256,1536]{1,0:T(8,128)(2,1)S(1)} custom-call(s32[2]{0:T(128)S(1)} %pad_add_fusion.1.refs_0_, bf16[256,768]{1,0:T(8,128)(2,1)S(1)} %collective-permute-done.19.refs_1_, bf16[256,768]{1,0:T(8,128)(2,1)S(1)} %collective-permute-done.20.refs_2_, bf16[768,6144]{1,0:T(8,128)(2,1)S(1)} %bitcast.12, bf16[768,3072]{1,0:T(8,128)(2,1)S(1)} %fetch.1.refs_4_), custom_call_target="tpu_custom_call" | custom-call | tf_op jit(solution)/shard_map/project_send/pallas_call | solution.py:43
  (53 shorter events, 9.4 us)
Async XLA Ops:
  1.3 16.3 %collective-permute-start.2 = (bf16[17,128,128]{2,1,0:T(8,128)(2,1)S(1)}, bf16[17,128,128]{2,1,0:T(8,128)(2,1)S(1)}, u32[]{:S(2)}, u32[]{:S(2)}) collective-permute-start(bf16[17,128,128]{2,1,0:T(8,128)(2,1)S(1)} %get-tuple-element.37), channel_id=1, source_target_pairs={{0,0},{1,4},{2,2},{3,6},{4,1},{5,5},{6,3},{7,7},{8,8},{9,12},{10,1... | collective-permute-start | bytes 1671176 | tf_op jit(solution)/shard_map/ppermute | solution.py:354
  7.5 10.0 %collective-permute-start = (bf16[4,128,128]{2,1,0:T(8,128)(2,1)S(1)}, bf16[4,128,128]{2,1,0:T(8,128)(2,1)S(1)}, u32[]{:S(2)}, u32[]{:S(2)}) collective-permute-start(bf16[4,128,128]{2,1,0:T(8,128)(2,1)S(1)} %get-tuple-element.36), channel_id=1, source_target_pairs={{0,8},{1,12},{2,10},{3,14},{4,9},{5,13},{6,11},{7,15},{8,16},{9,20... | collective-permute-start | bytes 393224 | tf_op jit(solution)/shard_map/ppermute | solution.py:353
  9.0 8.6 %collective-permute-start.1 = (bf16[4,128,128]{2,1,0:T(8,128)(2,1)S(1)}, bf16[4,128,128]{2,1,0:T(8,128)(2,1)S(1)}, u32[]{:S(2)}, u32[]{:S(2)}) collective-permute-start(bf16[4,128,128]{2,1,0:T(8,128)(2,1)S(1)} %get-tuple-element.36), channel_id=1, source_target_pairs={{0,56},{1,60},{2,58},{3,62},{4,57},{5,61},{6,59},{7,63},{8,0},{9,4... | collective-permute-start | bytes 393224 | tf_op jit(solution)/shard_map/ppermute | solution.py:353
  17.6 67.7 %collective-permute-start.18 = (bf16[768,3072]{1,0:T(8,128)(2,1)}, bf16[768,3072]{1,0:T(8,128)(2,1)}, u32[]{:S(2)}, u32[]{:S(2)}) collective-permute-start(bf16[768,3072]{1,0:T(8,128)(2,1)} %column_half.1), channel_id=1, source_target_pairs={{0,2},{1,7},{2,4},{3,1},{4,6},{5,3},{6,0},{7,5},{8,10},{9,15},{10,... | collective-permute-start | bytes 14155784 | tf_op jit(solution)/shard_map/ppermute | solution.py:358
  17.7 11.4 %collective-permute-start.3 = (bf16[4,128,128]{2,1,0:T(8,128)(2,1)S(1)}, bf16[4,128,128]{2,1,0:T(8,128)(2,1)S(1)}, u32[]{:S(2)}, u32[]{:S(2)}) collective-permute-start(bf16[4,128,128]{2,1,0:T(8,128)(2,1)S(1)} %collective-permute-done.refs_0_), channel_id=1, source_target_pairs={{0,8},{8,16},{16,24},{24,32},{32,40},{40,48},{48,56},{56,0},{1,9},... | collective-permute-start | bytes 393224 | tf_op jit(solution)/shard_map/ppermute | solution.py:359
  20.8 8.3 %collective-permute-start.4 = (bf16[4,128,128]{2,1,0:T(8,128)(2,1)S(1)}, bf16[4,128,128]{2,1,0:T(8,128)(2,1)S(1)}, u32[]{:S(2)}, u32[]{:S(2)}) collective-permute-start(bf16[4,128,128]{2,1,0:T(8,128)(2,1)S(1)} %collective-permute-done.1.refs_1_), channel_id=1, source_target_pairs={{0,56},{8,0},{16,8},{24,16},{32,24},{40,32},{48,40},{56,48},{1,57}... | collective-permute-start | bytes 393224 | tf_op jit(solution)/shard_map/ppermute | solution.py:360
  26.3 22.5 %collective-permute-start.8 = (bf16[17,128,128]{2,1,0:T(8,128)(2,1)S(1)}, bf16[17,128,128]{2,1,0:T(8,128)(2,1)S(1)}, u32[]{:S(2)}, u32[]{:S(2)}) collective-permute-start(bf16[17,128,128]{2,1,0:T(8,128)(2,1)S(1)} %collective-permute-done.2.refs_1_), channel_id=1, source_target_pairs={{0,1},{1,0},{2,3},{3,2},{4,5},{5,4},{6,7},{7,6},{8,9},{9,8},{10,11... | collective-permute-start | bytes 1671176 | tf_op jit(solution)/shard_map/ppermute | solution.py:370
  29.1 19.7 %collective-permute-start.10 = (bf16[16,128,128]{2,1,0:T(8,128)(2,1)S(1)}, bf16[16,128,128]{2,1,0:T(8,128)(2,1)S(1)}, u32[]{:S(2)}, u32[]{:S(2)}) collective-permute-start(bf16[16,128,128]{2,1,0:T(8,128)(2,1)S(1)} %join.3.refs_3_), channel_id=1, source_target_pairs={{0,192},{64,0},{128,64},{192,128},{1,193},{65,1},{129,65},{193,129... | collective-permute-start | bytes 1572872 | tf_op jit(solution)/shard_map/ppermute | solution.py:365
  31.7 17.2 %collective-permute-start.9 = (bf16[16,128,128]{2,1,0:T(8,128)(2,1)S(1)}, bf16[16,128,128]{2,1,0:T(8,128)(2,1)S(1)}, u32[]{:S(2)}, u32[]{:S(2)}) collective-permute-start(bf16[16,128,128]{2,1,0:T(8,128)(2,1)S(1)} %join.3.refs_3_), channel_id=1, source_target_pairs={{0,64},{64,128},{128,192},{192,0},{1,65},{65,129},{129,193},{193,1... | collective-permute-start | bytes 1572872 | tf_op jit(solution)/shard_map/ppermute | solution.py:364
  31.7 5.4 %collective-permute-start.5 = (bf16[4,128,128]{2,1,0:T(8,128)(2,1)S(1)}, bf16[4,128,128]{2,1,0:T(8,128)(2,1)S(1)}, u32[]{:S(2)}, u32[]{:S(2)}) collective-permute-start(bf16[4,128,128]{2,1,0:T(8,128)(2,1)S(1)} %collective-permute-done.3.refs_2_), channel_id=1, source_target_pairs={{0,8},{8,16},{16,24},{24,32},{32,40},{40,48},{48,56},{56,0},{1,9},... | collective-permute-start | bytes 393224 | tf_op jit(solution)/shard_map/ppermute | solution.py:366
  37.1 4.9 %collective-permute-start.6 = (bf16[4,128,128]{2,1,0:T(8,128)(2,1)S(1)}, bf16[4,128,128]{2,1,0:T(8,128)(2,1)S(1)}, u32[]{:S(2)}, u32[]{:S(2)}) collective-permute-start(bf16[4,128,128]{2,1,0:T(8,128)(2,1)S(1)} %collective-permute-done.4.refs_3_), channel_id=1, source_target_pairs={{0,56},{8,0},{16,8},{24,16},{32,24},{40,32},{48,40},{56,48},{1,57}... | collective-permute-start | bytes 393224 | tf_op jit(solution)/shard_map/ppermute | solution.py:367
  42.0 6.8 %collective-permute-start.7 = (bf16[4,128,128]{2,1,0:T(8,128)(2,1)S(1)}, bf16[4,128,128]{2,1,0:T(8,128)(2,1)S(1)}, u32[]{:S(2)}, u32[]{:S(2)}) collective-permute-start(bf16[4,128,128]{2,1,0:T(8,128)(2,1)S(1)} %collective-permute-done.5.refs_1_), channel_id=1, source_target_pairs={{0,8},{8,16},{16,24},{24,32},{32,40},{40,48},{48,56},{56,0},{1,9},... | collective-permute-start | bytes 393224 | tf_op jit(solution)/shard_map/ppermute | solution.py:368
  48.9 20.0 %collective-permute-start.13 = (bf16[16,128,128]{2,1,0:T(8,128)(2,1)S(1)}, bf16[16,128,128]{2,1,0:T(8,128)(2,1)S(1)}, u32[]{:S(2)}, u32[]{:S(2)}) collective-permute-start(bf16[16,128,128]{2,1,0:T(8,128)(2,1)S(1)} %join.2.refs_4_), channel_id=1, source_target_pairs={{0,64},{64,128},{128,192},{192,0},{1,65},{65,129},{129,193},{193,1... | collective-permute-start | bytes 1572872 | tf_op jit(solution)/shard_map/ppermute | solution.py:372
  49.3 19.6 %collective-permute-start.14 = (bf16[16,128,128]{2,1,0:T(8,128)(2,1)S(1)}, bf16[16,128,128]{2,1,0:T(8,128)(2,1)S(1)}, u32[]{:S(2)}, u32[]{:S(2)}) collective-permute-start(bf16[16,128,128]{2,1,0:T(8,128)(2,1)S(1)} %join.2.refs_4_), channel_id=1, source_target_pairs={{0,192},{64,0},{128,64},{192,128},{1,193},{65,1},{129,65},{193,129... | collective-permute-start | bytes 1572872 | tf_op jit(solution)/shard_map/ppermute | solution.py:373
  59.1 19.0 %collective-permute-start.11 = (bf16[8,128,128]{2,1,0:T(8,128)(2,1)S(1)}, bf16[8,128,128]{2,1,0:T(8,128)(2,1)S(1)}, u32[]{:S(2)}, u32[]{:S(2)}) collective-permute-start(bf16[8,128,128]{2,1,0:T(8,128)(2,1)S(1)} %slice.24), channel_id=1, source_target_pairs={{0,64},{64,128},{128,192},{192,0},{1,65},{65,129},{129,193},{193,1... | collective-permute-start | bytes 786440 | tf_op jit(solution)/shard_map/ppermute | solution.py:383
  59.2 18.9 %collective-permute-start.12 = (bf16[8,128,128]{2,1,0:T(8,128)(2,1)S(1)}, bf16[8,128,128]{2,1,0:T(8,128)(2,1)S(1)}, u32[]{:S(2)}, u32[]{:S(2)}) collective-permute-start(bf16[8,128,128]{2,1,0:T(8,128)(2,1)S(1)} %slice.25), channel_id=1, source_target_pairs={{0,192},{64,0},{128,64},{192,128},{1,193},{65,1},{129,65},{193,129... | collective-permute-start | bytes 786440 | tf_op jit(solution)/shard_map/ppermute | solution.py:384
  68.9 9.3 %collective-permute-start.15 = (bf16[8,128,128]{2,1,0:T(8,128)(2,1)S(1)}, bf16[8,128,128]{2,1,0:T(8,128)(2,1)S(1)}, u32[]{:S(2)}, u32[]{:S(2)}) collective-permute-start(bf16[8,128,128]{2,1,0:T(8,128)(2,1)S(1)} %slice.26), channel_id=1, source_target_pairs={{0,64},{64,128},{128,192},{192,0},{1,65},{65,129},{129,193},{193,1... | collective-permute-start | bytes 786440 | tf_op jit(solution)/shard_map/ppermute | solution.py:391
  69.0 9.2 %collective-permute-start.16 = (bf16[8,128,128]{2,1,0:T(8,128)(2,1)S(1)}, bf16[8,128,128]{2,1,0:T(8,128)(2,1)S(1)}, u32[]{:S(2)}, u32[]{:S(2)}) collective-permute-start(bf16[8,128,128]{2,1,0:T(8,128)(2,1)S(1)} %slice.27), channel_id=1, source_target_pairs={{0,192},{64,0},{128,64},{192,128},{1,193},{65,1},{129,65},{193,129... | collective-permute-start | bytes 786440 | tf_op jit(solution)/shard_map/ppermute | solution.py:392
  78.2 25.4 %slice-start = ((s8[9437184]{0:T(1024)(128)(4,1)}), s8[4194304]{0:T(1024)(128)(4,1)S(1)}, s32[]{:S(2)}) async-start(s8[9437184]{0:T(1024)(128)(4,1)} %bitcast.11), calls=%async_computation | async-start | bytes 8388608
  81.8 21.9 %slice-start.1 = ((s8[9437184]{0:T(1024)(128)(4,1)}), s8[4194304]{0:T(1024)(128)(4,1)S(1)}, s32[]{:S(2)}) async-start(s8[9437184]{0:T(1024)(128)(4,1)} %bitcast.11), calls=%async_computation.1 | async-start | bytes 8388608
  81.8 3.5 %collective-permute-start.17 = (f32[2,152,768]{2,1,0:T(8,128)S(1)}, f32[2,152,768]{2,1,0:T(8,128)S(1)}, u32[]{:S(2)}, u32[]{:S(2)}) collective-permute-start(f32[2,152,768]{2,1,0:T(8,128)S(1)} %last_send.1), channel_id=1, source_target_pairs={{0,1},{1,0},{2,3},{3,2},{4,5},{5,4},{6,7},{7,6},{8,9},{9,8},{10,11... | collective-permute-start | bytes 2801672 | tf_op jit(solution)/shard_map/ppermute | solution.py:400
  85.5 15.2 %collective-permute-start.19 = (bf16[256,768]{1,0:T(8,128)(2,1)S(1)}, bf16[256,768]{1,0:T(8,128)(2,1)S(1)}, u32[]{:S(2)}, u32[]{:S(2)}) collective-permute-start(bf16[256,768]{1,0:T(8,128)(2,1)S(1)} %merge.1), channel_id=1, source_target_pairs={{0,0},{1,4},{2,2},{3,6},{4,1},{5,5},{6,3},{7,7},{8,8},{9,12},{10,1... | collective-permute-start | bytes 1179656 | tf_op jit(solution)/shard_map/ppermute | solution.py:406
  92.4 11.2 %collective-permute-start.20 = (bf16[256,768]{1,0:T(8,128)(2,1)S(1)}, bf16[256,768]{1,0:T(8,128)(2,1)S(1)}, u32[]{:S(2)}, u32[]{:S(2)}) collective-permute-start(bf16[256,768]{1,0:T(8,128)(2,1)S(1)} %merge.1), channel_id=1, source_target_pairs={{0,2},{1,6},{2,0},{3,4},{4,3},{5,7},{6,1},{7,5},{8,10},{9,14},{10,... | collective-permute-start | bytes 1179656 | tf_op jit(solution)/shard_map/ppermute | solution.py:407
  105.6 2.4 %collective-permute-start.21 = (bf16[256,1536]{1,0:T(8,128)(2,1)S(1)}, bf16[256,1536]{1,0:T(8,128)(2,1)S(1)}, u32[]{:S(2)}, u32[]{:S(2)}) collective-permute-start(bf16[256,1536]{1,0:T(8,128)(2,1)S(1)} %project_send.1), channel_id=1, source_target_pairs={{0,1},{1,0},{2,3},{3,2},{4,5},{5,4},{6,7},{7,6},{8,9},{9,8},{10,11... | collective-permute-start | bytes 2359304 | tf_op jit(solution)/shard_map/ppermute | solution.py:411
  (1 other events, 8.9 us)

commit v8 on v7

--- a/solution.py
+++ b/solution.py
@@ -19,8 +19,8 @@
 MASK_AT = 2 * HEADS
 UNIT_AT = MASK_AT + 1
 EXP2_SCALE = math.log2(math.e) / math.sqrt(HD)
-EARLY = (-1, 1, -2, 2)
-LATE = (0, -3, 3, 4)
+EARLY = (-1, 1, 0, 4)
+LATE = (-2, 2, -3, 3)
 
 
 def vmem():
@@ -139,18 +139,22 @@
     return call(fetch_kernel, shape, (in_hbm(source),), [hbm()], scratch=scratch, name="fetch")
 
 
-def join_kernel(*refs):
+def join_kernel(starts, *refs):
     out_ref = refs[-1]
     at = 0
-    for ref in refs[:-1]:
-        out_ref[pl.ds(at, ref.shape[0])] = ref[...]
-        at += ref.shape[0]
+    for start, ref in zip(starts, refs[:-1]):
+        size = ref.shape[0] - start
+        out_ref[pl.ds(at, size)] = ref[pl.ds(start, size)]
+        at += size
 
 
 def join(parts):
-    total = sum(p.shape[0] for p in parts)
+    starts = [p[1] if isinstance(p, tuple) else 0 for p in parts]
+    parts = [p[0] if isinstance(p, tuple) else p for p in parts]
+    total = sum(p.shape[0] - start for p, start in zip(parts, starts))
     shape = jax.ShapeDtypeStruct((total, *parts[0].shape[1:]), parts[0].dtype)
-    return call(join_kernel, shape, parts, [vmem()] * len(parts), name="join")
+    kernel = lambda *refs: join_kernel(starts, *refs)
+    return call(kernel, shape, parts, [vmem()] * len(parts), name="join")
 
 
 def stage_kernel(columns, count, numbers, first, table_ref, mine_ref, theirs_ref, *refs):
@@ -352,25 +356,26 @@
     up, down = ring(NZ, 1), ring(NZ, -1)
     units = {-1: lax.ppermute(unit, YZ, turned(1)), 1: lax.ppermute(unit, YZ, turned(-1))}
     mine = lax.ppermute(bundle, Y, turn)
+    units[4] = lax.ppermute(unit, YZ, turned(4))
     half_away = column_half(out_weight, 1 - yl)
-    units[-1], units[1], mine, half_away = together((units[-1], units[1], mine, half_away))
+    units[-1], units[1], units[4], mine, half_away = together(
+        (units[-1], units[1], units[4], mine, half_away)
+    )
     away = along_y(lambda yh, yl, core: (*next_y(yh, yl, 1 - 2 * core), core))
     far_weight = lax.ppermute(half_away, Y, away)
-    units[-2] = lax.ppermute(units[-1], "z", up)
-    units[2] = lax.ppermute(units[1], "z", down)
-    units[-2], units[2] = together((units[-2], units[2]))
-    early = join([units[d] for d in EARLY])
+    early = join([units[-1], units[1], (mine, UNIT_AT), units[4]])
     forth, back = ring(NX, 1), ring(NX, -1)
     early_before = lax.ppermute(early, "x", forth)
     early_after = lax.ppermute(early, "x", back)
-    units[-3] = lax.ppermute(units[-2], "z", up)
-    units[3] = lax.ppermute(units[2], "z", down)
-    units[4] = lax.ppermute(units[-3], "z", up)
-    late = join([mine[UNIT_AT:]] + [units[d] for d in LATE[1:]])
-    theirs = lax.ppermute(mine, "core", swap)
-    late, theirs, early_before, early_after = together((late, theirs, early_before, early_after))
+    for step in (2, 3):
+        units[-step] = lax.ppermute(units[1 - step], "z", up)
+        units[step] = lax.ppermute(units[step - 1], "z", down)
+    late, mine, early_before, early_after = together(
+        (join([units[d] for d in LATE]), mine, early_before, early_after)
+    )
     late_before = lax.ppermute(late, "x", forth)
     late_after = lax.ppermute(late, "x", back)
+    theirs = lax.ppermute(mine, "core", swap)
     place = jnp.pad(jnp.stack([x, z, core]).astype(jnp.int32), (0, 125))[None]
     masks = jnp.concatenate([mine[MASK_AT, :2], theirs[MASK_AT, :2]]).astype(jnp.int32)
     table = jnp.concatenate([masks, place])
@@ -399,7 +404,6 @@
     (send,) = stage(*last, (send,), (2, 3), "last_send")
     received = lax.ppermute(send, "core", swap)
     (keep,) = stage(*last, (keep,), (0, 1), "last_keep")
-    keep, received, far_weight = together((keep, received, far_weight))
     shape = jax.ShapeDtypeStruct((2 * TILE, WIDE), jnp.bfloat16)
     attended = call(merge_kernel, shape, (keep, received), [vmem()] * 2, name="merge")
 

time: 108 us -> 98.4 us (0.911); the launches traced: 109 us -> 97.4 us
  waiting for transfers between devices: 25 us -> 16 us
  Pallas kernels: 40.6 us -> 34.1 us
  starting transfers between devices: 42.8 us -> 46.7 us
    ppermute x5, waiting for transfers between devices: 18.3 us -> 5.51 us  [the longest x2 5.5 us: per_device(): units[-step] = lax.ppermute(units[1 - step], 'z', up)]
    pallas_call x14, Pallas kernels: 40.6 us -> 34.1 us  [call(): pl.pallas_call(kernel, out_shape=out_shape, in_specs=in_specs, out_specs=...]
    ppermute x5, starting transfers between devices: 10.1 us -> 13.1 us  [the longest x1 6.6 us: per_device(): units[4] = lax.ppermute(unit, YZ, turned(4))]
    ppermute x1, waiting for transfers between devices: 3.5 us -> 5.69 us  [per_device(): near_part = lax.ppermute(attended, Y, turn)]
    ppermute x1, waiting for transfers between devices: 0.01 us -> 1.85 us  [per_device(): lax.ppermute(late_before[:half], 'x', forth)]
    ppermute x1, starting transfers between devices: 6.9 us -> 8.46 us  [per_device(): near_part = lax.ppermute(attended, Y, turn)]
    ppermute x1, starting transfers between devices: 0.01 us -> 1.29 us  [per_device(): early_before = lax.ppermute(early, 'x', forth)]
    ppermute x1, starting transfers between devices: 2.56 us -> 1.47 us  [per_device(): early_after = lax.ppermute(early, 'x', back)]
  transfers between devices with their start and end apart: 22 -> 22, of which waited for: 7 -> 6; matrix products, arithmetic and copies ran while one was open for 0% -> 0% of each run, Pallas kernels for 33% -> 31%
where the time goes in v8:
time: 98.4 us; the launch traced here: 97.4 us
  starting transfers between devices  46.7 us (47%)
  Pallas kernels  34.1 us (35%)
  waiting for transfers between devices  16 us (16%)
    pallas_call x14, Pallas kernels, call(): pl.pallas_call(kernel, out_shape=out_shape, in_specs=in_specs, out_specs=...  34.1 us
    ppermute x1, starting transfers between devices, per_device(): near_part = lax.ppermute(attended, Y, turn)  8.46 us
    ppermute x1, starting transfers between devices, per_device(): units[4] = lax.ppermute(unit, YZ, turned(4))  6.6 us
    ppermute x2, starting transfers between devices, per_device(): units[step] = lax.ppermute(units[step - 1], 'z', down)  6.53 us
    ppermute x1, starting transfers between devices, per_device(): mine = lax.ppermute(bundle, Y, turn)  6.21 us
    ppermute x1, waiting for transfers between devices, per_device(): near_part = lax.ppermute(attended, Y, turn)  5.69 us
    ppermute x2, waiting for transfers between devices, per_device(): units[-step] = lax.ppermute(units[1 - step], 'z', up)  5.5 us
    ppermute x1, starting transfers between devices, per_device(): lax.ppermute(unit, YZ, turned(-1))  4.03 us
  transfers between devices with their start and end apart: 22, of which 6 were waited for; matrix products, arithmetic and copies ran while one was open for 0% of the time, Pallas kernels for 31%

profile of v8, /device:TPU:1, one launch (start us, length us, event | category | flops | bytes accessed | tf_op | source)
XLA Modules:
  0.0 97.4 jit_solution(17448090121875533747)
XLA Ops:
  1.3 6.2 %collective-permute-start.3 = (bf16[17,128,128]{2,1,0:T(8,128)(2,1)S(1)}, bf16[17,128,128]{2,1,0:T(8,128)(2,1)S(1)}, u32[]{:S(2)}, u32[]{:S(2)}) collective-permute-start(bf16[17,128,128]{2,1,0:T(8,128)(2,1)S(1)} %get-tuple-element.33), channel_id=1, source_target_pairs={{0,0},{1,4},{2,2},{3,6},{4,1},{5,5},{6,3},{7,7},{8,8},{9,12},{10,1... | collective-permute-start | bytes 1671176 | tf_op jit(solution)/shard_map/ppermute | solution.py:358
  9.0 4.0 %collective-permute-start.1 = (bf16[4,128,128]{2,1,0:T(8,128)(2,1)S(1)}, bf16[4,128,128]{2,1,0:T(8,128)(2,1)S(1)}, u32[]{:S(2)}, u32[]{:S(2)}) collective-permute-start(bf16[4,128,128]{2,1,0:T(8,128)(2,1)S(1)} %get-tuple-element.32), channel_id=1, source_target_pairs={{0,56},{1,60},{2,58},{3,62},{4,57},{5,61},{6,59},{7,63},{8,0},{9,4... | collective-permute-start | bytes 393224 | tf_op jit(solution)/shard_map/ppermute | solution.py:357
  13.0 6.6 %collective-permute-start.2 = (bf16[4,128,128]{2,1,0:T(8,128)(2,1)S(1)}, bf16[4,128,128]{2,1,0:T(8,128)(2,1)S(1)}, u32[]{:S(2)}, u32[]{:S(2)}) collective-permute-start(bf16[4,128,128]{2,1,0:T(8,128)(2,1)S(1)} %get-tuple-element.32), channel_id=1, source_target_pairs={{0,32},{1,36},{2,34},{3,38},{4,33},{5,37},{6,35},{7,39},{8,40},{9,... | collective-permute-start | bytes 393224 | tf_op jit(solution)/shard_map/ppermute | solution.py:359
  19.6 4.5 %column_half.1 = bf16[768,3072]{1,0:T(8,128)(2,1)} custom-call(s32[1]{0:T(128)} %bitcast.2.half_ref, bf16[768,6144]{1,0:T(8,128)(2,1)} %refs_3_.3), custom_call_target="tpu_custom_call" | custom-call | tf_op jit(solution)/shard_map/column_half/pallas_call | solution.py:43
  25.6 1.5 %collective-permute-start.9 = (bf16[16,128,128]{2,1,0:T(8,128)(2,1)S(1)}, bf16[16,128,128]{2,1,0:T(8,128)(2,1)S(1)}, u32[]{:S(2)}, u32[]{:S(2)}) collective-permute-start(bf16[16,128,128]{2,1,0:T(8,128)(2,1)S(1)} %join.3.refs_3_), channel_id=1, source_target_pairs={{0,192},{64,0},{128,64},{192,128},{1,193},{65,1},{129,65},{193,129... | collective-permute-start | bytes 1572872 | tf_op jit(solution)/shard_map/ppermute | solution.py:369
  27.1 3.9 %collective-permute-start.5 = (bf16[4,128,128]{2,1,0:T(8,128)(2,1)S(1)}, bf16[4,128,128]{2,1,0:T(8,128)(2,1)S(1)}, u32[]{:S(2)}, u32[]{:S(2)}) collective-permute-start(bf16[4,128,128]{2,1,0:T(8,128)(2,1)S(1)} %collective-permute-done.1.refs_1_), channel_id=1, source_target_pairs={{0,56},{8,0},{16,8},{24,16},{32,24},{40,32},{48,40},{56,48},{1,57}... | collective-permute-start | bytes 393224 | tf_op jit(solution)/shard_map/ppermute | solution.py:372
  30.9 2.8 %collective-permute-done.4.refs_0_ = bf16[4,128,128]{2,1,0:T(8,128)(2,1)S(1)} collective-permute-done((bf16[4,128,128]{2,1,0:T(8,128)(2,1)S(1)}, bf16[4,128,128]{2,1,0:T(8,128)(2,1)S(1)}, u32[]{:S(2)}, u32[]{:S(2)}) %collective-permute-start.4) | collective-permute-done | bytes 131104 | tf_op jit(solution)/shard_map/ppermute | solution.py:371
  33.7 2.7 %collective-permute-start.7 = (bf16[4,128,128]{2,1,0:T(8,128)(2,1)S(1)}, bf16[4,128,128]{2,1,0:T(8,128)(2,1)S(1)}, u32[]{:S(2)}, u32[]{:S(2)}) collective-permute-start(bf16[4,128,128]{2,1,0:T(8,128)(2,1)S(1)} %collective-permute-done.5.refs_1_), channel_id=1, source_target_pairs={{0,56},{8,0},{16,8},{24,16},{32,24},{40,32},{48,40},{56,48},{1,57}... | collective-permute-start | bytes 393224 | tf_op jit(solution)/shard_map/ppermute | solution.py:372
  36.4 2.7 %collective-permute-done.6.refs_2_ = bf16[4,128,128]{2,1,0:T(8,128)(2,1)S(1)} collective-permute-done((bf16[4,128,128]{2,1,0:T(8,128)(2,1)S(1)}, bf16[4,128,128]{2,1,0:T(8,128)(2,1)S(1)}, u32[]{:S(2)}, u32[]{:S(2)}) %collective-permute-start.6) | collective-permute-done | bytes 131104 | tf_op jit(solution)/shard_map/ppermute | solution.py:371
  39.7 2.4 %collective-permute-start.14 = (bf16[16,128,128]{2,1,0:T(8,128)(2,1)S(1)}, bf16[16,128,128]{2,1,0:T(8,128)(2,1)S(1)}, u32[]{:S(2)}, u32[]{:S(2)}) collective-permute-start(bf16[16,128,128]{2,1,0:T(8,128)(2,1)S(1)} %join.2.refs_4_), channel_id=1, source_target_pairs={{0,192},{64,0},{128,64},{192,128},{1,193},{65,1},{129,65},{193,129... | collective-permute-start | bytes 1572872 | tf_op jit(solution)/shard_map/ppermute | solution.py:377
  42.2 2.7 %collective-permute-start.12 = (bf16[8,128,128]{2,1,0:T(8,128)(2,1)S(1)}, bf16[8,128,128]{2,1,0:T(8,128)(2,1)S(1)}, u32[]{:S(2)}, u32[]{:S(2)}) collective-permute-start(bf16[8,128,128]{2,1,0:T(8,128)(2,1)S(1)} %slice.21), channel_id=1, source_target_pairs={{0,192},{64,0},{128,64},{192,128},{1,193},{65,1},{129,65},{193,129... | collective-permute-start | bytes 786440 | tf_op jit(solution)/shard_map/ppermute | solution.py:389
  45.0 4.7 %own_column.1 = (f32[2,152,768]{2,1,0:T(8,128)S(1)}, f32[2,152,768]{2,1,0:T(8,128)S(1)}) custom-call(s32[5,128]{1,0:T(8,128)S(1)} %pad_add_fusion.refs_0_, bf16[17,128,128]{2,1,0:T(8,128)(2,1)S(1)} %collective-permute-done.3.refs_2_.refs_1_, bf16[17,128,128]{2,1,0:T(8,128)(2,1)S(1)} %collective-permute-done.10.refs_2_, ...), custom_call_target="tpu_custom_call" | custom-call | tf_op jit(solution)/shard_map/own_column/pallas_call | solution.py:43
  49.6 4.7 %early.1 = (f32[2,152,768]{2,1,0:T(8,128)S(1)}, f32[2,152,768]{2,1,0:T(8,128)S(1)}) custom-call(s32[5,128]{1,0:T(8,128)S(1)} %pad_add_fusion.refs_0_, bf16[17,128,128]{2,1,0:T(8,128)(2,1)S(1)} %collective-permute-done.3.refs_2_.refs_1_, bf16[17,128,128]{2,1,0:T(8,128)(2,1)S(1)} %collective-permute-done.10.refs_2_, ...), custom_call_target="tpu_custom_call", output_to_operand_aliasing={{0}: (5, {}), {1}: (6, {})} | custom-call | tf_op jit(solution)/shard_map/early/pallas_call | solution.py:43
  54.5 2.7 %collective-permute-start.16 = (bf16[8,128,128]{2,1,0:T(8,128)(2,1)S(1)}, bf16[8,128,128]{2,1,0:T(8,128)(2,1)S(1)}, u32[]{:S(2)}, u32[]{:S(2)}) collective-permute-start(bf16[8,128,128]{2,1,0:T(8,128)(2,1)S(1)} %slice.23), channel_id=1, source_target_pairs={{0,192},{64,0},{128,64},{192,128},{1,193},{65,1},{129,65},{193,129... | collective-permute-start | bytes 786440 | tf_op jit(solution)/shard_map/ppermute | solution.py:397
  57.2 5.9 %late.1 = (f32[2,152,768]{2,1,0:T(8,128)S(1)}, f32[2,152,768]{2,1,0:T(8,128)S(1)}) custom-call(s32[5,128]{1,0:T(8,128)S(1)} %pad_add_fusion.refs_0_, bf16[17,128,128]{2,1,0:T(8,128)(2,1)S(1)} %collective-permute-done.3.refs_2_.refs_1_, bf16[17,128,128]{2,1,0:T(8,128)(2,1)S(1)} %collective-permute-done.10.refs_2_, ...), custom_call_target="tpu_custom_call", output_to_operand_aliasing={{0}: (5, {}), {1}: (6, {})} | custom-call | tf_op jit(solution)/shard_map/late/pallas_call | solution.py:43
  63.1 1.9 %collective-permute-done.15.refs_5_ = bf16[8,128,128]{2,1,0:T(8,128)(2,1)S(1)} collective-permute-done((bf16[8,128,128]{2,1,0:T(8,128)(2,1)S(1)}, bf16[8,128,128]{2,1,0:T(8,128)(2,1)S(1)}, u32[]{:S(2)}, u32[]{:S(2)}) %collective-permute-start.15) | collective-permute-done | bytes 262176 | tf_op jit(solution)/shard_map/ppermute | solution.py:396
  65.0 2.8 %last_send.1 = f32[2,152,768]{2,1,0:T(8,128)S(1)} custom-call(s32[5,128]{1,0:T(8,128)S(1)} %pad_add_fusion.refs_0_, bf16[17,128,128]{2,1,0:T(8,128)(2,1)S(1)} %collective-permute-done.3.refs_2_.refs_1_, bf16[17,128,128]{2,1,0:T(8,128)(2,1)S(1)} %collective-permute-done.10.refs_2_, ...), custom_call_target="tpu_custom_call", output_to_operand_aliasing={{}: (7, {})} | custom-call | tf_op jit(solution)/shard_map/last_send/pallas_call | solution.py:43
  68.6 2.5 %last_keep.1.own_ref = f32[2,152,768]{2,1,0:T(8,128)S(1)} custom-call(s32[5,128]{1,0:T(8,128)S(1)} %pad_add_fusion.refs_0_, bf16[17,128,128]{2,1,0:T(8,128)(2,1)S(1)} %collective-permute-done.3.refs_2_.refs_1_, bf16[17,128,128]{2,1,0:T(8,128)(2,1)S(1)} %collective-permute-done.10.refs_2_, ...), custom_call_target="tpu_custom_call", output_to_operand_aliasing={{}: (7, {})} | custom-call | tf_op jit(solution)/shard_map/last_keep/pallas_call | solution.py:43
  71.3 8.5 %collective-permute-start.18 = (bf16[256,768]{1,0:T(8,128)(2,1)S(1)}, bf16[256,768]{1,0:T(8,128)(2,1)S(1)}, u32[]{:S(2)}, u32[]{:S(2)}) collective-permute-start(bf16[256,768]{1,0:T(8,128)(2,1)S(1)} %merge.1), channel_id=1, source_target_pairs={{0,0},{1,4},{2,2},{3,6},{4,1},{5,5},{6,3},{7,7},{8,8},{9,12},{10,1... | collective-permute-start | bytes 1179656 | tf_op jit(solution)/shard_map/ppermute | solution.py:410
  81.2 2.5 %fetch.1.refs_4_ = bf16[768,3072]{1,0:T(8,128)(2,1)S(1)} custom-call(bf16[768,3072]{1,0:T(8,128)(2,1)} %collective-permute-done.20.source_ref), custom_call_target="tpu_custom_call" | custom-call | tf_op jit(solution)/shard_map/fetch/pallas_call | solution.py:43
  83.6 5.7 %collective-permute-done.18.refs_1_ = bf16[256,768]{1,0:T(8,128)(2,1)S(1)} collective-permute-done((bf16[256,768]{1,0:T(8,128)(2,1)S(1)}, bf16[256,768]{1,0:T(8,128)(2,1)S(1)}, u32[]{:S(2)}, u32[]{:S(2)}) %collective-permute-start.18) | collective-permute-done | bytes 393248 | tf_op jit(solution)/shard_map/ppermute | solution.py:410
  89.3 2.6 %collective-permute-done.19.refs_2_ = bf16[256,768]{1,0:T(8,128)(2,1)S(1)} collective-permute-done((bf16[256,768]{1,0:T(8,128)(2,1)S(1)}, bf16[256,768]{1,0:T(8,128)(2,1)S(1)}, u32[]{:S(2)}, u32[]{:S(2)}) %collective-permute-start.19) | collective-permute-done | bytes 393248 | tf_op jit(solution)/shard_map/ppermute | solution.py:411
  92.0 2.0 %project_send.1 = bf16[256,1536]{1,0:T(8,128)(2,1)S(1)} custom-call(s32[2]{0:T(128)S(1)} %pad_add_fusion.1.refs_0_, bf16[256,768]{1,0:T(8,128)(2,1)S(1)} %collective-permute-done.18.refs_1_, bf16[256,768]{1,0:T(8,128)(2,1)S(1)} %collective-permute-done.19.refs_2_, bf16[768,6144]{1,0:T(8,128)(2,1)S(1)} %bitcast.12, bf16[768,3072]{1,0:T(8,128)(2,1)S(1)} %fetch.1.refs_4_), custom_call_target="tpu_custom_call" | custom-call | tf_op jit(solution)/shard_map/project_send/pallas_call | solution.py:43
  94.1 2.0 %project_keep.1.keep_ref = f32[256,1536]{1,0:T(8,128)S(1)} custom-call(s32[2]{0:T(128)S(1)} %pad_add_fusion.1.refs_0_, bf16[256,768]{1,0:T(8,128)(2,1)S(1)} %collective-permute-done.18.refs_1_, bf16[256,768]{1,0:T(8,128)(2,1)S(1)} %collective-permute-done.19.refs_2_, bf16[768,6144]{1,0:T(8,128)(2,1)S(1)} %bitcast.12, bf16[768,3072]{1,0:T(8,128)(2,1)S(1)} %fetch.1.refs_4_), custom_call_target="tpu_custom_call" | custom-call | tf_op jit(solution)/shard_map/project_keep/pallas_call | solution.py:43
  (52 shorter events, 8.8 us)
Async XLA Ops:
  1.3 22.9 %collective-permute-start.3 = (bf16[17,128,128]{2,1,0:T(8,128)(2,1)S(1)}, bf16[17,128,128]{2,1,0:T(8,128)(2,1)S(1)}, u32[]{:S(2)}, u32[]{:S(2)}) collective-permute-start(bf16[17,128,128]{2,1,0:T(8,128)(2,1)S(1)} %get-tuple-element.33), channel_id=1, source_target_pairs={{0,0},{1,4},{2,2},{3,6},{4,1},{5,5},{6,3},{7,7},{8,8},{9,12},{10,1... | collective-permute-start | bytes 1671176 | tf_op jit(solution)/shard_map/ppermute | solution.py:358
  7.5 16.6 %collective-permute-start = (bf16[4,128,128]{2,1,0:T(8,128)(2,1)S(1)}, bf16[4,128,128]{2,1,0:T(8,128)(2,1)S(1)}, u32[]{:S(2)}, u32[]{:S(2)}) collective-permute-start(bf16[4,128,128]{2,1,0:T(8,128)(2,1)S(1)} %get-tuple-element.32), channel_id=1, source_target_pairs={{0,8},{1,12},{2,10},{3,14},{4,9},{5,13},{6,11},{7,15},{8,16},{9,20... | collective-permute-start | bytes 393224 | tf_op jit(solution)/shard_map/ppermute | solution.py:357
  9.0 15.2 %collective-permute-start.1 = (bf16[4,128,128]{2,1,0:T(8,128)(2,1)S(1)}, bf16[4,128,128]{2,1,0:T(8,128)(2,1)S(1)}, u32[]{:S(2)}, u32[]{:S(2)}) collective-permute-start(bf16[4,128,128]{2,1,0:T(8,128)(2,1)S(1)} %get-tuple-element.32), channel_id=1, source_target_pairs={{0,56},{1,60},{2,58},{3,62},{4,57},{5,61},{6,59},{7,63},{8,0},{9,4... | collective-permute-start | bytes 393224 | tf_op jit(solution)/shard_map/ppermute | solution.py:357
  13.0 11.2 %collective-permute-start.2 = (bf16[4,128,128]{2,1,0:T(8,128)(2,1)S(1)}, bf16[4,128,128]{2,1,0:T(8,128)(2,1)S(1)}, u32[]{:S(2)}, u32[]{:S(2)}) collective-permute-start(bf16[4,128,128]{2,1,0:T(8,128)(2,1)S(1)} %get-tuple-element.32), channel_id=1, source_target_pairs={{0,32},{1,36},{2,34},{3,38},{4,33},{5,37},{6,35},{7,39},{8,40},{9,... | collective-permute-start | bytes 393224 | tf_op jit(solution)/shard_map/ppermute | solution.py:359
  24.2 57.0 %collective-permute-start.20 = (bf16[768,3072]{1,0:T(8,128)(2,1)}, bf16[768,3072]{1,0:T(8,128)(2,1)}, u32[]{:S(2)}, u32[]{:S(2)}) collective-permute-start(bf16[768,3072]{1,0:T(8,128)(2,1)} %column_half.1), channel_id=1, source_target_pairs={{0,2},{1,7},{2,4},{3,1},{4,6},{5,3},{6,0},{7,5},{8,10},{9,15},{10,... | collective-permute-start | bytes 14155784 | tf_op jit(solution)/shard_map/ppermute | solution.py:365
  24.3 14.8 %collective-permute-start.8 = (bf16[16,128,128]{2,1,0:T(8,128)(2,1)S(1)}, bf16[16,128,128]{2,1,0:T(8,128)(2,1)S(1)}, u32[]{:S(2)}, u32[]{:S(2)}) collective-permute-start(bf16[16,128,128]{2,1,0:T(8,128)(2,1)S(1)} %join.3.refs_3_), channel_id=1, source_target_pairs={{0,64},{64,128},{128,192},{192,0},{1,65},{65,129},{129,193},{193,1... | collective-permute-start | bytes 1572872 | tf_op jit(solution)/shard_map/ppermute | solution.py:368
  25.6 13.6 %collective-permute-start.9 = (bf16[16,128,128]{2,1,0:T(8,128)(2,1)S(1)}, bf16[16,128,128]{2,1,0:T(8,128)(2,1)S(1)}, u32[]{:S(2)}, u32[]{:S(2)}) collective-permute-start(bf16[16,128,128]{2,1,0:T(8,128)(2,1)S(1)} %join.3.refs_3_), channel_id=1, source_target_pairs={{0,192},{64,0},{128,64},{192,128},{1,193},{65,1},{129,65},{193,129... | collective-permute-start | bytes 1572872 | tf_op jit(solution)/shard_map/ppermute | solution.py:369
  27.1 6.6 %collective-permute-start.4 = (bf16[4,128,128]{2,1,0:T(8,128)(2,1)S(1)}, bf16[4,128,128]{2,1,0:T(8,128)(2,1)S(1)}, u32[]{:S(2)}, u32[]{:S(2)}) collective-permute-start(bf16[4,128,128]{2,1,0:T(8,128)(2,1)S(1)} %collective-permute-done.refs_0_), channel_id=1, source_target_pairs={{0,8},{8,16},{16,24},{24,32},{32,40},{40,48},{48,56},{56,0},{1,9},... | collective-permute-start | bytes 393224 | tf_op jit(solution)/shard_map/ppermute | solution.py:371
  27.1 6.6 %collective-permute-start.5 = (bf16[4,128,128]{2,1,0:T(8,128)(2,1)S(1)}, bf16[4,128,128]{2,1,0:T(8,128)(2,1)S(1)}, u32[]{:S(2)}, u32[]{:S(2)}) collective-permute-start(bf16[4,128,128]{2,1,0:T(8,128)(2,1)S(1)} %collective-permute-done.1.refs_1_), channel_id=1, source_target_pairs={{0,56},{8,0},{16,8},{24,16},{32,24},{40,32},{48,40},{56,48},{1,57}... | collective-permute-start | bytes 393224 | tf_op jit(solution)/shard_map/ppermute | solution.py:372
  33.7 5.4 %collective-permute-start.6 = (bf16[4,128,128]{2,1,0:T(8,128)(2,1)S(1)}, bf16[4,128,128]{2,1,0:T(8,128)(2,1)S(1)}, u32[]{:S(2)}, u32[]{:S(2)}) collective-permute-start(bf16[4,128,128]{2,1,0:T(8,128)(2,1)S(1)} %collective-permute-done.4.refs_0_), channel_id=1, source_target_pairs={{0,8},{8,16},{16,24},{24,32},{32,40},{40,48},{48,56},{56,0},{1,9},... | collective-permute-start | bytes 393224 | tf_op jit(solution)/shard_map/ppermute | solution.py:371
  33.7 5.4 %collective-permute-start.7 = (bf16[4,128,128]{2,1,0:T(8,128)(2,1)S(1)}, bf16[4,128,128]{2,1,0:T(8,128)(2,1)S(1)}, u32[]{:S(2)}, u32[]{:S(2)}) collective-permute-start(bf16[4,128,128]{2,1,0:T(8,128)(2,1)S(1)} %collective-permute-done.5.refs_1_), channel_id=1, source_target_pairs={{0,56},{8,0},{16,8},{24,16},{32,24},{40,32},{48,40},{56,48},{1,57}... | collective-permute-start | bytes 393224 | tf_op jit(solution)/shard_map/ppermute | solution.py:372
  39.2 3.0 %collective-permute-start.10 = (bf16[17,128,128]{2,1,0:T(8,128)(2,1)S(1)}, bf16[17,128,128]{2,1,0:T(8,128)(2,1)S(1)}, u32[]{:S(2)}, u32[]{:S(2)}) collective-permute-start(bf16[17,128,128]{2,1,0:T(8,128)(2,1)S(1)} %collective-permute-done.3.refs_2_.refs_1_), channel_id=1, source_target_pairs={{0,1},{1,0},{2,3},{3,2},{4,5},{5,4},{6,7},{7,6},{8,9},{9,8},{10,11... | collective-permute-start | bytes 1671176 | tf_op jit(solution)/shard_map/ppermute | solution.py:378
  39.4 14.9 %collective-permute-start.13 = (bf16[16,128,128]{2,1,0:T(8,128)(2,1)S(1)}, bf16[16,128,128]{2,1,0:T(8,128)(2,1)S(1)}, u32[]{:S(2)}, u32[]{:S(2)}) collective-permute-start(bf16[16,128,128]{2,1,0:T(8,128)(2,1)S(1)} %join.2.refs_4_), channel_id=1, source_target_pairs={{0,64},{64,128},{128,192},{192,0},{1,65},{65,129},{129,193},{193,1... | collective-permute-start | bytes 1572872 | tf_op jit(solution)/shard_map/ppermute | solution.py:376
  39.7 14.6 %collective-permute-start.14 = (bf16[16,128,128]{2,1,0:T(8,128)(2,1)S(1)}, bf16[16,128,128]{2,1,0:T(8,128)(2,1)S(1)}, u32[]{:S(2)}, u32[]{:S(2)}) collective-permute-start(bf16[16,128,128]{2,1,0:T(8,128)(2,1)S(1)} %join.2.refs_4_), channel_id=1, source_target_pairs={{0,192},{64,0},{128,64},{192,128},{1,193},{65,1},{129,65},{193,129... | collective-permute-start | bytes 1572872 | tf_op jit(solution)/shard_map/ppermute | solution.py:377
  42.1 21.0 %collective-permute-start.11 = (bf16[8,128,128]{2,1,0:T(8,128)(2,1)S(1)}, bf16[8,128,128]{2,1,0:T(8,128)(2,1)S(1)}, u32[]{:S(2)}, u32[]{:S(2)}) collective-permute-start(bf16[8,128,128]{2,1,0:T(8,128)(2,1)S(1)} %slice.20), channel_id=1, source_target_pairs={{0,64},{64,128},{128,192},{192,0},{1,65},{65,129},{129,193},{193,1... | collective-permute-start | bytes 786440 | tf_op jit(solution)/shard_map/ppermute | solution.py:388
  42.2 20.9 %collective-permute-start.12 = (bf16[8,128,128]{2,1,0:T(8,128)(2,1)S(1)}, bf16[8,128,128]{2,1,0:T(8,128)(2,1)S(1)}, u32[]{:S(2)}, u32[]{:S(2)}) collective-permute-start(bf16[8,128,128]{2,1,0:T(8,128)(2,1)S(1)} %slice.21), channel_id=1, source_target_pairs={{0,192},{64,0},{128,64},{192,128},{1,193},{65,1},{129,65},{193,129... | collective-permute-start | bytes 786440 | tf_op jit(solution)/shard_map/ppermute | solution.py:389
  54.4 10.6 %collective-permute-start.15 = (bf16[8,128,128]{2,1,0:T(8,128)(2,1)S(1)}, bf16[8,128,128]{2,1,0:T(8,128)(2,1)S(1)}, u32[]{:S(2)}, u32[]{:S(2)}) collective-permute-start(bf16[8,128,128]{2,1,0:T(8,128)(2,1)S(1)} %slice.22), channel_id=1, source_target_pairs={{0,64},{64,128},{128,192},{192,0},{1,65},{65,129},{129,193},{193,1... | collective-permute-start | bytes 786440 | tf_op jit(solution)/shard_map/ppermute | solution.py:396
  54.5 10.5 %collective-permute-start.16 = (bf16[8,128,128]{2,1,0:T(8,128)(2,1)S(1)}, bf16[8,128,128]{2,1,0:T(8,128)(2,1)S(1)}, u32[]{:S(2)}, u32[]{:S(2)}) collective-permute-start(bf16[8,128,128]{2,1,0:T(8,128)(2,1)S(1)} %slice.23), channel_id=1, source_target_pairs={{0,192},{64,0},{128,64},{192,128},{1,193},{65,1},{129,65},{193,129... | collective-permute-start | bytes 786440 | tf_op jit(solution)/shard_map/ppermute | solution.py:397
  65.0 27.0 %slice-start = ((s8[9437184]{0:T(1024)(128)(4,1)}), s8[4194304]{0:T(1024)(128)(4,1)S(1)}, s32[]{:S(2)}) async-start(s8[9437184]{0:T(1024)(128)(4,1)} %bitcast.11), calls=%async_computation | async-start | bytes 8388608
  67.7 24.2 %slice-start.1 = ((s8[9437184]{0:T(1024)(128)(4,1)}), s8[4194304]{0:T(1024)(128)(4,1)S(1)}, s32[]{:S(2)}) async-start(s8[9437184]{0:T(1024)(128)(4,1)} %bitcast.11), calls=%async_computation.1 | async-start | bytes 8388608
  67.8 3.3 %collective-permute-start.17 = (f32[2,152,768]{2,1,0:T(8,128)S(1)}, f32[2,152,768]{2,1,0:T(8,128)S(1)}, u32[]{:S(2)}, u32[]{:S(2)}) collective-permute-start(f32[2,152,768]{2,1,0:T(8,128)S(1)} %last_send.1), channel_id=1, source_target_pairs={{0,1},{1,0},{2,3},{3,2},{4,5},{5,4},{6,7},{7,6},{8,9},{9,8},{10,11... | collective-permute-start | bytes 2801672 | tf_op jit(solution)/shard_map/ppermute | solution.py:405
  71.3 18.0 %collective-permute-start.18 = (bf16[256,768]{1,0:T(8,128)(2,1)S(1)}, bf16[256,768]{1,0:T(8,128)(2,1)S(1)}, u32[]{:S(2)}, u32[]{:S(2)}) collective-permute-start(bf16[256,768]{1,0:T(8,128)(2,1)S(1)} %merge.1), channel_id=1, source_target_pairs={{0,0},{1,4},{2,2},{3,6},{4,1},{5,5},{6,3},{7,7},{8,8},{9,12},{10,1... | collective-permute-start | bytes 1179656 | tf_op jit(solution)/shard_map/ppermute | solution.py:410
  79.8 12.2 %collective-permute-start.19 = (bf16[256,768]{1,0:T(8,128)(2,1)S(1)}, bf16[256,768]{1,0:T(8,128)(2,1)S(1)}, u32[]{:S(2)}, u32[]{:S(2)}) collective-permute-start(bf16[256,768]{1,0:T(8,128)(2,1)S(1)} %merge.1), channel_id=1, source_target_pairs={{0,2},{1,6},{2,0},{3,4},{4,3},{5,7},{6,1},{7,5},{8,10},{9,14},{10,... | collective-permute-start | bytes 1179656 | tf_op jit(solution)/shard_map/ppermute | solution.py:411
  94.0 2.4 %collective-permute-start.21 = (bf16[256,1536]{1,0:T(8,128)(2,1)S(1)}, bf16[256,1536]{1,0:T(8,128)(2,1)S(1)}, u32[]{:S(2)}, u32[]{:S(2)}) collective-permute-start(bf16[256,1536]{1,0:T(8,128)(2,1)S(1)} %project_send.1), channel_id=1, source_target_pairs={{0,1},{1,0},{2,3},{3,2},{4,5},{5,4},{6,7},{7,6},{8,9},{9,8},{10,11... | collective-permute-start | bytes 2359304 | tf_op jit(solution)/shard_map/ppermute | solution.py:415
  (1 other events, 10.8 us)

commit v9 on v8

--- a/solution.py
+++ b/solution.py
@@ -382,15 +382,14 @@
 
     near = (table, mine, theirs)
     every = (0, 1, 2, 3)
-    state = stage(((0, EARLY), (0, LATE)), near, [early, late], None, every, "own_column")
     half = early.shape[0] // 2
     early_far = [
         lax.ppermute(early_before[:half], "x", forth),
         lax.ppermute(early_after[half:], "x", back),
     ]
-    state = stage(
-        ((-1, EARLY), (1, EARLY)), near, [early_before, early_after], state, every, "early"
-    )
+    columns = ((0, EARLY), (0, LATE), (-1, EARLY), (1, EARLY))
+    parts = [early, late, early_before, early_after]
+    state = stage(columns, near, parts, None, every, "first")
     late_before, late_after, *state = together((late_before, late_after, *state))
     late_far = [
         lax.ppermute(late_before[:half], "x", forth),

time: 98.4 us -> 94.9 us (0.964)
  waiting for transfers between devices: 16 us -> 23.1 us
  Pallas kernels: 34.1 us -> 27.5 us
  starting transfers between devices: 46.7 us -> 43 us
    pallas_call x14 -> x13, Pallas kernels: 34.1 us -> 27.5 us  [call(): pl.pallas_call(kernel, out_shape=out_shape, in_specs=in_specs, out_specs=...]
    ppermute x1, starting transfers between devices: 8.46 us -> 4.61 us  [per_device(): near_part = lax.ppermute(attended, Y, turn)]
    ppermute x1, waiting for transfers between devices: 1.85 us -> 4.77 us  [per_device(): lax.ppermute(late_before[:half], 'x', forth)]
    ppermute x1, waiting for transfers between devices: 0.01 us -> 2.64 us  [per_device(): late_after = lax.ppermute(late, 'x', back)]
    ppermute x1, waiting for transfers between devices: 2.63 us -> 0.01 us  [per_device(): lax.ppermute(attended, Y, along_y(lambda yh, yl, core: (core, 1 - yl, yh)))]
    ppermute x1, starting transfers between devices: 0.8 us -> 3.41 us  [per_device(): received = lax.ppermute(send, 'core', swap)]
    ppermute x1, starting transfers between devices: 1.31 us -> 3.32 us  [per_device(): lax.ppermute(attended, Y, along_y(lambda yh, yl, core: (core, 1 - yl, yh)))]
    ppermute x1, waiting for transfers between devices: 0.01 us -> 1.93 us  [per_device(): late_before = lax.ppermute(late, 'x', forth)]
  transfers between devices with their start and end apart: 22 -> 22, of which waited for: 6 -> 10; matrix products, arithmetic and copies ran while one was open for 0% -> 0% of each run, Pallas kernels for 31% -> 25%
where the time goes in v9:
time: 94.9 us; the launch traced here: 94.1 us
  starting transfers between devices  43 us (45%)
  Pallas kernels  27.5 us (29%)
  waiting for transfers between devices  23.1 us (24%)
    pallas_call x13, Pallas kernels, call(): pl.pallas_call(kernel, out_shape=out_shape, in_specs=in_specs, out_specs=...  27.5 us
    ppermute x1, starting transfers between devices, per_device(): units[4] = lax.ppermute(unit, YZ, turned(4))  6.72 us
    ppermute x1, starting transfers between devices, per_device(): mine = lax.ppermute(bundle, Y, turn)  6.21 us
    ppermute x2, waiting for transfers between devices, per_device(): units[-step] = lax.ppermute(units[1 - step], 'z', up)  5.5 us
    ppermute x2, starting transfers between devices, per_device(): units[step] = lax.ppermute(units[step - 1], 'z', down)  4.92 us
    ppermute x1, waiting for transfers between devices, per_device(): lax.ppermute(late_before[:half], 'x', forth)  4.77 us
    ppermute x1, starting transfers between devices, per_device(): near_part = lax.ppermute(attended, Y, turn)  4.61 us
    ppermute x1, waiting for transfers between devices, per_device(): near_part = lax.ppermute(attended, Y, turn)  4.04 us
  transfers between devices with their start and end apart: 22, of which 10 were waited for; matrix products, arithmetic and copies ran while one was open for 0% of the time, Pallas kernels for 25%

profile of v9, /device:TPU:1, one launch (start us, length us, event | category | flops | bytes accessed | tf_op | source)
XLA Modules:
  0.0 94.1 jit_solution(5915272431258056166)
XLA Ops:
  1.3 6.2 %collective-permute-start.3 = (bf16[17,128,128]{2,1,0:T(8,128)(2,1)S(1)}, bf16[17,128,128]{2,1,0:T(8,128)(2,1)S(1)}, u32[]{:S(2)}, u32[]{:S(2)}) collective-permute-start(bf16[17,128,128]{2,1,0:T(8,128)(2,1)S(1)} %get-tuple-element.31), channel_id=1, source_target_pairs={{0,0},{1,4},{2,2},{3,6},{4,1},{5,5},{6,3},{7,7},{8,8},{9,12},{10,1... | collective-permute-start | bytes 1671176 | tf_op jit(solution)/shard_map/ppermute | solution.py:358
  7.5 6.7 %collective-permute-start.2 = (bf16[4,128,128]{2,1,0:T(8,128)(2,1)S(1)}, bf16[4,128,128]{2,1,0:T(8,128)(2,1)S(1)}, u32[]{:S(2)}, u32[]{:S(2)}) collective-permute-start(bf16[4,128,128]{2,1,0:T(8,128)(2,1)S(1)} %get-tuple-element.30), channel_id=1, source_target_pairs={{0,32},{1,36},{2,34},{3,38},{4,33},{5,37},{6,35},{7,39},{8,40},{9,... | collective-permute-start | bytes 393224 | tf_op jit(solution)/shard_map/ppermute | solution.py:359
  14.3 2.8 %collective-permute-start.1 = (bf16[4,128,128]{2,1,0:T(8,128)(2,1)S(1)}, bf16[4,128,128]{2,1,0:T(8,128)(2,1)S(1)}, u32[]{:S(2)}, u32[]{:S(2)}) collective-permute-start(bf16[4,128,128]{2,1,0:T(8,128)(2,1)S(1)} %get-tuple-element.30), channel_id=1, source_target_pairs={{0,56},{1,60},{2,58},{3,62},{4,57},{5,61},{6,59},{7,63},{8,0},{9,4... | collective-permute-start | bytes 393224 | tf_op jit(solution)/shard_map/ppermute | solution.py:357
  18.4 4.5 %column_half.1 = bf16[768,3072]{1,0:T(8,128)(2,1)} custom-call(s32[1]{0:T(128)} %bitcast.2.half_ref, bf16[768,6144]{1,0:T(8,128)(2,1)} %refs_3_.3), custom_call_target="tpu_custom_call" | custom-call | tf_op jit(solution)/shard_map/column_half/pallas_call | solution.py:43
  25.1 2.6 %collective-permute-start.9 = (bf16[16,128,128]{2,1,0:T(8,128)(2,1)S(1)}, bf16[16,128,128]{2,1,0:T(8,128)(2,1)S(1)}, u32[]{:S(2)}, u32[]{:S(2)}) collective-permute-start(bf16[16,128,128]{2,1,0:T(8,128)(2,1)S(1)} %join.3.refs_3_), channel_id=1, source_target_pairs={{0,192},{64,0},{128,64},{192,128},{1,193},{65,1},{129,65},{193,129... | collective-permute-start | bytes 1572872 | tf_op jit(solution)/shard_map/ppermute | solution.py:369
  28.1 2.2 %collective-permute-start.5 = (bf16[4,128,128]{2,1,0:T(8,128)(2,1)S(1)}, bf16[4,128,128]{2,1,0:T(8,128)(2,1)S(1)}, u32[]{:S(2)}, u32[]{:S(2)}) collective-permute-start(bf16[4,128,128]{2,1,0:T(8,128)(2,1)S(1)} %collective-permute-done.1.refs_1_), channel_id=1, source_target_pairs={{0,56},{8,0},{16,8},{24,16},{32,24},{40,32},{48,40},{56,48},{1,57}... | collective-permute-start | bytes 393224 | tf_op jit(solution)/shard_map/ppermute | solution.py:372
  30.3 2.8 %collective-permute-done.4.refs_0_ = bf16[4,128,128]{2,1,0:T(8,128)(2,1)S(1)} collective-permute-done((bf16[4,128,128]{2,1,0:T(8,128)(2,1)S(1)}, bf16[4,128,128]{2,1,0:T(8,128)(2,1)S(1)}, u32[]{:S(2)}, u32[]{:S(2)}) %collective-permute-start.4) | collective-permute-done | bytes 131104 | tf_op jit(solution)/shard_map/ppermute | solution.py:371
  33.1 2.7 %collective-permute-start.7 = (bf16[4,128,128]{2,1,0:T(8,128)(2,1)S(1)}, bf16[4,128,128]{2,1,0:T(8,128)(2,1)S(1)}, u32[]{:S(2)}, u32[]{:S(2)}) collective-permute-start(bf16[4,128,128]{2,1,0:T(8,128)(2,1)S(1)} %collective-permute-done.5.refs_1_), channel_id=1, source_target_pairs={{0,56},{8,0},{16,8},{24,16},{32,24},{40,32},{48,40},{56,48},{1,57}... | collective-permute-start | bytes 393224 | tf_op jit(solution)/shard_map/ppermute | solution.py:372
  35.8 2.7 %collective-permute-done.6.refs_2_ = bf16[4,128,128]{2,1,0:T(8,128)(2,1)S(1)} collective-permute-done((bf16[4,128,128]{2,1,0:T(8,128)(2,1)S(1)}, bf16[4,128,128]{2,1,0:T(8,128)(2,1)S(1)}, u32[]{:S(2)}, u32[]{:S(2)}) %collective-permute-start.6) | collective-permute-done | bytes 131104 | tf_op jit(solution)/shard_map/ppermute | solution.py:371
  42.0 2.3 %collective-permute-start.12 = (bf16[8,128,128]{2,1,0:T(8,128)(2,1)S(1)}, bf16[8,128,128]{2,1,0:T(8,128)(2,1)S(1)}, u32[]{:S(2)}, u32[]{:S(2)}) collective-permute-start(bf16[8,128,128]{2,1,0:T(8,128)(2,1)S(1)} %slice.21), channel_id=1, source_target_pairs={{0,192},{64,0},{128,64},{192,128},{1,193},{65,1},{129,65},{193,129... | collective-permute-start | bytes 786440 | tf_op jit(solution)/shard_map/ppermute | solution.py:388
  44.3 6.6 %first.1 = (f32[2,152,768]{2,1,0:T(8,128)S(1)}, f32[2,152,768]{2,1,0:T(8,128)S(1)}) custom-call(s32[5,128]{1,0:T(8,128)S(1)} %pad_add_fusion.refs_0_, bf16[17,128,128]{2,1,0:T(8,128)(2,1)S(1)} %collective-permute-done.3.refs_2_.refs_1_, bf16[17,128,128]{2,1,0:T(8,128)(2,1)S(1)} %collective-permute-done.10.refs_2_, bf16[16,128,128]{2,1,0:T(8,128)(2,1)S(1)} %join.3.refs_3_, ...), custom_call_target="tpu_custom_call" | custom-call | tf_op jit(solution)/shard_map/first/pallas_call | solution.py:43
  50.9 2.6 %collective-permute-done.14.refs_4_ = bf16[16,128,128]{2,1,0:T(8,128)(2,1)S(1)} collective-permute-done((bf16[16,128,128]{2,1,0:T(8,128)(2,1)S(1)}, bf16[16,128,128]{2,1,0:T(8,128)(2,1)S(1)}, u32[]{:S(2)}, u32[]{:S(2)}) %collective-permute-start.14) | collective-permute-done | bytes 524320 | tf_op jit(solution)/shard_map/ppermute | solution.py:377
  53.5 1.9 %collective-permute-done.13.refs_3_ = bf16[16,128,128]{2,1,0:T(8,128)(2,1)S(1)} collective-permute-done((bf16[16,128,128]{2,1,0:T(8,128)(2,1)S(1)}, bf16[16,128,128]{2,1,0:T(8,128)(2,1)S(1)}, u32[]{:S(2)}, u32[]{:S(2)}) %collective-permute-start.13) | collective-permute-done | bytes 524320 | tf_op jit(solution)/shard_map/ppermute | solution.py:376
  55.6 2.7 %collective-permute-start.16 = (bf16[8,128,128]{2,1,0:T(8,128)(2,1)S(1)}, bf16[8,128,128]{2,1,0:T(8,128)(2,1)S(1)}, u32[]{:S(2)}, u32[]{:S(2)}) collective-permute-start(bf16[8,128,128]{2,1,0:T(8,128)(2,1)S(1)} %slice.23), channel_id=1, source_target_pairs={{0,192},{64,0},{128,64},{192,128},{1,193},{65,1},{129,65},{193,129... | collective-permute-start | bytes 786440 | tf_op jit(solution)/shard_map/ppermute | solution.py:396
  58.3 3.6 %late.1 = (f32[2,152,768]{2,1,0:T(8,128)S(1)}, f32[2,152,768]{2,1,0:T(8,128)S(1)}) custom-call(s32[5,128]{1,0:T(8,128)S(1)} %pad_add_fusion.refs_0_, bf16[17,128,128]{2,1,0:T(8,128)(2,1)S(1)} %collective-permute-done.3.refs_2_.refs_1_, bf16[17,128,128]{2,1,0:T(8,128)(2,1)S(1)} %collective-permute-done.10.refs_2_, ...), custom_call_target="tpu_custom_call", output_to_operand_aliasing={{0}: (5, {}), {1}: (6, {})} | custom-call | tf_op jit(solution)/shard_map/late/pallas_call | solution.py:43
  61.9 4.8 %collective-permute-done.15.refs_5_ = bf16[8,128,128]{2,1,0:T(8,128)(2,1)S(1)} collective-permute-done((bf16[8,128,128]{2,1,0:T(8,128)(2,1)S(1)}, bf16[8,128,128]{2,1,0:T(8,128)(2,1)S(1)}, u32[]{:S(2)}, u32[]{:S(2)}) %collective-permute-start.15) | collective-permute-done | bytes 262176 | tf_op jit(solution)/shard_map/ppermute | solution.py:395
  67.7 3.4 %collective-permute-start.17 = (f32[2,152,768]{2,1,0:T(8,128)S(1)}, f32[2,152,768]{2,1,0:T(8,128)S(1)}, u32[]{:S(2)}, u32[]{:S(2)}) collective-permute-start(f32[2,152,768]{2,1,0:T(8,128)S(1)} %last_send.1), channel_id=1, source_target_pairs={{0,1},{1,0},{2,3},{3,2},{4,5},{5,4},{6,7},{7,6},{8,9},{9,8},{10,11... | collective-permute-start | bytes 2801672 | tf_op jit(solution)/shard_map/ppermute | solution.py:404
  71.1 2.8 %last_keep.1.own_ref = f32[2,152,768]{2,1,0:T(8,128)S(1)} custom-call(s32[5,128]{1,0:T(8,128)S(1)} %pad_add_fusion.refs_0_, bf16[17,128,128]{2,1,0:T(8,128)(2,1)S(1)} %collective-permute-done.3.refs_2_.refs_1_, bf16[17,128,128]{2,1,0:T(8,128)(2,1)S(1)} %collective-permute-done.10.refs_2_, ...), custom_call_target="tpu_custom_call", output_to_operand_aliasing={{}: (7, {})} | custom-call | tf_op jit(solution)/shard_map/last_keep/pallas_call | solution.py:43
  74.1 3.3 %collective-permute-start.19 = (bf16[256,768]{1,0:T(8,128)(2,1)S(1)}, bf16[256,768]{1,0:T(8,128)(2,1)S(1)}, u32[]{:S(2)}, u32[]{:S(2)}) collective-permute-start(bf16[256,768]{1,0:T(8,128)(2,1)S(1)} %merge.1), channel_id=1, source_target_pairs={{0,2},{1,6},{2,0},{3,4},{4,3},{5,7},{6,1},{7,5},{8,10},{9,14},{10,... | collective-permute-start | bytes 1179656 | tf_op jit(solution)/shard_map/ppermute | solution.py:410
  77.5 4.6 %collective-permute-start.18 = (bf16[256,768]{1,0:T(8,128)(2,1)S(1)}, bf16[256,768]{1,0:T(8,128)(2,1)S(1)}, u32[]{:S(2)}, u32[]{:S(2)}) collective-permute-start(bf16[256,768]{1,0:T(8,128)(2,1)S(1)} %merge.1), channel_id=1, source_target_pairs={{0,0},{1,4},{2,2},{3,6},{4,1},{5,5},{6,3},{7,7},{8,8},{9,12},{10,1... | collective-permute-start | bytes 1179656 | tf_op jit(solution)/shard_map/ppermute | solution.py:409
  82.2 2.5 %fetch.1.refs_4_ = bf16[768,3072]{1,0:T(8,128)(2,1)S(1)} custom-call(bf16[768,3072]{1,0:T(8,128)(2,1)} %collective-permute-done.20.source_ref), custom_call_target="tpu_custom_call" | custom-call | tf_op jit(solution)/shard_map/fetch/pallas_call | solution.py:43
  84.6 4.0 %collective-permute-done.18.refs_1_ = bf16[256,768]{1,0:T(8,128)(2,1)S(1)} collective-permute-done((bf16[256,768]{1,0:T(8,128)(2,1)S(1)}, bf16[256,768]{1,0:T(8,128)(2,1)S(1)}, u32[]{:S(2)}, u32[]{:S(2)}) %collective-permute-start.18) | collective-permute-done | bytes 393248 | tf_op jit(solution)/shard_map/ppermute | solution.py:409
  88.7 2.0 %project_send.1 = bf16[256,1536]{1,0:T(8,128)(2,1)S(1)} custom-call(s32[2]{0:T(128)S(1)} %pad_add_fusion.1.refs_0_, bf16[256,768]{1,0:T(8,128)(2,1)S(1)} %collective-permute-done.18.refs_1_, bf16[256,768]{1,0:T(8,128)(2,1)S(1)} %collective-permute-done.19.refs_2_, bf16[768,6144]{1,0:T(8,128)(2,1)S(1)} %bitcast.12, bf16[768,3072]{1,0:T(8,128)(2,1)S(1)} %fetch.1.refs_4_), custom_call_target="tpu_custom_call" | custom-call | tf_op jit(solution)/shard_map/project_send/pallas_call | solution.py:43
  90.8 2.0 %project_keep.1.keep_ref = f32[256,1536]{1,0:T(8,128)S(1)} custom-call(s32[2]{0:T(128)S(1)} %pad_add_fusion.1.refs_0_, bf16[256,768]{1,0:T(8,128)(2,1)S(1)} %collective-permute-done.18.refs_1_, bf16[256,768]{1,0:T(8,128)(2,1)S(1)} %collective-permute-done.19.refs_2_, bf16[768,6144]{1,0:T(8,128)(2,1)S(1)} %bitcast.12, bf16[768,3072]{1,0:T(8,128)(2,1)S(1)} %fetch.1.refs_4_), custom_call_target="tpu_custom_call" | custom-call | tf_op jit(solution)/shard_map/project_keep/pallas_call | solution.py:43
  (51 shorter events, 11.6 us)
Async XLA Ops:
  1.3 23.7 %collective-permute-start.3 = (bf16[17,128,128]{2,1,0:T(8,128)(2,1)S(1)}, bf16[17,128,128]{2,1,0:T(8,128)(2,1)S(1)}, u32[]{:S(2)}, u32[]{:S(2)}) collective-permute-start(bf16[17,128,128]{2,1,0:T(8,128)(2,1)S(1)} %get-tuple-element.31), channel_id=1, source_target_pairs={{0,0},{1,4},{2,2},{3,6},{4,1},{5,5},{6,3},{7,7},{8,8},{9,12},{10,1... | collective-permute-start | bytes 1671176 | tf_op jit(solution)/shard_map/ppermute | solution.py:358
  7.5 15.4 %collective-permute-start.2 = (bf16[4,128,128]{2,1,0:T(8,128)(2,1)S(1)}, bf16[4,128,128]{2,1,0:T(8,128)(2,1)S(1)}, u32[]{:S(2)}, u32[]{:S(2)}) collective-permute-start(bf16[4,128,128]{2,1,0:T(8,128)(2,1)S(1)} %get-tuple-element.30), channel_id=1, source_target_pairs={{0,32},{1,36},{2,34},{3,38},{4,33},{5,37},{6,35},{7,39},{8,40},{9,... | collective-permute-start | bytes 393224 | tf_op jit(solution)/shard_map/ppermute | solution.py:359
  14.3 9.2 %collective-permute-start.1 = (bf16[4,128,128]{2,1,0:T(8,128)(2,1)S(1)}, bf16[4,128,128]{2,1,0:T(8,128)(2,1)S(1)}, u32[]{:S(2)}, u32[]{:S(2)}) collective-permute-start(bf16[4,128,128]{2,1,0:T(8,128)(2,1)S(1)} %get-tuple-element.30), channel_id=1, source_target_pairs={{0,56},{1,60},{2,58},{3,62},{4,57},{5,61},{6,59},{7,63},{8,0},{9,4... | collective-permute-start | bytes 393224 | tf_op jit(solution)/shard_map/ppermute | solution.py:357
  17.0 8.0 %collective-permute-start = (bf16[4,128,128]{2,1,0:T(8,128)(2,1)S(1)}, bf16[4,128,128]{2,1,0:T(8,128)(2,1)S(1)}, u32[]{:S(2)}, u32[]{:S(2)}) collective-permute-start(bf16[4,128,128]{2,1,0:T(8,128)(2,1)S(1)} %get-tuple-element.30), channel_id=1, source_target_pairs={{0,8},{1,12},{2,10},{3,14},{4,9},{5,13},{6,11},{7,15},{8,16},{9,20... | collective-permute-start | bytes 393224 | tf_op jit(solution)/shard_map/ppermute | solution.py:357
  25.0 57.1 %collective-permute-start.20 = (bf16[768,3072]{1,0:T(8,128)(2,1)}, bf16[768,3072]{1,0:T(8,128)(2,1)}, u32[]{:S(2)}, u32[]{:S(2)}) collective-permute-start(bf16[768,3072]{1,0:T(8,128)(2,1)} %column_half.1), channel_id=1, source_target_pairs={{0,2},{1,7},{2,4},{3,1},{4,6},{5,3},{6,0},{7,5},{8,10},{9,15},{10,... | collective-permute-start | bytes 14155784 | tf_op jit(solution)/shard_map/ppermute | solution.py:365
  25.1 13.5 %collective-permute-start.9 = (bf16[16,128,128]{2,1,0:T(8,128)(2,1)S(1)}, bf16[16,128,128]{2,1,0:T(8,128)(2,1)S(1)}, u32[]{:S(2)}, u32[]{:S(2)}) collective-permute-start(bf16[16,128,128]{2,1,0:T(8,128)(2,1)S(1)} %join.3.refs_3_), channel_id=1, source_target_pairs={{0,192},{64,0},{128,64},{192,128},{1,193},{65,1},{129,65},{193,129... | collective-permute-start | bytes 1572872 | tf_op jit(solution)/shard_map/ppermute | solution.py:369
  27.6 12.7 %collective-permute-start.8 = (bf16[16,128,128]{2,1,0:T(8,128)(2,1)S(1)}, bf16[16,128,128]{2,1,0:T(8,128)(2,1)S(1)}, u32[]{:S(2)}, u32[]{:S(2)}) collective-permute-start(bf16[16,128,128]{2,1,0:T(8,128)(2,1)S(1)} %join.3.refs_3_), channel_id=1, source_target_pairs={{0,64},{64,128},{128,192},{192,0},{1,65},{65,129},{129,193},{193,1... | collective-permute-start | bytes 1572872 | tf_op jit(solution)/shard_map/ppermute | solution.py:368
  27.7 5.4 %collective-permute-start.4 = (bf16[4,128,128]{2,1,0:T(8,128)(2,1)S(1)}, bf16[4,128,128]{2,1,0:T(8,128)(2,1)S(1)}, u32[]{:S(2)}, u32[]{:S(2)}) collective-permute-start(bf16[4,128,128]{2,1,0:T(8,128)(2,1)S(1)} %collective-permute-done.refs_0_), channel_id=1, source_target_pairs={{0,8},{8,16},{16,24},{24,32},{32,40},{40,48},{48,56},{56,0},{1,9},... | collective-permute-start | bytes 393224 | tf_op jit(solution)/shard_map/ppermute | solution.py:371
  28.1 5.0 %collective-permute-start.5 = (bf16[4,128,128]{2,1,0:T(8,128)(2,1)S(1)}, bf16[4,128,128]{2,1,0:T(8,128)(2,1)S(1)}, u32[]{:S(2)}, u32[]{:S(2)}) collective-permute-start(bf16[4,128,128]{2,1,0:T(8,128)(2,1)S(1)} %collective-permute-done.1.refs_1_), channel_id=1, source_target_pairs={{0,56},{8,0},{16,8},{24,16},{32,24},{40,32},{48,40},{56,48},{1,57}... | collective-permute-start | bytes 393224 | tf_op jit(solution)/shard_map/ppermute | solution.py:372
  33.1 5.4 %collective-permute-start.6 = (bf16[4,128,128]{2,1,0:T(8,128)(2,1)S(1)}, bf16[4,128,128]{2,1,0:T(8,128)(2,1)S(1)}, u32[]{:S(2)}, u32[]{:S(2)}) collective-permute-start(bf16[4,128,128]{2,1,0:T(8,128)(2,1)S(1)} %collective-permute-done.4.refs_0_), channel_id=1, source_target_pairs={{0,8},{8,16},{16,24},{24,32},{32,40},{40,48},{48,56},{56,0},{1,9},... | collective-permute-start | bytes 393224 | tf_op jit(solution)/shard_map/ppermute | solution.py:371
  33.1 5.4 %collective-permute-start.7 = (bf16[4,128,128]{2,1,0:T(8,128)(2,1)S(1)}, bf16[4,128,128]{2,1,0:T(8,128)(2,1)S(1)}, u32[]{:S(2)}, u32[]{:S(2)}) collective-permute-start(bf16[4,128,128]{2,1,0:T(8,128)(2,1)S(1)} %collective-permute-done.5.refs_1_), channel_id=1, source_target_pairs={{0,56},{8,0},{16,8},{24,16},{32,24},{40,32},{48,40},{56,48},{1,57}... | collective-permute-start | bytes 393224 | tf_op jit(solution)/shard_map/ppermute | solution.py:372
  40.3 3.9 %collective-permute-start.10 = (bf16[17,128,128]{2,1,0:T(8,128)(2,1)S(1)}, bf16[17,128,128]{2,1,0:T(8,128)(2,1)S(1)}, u32[]{:S(2)}, u32[]{:S(2)}) collective-permute-start(bf16[17,128,128]{2,1,0:T(8,128)(2,1)S(1)} %collective-permute-done.3.refs_2_.refs_1_), channel_id=1, source_target_pairs={{0,1},{1,0},{2,3},{3,2},{4,5},{5,4},{6,7},{7,6},{8,9},{9,8},{10,11... | collective-permute-start | bytes 1671176 | tf_op jit(solution)/shard_map/ppermute | solution.py:378
  40.4 13.1 %collective-permute-start.14 = (bf16[16,128,128]{2,1,0:T(8,128)(2,1)S(1)}, bf16[16,128,128]{2,1,0:T(8,128)(2,1)S(1)}, u32[]{:S(2)}, u32[]{:S(2)}) collective-permute-start(bf16[16,128,128]{2,1,0:T(8,128)(2,1)S(1)} %join.2.refs_4_), channel_id=1, source_target_pairs={{0,192},{64,0},{128,64},{192,128},{1,193},{65,1},{129,65},{193,129... | collective-permute-start | bytes 1572872 | tf_op jit(solution)/shard_map/ppermute | solution.py:377
  41.5 14.0 %collective-permute-start.13 = (bf16[16,128,128]{2,1,0:T(8,128)(2,1)S(1)}, bf16[16,128,128]{2,1,0:T(8,128)(2,1)S(1)}, u32[]{:S(2)}, u32[]{:S(2)}) collective-permute-start(bf16[16,128,128]{2,1,0:T(8,128)(2,1)S(1)} %join.2.refs_4_), channel_id=1, source_target_pairs={{0,64},{64,128},{128,192},{192,0},{1,65},{65,129},{129,193},{193,1... | collective-permute-start | bytes 1572872 | tf_op jit(solution)/shard_map/ppermute | solution.py:376
  42.0 19.9 %collective-permute-start.12 = (bf16[8,128,128]{2,1,0:T(8,128)(2,1)S(1)}, bf16[8,128,128]{2,1,0:T(8,128)(2,1)S(1)}, u32[]{:S(2)}, u32[]{:S(2)}) collective-permute-start(bf16[8,128,128]{2,1,0:T(8,128)(2,1)S(1)} %slice.21), channel_id=1, source_target_pairs={{0,192},{64,0},{128,64},{192,128},{1,193},{65,1},{129,65},{193,129... | collective-permute-start | bytes 786440 | tf_op jit(solution)/shard_map/ppermute | solution.py:388
  44.3 17.6 %collective-permute-start.11 = (bf16[8,128,128]{2,1,0:T(8,128)(2,1)S(1)}, bf16[8,128,128]{2,1,0:T(8,128)(2,1)S(1)}, u32[]{:S(2)}, u32[]{:S(2)}) collective-permute-start(bf16[8,128,128]{2,1,0:T(8,128)(2,1)S(1)} %slice.20), channel_id=1, source_target_pairs={{0,64},{64,128},{128,192},{192,0},{1,65},{65,129},{129,193},{193,1... | collective-permute-start | bytes 786440 | tf_op jit(solution)/shard_map/ppermute | solution.py:387
  55.5 11.2 %collective-permute-start.15 = (bf16[8,128,128]{2,1,0:T(8,128)(2,1)S(1)}, bf16[8,128,128]{2,1,0:T(8,128)(2,1)S(1)}, u32[]{:S(2)}, u32[]{:S(2)}) collective-permute-start(bf16[8,128,128]{2,1,0:T(8,128)(2,1)S(1)} %slice.22), channel_id=1, source_target_pairs={{0,64},{64,128},{128,192},{192,0},{1,65},{65,129},{129,193},{193,1... | collective-permute-start | bytes 786440 | tf_op jit(solution)/shard_map/ppermute | solution.py:395
  55.6 11.1 %collective-permute-start.16 = (bf16[8,128,128]{2,1,0:T(8,128)(2,1)S(1)}, bf16[8,128,128]{2,1,0:T(8,128)(2,1)S(1)}, u32[]{:S(2)}, u32[]{:S(2)}) collective-permute-start(bf16[8,128,128]{2,1,0:T(8,128)(2,1)S(1)} %slice.23), channel_id=1, source_target_pairs={{0,192},{64,0},{128,64},{192,128},{1,193},{65,1},{129,65},{193,129... | collective-permute-start | bytes 786440 | tf_op jit(solution)/shard_map/ppermute | solution.py:396
  66.7 22.0 %slice-start = ((s8[9437184]{0:T(1024)(128)(4,1)}), s8[4194304]{0:T(1024)(128)(4,1)S(1)}, s32[]{:S(2)}) async-start(s8[9437184]{0:T(1024)(128)(4,1)} %bitcast.11), calls=%async_computation | async-start | bytes 8388608
  67.7 21.0 %slice-start.1 = ((s8[9437184]{0:T(1024)(128)(4,1)}), s8[4194304]{0:T(1024)(128)(4,1)S(1)}, s32[]{:S(2)}) async-start(s8[9437184]{0:T(1024)(128)(4,1)} %bitcast.11), calls=%async_computation.1 | async-start | bytes 8388608
  67.7 6.2 %collective-permute-start.17 = (f32[2,152,768]{2,1,0:T(8,128)S(1)}, f32[2,152,768]{2,1,0:T(8,128)S(1)}, u32[]{:S(2)}, u32[]{:S(2)}) collective-permute-start(f32[2,152,768]{2,1,0:T(8,128)S(1)} %last_send.1), channel_id=1, source_target_pairs={{0,1},{1,0},{2,3},{3,2},{4,5},{5,4},{6,7},{7,6},{8,9},{9,8},{10,11... | collective-permute-start | bytes 2801672 | tf_op jit(solution)/shard_map/ppermute | solution.py:404
  74.1 10.5 %collective-permute-start.19 = (bf16[256,768]{1,0:T(8,128)(2,1)S(1)}, bf16[256,768]{1,0:T(8,128)(2,1)S(1)}, u32[]{:S(2)}, u32[]{:S(2)}) collective-permute-start(bf16[256,768]{1,0:T(8,128)(2,1)S(1)} %merge.1), channel_id=1, source_target_pairs={{0,2},{1,6},{2,0},{3,4},{4,3},{5,7},{6,1},{7,5},{8,10},{9,14},{10,... | collective-permute-start | bytes 1179656 | tf_op jit(solution)/shard_map/ppermute | solution.py:410
  77.5 11.2 %collective-permute-start.18 = (bf16[256,768]{1,0:T(8,128)(2,1)S(1)}, bf16[256,768]{1,0:T(8,128)(2,1)S(1)}, u32[]{:S(2)}, u32[]{:S(2)}) collective-permute-start(bf16[256,768]{1,0:T(8,128)(2,1)S(1)} %merge.1), channel_id=1, source_target_pairs={{0,0},{1,4},{2,2},{3,6},{4,1},{5,5},{6,3},{7,7},{8,8},{9,12},{10,1... | collective-permute-start | bytes 1179656 | tf_op jit(solution)/shard_map/ppermute | solution.py:409
  90.7 2.4 %collective-permute-start.21 = (bf16[256,1536]{1,0:T(8,128)(2,1)S(1)}, bf16[256,1536]{1,0:T(8,128)(2,1)S(1)}, u32[]{:S(2)}, u32[]{:S(2)}) collective-permute-start(bf16[256,1536]{1,0:T(8,128)(2,1)S(1)} %project_send.1), channel_id=1, source_target_pairs={{0,1},{1,0},{2,3},{3,2},{4,5},{5,4},{6,7},{7,6},{8,9},{9,8},{10,11... | collective-permute-start | bytes 2359304 | tf_op jit(solution)/shard_map/ppermute | solution.py:414
  (1 other events, 6.5 us)

commit v10 on v9

--- a/solution.py
+++ b/solution.py
@@ -395,11 +395,11 @@
         lax.ppermute(late_before[:half], "x", forth),
         lax.ppermute(late_after[half:], "x", back),
     ]
-    keep, send = stage(
-        ((-1, LATE), (1, LATE)), near, [late_before, late_after], state, every, "late"
-    )
-    *far, keep, send = together((*early_far, *late_far, keep, send))
-    last = (((2, EARLY), (2, LATE)), near, far)
+    columns = ((-1, LATE), (1, LATE), (2, EARLY))
+    parts = [late_before, late_after, *early_far]
+    keep, send = stage(columns, near, parts, state, every, "late")
+    *late_far, keep, send = together((*late_far, keep, send))
+    last = (((2, LATE),), near, late_far)
     (send,) = stage(*last, (send,), (2, 3), "last_send")
     received = lax.ppermute(send, "core", swap)
     (keep,) = stage(*last, (keep,), (0, 1), "last_keep")

time: 94.9 us -> 101 us (1.064)
  the two profiles are of different devices: /device:TPU:1 before, /device:TPU:97 now
where the time goes in v10:
time: 101 us
  starting transfers between devices  43.6 us (43%)
  Pallas kernels  38.6 us (38%)
  waiting for transfers between devices  18.1 us (18%)
    pallas_call x13, Pallas kernels, call(): pl.pallas_call(kernel, out_shape=out_shape, in_specs=in_specs, out_specs=...  38.6 us
    ppermute x2, starting transfers between devices, per_device(): units[-step] = lax.ppermute(units[1 - step], 'z', up)  8.26 us
    ppermute x1, starting transfers between devices, per_device(): mine = lax.ppermute(bundle, Y, turn)  5.38 us
    ppermute x2, waiting for transfers between devices, per_device(): units[-step] = lax.ppermute(units[1 - step], 'z', up)  5.13 us
    ppermute x1, starting transfers between devices, per_device(): near_part = lax.ppermute(attended, Y, turn)  4.96 us
    ppermute x1, waiting for transfers between devices, per_device(): near_part = lax.ppermute(attended, Y, turn)  4.81 us
    ppermute x1, starting transfers between devices, per_device(): units[4] = lax.ppermute(unit, YZ, turned(4))  3.94 us
    ppermute x1, starting transfers between devices, per_device(): received = lax.ppermute(send, 'core', swap)  3.74 us
  transfers between devices with their start and end apart: 22, of which 8 were waited for; matrix products, arithmetic and copies ran while one was open for 0% of the time, Pallas kernels for 34%

profile of v10, /device:TPU:97, one launch (start us, length us, event | category | flops | bytes accessed | tf_op | source)
XLA Modules:
  0.0 100.9 jit_solution(59860938504109974)
XLA Ops:
  1.3 5.4 %collective-permute-start.3 = (bf16[17,128,128]{2,1,0:T(8,128)(2,1)S(1)}, bf16[17,128,128]{2,1,0:T(8,128)(2,1)S(1)}, u32[]{:S(2)}, u32[]{:S(2)}) collective-permute-start(bf16[17,128,128]{2,1,0:T(8,128)(2,1)S(1)} %get-tuple-element.29), channel_id=1, source_target_pairs={{0,0},{1,4},{2,2},{3,6},{4,1},{5,5},{6,3},{7,7},{8,8},{9,12},{10,1... | collective-permute-start | bytes 1671176 | tf_op jit(solution)/shard_map/ppermute | solution.py:358
  6.7 2.7 %collective-permute-start = (bf16[4,128,128]{2,1,0:T(8,128)(2,1)S(1)}, bf16[4,128,128]{2,1,0:T(8,128)(2,1)S(1)}, u32[]{:S(2)}, u32[]{:S(2)}) collective-permute-start(bf16[4,128,128]{2,1,0:T(8,128)(2,1)S(1)} %get-tuple-element.28), channel_id=1, source_target_pairs={{0,8},{1,12},{2,10},{3,14},{4,9},{5,13},{6,11},{7,15},{8,16},{9,20... | collective-permute-start | bytes 393224 | tf_op jit(solution)/shard_map/ppermute | solution.py:357
  10.9 3.9 %collective-permute-start.2 = (bf16[4,128,128]{2,1,0:T(8,128)(2,1)S(1)}, bf16[4,128,128]{2,1,0:T(8,128)(2,1)S(1)}, u32[]{:S(2)}, u32[]{:S(2)}) collective-permute-start(bf16[4,128,128]{2,1,0:T(8,128)(2,1)S(1)} %get-tuple-element.28), channel_id=1, source_target_pairs={{0,32},{1,36},{2,34},{3,38},{4,33},{5,37},{6,35},{7,39},{8,40},{9,... | collective-permute-start | bytes 393224 | tf_op jit(solution)/shard_map/ppermute | solution.py:359
  14.9 4.5 %column_half.1 = bf16[768,3072]{1,0:T(8,128)(2,1)} custom-call(s32[1]{0:T(128)} %bitcast.2.half_ref, bf16[768,6144]{1,0:T(8,128)(2,1)} %refs_3_.3), custom_call_target="tpu_custom_call" | custom-call | tf_op jit(solution)/shard_map/column_half/pallas_call | solution.py:43
  19.4 2.2 %collective-permute-done.2.refs_3_ = bf16[4,128,128]{2,1,0:T(8,128)(2,1)S(1)} collective-permute-done((bf16[4,128,128]{2,1,0:T(8,128)(2,1)S(1)}, bf16[4,128,128]{2,1,0:T(8,128)(2,1)S(1)}, u32[]{:S(2)}, u32[]{:S(2)}) %collective-permute-start.2) | collective-permute-done | bytes 131104 | tf_op jit(solution)/shard_map/ppermute | solution.py:359
  24.4 4.7 %collective-permute-start.4 = (bf16[4,128,128]{2,1,0:T(8,128)(2,1)S(1)}, bf16[4,128,128]{2,1,0:T(8,128)(2,1)S(1)}, u32[]{:S(2)}, u32[]{:S(2)}) collective-permute-start(bf16[4,128,128]{2,1,0:T(8,128)(2,1)S(1)} %collective-permute-done.refs_0_), channel_id=1, source_target_pairs={{0,8},{8,16},{16,24},{24,32},{32,40},{40,48},{48,56},{56,0},{1,9},... | collective-permute-start | bytes 393224 | tf_op jit(solution)/shard_map/ppermute | solution.py:371
  29.2 3.2 %collective-permute-done.4.refs_0_ = bf16[4,128,128]{2,1,0:T(8,128)(2,1)S(1)} collective-permute-done((bf16[4,128,128]{2,1,0:T(8,128)(2,1)S(1)}, bf16[4,128,128]{2,1,0:T(8,128)(2,1)S(1)}, u32[]{:S(2)}, u32[]{:S(2)}) %collective-permute-start.4) | collective-permute-done | bytes 131104 | tf_op jit(solution)/shard_map/ppermute | solution.py:371
  32.4 3.5 %collective-permute-start.6 = (bf16[4,128,128]{2,1,0:T(8,128)(2,1)S(1)}, bf16[4,128,128]{2,1,0:T(8,128)(2,1)S(1)}, u32[]{:S(2)}, u32[]{:S(2)}) collective-permute-start(bf16[4,128,128]{2,1,0:T(8,128)(2,1)S(1)} %collective-permute-done.4.refs_0_), channel_id=1, source_target_pairs={{0,8},{8,16},{16,24},{24,32},{32,40},{40,48},{48,56},{56,0},{1,9},... | collective-permute-start | bytes 393224 | tf_op jit(solution)/shard_map/ppermute | solution.py:371
  35.9 1.9 %collective-permute-done.6.refs_2_ = bf16[4,128,128]{2,1,0:T(8,128)(2,1)S(1)} collective-permute-done((bf16[4,128,128]{2,1,0:T(8,128)(2,1)S(1)}, bf16[4,128,128]{2,1,0:T(8,128)(2,1)S(1)}, u32[]{:S(2)}, u32[]{:S(2)}) %collective-permute-start.6) | collective-permute-done | bytes 131104 | tf_op jit(solution)/shard_map/ppermute | solution.py:371
  37.8 3.5 %collective-permute-done.7.refs_3_ = bf16[4,128,128]{2,1,0:T(8,128)(2,1)S(1)} collective-permute-done((bf16[4,128,128]{2,1,0:T(8,128)(2,1)S(1)}, bf16[4,128,128]{2,1,0:T(8,128)(2,1)S(1)}, u32[]{:S(2)}, u32[]{:S(2)}) %collective-permute-start.7) | collective-permute-done | bytes 131104 | tf_op jit(solution)/shard_map/ppermute | solution.py:372
  41.6 2.7 %collective-permute-start.12 = (bf16[16,128,128]{2,1,0:T(8,128)(2,1)S(1)}, bf16[16,128,128]{2,1,0:T(8,128)(2,1)S(1)}, u32[]{:S(2)}, u32[]{:S(2)}) collective-permute-start(bf16[16,128,128]{2,1,0:T(8,128)(2,1)S(1)} %join.2.refs_4_), channel_id=1, source_target_pairs={{0,192},{64,0},{128,64},{192,128},{1,193},{65,1},{129,65},{193,129... | collective-permute-start | bytes 1572872 | tf_op jit(solution)/shard_map/ppermute | solution.py:377
  44.4 2.7 %collective-permute-start.16 = (bf16[8,128,128]{2,1,0:T(8,128)(2,1)S(1)}, bf16[8,128,128]{2,1,0:T(8,128)(2,1)S(1)}, u32[]{:S(2)}, u32[]{:S(2)}) collective-permute-start(bf16[8,128,128]{2,1,0:T(8,128)(2,1)S(1)} %slice.23), channel_id=1, source_target_pairs={{0,192},{64,0},{128,64},{192,128},{1,193},{65,1},{129,65},{193,129... | collective-permute-start | bytes 786440 | tf_op jit(solution)/shard_map/ppermute | solution.py:388
  47.2 11.4 %first.1 = (f32[2,152,768]{2,1,0:T(8,128)S(1)}, f32[2,152,768]{2,1,0:T(8,128)S(1)}) custom-call(s32[5,128]{1,0:T(8,128)S(1)} %pad_add_fusion.refs_0_, bf16[17,128,128]{2,1,0:T(8,128)(2,1)S(1)} %collective-permute-done.3.refs_2_.refs_1_, bf16[17,128,128]{2,1,0:T(8,128)(2,1)S(1)} %collective-permute-done.10.refs_2_, bf16[16,128,128]{2,1,0:T(8,128)(2,1)S(1)} %join.3.refs_3_, ...), custom_call_target="tpu_custom_call" | custom-call | tf_op jit(solution)/shard_map/first/pallas_call | solution.py:43
  58.7 2.7 %collective-permute-start.14 = (bf16[8,128,128]{2,1,0:T(8,128)(2,1)S(1)}, bf16[8,128,128]{2,1,0:T(8,128)(2,1)S(1)}, u32[]{:S(2)}, u32[]{:S(2)}) collective-permute-start(bf16[8,128,128]{2,1,0:T(8,128)(2,1)S(1)} %slice.21), channel_id=1, source_target_pairs={{0,192},{64,0},{128,64},{192,128},{1,193},{65,1},{129,65},{193,129... | collective-permute-start | bytes 786440 | tf_op jit(solution)/shard_map/ppermute | solution.py:396
  61.5 8.0 %late.1 = (f32[2,152,768]{2,1,0:T(8,128)S(1)}, f32[2,152,768]{2,1,0:T(8,128)S(1)}) custom-call(s32[5,128]{1,0:T(8,128)S(1)} %pad_add_fusion.refs_0_, bf16[17,128,128]{2,1,0:T(8,128)(2,1)S(1)} %collective-permute-done.3.refs_2_.refs_1_, bf16[17,128,128]{2,1,0:T(8,128)(2,1)S(1)} %collective-permute-done.10.refs_2_, ...), custom_call_target="tpu_custom_call", output_to_operand_aliasing={{0}: (7, {}), {1}: (8, {})} | custom-call | tf_op jit(solution)/shard_map/late/pallas_call | solution.py:43
  69.6 2.4 %last_send.1 = f32[2,152,768]{2,1,0:T(8,128)S(1)} custom-call(s32[5,128]{1,0:T(8,128)S(1)} %pad_add_fusion.refs_0_, bf16[17,128,128]{2,1,0:T(8,128)(2,1)S(1)} %collective-permute-done.3.refs_2_.refs_1_, bf16[17,128,128]{2,1,0:T(8,128)(2,1)S(1)} %collective-permute-done.10.refs_2_, ...), custom_call_target="tpu_custom_call", output_to_operand_aliasing={{}: (5, {})} | custom-call | tf_op jit(solution)/shard_map/last_send/pallas_call | solution.py:43
  72.0 3.7 %collective-permute-start.17 = (f32[2,152,768]{2,1,0:T(8,128)S(1)}, f32[2,152,768]{2,1,0:T(8,128)S(1)}, u32[]{:S(2)}, u32[]{:S(2)}) collective-permute-start(f32[2,152,768]{2,1,0:T(8,128)S(1)} %last_send.1), channel_id=1, source_target_pairs={{0,1},{1,0},{2,3},{3,2},{4,5},{5,4},{6,7},{7,6},{8,9},{9,8},{10,11... | collective-permute-start | bytes 2801672 | tf_op jit(solution)/shard_map/ppermute | solution.py:404
  75.7 3.2 %last_keep.1.own_ref = f32[2,152,768]{2,1,0:T(8,128)S(1)} custom-call(s32[5,128]{1,0:T(8,128)S(1)} %pad_add_fusion.refs_0_, bf16[17,128,128]{2,1,0:T(8,128)(2,1)S(1)} %collective-permute-done.3.refs_2_.refs_1_, bf16[17,128,128]{2,1,0:T(8,128)(2,1)S(1)} %collective-permute-done.10.refs_2_, ...), custom_call_target="tpu_custom_call", output_to_operand_aliasing={{}: (5, {})} | custom-call | tf_op jit(solution)/shard_map/last_keep/pallas_call | solution.py:43
  79.2 5.0 %collective-permute-start.18 = (bf16[256,768]{1,0:T(8,128)(2,1)S(1)}, bf16[256,768]{1,0:T(8,128)(2,1)S(1)}, u32[]{:S(2)}, u32[]{:S(2)}) collective-permute-start(bf16[256,768]{1,0:T(8,128)(2,1)S(1)} %merge.1), channel_id=1, source_target_pairs={{0,0},{1,4},{2,2},{3,6},{4,1},{5,5},{6,3},{7,7},{8,8},{9,12},{10,1... | collective-permute-start | bytes 1179656 | tf_op jit(solution)/shard_map/ppermute | solution.py:409
  86.1 2.5 %fetch.1.refs_4_ = bf16[768,3072]{1,0:T(8,128)(2,1)S(1)} custom-call(bf16[768,3072]{1,0:T(8,128)(2,1)} %collective-permute-done.20.source_ref), custom_call_target="tpu_custom_call" | custom-call | tf_op jit(solution)/shard_map/fetch/pallas_call | solution.py:43
  88.6 4.8 %collective-permute-done.18.refs_1_ = bf16[256,768]{1,0:T(8,128)(2,1)S(1)} collective-permute-done((bf16[256,768]{1,0:T(8,128)(2,1)S(1)}, bf16[256,768]{1,0:T(8,128)(2,1)S(1)}, u32[]{:S(2)}, u32[]{:S(2)}) %collective-permute-start.18) | collective-permute-done | bytes 393248 | tf_op jit(solution)/shard_map/ppermute | solution.py:409
  93.4 2.1 %collective-permute-done.19.refs_2_ = bf16[256,768]{1,0:T(8,128)(2,1)S(1)} collective-permute-done((bf16[256,768]{1,0:T(8,128)(2,1)S(1)}, bf16[256,768]{1,0:T(8,128)(2,1)S(1)}, u32[]{:S(2)}, u32[]{:S(2)}) %collective-permute-start.19) | collective-permute-done | bytes 393248 | tf_op jit(solution)/shard_map/ppermute | solution.py:410
  95.4 2.0 %project_send.1 = bf16[256,1536]{1,0:T(8,128)(2,1)S(1)} custom-call(s32[2]{0:T(128)S(1)} %pad_add_fusion.1.refs_0_, bf16[256,768]{1,0:T(8,128)(2,1)S(1)} %collective-permute-done.18.refs_1_, bf16[256,768]{1,0:T(8,128)(2,1)S(1)} %collective-permute-done.19.refs_2_, bf16[768,6144]{1,0:T(8,128)(2,1)S(1)} %bitcast.12, bf16[768,3072]{1,0:T(8,128)(2,1)S(1)} %fetch.1.refs_4_), custom_call_target="tpu_custom_call" | custom-call | tf_op jit(solution)/shard_map/project_send/pallas_call | solution.py:43
  97.5 2.0 %project_keep.1.keep_ref = f32[256,1536]{1,0:T(8,128)S(1)} custom-call(s32[2]{0:T(128)S(1)} %pad_add_fusion.1.refs_0_, bf16[256,768]{1,0:T(8,128)(2,1)S(1)} %collective-permute-done.18.refs_1_, bf16[256,768]{1,0:T(8,128)(2,1)S(1)} %collective-permute-done.19.refs_2_, bf16[768,6144]{1,0:T(8,128)(2,1)S(1)} %bitcast.12, bf16[768,3072]{1,0:T(8,128)(2,1)S(1)} %fetch.1.refs_4_), custom_call_target="tpu_custom_call" | custom-call | tf_op jit(solution)/shard_map/project_keep/pallas_call | solution.py:43
  (51 shorter events, 9.9 us)
Async XLA Ops:
  1.3 20.3 %collective-permute-start.3 = (bf16[17,128,128]{2,1,0:T(8,128)(2,1)S(1)}, bf16[17,128,128]{2,1,0:T(8,128)(2,1)S(1)}, u32[]{:S(2)}, u32[]{:S(2)}) collective-permute-start(bf16[17,128,128]{2,1,0:T(8,128)(2,1)S(1)} %get-tuple-element.29), channel_id=1, source_target_pairs={{0,0},{1,4},{2,2},{3,6},{4,1},{5,5},{6,3},{7,7},{8,8},{9,12},{10,1... | collective-permute-start | bytes 1671176 | tf_op jit(solution)/shard_map/ppermute | solution.py:358
  6.7 12.7 %collective-permute-start = (bf16[4,128,128]{2,1,0:T(8,128)(2,1)S(1)}, bf16[4,128,128]{2,1,0:T(8,128)(2,1)S(1)}, u32[]{:S(2)}, u32[]{:S(2)}) collective-permute-start(bf16[4,128,128]{2,1,0:T(8,128)(2,1)S(1)} %get-tuple-element.28), channel_id=1, source_target_pairs={{0,8},{1,12},{2,10},{3,14},{4,9},{5,13},{6,11},{7,15},{8,16},{9,20... | collective-permute-start | bytes 393224 | tf_op jit(solution)/shard_map/ppermute | solution.py:357
  9.4 10.1 %collective-permute-start.1 = (bf16[4,128,128]{2,1,0:T(8,128)(2,1)S(1)}, bf16[4,128,128]{2,1,0:T(8,128)(2,1)S(1)}, u32[]{:S(2)}, u32[]{:S(2)}) collective-permute-start(bf16[4,128,128]{2,1,0:T(8,128)(2,1)S(1)} %get-tuple-element.28), channel_id=1, source_target_pairs={{0,56},{1,60},{2,58},{3,62},{4,57},{5,61},{6,59},{7,63},{8,0},{9,4... | collective-permute-start | bytes 393224 | tf_op jit(solution)/shard_map/ppermute | solution.py:357
  10.9 10.7 %collective-permute-start.2 = (bf16[4,128,128]{2,1,0:T(8,128)(2,1)S(1)}, bf16[4,128,128]{2,1,0:T(8,128)(2,1)S(1)}, u32[]{:S(2)}, u32[]{:S(2)}) collective-permute-start(bf16[4,128,128]{2,1,0:T(8,128)(2,1)S(1)} %get-tuple-element.28), channel_id=1, source_target_pairs={{0,32},{1,36},{2,34},{3,38},{4,33},{5,37},{6,35},{7,39},{8,40},{9,... | collective-permute-start | bytes 393224 | tf_op jit(solution)/shard_map/ppermute | solution.py:359
  21.6 64.5 %collective-permute-start.20 = (bf16[768,3072]{1,0:T(8,128)(2,1)}, bf16[768,3072]{1,0:T(8,128)(2,1)}, u32[]{:S(2)}, u32[]{:S(2)}) collective-permute-start(bf16[768,3072]{1,0:T(8,128)(2,1)} %column_half.1), channel_id=1, source_target_pairs={{0,2},{1,7},{2,4},{3,1},{4,6},{5,3},{6,0},{7,5},{8,10},{9,15},{10,... | collective-permute-start | bytes 14155784 | tf_op jit(solution)/shard_map/ppermute | solution.py:365
  21.7 19.7 %collective-permute-start.8 = (bf16[16,128,128]{2,1,0:T(8,128)(2,1)S(1)}, bf16[16,128,128]{2,1,0:T(8,128)(2,1)S(1)}, u32[]{:S(2)}, u32[]{:S(2)}) collective-permute-start(bf16[16,128,128]{2,1,0:T(8,128)(2,1)S(1)} %join.3.refs_3_), channel_id=1, source_target_pairs={{0,64},{64,128},{128,192},{192,0},{1,65},{65,129},{129,193},{193,1... | collective-permute-start | bytes 1572872 | tf_op jit(solution)/shard_map/ppermute | solution.py:368
  23.0 18.4 %collective-permute-start.9 = (bf16[16,128,128]{2,1,0:T(8,128)(2,1)S(1)}, bf16[16,128,128]{2,1,0:T(8,128)(2,1)S(1)}, u32[]{:S(2)}, u32[]{:S(2)}) collective-permute-start(bf16[16,128,128]{2,1,0:T(8,128)(2,1)S(1)} %join.3.refs_3_), channel_id=1, source_target_pairs={{0,192},{64,0},{128,64},{192,128},{1,193},{65,1},{129,65},{193,129... | collective-permute-start | bytes 1572872 | tf_op jit(solution)/shard_map/ppermute | solution.py:369
  24.4 7.9 %collective-permute-start.4 = (bf16[4,128,128]{2,1,0:T(8,128)(2,1)S(1)}, bf16[4,128,128]{2,1,0:T(8,128)(2,1)S(1)}, u32[]{:S(2)}, u32[]{:S(2)}) collective-permute-start(bf16[4,128,128]{2,1,0:T(8,128)(2,1)S(1)} %collective-permute-done.refs_0_), channel_id=1, source_target_pairs={{0,8},{8,16},{16,24},{24,32},{32,40},{40,48},{48,56},{56,0},{1,9},... | collective-permute-start | bytes 393224 | tf_op jit(solution)/shard_map/ppermute | solution.py:371
  29.2 6.7 %collective-permute-start.5 = (bf16[4,128,128]{2,1,0:T(8,128)(2,1)S(1)}, bf16[4,128,128]{2,1,0:T(8,128)(2,1)S(1)}, u32[]{:S(2)}, u32[]{:S(2)}) collective-permute-start(bf16[4,128,128]{2,1,0:T(8,128)(2,1)S(1)} %collective-permute-done.1.refs_1_), channel_id=1, source_target_pairs={{0,56},{8,0},{16,8},{24,16},{32,24},{40,32},{48,40},{56,48},{1,57}... | collective-permute-start | bytes 393224 | tf_op jit(solution)/shard_map/ppermute | solution.py:372
  32.4 5.5 %collective-permute-start.6 = (bf16[4,128,128]{2,1,0:T(8,128)(2,1)S(1)}, bf16[4,128,128]{2,1,0:T(8,128)(2,1)S(1)}, u32[]{:S(2)}, u32[]{:S(2)}) collective-permute-start(bf16[4,128,128]{2,1,0:T(8,128)(2,1)S(1)} %collective-permute-done.4.refs_0_), channel_id=1, source_target_pairs={{0,8},{8,16},{16,24},{24,32},{32,40},{40,48},{48,56},{56,0},{1,9},... | collective-permute-start | bytes 393224 | tf_op jit(solution)/shard_map/ppermute | solution.py:371
  35.9 5.4 %collective-permute-start.7 = (bf16[4,128,128]{2,1,0:T(8,128)(2,1)S(1)}, bf16[4,128,128]{2,1,0:T(8,128)(2,1)S(1)}, u32[]{:S(2)}, u32[]{:S(2)}) collective-permute-start(bf16[4,128,128]{2,1,0:T(8,128)(2,1)S(1)} %collective-permute-done.5.refs_1_), channel_id=1, source_target_pairs={{0,56},{8,0},{16,8},{24,16},{32,24},{40,32},{48,40},{56,48},{1,57}... | collective-permute-start | bytes 393224 | tf_op jit(solution)/shard_map/ppermute | solution.py:372
  41.4 3.0 %collective-permute-start.10 = (bf16[17,128,128]{2,1,0:T(8,128)(2,1)S(1)}, bf16[17,128,128]{2,1,0:T(8,128)(2,1)S(1)}, u32[]{:S(2)}, u32[]{:S(2)}) collective-permute-start(bf16[17,128,128]{2,1,0:T(8,128)(2,1)S(1)} %collective-permute-done.3.refs_2_.refs_1_), channel_id=1, source_target_pairs={{0,1},{1,0},{2,3},{3,2},{4,5},{5,4},{6,7},{7,6},{8,9},{9,8},{10,11... | collective-permute-start | bytes 1671176 | tf_op jit(solution)/shard_map/ppermute | solution.py:378
  41.6 17.0 %collective-permute-start.11 = (bf16[16,128,128]{2,1,0:T(8,128)(2,1)S(1)}, bf16[16,128,128]{2,1,0:T(8,128)(2,1)S(1)}, u32[]{:S(2)}, u32[]{:S(2)}) collective-permute-start(bf16[16,128,128]{2,1,0:T(8,128)(2,1)S(1)} %join.2.refs_4_), channel_id=1, source_target_pairs={{0,64},{64,128},{128,192},{192,0},{1,65},{65,129},{129,193},{193,1... | collective-permute-start | bytes 1572872 | tf_op jit(solution)/shard_map/ppermute | solution.py:376
  41.6 17.0 %collective-permute-start.12 = (bf16[16,128,128]{2,1,0:T(8,128)(2,1)S(1)}, bf16[16,128,128]{2,1,0:T(8,128)(2,1)S(1)}, u32[]{:S(2)}, u32[]{:S(2)}) collective-permute-start(bf16[16,128,128]{2,1,0:T(8,128)(2,1)S(1)} %join.2.refs_4_), channel_id=1, source_target_pairs={{0,192},{64,0},{128,64},{192,128},{1,193},{65,1},{129,65},{193,129... | collective-permute-start | bytes 1572872 | tf_op jit(solution)/shard_map/ppermute | solution.py:377
  44.3 17.2 %collective-permute-start.15 = (bf16[8,128,128]{2,1,0:T(8,128)(2,1)S(1)}, bf16[8,128,128]{2,1,0:T(8,128)(2,1)S(1)}, u32[]{:S(2)}, u32[]{:S(2)}) collective-permute-start(bf16[8,128,128]{2,1,0:T(8,128)(2,1)S(1)} %slice.22), channel_id=1, source_target_pairs={{0,64},{64,128},{128,192},{192,0},{1,65},{65,129},{129,193},{193,1... | collective-permute-start | bytes 786440 | tf_op jit(solution)/shard_map/ppermute | solution.py:387
  44.4 17.1 %collective-permute-start.16 = (bf16[8,128,128]{2,1,0:T(8,128)(2,1)S(1)}, bf16[8,128,128]{2,1,0:T(8,128)(2,1)S(1)}, u32[]{:S(2)}, u32[]{:S(2)}) collective-permute-start(bf16[8,128,128]{2,1,0:T(8,128)(2,1)S(1)} %slice.23), channel_id=1, source_target_pairs={{0,192},{64,0},{128,64},{192,128},{1,193},{65,1},{129,65},{193,129... | collective-permute-start | bytes 786440 | tf_op jit(solution)/shard_map/ppermute | solution.py:388
  58.6 10.9 %collective-permute-start.13 = (bf16[8,128,128]{2,1,0:T(8,128)(2,1)S(1)}, bf16[8,128,128]{2,1,0:T(8,128)(2,1)S(1)}, u32[]{:S(2)}, u32[]{:S(2)}) collective-permute-start(bf16[8,128,128]{2,1,0:T(8,128)(2,1)S(1)} %slice.20), channel_id=1, source_target_pairs={{0,64},{64,128},{128,192},{192,0},{1,65},{65,129},{129,193},{193,1... | collective-permute-start | bytes 786440 | tf_op jit(solution)/shard_map/ppermute | solution.py:395
  58.7 10.8 %collective-permute-start.14 = (bf16[8,128,128]{2,1,0:T(8,128)(2,1)S(1)}, bf16[8,128,128]{2,1,0:T(8,128)(2,1)S(1)}, u32[]{:S(2)}, u32[]{:S(2)}) collective-permute-start(bf16[8,128,128]{2,1,0:T(8,128)(2,1)S(1)} %slice.21), channel_id=1, source_target_pairs={{0,192},{64,0},{128,64},{192,128},{1,193},{65,1},{129,65},{193,129... | collective-permute-start | bytes 786440 | tf_op jit(solution)/shard_map/ppermute | solution.py:396
  69.6 25.9 %slice-start = ((s8[9437184]{0:T(1024)(128)(4,1)}), s8[4194304]{0:T(1024)(128)(4,1)S(1)}, s32[]{:S(2)}) async-start(s8[9437184]{0:T(1024)(128)(4,1)} %bitcast.11), calls=%async_computation | async-start | bytes 8388608
  72.0 23.4 %slice-start.1 = ((s8[9437184]{0:T(1024)(128)(4,1)}), s8[4194304]{0:T(1024)(128)(4,1)S(1)}, s32[]{:S(2)}) async-start(s8[9437184]{0:T(1024)(128)(4,1)} %bitcast.11), calls=%async_computation.1 | async-start | bytes 8388608
  72.0 7.0 %collective-permute-start.17 = (f32[2,152,768]{2,1,0:T(8,128)S(1)}, f32[2,152,768]{2,1,0:T(8,128)S(1)}, u32[]{:S(2)}, u32[]{:S(2)}) collective-permute-start(f32[2,152,768]{2,1,0:T(8,128)S(1)} %last_send.1), channel_id=1, source_target_pairs={{0,1},{1,0},{2,3},{3,2},{4,5},{5,4},{6,7},{7,6},{8,9},{9,8},{10,11... | collective-permute-start | bytes 2801672 | tf_op jit(solution)/shard_map/ppermute | solution.py:404
  79.2 14.2 %collective-permute-start.18 = (bf16[256,768]{1,0:T(8,128)(2,1)S(1)}, bf16[256,768]{1,0:T(8,128)(2,1)S(1)}, u32[]{:S(2)}, u32[]{:S(2)}) collective-permute-start(bf16[256,768]{1,0:T(8,128)(2,1)S(1)} %merge.1), channel_id=1, source_target_pairs={{0,0},{1,4},{2,2},{3,6},{4,1},{5,5},{6,3},{7,7},{8,8},{9,12},{10,1... | collective-permute-start | bytes 1179656 | tf_op jit(solution)/shard_map/ppermute | solution.py:409
  84.2 11.3 %collective-permute-start.19 = (bf16[256,768]{1,0:T(8,128)(2,1)S(1)}, bf16[256,768]{1,0:T(8,128)(2,1)S(1)}, u32[]{:S(2)}, u32[]{:S(2)}) collective-permute-start(bf16[256,768]{1,0:T(8,128)(2,1)S(1)} %merge.1), channel_id=1, source_target_pairs={{0,2},{1,6},{2,0},{3,4},{4,3},{5,7},{6,1},{7,5},{8,10},{9,14},{10,... | collective-permute-start | bytes 1179656 | tf_op jit(solution)/shard_map/ppermute | solution.py:410
  97.4 2.4 %collective-permute-start.21 = (bf16[256,1536]{1,0:T(8,128)(2,1)S(1)}, bf16[256,1536]{1,0:T(8,128)(2,1)S(1)}, u32[]{:S(2)}, u32[]{:S(2)}) collective-permute-start(bf16[256,1536]{1,0:T(8,128)(2,1)S(1)} %project_send.1), channel_id=1, source_target_pairs={{0,1},{1,0},{2,3},{3,2},{4,5},{5,4},{6,7},{7,6},{8,9},{9,8},{10,11... | collective-permute-start | bytes 2359304 | tf_op jit(solution)/shard_map/ppermute | solution.py:414
  (1 other events, 9.3 us)

commit v11 on v10

--- a/solution.py
+++ b/solution.py
@@ -317,26 +317,39 @@
     return [(z * 8 + a, (z + shift) % NZ * 8 + b) for z in range(NZ) for a, b in turn]
 
 
-def project_kernel(flip, place_ref, near_ref, far_ref, weight_ref, far_weight_ref, out_ref):
+def near_kernel(place_ref, near_ref, weight_ref, out_ref):
+    for n in range(out_ref.shape[1] // 256):
+        at = pl.multiple_of(place_ref[0] * out_ref.shape[1] + n * 256, 256)
+        out_ref[:, n * 256 : (n + 1) * 256] = jnp.dot(
+            near_ref[...], weight_ref[:, pl.ds(at, 256)], preferred_element_type=jnp.float32
+        )
+
+
+def project_near(place, near, weight):
+    shape = jax.ShapeDtypeStruct((near.shape[0], weight.shape[1] // 2), jnp.float32)
+    return call(
+        near_kernel, shape, (place, near, weight), [smem()] + [vmem()] * 2, name="project_near"
+    )
+
+
+def project_kernel(flip, place_ref, far_ref, far_weight_ref, before_ref, out_ref):
     width = out_ref.shape[1]
     which = place_ref[1] + flip - 2 * flip * place_ref[1]
     for n in range(width // 256):
-        at = pl.multiple_of(which * width + n * 256, 256)
-        far = far_weight_ref[:, pl.ds(at, 256)]
-        total = jnp.dot(far_ref[...], far, preferred_element_type=jnp.float32)
-        at = pl.multiple_of(place_ref[0] * (2 * width) + which * width + n * 256, 256)
-        near = weight_ref[:, pl.ds(at, 256)]
-        total = total + jnp.dot(near_ref[...], near, preferred_element_type=jnp.float32)
+        lanes = pl.ds(pl.multiple_of(which * width + n * 256, 256), 256)
+        total = before_ref[:, lanes] + jnp.dot(
+            far_ref[...], far_weight_ref[:, lanes], preferred_element_type=jnp.float32
+        )
         out_ref[:, n * 256 : (n + 1) * 256] = total.astype(out_ref.dtype)
 
 
-def project(flip, place, near, far, weight, far_weight, dtype, name):
-    shape = jax.ShapeDtypeStruct((near.shape[0], far_weight.shape[1] // 2), dtype)
+def project(flip, place, far, far_weight, before, dtype, name):
+    shape = jax.ShapeDtypeStruct((far.shape[0], far_weight.shape[1] // 2), dtype)
     return call(
         lambda *refs: project_kernel(flip, *refs),
         shape,
-        (place, near, far, weight, far_weight),
-        [smem()] + [vmem()] * 4,
+        (place, far, far_weight, before),
+        [smem()] + [vmem()] * 3,
         name=name,
     )
 
@@ -409,7 +422,8 @@
     near_part = lax.ppermute(attended, Y, turn)
     far_part = lax.ppermute(attended, Y, along_y(lambda yh, yl, core: (core, 1 - yl, yh)))
     where = jnp.stack([yl, core]).astype(jnp.int32)
-    sides = (where, near_part, far_part, out_weight, fetch(far_weight))
+    near_part, far_weight = together((near_part, fetch(far_weight)))
+    sides = (where, far_part, far_weight, project_near(where, near_part, out_weight))
     other = project(1, *sides, jnp.bfloat16, "project_send")
     other = lax.ppermute(other, "core", swap)
     own = project(0, *sides, jnp.float32, "project_keep")

time: 101 us -> 97.5 us (0.965)
  the two profiles are of different devices: /device:TPU:97 before, /device:TPU:1 now
where the time goes in v11:
time: 97.5 us; the launch traced here: 96.2 us
  starting transfers between devices  47.3 us (49%)
  Pallas kernels  29.9 us (31%)
  waiting for transfers between devices  18.5 us (19%)
    pallas_call x14, Pallas kernels, call(): pl.pallas_call(kernel, out_shape=out_shape, in_specs=in_specs, out_specs=...  29.9 us
    ppermute x1, starting transfers between devices, per_device(): near_part = lax.ppermute(attended, Y, turn)  7.52 us
    ppermute x1, starting transfers between devices, per_device(): units[4] = lax.ppermute(unit, YZ, turned(4))  6.6 us
    ppermute x2, starting transfers between devices, per_device(): units[step] = lax.ppermute(units[step - 1], 'z', down)  6.53 us
    ppermute x1, waiting for transfers between devices, per_device(): near_part = lax.ppermute(attended, Y, turn)  6.35 us
    ppermute x1, starting transfers between devices, per_device(): mine = lax.ppermute(bundle, Y, turn)  6.21 us
    ppermute x2, waiting for transfers between devices, per_device(): units[-step] = lax.ppermute(units[1 - step], 'z', up)  5.5 us
    ppermute x1, starting transfers between devices, per_device(): lax.ppermute(unit, YZ, turned(-1))  4.03 us
  transfers between devices with their start and end apart: 22, of which 8 were waited for; matrix products, arithmetic and copies ran while one was open for 0% of the time, Pallas kernels for 27%

profile of v11, /device:TPU:1, one launch (start us, length us, event | category | flops | bytes accessed | tf_op | source)
XLA Modules:
  0.0 96.2 jit_solution(11634749848037194136)
XLA Ops:
  1.3 6.2 %collective-permute-start.3 = (bf16[17,128,128]{2,1,0:T(8,128)(2,1)S(1)}, bf16[17,128,128]{2,1,0:T(8,128)(2,1)S(1)}, u32[]{:S(2)}, u32[]{:S(2)}) collective-permute-start(bf16[17,128,128]{2,1,0:T(8,128)(2,1)S(1)} %get-tuple-element.31), channel_id=1, source_target_pairs={{0,0},{1,4},{2,2},{3,6},{4,1},{5,5},{6,3},{7,7},{8,8},{9,12},{10,1... | collective-permute-start | bytes 1671176 | tf_op jit(solution)/shard_map/ppermute | solution.py:371
  7.5 1.4 %collective-permute-start = (bf16[4,128,128]{2,1,0:T(8,128)(2,1)S(1)}, bf16[4,128,128]{2,1,0:T(8,128)(2,1)S(1)}, u32[]{:S(2)}, u32[]{:S(2)}) collective-permute-start(bf16[4,128,128]{2,1,0:T(8,128)(2,1)S(1)} %get-tuple-element.30), channel_id=1, source_target_pairs={{0,8},{1,12},{2,10},{3,14},{4,9},{5,13},{6,11},{7,15},{8,16},{9,20... | collective-permute-start | bytes 393224 | tf_op jit(solution)/shard_map/ppermute | solution.py:370
  9.0 4.0 %collective-permute-start.1 = (bf16[4,128,128]{2,1,0:T(8,128)(2,1)S(1)}, bf16[4,128,128]{2,1,0:T(8,128)(2,1)S(1)}, u32[]{:S(2)}, u32[]{:S(2)}) collective-permute-start(bf16[4,128,128]{2,1,0:T(8,128)(2,1)S(1)} %get-tuple-element.30), channel_id=1, source_target_pairs={{0,56},{1,60},{2,58},{3,62},{4,57},{5,61},{6,59},{7,63},{8,0},{9,4... | collective-permute-start | bytes 393224 | tf_op jit(solution)/shard_map/ppermute | solution.py:370
  13.0 6.6 %collective-permute-start.2 = (bf16[4,128,128]{2,1,0:T(8,128)(2,1)S(1)}, bf16[4,128,128]{2,1,0:T(8,128)(2,1)S(1)}, u32[]{:S(2)}, u32[]{:S(2)}) collective-permute-start(bf16[4,128,128]{2,1,0:T(8,128)(2,1)S(1)} %get-tuple-element.30), channel_id=1, source_target_pairs={{0,32},{1,36},{2,34},{3,38},{4,33},{5,37},{6,35},{7,39},{8,40},{9,... | collective-permute-start | bytes 393224 | tf_op jit(solution)/shard_map/ppermute | solution.py:372
  19.6 4.5 %column_half.1 = bf16[768,3072]{1,0:T(8,128)(2,1)} custom-call(s32[1]{0:T(128)} %bitcast.2.half_ref, bf16[768,6144]{1,0:T(8,128)(2,1)} %weight_ref.1), custom_call_target="tpu_custom_call" | custom-call | tf_op jit(solution)/shard_map/column_half/pallas_call | solution.py:43
  25.6 1.5 %collective-permute-start.9 = (bf16[16,128,128]{2,1,0:T(8,128)(2,1)S(1)}, bf16[16,128,128]{2,1,0:T(8,128)(2,1)S(1)}, u32[]{:S(2)}, u32[]{:S(2)}) collective-permute-start(bf16[16,128,128]{2,1,0:T(8,128)(2,1)S(1)} %join.3.refs_3_), channel_id=1, source_target_pairs={{0,192},{64,0},{128,64},{192,128},{1,193},{65,1},{129,65},{193,129... | collective-permute-start | bytes 1572872 | tf_op jit(solution)/shard_map/ppermute | solution.py:382
  27.1 3.9 %collective-permute-start.5 = (bf16[4,128,128]{2,1,0:T(8,128)(2,1)S(1)}, bf16[4,128,128]{2,1,0:T(8,128)(2,1)S(1)}, u32[]{:S(2)}, u32[]{:S(2)}) collective-permute-start(bf16[4,128,128]{2,1,0:T(8,128)(2,1)S(1)} %collective-permute-done.1.refs_1_), channel_id=1, source_target_pairs={{0,56},{8,0},{16,8},{24,16},{32,24},{40,32},{48,40},{56,48},{1,57}... | collective-permute-start | bytes 393224 | tf_op jit(solution)/shard_map/ppermute | solution.py:385
  30.9 2.8 %collective-permute-done.4.refs_0_ = bf16[4,128,128]{2,1,0:T(8,128)(2,1)S(1)} collective-permute-done((bf16[4,128,128]{2,1,0:T(8,128)(2,1)S(1)}, bf16[4,128,128]{2,1,0:T(8,128)(2,1)S(1)}, u32[]{:S(2)}, u32[]{:S(2)}) %collective-permute-start.4) | collective-permute-done | bytes 131104 | tf_op jit(solution)/shard_map/ppermute | solution.py:384
  33.7 2.7 %collective-permute-start.7 = (bf16[4,128,128]{2,1,0:T(8,128)(2,1)S(1)}, bf16[4,128,128]{2,1,0:T(8,128)(2,1)S(1)}, u32[]{:S(2)}, u32[]{:S(2)}) collective-permute-start(bf16[4,128,128]{2,1,0:T(8,128)(2,1)S(1)} %collective-permute-done.5.refs_1_), channel_id=1, source_target_pairs={{0,56},{8,0},{16,8},{24,16},{32,24},{40,32},{48,40},{56,48},{1,57}... | collective-permute-start | bytes 393224 | tf_op jit(solution)/shard_map/ppermute | solution.py:385
  36.4 2.7 %collective-permute-done.6.refs_2_ = bf16[4,128,128]{2,1,0:T(8,128)(2,1)S(1)} collective-permute-done((bf16[4,128,128]{2,1,0:T(8,128)(2,1)S(1)}, bf16[4,128,128]{2,1,0:T(8,128)(2,1)S(1)}, u32[]{:S(2)}, u32[]{:S(2)}) %collective-permute-start.6) | collective-permute-done | bytes 131104 | tf_op jit(solution)/shard_map/ppermute | solution.py:384
  39.7 2.4 %collective-permute-start.12 = (bf16[16,128,128]{2,1,0:T(8,128)(2,1)S(1)}, bf16[16,128,128]{2,1,0:T(8,128)(2,1)S(1)}, u32[]{:S(2)}, u32[]{:S(2)}) collective-permute-start(bf16[16,128,128]{2,1,0:T(8,128)(2,1)S(1)} %join.2.refs_4_), channel_id=1, source_target_pairs={{0,192},{64,0},{128,64},{192,128},{1,193},{65,1},{129,65},{193,129... | collective-permute-start | bytes 1572872 | tf_op jit(solution)/shard_map/ppermute | solution.py:390
  42.2 2.7 %collective-permute-start.16 = (bf16[8,128,128]{2,1,0:T(8,128)(2,1)S(1)}, bf16[8,128,128]{2,1,0:T(8,128)(2,1)S(1)}, u32[]{:S(2)}, u32[]{:S(2)}) collective-permute-start(bf16[8,128,128]{2,1,0:T(8,128)(2,1)S(1)} %slice.23), channel_id=1, source_target_pairs={{0,192},{64,0},{128,64},{192,128},{1,193},{65,1},{129,65},{193,129... | collective-permute-start | bytes 786440 | tf_op jit(solution)/shard_map/ppermute | solution.py:401
  45.0 7.9 %first.1 = (f32[2,152,768]{2,1,0:T(8,128)S(1)}, f32[2,152,768]{2,1,0:T(8,128)S(1)}) custom-call(s32[5,128]{1,0:T(8,128)S(1)} %pad_add_fusion.refs_0_, bf16[17,128,128]{2,1,0:T(8,128)(2,1)S(1)} %collective-permute-done.3.refs_2_.refs_1_, bf16[17,128,128]{2,1,0:T(8,128)(2,1)S(1)} %collective-permute-done.10.refs_2_, bf16[16,128,128]{2,1,0:T(8,128)(2,1)S(1)} %join.3.refs_3_, ...), custom_call_target="tpu_custom_call" | custom-call | tf_op jit(solution)/shard_map/first/pallas_call | solution.py:43
  53.9 2.7 %collective-permute-start.14 = (bf16[8,128,128]{2,1,0:T(8,128)(2,1)S(1)}, bf16[8,128,128]{2,1,0:T(8,128)(2,1)S(1)}, u32[]{:S(2)}, u32[]{:S(2)}) collective-permute-start(bf16[8,128,128]{2,1,0:T(8,128)(2,1)S(1)} %slice.21), channel_id=1, source_target_pairs={{0,192},{64,0},{128,64},{192,128},{1,193},{65,1},{129,65},{193,129... | collective-permute-start | bytes 786440 | tf_op jit(solution)/shard_map/ppermute | solution.py:409
  56.6 2.7 %collective-permute-done.15.refs_5_ = bf16[8,128,128]{2,1,0:T(8,128)(2,1)S(1)} collective-permute-done((bf16[8,128,128]{2,1,0:T(8,128)(2,1)S(1)}, bf16[8,128,128]{2,1,0:T(8,128)(2,1)S(1)}, u32[]{:S(2)}, u32[]{:S(2)}) %collective-permute-start.15) | collective-permute-done | bytes 262176 | tf_op jit(solution)/shard_map/ppermute | solution.py:400
  59.3 3.9 %late.1 = (f32[2,152,768]{2,1,0:T(8,128)S(1)}, f32[2,152,768]{2,1,0:T(8,128)S(1)}) custom-call(s32[5,128]{1,0:T(8,128)S(1)} %pad_add_fusion.refs_0_, bf16[17,128,128]{2,1,0:T(8,128)(2,1)S(1)} %collective-permute-done.3.refs_2_.refs_1_, bf16[17,128,128]{2,1,0:T(8,128)(2,1)S(1)} %collective-permute-done.10.refs_2_, ...), custom_call_target="tpu_custom_call", output_to_operand_aliasing={{0}: (7, {}), {1}: (8, {})} | custom-call | tf_op jit(solution)/shard_map/late/pallas_call | solution.py:43
  63.3 1.7 %collective-permute-done.13.refs_3_ = bf16[8,128,128]{2,1,0:T(8,128)(2,1)S(1)} collective-permute-done((bf16[8,128,128]{2,1,0:T(8,128)(2,1)S(1)}, bf16[8,128,128]{2,1,0:T(8,128)(2,1)S(1)}, u32[]{:S(2)}, u32[]{:S(2)}) %collective-permute-start.13) | collective-permute-done | bytes 262176 | tf_op jit(solution)/shard_map/ppermute | solution.py:408
  65.0 2.0 %last_send.1 = f32[2,152,768]{2,1,0:T(8,128)S(1)} custom-call(s32[5,128]{1,0:T(8,128)S(1)} %pad_add_fusion.refs_0_, bf16[17,128,128]{2,1,0:T(8,128)(2,1)S(1)} %collective-permute-done.3.refs_2_.refs_1_, bf16[17,128,128]{2,1,0:T(8,128)(2,1)S(1)} %collective-permute-done.10.refs_2_, ...), custom_call_target="tpu_custom_call", output_to_operand_aliasing={{}: (5, {})} | custom-call | tf_op jit(solution)/shard_map/last_send/pallas_call | solution.py:43
  68.4 1.7 %last_keep.1.own_ref = f32[2,152,768]{2,1,0:T(8,128)S(1)} custom-call(s32[5,128]{1,0:T(8,128)S(1)} %pad_add_fusion.refs_0_, bf16[17,128,128]{2,1,0:T(8,128)(2,1)S(1)} %collective-permute-done.3.refs_2_.refs_1_, bf16[17,128,128]{2,1,0:T(8,128)(2,1)S(1)} %collective-permute-done.10.refs_2_, ...), custom_call_target="tpu_custom_call", output_to_operand_aliasing={{}: (5, {})} | custom-call | tf_op jit(solution)/shard_map/last_keep/pallas_call | solution.py:43
  70.7 7.5 %collective-permute-start.19 = (bf16[256,768]{1,0:T(8,128)(2,1)S(1)}, bf16[256,768]{1,0:T(8,128)(2,1)S(1)}, u32[]{:S(2)}, u32[]{:S(2)}) collective-permute-start(bf16[256,768]{1,0:T(8,128)(2,1)S(1)} %merge.1), channel_id=1, source_target_pairs={{0,0},{1,4},{2,2},{3,6},{4,1},{5,5},{6,3},{7,7},{8,8},{9,12},{10,1... | collective-permute-start | bytes 1179656 | tf_op jit(solution)/shard_map/ppermute | solution.py:422
  78.3 2.1 %collective-permute-start.18 = (bf16[256,768]{1,0:T(8,128)(2,1)S(1)}, bf16[256,768]{1,0:T(8,128)(2,1)S(1)}, u32[]{:S(2)}, u32[]{:S(2)}) collective-permute-start(bf16[256,768]{1,0:T(8,128)(2,1)S(1)} %merge.1), channel_id=1, source_target_pairs={{0,2},{1,6},{2,0},{3,4},{4,3},{5,7},{6,1},{7,5},{8,10},{9,14},{10,... | collective-permute-start | bytes 1179656 | tf_op jit(solution)/shard_map/ppermute | solution.py:423
  80.5 2.5 %fetch.1.refs_2_ = bf16[768,3072]{1,0:T(8,128)(2,1)S(1)} custom-call(bf16[768,3072]{1,0:T(8,128)(2,1)} %collective-permute-done.20.source_ref), custom_call_target="tpu_custom_call" | custom-call | tf_op jit(solution)/shard_map/fetch/pallas_call | solution.py:43
  83.0 6.3 %collective-permute-done.19.near_ref = bf16[256,768]{1,0:T(8,128)(2,1)S(1)} collective-permute-done((bf16[256,768]{1,0:T(8,128)(2,1)S(1)}, bf16[256,768]{1,0:T(8,128)(2,1)S(1)}, u32[]{:S(2)}, u32[]{:S(2)}) %collective-permute-start.19) | collective-permute-done | bytes 393248 | tf_op jit(solution)/shard_map/ppermute | solution.py:422
  89.4 2.0 %project_near.1.refs_3_ = f32[256,3072]{1,0:T(8,128)S(1)} custom-call(s32[2]{0:T(128)S(1)} %pad_add_fusion.1.place_ref.refs_0_, bf16[256,768]{1,0:T(8,128)(2,1)S(1)} %collective-permute-done.19.near_ref, bf16[768,6144]{1,0:T(8,128)(2,1)S(1)} %bitcast.12), custom_call_target="tpu_custom_call" | custom-call | tf_op jit(solution)/shard_map/project_near/pallas_call | solution.py:43
  (52 shorter events, 11.3 us)
Async XLA Ops:
  1.3 22.9 %collective-permute-start.3 = (bf16[17,128,128]{2,1,0:T(8,128)(2,1)S(1)}, bf16[17,128,128]{2,1,0:T(8,128)(2,1)S(1)}, u32[]{:S(2)}, u32[]{:S(2)}) collective-permute-start(bf16[17,128,128]{2,1,0:T(8,128)(2,1)S(1)} %get-tuple-element.31), channel_id=1, source_target_pairs={{0,0},{1,4},{2,2},{3,6},{4,1},{5,5},{6,3},{7,7},{8,8},{9,12},{10,1... | collective-permute-start | bytes 1671176 | tf_op jit(solution)/shard_map/ppermute | solution.py:371
  7.5 16.6 %collective-permute-start = (bf16[4,128,128]{2,1,0:T(8,128)(2,1)S(1)}, bf16[4,128,128]{2,1,0:T(8,128)(2,1)S(1)}, u32[]{:S(2)}, u32[]{:S(2)}) collective-permute-start(bf16[4,128,128]{2,1,0:T(8,128)(2,1)S(1)} %get-tuple-element.30), channel_id=1, source_target_pairs={{0,8},{1,12},{2,10},{3,14},{4,9},{5,13},{6,11},{7,15},{8,16},{9,20... | collective-permute-start | bytes 393224 | tf_op jit(solution)/shard_map/ppermute | solution.py:370
  9.0 15.2 %collective-permute-start.1 = (bf16[4,128,128]{2,1,0:T(8,128)(2,1)S(1)}, bf16[4,128,128]{2,1,0:T(8,128)(2,1)S(1)}, u32[]{:S(2)}, u32[]{:S(2)}) collective-permute-start(bf16[4,128,128]{2,1,0:T(8,128)(2,1)S(1)} %get-tuple-element.30), channel_id=1, source_target_pairs={{0,56},{1,60},{2,58},{3,62},{4,57},{5,61},{6,59},{7,63},{8,0},{9,4... | collective-permute-start | bytes 393224 | tf_op jit(solution)/shard_map/ppermute | solution.py:370
  13.0 11.2 %collective-permute-start.2 = (bf16[4,128,128]{2,1,0:T(8,128)(2,1)S(1)}, bf16[4,128,128]{2,1,0:T(8,128)(2,1)S(1)}, u32[]{:S(2)}, u32[]{:S(2)}) collective-permute-start(bf16[4,128,128]{2,1,0:T(8,128)(2,1)S(1)} %get-tuple-element.30), channel_id=1, source_target_pairs={{0,32},{1,36},{2,34},{3,38},{4,33},{5,37},{6,35},{7,39},{8,40},{9,... | collective-permute-start | bytes 393224 | tf_op jit(solution)/shard_map/ppermute | solution.py:372
  24.2 56.3 %collective-permute-start.20 = (bf16[768,3072]{1,0:T(8,128)(2,1)}, bf16[768,3072]{1,0:T(8,128)(2,1)}, u32[]{:S(2)}, u32[]{:S(2)}) collective-permute-start(bf16[768,3072]{1,0:T(8,128)(2,1)} %column_half.1), channel_id=1, source_target_pairs={{0,2},{1,7},{2,4},{3,1},{4,6},{5,3},{6,0},{7,5},{8,10},{9,15},{10,... | collective-permute-start | bytes 14155784 | tf_op jit(solution)/shard_map/ppermute | solution.py:378
  24.3 14.8 %collective-permute-start.8 = (bf16[16,128,128]{2,1,0:T(8,128)(2,1)S(1)}, bf16[16,128,128]{2,1,0:T(8,128)(2,1)S(1)}, u32[]{:S(2)}, u32[]{:S(2)}) collective-permute-start(bf16[16,128,128]{2,1,0:T(8,128)(2,1)S(1)} %join.3.refs_3_), channel_id=1, source_target_pairs={{0,64},{64,128},{128,192},{192,0},{1,65},{65,129},{129,193},{193,1... | collective-permute-start | bytes 1572872 | tf_op jit(solution)/shard_map/ppermute | solution.py:381
  25.6 13.6 %collective-permute-start.9 = (bf16[16,128,128]{2,1,0:T(8,128)(2,1)S(1)}, bf16[16,128,128]{2,1,0:T(8,128)(2,1)S(1)}, u32[]{:S(2)}, u32[]{:S(2)}) collective-permute-start(bf16[16,128,128]{2,1,0:T(8,128)(2,1)S(1)} %join.3.refs_3_), channel_id=1, source_target_pairs={{0,192},{64,0},{128,64},{192,128},{1,193},{65,1},{129,65},{193,129... | collective-permute-start | bytes 1572872 | tf_op jit(solution)/shard_map/ppermute | solution.py:382
  27.1 6.6 %collective-permute-start.4 = (bf16[4,128,128]{2,1,0:T(8,128)(2,1)S(1)}, bf16[4,128,128]{2,1,0:T(8,128)(2,1)S(1)}, u32[]{:S(2)}, u32[]{:S(2)}) collective-permute-start(bf16[4,128,128]{2,1,0:T(8,128)(2,1)S(1)} %collective-permute-done.refs_0_), channel_id=1, source_target_pairs={{0,8},{8,16},{16,24},{24,32},{32,40},{40,48},{48,56},{56,0},{1,9},... | collective-permute-start | bytes 393224 | tf_op jit(solution)/shard_map/ppermute | solution.py:384
  27.1 6.6 %collective-permute-start.5 = (bf16[4,128,128]{2,1,0:T(8,128)(2,1)S(1)}, bf16[4,128,128]{2,1,0:T(8,128)(2,1)S(1)}, u32[]{:S(2)}, u32[]{:S(2)}) collective-permute-start(bf16[4,128,128]{2,1,0:T(8,128)(2,1)S(1)} %collective-permute-done.1.refs_1_), channel_id=1, source_target_pairs={{0,56},{8,0},{16,8},{24,16},{32,24},{40,32},{48,40},{56,48},{1,57}... | collective-permute-start | bytes 393224 | tf_op jit(solution)/shard_map/ppermute | solution.py:385
  33.7 5.4 %collective-permute-start.6 = (bf16[4,128,128]{2,1,0:T(8,128)(2,1)S(1)}, bf16[4,128,128]{2,1,0:T(8,128)(2,1)S(1)}, u32[]{:S(2)}, u32[]{:S(2)}) collective-permute-start(bf16[4,128,128]{2,1,0:T(8,128)(2,1)S(1)} %collective-permute-done.4.refs_0_), channel_id=1, source_target_pairs={{0,8},{8,16},{16,24},{24,32},{32,40},{40,48},{48,56},{56,0},{1,9},... | collective-permute-start | bytes 393224 | tf_op jit(solution)/shard_map/ppermute | solution.py:384
  33.7 5.4 %collective-permute-start.7 = (bf16[4,128,128]{2,1,0:T(8,128)(2,1)S(1)}, bf16[4,128,128]{2,1,0:T(8,128)(2,1)S(1)}, u32[]{:S(2)}, u32[]{:S(2)}) collective-permute-start(bf16[4,128,128]{2,1,0:T(8,128)(2,1)S(1)} %collective-permute-done.5.refs_1_), channel_id=1, source_target_pairs={{0,56},{8,0},{16,8},{24,16},{32,24},{40,32},{48,40},{56,48},{1,57}... | collective-permute-start | bytes 393224 | tf_op jit(solution)/shard_map/ppermute | solution.py:385
  39.2 3.0 %collective-permute-start.10 = (bf16[17,128,128]{2,1,0:T(8,128)(2,1)S(1)}, bf16[17,128,128]{2,1,0:T(8,128)(2,1)S(1)}, u32[]{:S(2)}, u32[]{:S(2)}) collective-permute-start(bf16[17,128,128]{2,1,0:T(8,128)(2,1)S(1)} %collective-permute-done.3.refs_2_.refs_1_), channel_id=1, source_target_pairs={{0,1},{1,0},{2,3},{3,2},{4,5},{5,4},{6,7},{7,6},{8,9},{9,8},{10,11... | collective-permute-start | bytes 1671176 | tf_op jit(solution)/shard_map/ppermute | solution.py:391
  39.4 14.3 %collective-permute-start.11 = (bf16[16,128,128]{2,1,0:T(8,128)(2,1)S(1)}, bf16[16,128,128]{2,1,0:T(8,128)(2,1)S(1)}, u32[]{:S(2)}, u32[]{:S(2)}) collective-permute-start(bf16[16,128,128]{2,1,0:T(8,128)(2,1)S(1)} %join.2.refs_4_), channel_id=1, source_target_pairs={{0,64},{64,128},{128,192},{192,0},{1,65},{65,129},{129,193},{193,1... | collective-permute-start | bytes 1572872 | tf_op jit(solution)/shard_map/ppermute | solution.py:389
  39.7 14.0 %collective-permute-start.12 = (bf16[16,128,128]{2,1,0:T(8,128)(2,1)S(1)}, bf16[16,128,128]{2,1,0:T(8,128)(2,1)S(1)}, u32[]{:S(2)}, u32[]{:S(2)}) collective-permute-start(bf16[16,128,128]{2,1,0:T(8,128)(2,1)S(1)} %join.2.refs_4_), channel_id=1, source_target_pairs={{0,192},{64,0},{128,64},{192,128},{1,193},{65,1},{129,65},{193,129... | collective-permute-start | bytes 1572872 | tf_op jit(solution)/shard_map/ppermute | solution.py:390
  42.1 17.2 %collective-permute-start.15 = (bf16[8,128,128]{2,1,0:T(8,128)(2,1)S(1)}, bf16[8,128,128]{2,1,0:T(8,128)(2,1)S(1)}, u32[]{:S(2)}, u32[]{:S(2)}) collective-permute-start(bf16[8,128,128]{2,1,0:T(8,128)(2,1)S(1)} %slice.22), channel_id=1, source_target_pairs={{0,64},{64,128},{128,192},{192,0},{1,65},{65,129},{129,193},{193,1... | collective-permute-start | bytes 786440 | tf_op jit(solution)/shard_map/ppermute | solution.py:400
  42.2 17.1 %collective-permute-start.16 = (bf16[8,128,128]{2,1,0:T(8,128)(2,1)S(1)}, bf16[8,128,128]{2,1,0:T(8,128)(2,1)S(1)}, u32[]{:S(2)}, u32[]{:S(2)}) collective-permute-start(bf16[8,128,128]{2,1,0:T(8,128)(2,1)S(1)} %slice.23), channel_id=1, source_target_pairs={{0,192},{64,0},{128,64},{192,128},{1,193},{65,1},{129,65},{193,129... | collective-permute-start | bytes 786440 | tf_op jit(solution)/shard_map/ppermute | solution.py:401
  53.7 11.2 %collective-permute-start.13 = (bf16[8,128,128]{2,1,0:T(8,128)(2,1)S(1)}, bf16[8,128,128]{2,1,0:T(8,128)(2,1)S(1)}, u32[]{:S(2)}, u32[]{:S(2)}) collective-permute-start(bf16[8,128,128]{2,1,0:T(8,128)(2,1)S(1)} %slice.20), channel_id=1, source_target_pairs={{0,64},{64,128},{128,192},{192,0},{1,65},{65,129},{129,193},{193,1... | collective-permute-start | bytes 786440 | tf_op jit(solution)/shard_map/ppermute | solution.py:408
  53.9 11.1 %collective-permute-start.14 = (bf16[8,128,128]{2,1,0:T(8,128)(2,1)S(1)}, bf16[8,128,128]{2,1,0:T(8,128)(2,1)S(1)}, u32[]{:S(2)}, u32[]{:S(2)}) collective-permute-start(bf16[8,128,128]{2,1,0:T(8,128)(2,1)S(1)} %slice.21), channel_id=1, source_target_pairs={{0,192},{64,0},{128,64},{192,128},{1,193},{65,1},{129,65},{193,129... | collective-permute-start | bytes 786440 | tf_op jit(solution)/shard_map/ppermute | solution.py:409
  65.0 24.4 %slice-start = ((s8[9437184]{0:T(1024)(128)(4,1)}), s8[1048576]{0:T(1024)(128)(4,1)S(1)}, s32[]{:S(2)}) async-start(s8[9437184]{0:T(1024)(128)(4,1)} %bitcast.11), calls=%async_computation | async-start | bytes 2097152
  66.9 22.4 %slice-start.1 = ((s8[9437184]{0:T(1024)(128)(4,1)}), s8[4194304]{0:T(1024)(128)(4,1)S(1)}, s32[]{:S(2)}) async-start(s8[9437184]{0:T(1024)(128)(4,1)} %bitcast.11), calls=%async_computation.1 | async-start | bytes 8388608
  67.0 3.5 %collective-permute-start.17 = (f32[2,152,768]{2,1,0:T(8,128)S(1)}, f32[2,152,768]{2,1,0:T(8,128)S(1)}, u32[]{:S(2)}, u32[]{:S(2)}) collective-permute-start(f32[2,152,768]{2,1,0:T(8,128)S(1)} %last_send.1), channel_id=1, source_target_pairs={{0,1},{1,0},{2,3},{3,2},{4,5},{5,4},{6,7},{7,6},{8,9},{9,8},{10,11... | collective-permute-start | bytes 2801672 | tf_op jit(solution)/shard_map/ppermute | solution.py:417
  70.7 18.6 %collective-permute-start.19 = (bf16[256,768]{1,0:T(8,128)(2,1)S(1)}, bf16[256,768]{1,0:T(8,128)(2,1)S(1)}, u32[]{:S(2)}, u32[]{:S(2)}) collective-permute-start(bf16[256,768]{1,0:T(8,128)(2,1)S(1)} %merge.1), channel_id=1, source_target_pairs={{0,0},{1,4},{2,2},{3,6},{4,1},{5,5},{6,3},{7,7},{8,8},{9,12},{10,1... | collective-permute-start | bytes 1179656 | tf_op jit(solution)/shard_map/ppermute | solution.py:422
  78.3 13.1 %collective-permute-start.18 = (bf16[256,768]{1,0:T(8,128)(2,1)S(1)}, bf16[256,768]{1,0:T(8,128)(2,1)S(1)}, u32[]{:S(2)}, u32[]{:S(2)}) collective-permute-start(bf16[256,768]{1,0:T(8,128)(2,1)S(1)} %merge.1), channel_id=1, source_target_pairs={{0,2},{1,6},{2,0},{3,4},{4,3},{5,7},{6,1},{7,5},{8,10},{9,14},{10,... | collective-permute-start | bytes 1179656 | tf_op jit(solution)/shard_map/ppermute | solution.py:423
  92.8 2.4 %collective-permute-start.21 = (bf16[256,1536]{1,0:T(8,128)(2,1)S(1)}, bf16[256,1536]{1,0:T(8,128)(2,1)S(1)}, u32[]{:S(2)}, u32[]{:S(2)}) collective-permute-start(bf16[256,1536]{1,0:T(8,128)(2,1)S(1)} %project_send.1), channel_id=1, source_target_pairs={{0,1},{1,0},{2,3},{3,2},{4,5},{5,4},{6,7},{7,6},{8,9},{9,8},{10,11... | collective-permute-start | bytes 2359304 | tf_op jit(solution)/shard_map/ppermute | solution.py:428
  (1 other events, 8.9 us)

commit v12 on v9

--- a/solution.py
+++ b/solution.py
@@ -192,12 +192,14 @@
         state_ref = states[targets.index(target)]
         source = theirs_ref if target else mine_ref
         number = 2 * target + row
-        at = [list_ref[number, base + j] for j in range(size - 1)]
-        live = base + size - 1 < list_ref[number, slot]
-        at.append(jnp.where(live, list_ref[number, base + size - 1], at[0]))
+        at = [list_ref[number, base + j] for j in range(max(size - 1, 1))]
         ones = jnp.ones((16, TILE), jnp.bfloat16)
+        if size > 1:
+            live = base + size - 1 < list_ref[number, slot]
+            at.append(jnp.where(live, list_ref[number, base + size - 1], at[0]))
         values = [jnp.concatenate([tiles_ref[i + 2], ones], axis=0) for i in at]
-        values[-1] = values[-1] * jnp.where(live, 1.0, 0.0).astype(jnp.bfloat16)
+        if size > 1:
+            values[-1] = values[-1] * jnp.where(live, 1.0, 0.0).astype(jnp.bfloat16)
         values = jnp.concatenate(values, axis=1)
         keys = jnp.concatenate([tiles_ref[i] for i in at], axis=0)
         chunks = [pl.ds(h * TILE, TILE) for h in range(HEADS)]
@@ -236,7 +238,11 @@
 
         lax.fori_loop(0, blocks, full, 0)
 
-        @pl.when(rest > 0)
+        @pl.when(rest == 1)
+        def _():
+            block(target, row, 4 * blocks, 1)
+
+        @pl.when(rest == 2)
         def _():
             block(target, row, 4 * blocks, 2)
 
@@ -341,10 +347,6 @@
     )
 
 
-def add_kernel(keep_ref, other_ref, out_ref):
-    out_ref[...] = (keep_ref[...] + other_ref[...].astype(jnp.float32)).astype(out_ref.dtype)
-
-
 def per_device(queries, key_rows, value_rows, tile_mask, out_weight):
     x, z = lax.axis_index("x"), lax.axis_index("z")
     yh, yl, core = lax.axis_index("yh"), lax.axis_index("yl"), lax.axis_index("core")
@@ -413,8 +415,7 @@
     other = project(1, *sides, jnp.bfloat16, "project_send")
     other = lax.ppermute(other, "core", swap)
     own = project(0, *sides, jnp.float32, "project_keep")
-    shape = jax.ShapeDtypeStruct(own.shape, jnp.bfloat16)
-    return call(add_kernel, shape, (own, other), [vmem()] * 2, name="add")
+    return (own + other.astype(jnp.float32)).astype(jnp.bfloat16)
 
 
 def solution(mesh):

time: 94.9 us -> 94.7 us (level); the launches traced: 94.1 us -> 95 us
  Pallas kernels: 27.5 us -> 32.2 us
  waiting for transfers between devices: 23.1 us -> 19.2 us
  other arithmetic: 0.17 us -> 1.27 us
  starting transfers between devices: 43 us -> 42 us
    pallas_call x13 -> x12, Pallas kernels: 27.5 us -> 32.2 us  [call(): pl.pallas_call(kernel, out_shape=out_shape, in_specs=in_specs, out_specs=...]
    ppermute x1, waiting for transfers between devices: 2.64 us -> 0.01 us  [per_device(): late_after = lax.ppermute(late, 'x', back)]
    ppermute x1, waiting for transfers between devices: 4.77 us -> 3.06 us  [per_device(): lax.ppermute(late_before[:half], 'x', forth)]
    ppermute x1, starting transfers between devices: 3.32 us -> 4.89 us  [per_device(): lax.ppermute(attended, Y, along_y(lambda yh, yl, core: (core, 1 - yl, yh)))]
    ppermute x1, starting transfers between devices: 3.41 us -> 2.08 us  [per_device(): received = lax.ppermute(send, 'core', swap)]
    ppermute x1, starting transfers between devices: 4.61 us -> 3.38 us  [per_device(): near_part = lax.ppermute(attended, Y, turn)]
    convert_element_type x0 -> x1, other arithmetic: none -> 1.1 us  [per_device(): return (own + other.astype(jnp.float32)).astype(jnp.bfloat16)]
  transfers between devices with their start and end apart: 22 -> 22, of which waited for: 10 -> 9; matrix products, arithmetic and copies ran while one was open for 0% -> 0% of each run, Pallas kernels for 25% -> 30%
where the time goes in v12:
time: 94.7 us; the launch traced here: 95 us
  starting transfers between devices  42 us (44%)
  Pallas kernels  32.2 us (34%)
  waiting for transfers between devices  19.2 us (20%)
  other arithmetic  1.27 us (1%)
    pallas_call x12, Pallas kernels, call(): pl.pallas_call(kernel, out_shape=out_shape, in_specs=in_specs, out_specs=...  32.2 us
    ppermute x1, starting transfers between devices, per_device(): units[4] = lax.ppermute(unit, YZ, turned(4))  6.72 us
    ppermute x1, starting transfers between devices, per_device(): mine = lax.ppermute(bundle, Y, turn)  6.21 us
    ppermute x2, waiting for transfers between devices, per_device(): units[-step] = lax.ppermute(units[1 - step], 'z', up)  5.5 us
    ppermute x2, starting transfers between devices, per_device(): units[step] = lax.ppermute(units[step - 1], 'z', down)  4.92 us
    ppermute x1, starting transfers between devices, per_device(): lax.ppermute(attended, Y, along_y(lambda yh, yl, core: (core, 1 - yl, yh)))  4.89 us
    ppermute x1, waiting for transfers between devices, per_device(): near_part = lax.ppermute(attended, Y, turn)  4.62 us
    ppermute x1, starting transfers between devices, per_device(): near_part = lax.ppermute(attended, Y, turn)  3.38 us
  transfers between devices with their start and end apart: 22, of which 9 were waited for; matrix products, arithmetic and copies ran while one was open for 0% of the time, Pallas kernels for 30%

profile of v12, /device:TPU:1, one launch (start us, length us, event | category | flops | bytes accessed | tf_op | source)
XLA Modules:
  0.0 95.0 jit_solution(17221614658941602662)
XLA Ops:
  1.3 6.2 %collective-permute-start.3 = (bf16[17,128,128]{2,1,0:T(8,128)(2,1)S(1)}, bf16[17,128,128]{2,1,0:T(8,128)(2,1)S(1)}, u32[]{:S(2)}, u32[]{:S(2)}) collective-permute-start(bf16[17,128,128]{2,1,0:T(8,128)(2,1)S(1)} %get-tuple-element.31), channel_id=1, source_target_pairs={{0,0},{1,4},{2,2},{3,6},{4,1},{5,5},{6,3},{7,7},{8,8},{9,12},{10,1... | collective-permute-start | bytes 1671176 | tf_op jit(solution)/shard_map/ppermute | solution.py:360
  7.5 6.7 %collective-permute-start.2 = (bf16[4,128,128]{2,1,0:T(8,128)(2,1)S(1)}, bf16[4,128,128]{2,1,0:T(8,128)(2,1)S(1)}, u32[]{:S(2)}, u32[]{:S(2)}) collective-permute-start(bf16[4,128,128]{2,1,0:T(8,128)(2,1)S(1)} %get-tuple-element.30), channel_id=1, source_target_pairs={{0,32},{1,36},{2,34},{3,38},{4,33},{5,37},{6,35},{7,39},{8,40},{9,... | collective-permute-start | bytes 393224 | tf_op jit(solution)/shard_map/ppermute | solution.py:361
  14.3 2.8 %collective-permute-start.1 = (bf16[4,128,128]{2,1,0:T(8,128)(2,1)S(1)}, bf16[4,128,128]{2,1,0:T(8,128)(2,1)S(1)}, u32[]{:S(2)}, u32[]{:S(2)}) collective-permute-start(bf16[4,128,128]{2,1,0:T(8,128)(2,1)S(1)} %get-tuple-element.30), channel_id=1, source_target_pairs={{0,56},{1,60},{2,58},{3,62},{4,57},{5,61},{6,59},{7,63},{8,0},{9,4... | collective-permute-start | bytes 393224 | tf_op jit(solution)/shard_map/ppermute | solution.py:359
  18.4 4.5 %column_half.1 = bf16[768,3072]{1,0:T(8,128)(2,1)} custom-call(s32[1]{0:T(128)} %bitcast.2.half_ref, bf16[768,6144]{1,0:T(8,128)(2,1)} %refs_3_.3), custom_call_target="tpu_custom_call" | custom-call | tf_op jit(solution)/shard_map/column_half/pallas_call | solution.py:43
  25.1 2.6 %collective-permute-start.9 = (bf16[16,128,128]{2,1,0:T(8,128)(2,1)S(1)}, bf16[16,128,128]{2,1,0:T(8,128)(2,1)S(1)}, u32[]{:S(2)}, u32[]{:S(2)}) collective-permute-start(bf16[16,128,128]{2,1,0:T(8,128)(2,1)S(1)} %join.3.refs_3_), channel_id=1, source_target_pairs={{0,192},{64,0},{128,64},{192,128},{1,193},{65,1},{129,65},{193,129... | collective-permute-start | bytes 1572872 | tf_op jit(solution)/shard_map/ppermute | solution.py:371
  28.1 2.2 %collective-permute-start.5 = (bf16[4,128,128]{2,1,0:T(8,128)(2,1)S(1)}, bf16[4,128,128]{2,1,0:T(8,128)(2,1)S(1)}, u32[]{:S(2)}, u32[]{:S(2)}) collective-permute-start(bf16[4,128,128]{2,1,0:T(8,128)(2,1)S(1)} %collective-permute-done.1.refs_1_), channel_id=1, source_target_pairs={{0,56},{8,0},{16,8},{24,16},{32,24},{40,32},{48,40},{56,48},{1,57}... | collective-permute-start | bytes 393224 | tf_op jit(solution)/shard_map/ppermute | solution.py:374
  30.3 2.8 %collective-permute-done.4.refs_0_ = bf16[4,128,128]{2,1,0:T(8,128)(2,1)S(1)} collective-permute-done((bf16[4,128,128]{2,1,0:T(8,128)(2,1)S(1)}, bf16[4,128,128]{2,1,0:T(8,128)(2,1)S(1)}, u32[]{:S(2)}, u32[]{:S(2)}) %collective-permute-start.4) | collective-permute-done | bytes 131104 | tf_op jit(solution)/shard_map/ppermute | solution.py:373
  33.1 2.7 %collective-permute-start.7 = (bf16[4,128,128]{2,1,0:T(8,128)(2,1)S(1)}, bf16[4,128,128]{2,1,0:T(8,128)(2,1)S(1)}, u32[]{:S(2)}, u32[]{:S(2)}) collective-permute-start(bf16[4,128,128]{2,1,0:T(8,128)(2,1)S(1)} %collective-permute-done.5.refs_1_), channel_id=1, source_target_pairs={{0,56},{8,0},{16,8},{24,16},{32,24},{40,32},{48,40},{56,48},{1,57}... | collective-permute-start | bytes 393224 | tf_op jit(solution)/shard_map/ppermute | solution.py:374
  35.8 2.7 %collective-permute-done.6.refs_2_ = bf16[4,128,128]{2,1,0:T(8,128)(2,1)S(1)} collective-permute-done((bf16[4,128,128]{2,1,0:T(8,128)(2,1)S(1)}, bf16[4,128,128]{2,1,0:T(8,128)(2,1)S(1)}, u32[]{:S(2)}, u32[]{:S(2)}) %collective-permute-start.6) | collective-permute-done | bytes 131104 | tf_op jit(solution)/shard_map/ppermute | solution.py:373
  42.0 2.3 %collective-permute-start.12 = (bf16[8,128,128]{2,1,0:T(8,128)(2,1)S(1)}, bf16[8,128,128]{2,1,0:T(8,128)(2,1)S(1)}, u32[]{:S(2)}, u32[]{:S(2)}) collective-permute-start(bf16[8,128,128]{2,1,0:T(8,128)(2,1)S(1)} %slice.21), channel_id=1, source_target_pairs={{0,192},{64,0},{128,64},{192,128},{1,193},{65,1},{129,65},{193,129... | collective-permute-start | bytes 786440 | tf_op jit(solution)/shard_map/ppermute | solution.py:390
  44.3 9.3 %first.1 = (f32[2,152,768]{2,1,0:T(8,128)S(1)}, f32[2,152,768]{2,1,0:T(8,128)S(1)}) custom-call(s32[5,128]{1,0:T(8,128)S(1)} %pad_add_fusion.refs_0_, bf16[17,128,128]{2,1,0:T(8,128)(2,1)S(1)} %collective-permute-done.3.refs_2_.refs_1_, bf16[17,128,128]{2,1,0:T(8,128)(2,1)S(1)} %collective-permute-done.10.refs_2_, bf16[16,128,128]{2,1,0:T(8,128)(2,1)S(1)} %join.3.refs_3_, ...), custom_call_target="tpu_custom_call" | custom-call | tf_op jit(solution)/shard_map/first/pallas_call | solution.py:43
  53.6 1.8 %collective-permute-done.13.refs_3_ = bf16[16,128,128]{2,1,0:T(8,128)(2,1)S(1)} collective-permute-done((bf16[16,128,128]{2,1,0:T(8,128)(2,1)S(1)}, bf16[16,128,128]{2,1,0:T(8,128)(2,1)S(1)}, u32[]{:S(2)}, u32[]{:S(2)}) %collective-permute-start.13) | collective-permute-done | bytes 524320 | tf_op jit(solution)/shard_map/ppermute | solution.py:378
  55.6 2.7 %collective-permute-start.16 = (bf16[8,128,128]{2,1,0:T(8,128)(2,1)S(1)}, bf16[8,128,128]{2,1,0:T(8,128)(2,1)S(1)}, u32[]{:S(2)}, u32[]{:S(2)}) collective-permute-start(bf16[8,128,128]{2,1,0:T(8,128)(2,1)S(1)} %slice.23), channel_id=1, source_target_pairs={{0,192},{64,0},{128,64},{192,128},{1,193},{65,1},{129,65},{193,129... | collective-permute-start | bytes 786440 | tf_op jit(solution)/shard_map/ppermute | solution.py:398
  58.3 5.3 %late.1 = (f32[2,152,768]{2,1,0:T(8,128)S(1)}, f32[2,152,768]{2,1,0:T(8,128)S(1)}) custom-call(s32[5,128]{1,0:T(8,128)S(1)} %pad_add_fusion.refs_0_, bf16[17,128,128]{2,1,0:T(8,128)(2,1)S(1)} %collective-permute-done.3.refs_2_.refs_1_, bf16[17,128,128]{2,1,0:T(8,128)(2,1)S(1)} %collective-permute-done.10.refs_2_, ...), custom_call_target="tpu_custom_call", output_to_operand_aliasing={{0}: (5, {}), {1}: (6, {})} | custom-call | tf_op jit(solution)/shard_map/late/pallas_call | solution.py:43
  63.6 3.1 %collective-permute-done.15.refs_5_ = bf16[8,128,128]{2,1,0:T(8,128)(2,1)S(1)} collective-permute-done((bf16[8,128,128]{2,1,0:T(8,128)(2,1)S(1)}, bf16[8,128,128]{2,1,0:T(8,128)(2,1)S(1)}, u32[]{:S(2)}, u32[]{:S(2)}) %collective-permute-start.15) | collective-permute-done | bytes 262176 | tf_op jit(solution)/shard_map/ppermute | solution.py:397
  66.7 2.8 %last_send.1 = f32[2,152,768]{2,1,0:T(8,128)S(1)} custom-call(s32[5,128]{1,0:T(8,128)S(1)} %pad_add_fusion.refs_0_, bf16[17,128,128]{2,1,0:T(8,128)(2,1)S(1)} %collective-permute-done.3.refs_2_.refs_1_, bf16[17,128,128]{2,1,0:T(8,128)(2,1)S(1)} %collective-permute-done.10.refs_2_, ...), custom_call_target="tpu_custom_call", output_to_operand_aliasing={{}: (7, {})} | custom-call | tf_op jit(solution)/shard_map/last_send/pallas_call | solution.py:43
  69.5 2.1 %collective-permute-start.17 = (f32[2,152,768]{2,1,0:T(8,128)S(1)}, f32[2,152,768]{2,1,0:T(8,128)S(1)}, u32[]{:S(2)}, u32[]{:S(2)}) collective-permute-start(f32[2,152,768]{2,1,0:T(8,128)S(1)} %last_send.1), channel_id=1, source_target_pairs={{0,1},{1,0},{2,3},{3,2},{4,5},{5,4},{6,7},{7,6},{8,9},{9,8},{10,11... | collective-permute-start | bytes 2801672 | tf_op jit(solution)/shard_map/ppermute | solution.py:406
  71.6 2.2 %last_keep.1.own_ref = f32[2,152,768]{2,1,0:T(8,128)S(1)} custom-call(s32[5,128]{1,0:T(8,128)S(1)} %pad_add_fusion.refs_0_, bf16[17,128,128]{2,1,0:T(8,128)(2,1)S(1)} %collective-permute-done.3.refs_2_.refs_1_, bf16[17,128,128]{2,1,0:T(8,128)(2,1)S(1)} %collective-permute-done.10.refs_2_, ...), custom_call_target="tpu_custom_call", output_to_operand_aliasing={{}: (7, {})} | custom-call | tf_op jit(solution)/shard_map/last_keep/pallas_call | solution.py:43
  74.1 4.9 %collective-permute-start.19 = (bf16[256,768]{1,0:T(8,128)(2,1)S(1)}, bf16[256,768]{1,0:T(8,128)(2,1)S(1)}, u32[]{:S(2)}, u32[]{:S(2)}) collective-permute-start(bf16[256,768]{1,0:T(8,128)(2,1)S(1)} %merge.1), channel_id=1, source_target_pairs={{0,2},{1,6},{2,0},{3,4},{4,3},{5,7},{6,1},{7,5},{8,10},{9,14},{10,... | collective-permute-start | bytes 1179656 | tf_op jit(solution)/shard_map/ppermute | solution.py:412
  79.0 3.4 %collective-permute-start.18 = (bf16[256,768]{1,0:T(8,128)(2,1)S(1)}, bf16[256,768]{1,0:T(8,128)(2,1)S(1)}, u32[]{:S(2)}, u32[]{:S(2)}) collective-permute-start(bf16[256,768]{1,0:T(8,128)(2,1)S(1)} %merge.1), channel_id=1, source_target_pairs={{0,0},{1,4},{2,2},{3,6},{4,1},{5,5},{6,3},{7,7},{8,8},{9,12},{10,1... | collective-permute-start | bytes 1179656 | tf_op jit(solution)/shard_map/ppermute | solution.py:411
  82.4 2.5 %fetch.1.refs_4_ = bf16[768,3072]{1,0:T(8,128)(2,1)S(1)} custom-call(bf16[768,3072]{1,0:T(8,128)(2,1)} %collective-permute-done.20.source_ref), custom_call_target="tpu_custom_call" | custom-call | tf_op jit(solution)/shard_map/fetch/pallas_call | solution.py:43
  84.9 4.6 %collective-permute-done.18.refs_1_ = bf16[256,768]{1,0:T(8,128)(2,1)S(1)} collective-permute-done((bf16[256,768]{1,0:T(8,128)(2,1)S(1)}, bf16[256,768]{1,0:T(8,128)(2,1)S(1)}, u32[]{:S(2)}, u32[]{:S(2)}) %collective-permute-start.18) | collective-permute-done | bytes 393248 | tf_op jit(solution)/shard_map/ppermute | solution.py:411
  89.6 2.0 %project_send.1 = bf16[256,1536]{1,0:T(8,128)(2,1)S(1)} custom-call(s32[2]{0:T(128)S(1)} %pad_add_fusion.1.refs_0_, bf16[256,768]{1,0:T(8,128)(2,1)S(1)} %collective-permute-done.18.refs_1_, bf16[256,768]{1,0:T(8,128)(2,1)S(1)} %collective-permute-done.19.refs_2_, bf16[768,6144]{1,0:T(8,128)(2,1)S(1)} %bitcast.12, bf16[768,3072]{1,0:T(8,128)(2,1)S(1)} %fetch.1.refs_4_), custom_call_target="tpu_custom_call" | custom-call | tf_op jit(solution)/shard_map/project_send/pallas_call | solution.py:43
  91.7 2.0 %project_keep.1 = f32[256,1536]{1,0:T(8,128)S(1)} custom-call(s32[2]{0:T(128)S(1)} %pad_add_fusion.1.refs_0_, bf16[256,768]{1,0:T(8,128)(2,1)S(1)} %collective-permute-done.18.refs_1_, bf16[256,768]{1,0:T(8,128)(2,1)S(1)} %collective-permute-done.19.refs_2_, bf16[768,6144]{1,0:T(8,128)(2,1)S(1)} %bitcast.12, bf16[768,3072]{1,0:T(8,128)(2,1)S(1)} %fetch.1.refs_4_), custom_call_target="tpu_custom_call" | custom-call | tf_op jit(solution)/shard_map/project_keep/pallas_call | solution.py:43
  (51 shorter events, 10.6 us)
Async XLA Ops:
  1.3 23.7 %collective-permute-start.3 = (bf16[17,128,128]{2,1,0:T(8,128)(2,1)S(1)}, bf16[17,128,128]{2,1,0:T(8,128)(2,1)S(1)}, u32[]{:S(2)}, u32[]{:S(2)}) collective-permute-start(bf16[17,128,128]{2,1,0:T(8,128)(2,1)S(1)} %get-tuple-element.31), channel_id=1, source_target_pairs={{0,0},{1,4},{2,2},{3,6},{4,1},{5,5},{6,3},{7,7},{8,8},{9,12},{10,1... | collective-permute-start | bytes 1671176 | tf_op jit(solution)/shard_map/ppermute | solution.py:360
  7.5 15.4 %collective-permute-start.2 = (bf16[4,128,128]{2,1,0:T(8,128)(2,1)S(1)}, bf16[4,128,128]{2,1,0:T(8,128)(2,1)S(1)}, u32[]{:S(2)}, u32[]{:S(2)}) collective-permute-start(bf16[4,128,128]{2,1,0:T(8,128)(2,1)S(1)} %get-tuple-element.30), channel_id=1, source_target_pairs={{0,32},{1,36},{2,34},{3,38},{4,33},{5,37},{6,35},{7,39},{8,40},{9,... | collective-permute-start | bytes 393224 | tf_op jit(solution)/shard_map/ppermute | solution.py:361
  14.3 9.2 %collective-permute-start.1 = (bf16[4,128,128]{2,1,0:T(8,128)(2,1)S(1)}, bf16[4,128,128]{2,1,0:T(8,128)(2,1)S(1)}, u32[]{:S(2)}, u32[]{:S(2)}) collective-permute-start(bf16[4,128,128]{2,1,0:T(8,128)(2,1)S(1)} %get-tuple-element.30), channel_id=1, source_target_pairs={{0,56},{1,60},{2,58},{3,62},{4,57},{5,61},{6,59},{7,63},{8,0},{9,4... | collective-permute-start | bytes 393224 | tf_op jit(solution)/shard_map/ppermute | solution.py:359
  17.0 8.0 %collective-permute-start = (bf16[4,128,128]{2,1,0:T(8,128)(2,1)S(1)}, bf16[4,128,128]{2,1,0:T(8,128)(2,1)S(1)}, u32[]{:S(2)}, u32[]{:S(2)}) collective-permute-start(bf16[4,128,128]{2,1,0:T(8,128)(2,1)S(1)} %get-tuple-element.30), channel_id=1, source_target_pairs={{0,8},{1,12},{2,10},{3,14},{4,9},{5,13},{6,11},{7,15},{8,16},{9,20... | collective-permute-start | bytes 393224 | tf_op jit(solution)/shard_map/ppermute | solution.py:359
  25.0 57.4 %collective-permute-start.20 = (bf16[768,3072]{1,0:T(8,128)(2,1)}, bf16[768,3072]{1,0:T(8,128)(2,1)}, u32[]{:S(2)}, u32[]{:S(2)}) collective-permute-start(bf16[768,3072]{1,0:T(8,128)(2,1)} %column_half.1), channel_id=1, source_target_pairs={{0,2},{1,7},{2,4},{3,1},{4,6},{5,3},{6,0},{7,5},{8,10},{9,15},{10,... | collective-permute-start | bytes 14155784 | tf_op jit(solution)/shard_map/ppermute | solution.py:367
  25.1 13.5 %collective-permute-start.9 = (bf16[16,128,128]{2,1,0:T(8,128)(2,1)S(1)}, bf16[16,128,128]{2,1,0:T(8,128)(2,1)S(1)}, u32[]{:S(2)}, u32[]{:S(2)}) collective-permute-start(bf16[16,128,128]{2,1,0:T(8,128)(2,1)S(1)} %join.3.refs_3_), channel_id=1, source_target_pairs={{0,192},{64,0},{128,64},{192,128},{1,193},{65,1},{129,65},{193,129... | collective-permute-start | bytes 1572872 | tf_op jit(solution)/shard_map/ppermute | solution.py:371
  27.6 12.7 %collective-permute-start.8 = (bf16[16,128,128]{2,1,0:T(8,128)(2,1)S(1)}, bf16[16,128,128]{2,1,0:T(8,128)(2,1)S(1)}, u32[]{:S(2)}, u32[]{:S(2)}) collective-permute-start(bf16[16,128,128]{2,1,0:T(8,128)(2,1)S(1)} %join.3.refs_3_), channel_id=1, source_target_pairs={{0,64},{64,128},{128,192},{192,0},{1,65},{65,129},{129,193},{193,1... | collective-permute-start | bytes 1572872 | tf_op jit(solution)/shard_map/ppermute | solution.py:370
  27.7 5.4 %collective-permute-start.4 = (bf16[4,128,128]{2,1,0:T(8,128)(2,1)S(1)}, bf16[4,128,128]{2,1,0:T(8,128)(2,1)S(1)}, u32[]{:S(2)}, u32[]{:S(2)}) collective-permute-start(bf16[4,128,128]{2,1,0:T(8,128)(2,1)S(1)} %collective-permute-done.refs_0_), channel_id=1, source_target_pairs={{0,8},{8,16},{16,24},{24,32},{32,40},{40,48},{48,56},{56,0},{1,9},... | collective-permute-start | bytes 393224 | tf_op jit(solution)/shard_map/ppermute | solution.py:373
  28.1 5.0 %collective-permute-start.5 = (bf16[4,128,128]{2,1,0:T(8,128)(2,1)S(1)}, bf16[4,128,128]{2,1,0:T(8,128)(2,1)S(1)}, u32[]{:S(2)}, u32[]{:S(2)}) collective-permute-start(bf16[4,128,128]{2,1,0:T(8,128)(2,1)S(1)} %collective-permute-done.1.refs_1_), channel_id=1, source_target_pairs={{0,56},{8,0},{16,8},{24,16},{32,24},{40,32},{48,40},{56,48},{1,57}... | collective-permute-start | bytes 393224 | tf_op jit(solution)/shard_map/ppermute | solution.py:374
  33.1 5.4 %collective-permute-start.6 = (bf16[4,128,128]{2,1,0:T(8,128)(2,1)S(1)}, bf16[4,128,128]{2,1,0:T(8,128)(2,1)S(1)}, u32[]{:S(2)}, u32[]{:S(2)}) collective-permute-start(bf16[4,128,128]{2,1,0:T(8,128)(2,1)S(1)} %collective-permute-done.4.refs_0_), channel_id=1, source_target_pairs={{0,8},{8,16},{16,24},{24,32},{32,40},{40,48},{48,56},{56,0},{1,9},... | collective-permute-start | bytes 393224 | tf_op jit(solution)/shard_map/ppermute | solution.py:373
  33.1 5.4 %collective-permute-start.7 = (bf16[4,128,128]{2,1,0:T(8,128)(2,1)S(1)}, bf16[4,128,128]{2,1,0:T(8,128)(2,1)S(1)}, u32[]{:S(2)}, u32[]{:S(2)}) collective-permute-start(bf16[4,128,128]{2,1,0:T(8,128)(2,1)S(1)} %collective-permute-done.5.refs_1_), channel_id=1, source_target_pairs={{0,56},{8,0},{16,8},{24,16},{32,24},{40,32},{48,40},{56,48},{1,57}... | collective-permute-start | bytes 393224 | tf_op jit(solution)/shard_map/ppermute | solution.py:374
  40.3 3.9 %collective-permute-start.10 = (bf16[17,128,128]{2,1,0:T(8,128)(2,1)S(1)}, bf16[17,128,128]{2,1,0:T(8,128)(2,1)S(1)}, u32[]{:S(2)}, u32[]{:S(2)}) collective-permute-start(bf16[17,128,128]{2,1,0:T(8,128)(2,1)S(1)} %collective-permute-done.3.refs_2_.refs_1_), channel_id=1, source_target_pairs={{0,1},{1,0},{2,3},{3,2},{4,5},{5,4},{6,7},{7,6},{8,9},{9,8},{10,11... | collective-permute-start | bytes 1671176 | tf_op jit(solution)/shard_map/ppermute | solution.py:380
  40.4 13.2 %collective-permute-start.14 = (bf16[16,128,128]{2,1,0:T(8,128)(2,1)S(1)}, bf16[16,128,128]{2,1,0:T(8,128)(2,1)S(1)}, u32[]{:S(2)}, u32[]{:S(2)}) collective-permute-start(bf16[16,128,128]{2,1,0:T(8,128)(2,1)S(1)} %join.2.refs_4_), channel_id=1, source_target_pairs={{0,192},{64,0},{128,64},{192,128},{1,193},{65,1},{129,65},{193,129... | collective-permute-start | bytes 1572872 | tf_op jit(solution)/shard_map/ppermute | solution.py:379
  41.5 14.0 %collective-permute-start.13 = (bf16[16,128,128]{2,1,0:T(8,128)(2,1)S(1)}, bf16[16,128,128]{2,1,0:T(8,128)(2,1)S(1)}, u32[]{:S(2)}, u32[]{:S(2)}) collective-permute-start(bf16[16,128,128]{2,1,0:T(8,128)(2,1)S(1)} %join.2.refs_4_), channel_id=1, source_target_pairs={{0,64},{64,128},{128,192},{192,0},{1,65},{65,129},{129,193},{193,1... | collective-permute-start | bytes 1572872 | tf_op jit(solution)/shard_map/ppermute | solution.py:378
  42.0 21.6 %collective-permute-start.12 = (bf16[8,128,128]{2,1,0:T(8,128)(2,1)S(1)}, bf16[8,128,128]{2,1,0:T(8,128)(2,1)S(1)}, u32[]{:S(2)}, u32[]{:S(2)}) collective-permute-start(bf16[8,128,128]{2,1,0:T(8,128)(2,1)S(1)} %slice.21), channel_id=1, source_target_pairs={{0,192},{64,0},{128,64},{192,128},{1,193},{65,1},{129,65},{193,129... | collective-permute-start | bytes 786440 | tf_op jit(solution)/shard_map/ppermute | solution.py:390
  44.3 19.4 %collective-permute-start.11 = (bf16[8,128,128]{2,1,0:T(8,128)(2,1)S(1)}, bf16[8,128,128]{2,1,0:T(8,128)(2,1)S(1)}, u32[]{:S(2)}, u32[]{:S(2)}) collective-permute-start(bf16[8,128,128]{2,1,0:T(8,128)(2,1)S(1)} %slice.20), channel_id=1, source_target_pairs={{0,64},{64,128},{128,192},{192,0},{1,65},{65,129},{129,193},{193,1... | collective-permute-start | bytes 786440 | tf_op jit(solution)/shard_map/ppermute | solution.py:389
  55.5 11.2 %collective-permute-start.15 = (bf16[8,128,128]{2,1,0:T(8,128)(2,1)S(1)}, bf16[8,128,128]{2,1,0:T(8,128)(2,1)S(1)}, u32[]{:S(2)}, u32[]{:S(2)}) collective-permute-start(bf16[8,128,128]{2,1,0:T(8,128)(2,1)S(1)} %slice.22), channel_id=1, source_target_pairs={{0,64},{64,128},{128,192},{192,0},{1,65},{65,129},{129,193},{193,1... | collective-permute-start | bytes 786440 | tf_op jit(solution)/shard_map/ppermute | solution.py:397
  55.6 11.1 %collective-permute-start.16 = (bf16[8,128,128]{2,1,0:T(8,128)(2,1)S(1)}, bf16[8,128,128]{2,1,0:T(8,128)(2,1)S(1)}, u32[]{:S(2)}, u32[]{:S(2)}) collective-permute-start(bf16[8,128,128]{2,1,0:T(8,128)(2,1)S(1)} %slice.23), channel_id=1, source_target_pairs={{0,192},{64,0},{128,64},{192,128},{1,193},{65,1},{129,65},{193,129... | collective-permute-start | bytes 786440 | tf_op jit(solution)/shard_map/ppermute | solution.py:398
  66.7 22.9 %slice-start = ((s8[9437184]{0:T(1024)(128)(4,1)}), s8[4194304]{0:T(1024)(128)(4,1)S(1)}, s32[]{:S(2)}) async-start(s8[9437184]{0:T(1024)(128)(4,1)} %bitcast.11), calls=%async_computation | async-start | bytes 8388608
  69.5 20.1 %slice-start.1 = ((s8[9437184]{0:T(1024)(128)(4,1)}), s8[4194304]{0:T(1024)(128)(4,1)S(1)}, s32[]{:S(2)}) async-start(s8[9437184]{0:T(1024)(128)(4,1)} %bitcast.11), calls=%async_computation.1 | async-start | bytes 8388608
  69.5 4.3 %collective-permute-start.17 = (f32[2,152,768]{2,1,0:T(8,128)S(1)}, f32[2,152,768]{2,1,0:T(8,128)S(1)}, u32[]{:S(2)}, u32[]{:S(2)}) collective-permute-start(f32[2,152,768]{2,1,0:T(8,128)S(1)} %last_send.1), channel_id=1, source_target_pairs={{0,1},{1,0},{2,3},{3,2},{4,5},{5,4},{6,7},{7,6},{8,9},{9,8},{10,11... | collective-permute-start | bytes 2801672 | tf_op jit(solution)/shard_map/ppermute | solution.py:406
  74.1 10.9 %collective-permute-start.19 = (bf16[256,768]{1,0:T(8,128)(2,1)S(1)}, bf16[256,768]{1,0:T(8,128)(2,1)S(1)}, u32[]{:S(2)}, u32[]{:S(2)}) collective-permute-start(bf16[256,768]{1,0:T(8,128)(2,1)S(1)} %merge.1), channel_id=1, source_target_pairs={{0,2},{1,6},{2,0},{3,4},{4,3},{5,7},{6,1},{7,5},{8,10},{9,14},{10,... | collective-permute-start | bytes 1179656 | tf_op jit(solution)/shard_map/ppermute | solution.py:412
  79.0 10.6 %collective-permute-start.18 = (bf16[256,768]{1,0:T(8,128)(2,1)S(1)}, bf16[256,768]{1,0:T(8,128)(2,1)S(1)}, u32[]{:S(2)}, u32[]{:S(2)}) collective-permute-start(bf16[256,768]{1,0:T(8,128)(2,1)S(1)} %merge.1), channel_id=1, source_target_pairs={{0,0},{1,4},{2,2},{3,6},{4,1},{5,5},{6,3},{7,7},{8,8},{9,12},{10,1... | collective-permute-start | bytes 1179656 | tf_op jit(solution)/shard_map/ppermute | solution.py:411
  91.6 2.4 %collective-permute-start.21 = (bf16[256,1536]{1,0:T(8,128)(2,1)S(1)}, bf16[256,1536]{1,0:T(8,128)(2,1)S(1)}, u32[]{:S(2)}, u32[]{:S(2)}) collective-permute-start(bf16[256,1536]{1,0:T(8,128)(2,1)S(1)} %project_send.1), channel_id=1, source_target_pairs={{0,1},{1,0},{2,3},{3,2},{4,5},{5,4},{6,7},{7,6},{8,9},{9,8},{10,11... | collective-permute-start | bytes 2359304 | tf_op jit(solution)/shard_map/ppermute | solution.py:416
  (1 other events, 7.1 us)

commit v13 on v12

--- a/solution.py
+++ b/solution.py
@@ -238,11 +238,7 @@
 
         lax.fori_loop(0, blocks, full, 0)
 
-        @pl.when(rest == 1)
-        def _():
-            block(target, row, 4 * blocks, 1)
-
-        @pl.when(rest == 2)
+        @pl.when(rest > 0)
         def _():
             block(target, row, 4 * blocks, 2)
 
@@ -397,11 +393,12 @@
         lax.ppermute(late_before[:half], "x", forth),
         lax.ppermute(late_after[half:], "x", back),
     ]
-    keep, send = stage(
+    state = stage(
         ((-1, LATE), (1, LATE)), near, [late_before, late_after], state, every, "late"
     )
-    *far, keep, send = together((*early_far, *late_far, keep, send))
-    last = (((2, EARLY), (2, LATE)), near, far)
+    keep, send = stage(((2, EARLY),), near, early_far, state, every, "opposite")
+    *late_far, keep, send = together((*late_far, keep, send))
+    last = (((2, LATE),), near, late_far)
     (send,) = stage(*last, (send,), (2, 3), "last_send")
     received = lax.ppermute(send, "core", swap)
     (keep,) = stage(*last, (keep,), (0, 1), "last_keep")

time: 94.7 us -> 96.5 us (1.019); the launches traced: 95 us -> 95.5 us
  starting transfers between devices: 42 us -> 44.4 us
  waiting for transfers between devices: 19.2 us -> 17.2 us
    ppermute x1, starting transfers between devices: 2.08 us -> 5.36 us  [per_device(): received = lax.ppermute(send, 'core', swap)]
    ppermute x1, waiting for transfers between devices: 3.06 us -> 0.73 us  [per_device(): lax.ppermute(late_before[:half], 'x', forth)]
    ppermute x1, starting transfers between devices: 4.89 us -> 3.07 us  [per_device(): lax.ppermute(attended, Y, along_y(lambda yh, yl, core: (core, 1 - yl, yh)))]
    pallas_call x12 -> x13, Pallas kernels: 32.2 us -> 32.3 us  [call(): pl.pallas_call(kernel, out_shape=out_shape, in_specs=in_specs, out_specs=...]
  transfers between devices with their start and end apart: 22 -> 22, of which waited for: 9 -> 10; matrix products, arithmetic and copies ran while one was open for 0% -> 0% of each run, Pallas kernels for 30% -> 30%
where the time goes in v13:
time: 96.5 us; the launch traced here: 95.5 us
  starting transfers between devices  44.4 us (46%)
  Pallas kernels  32.3 us (33%)
  waiting for transfers between devices  17.2 us (18%)
  other arithmetic  1.27 us (1%)
    pallas_call x13, Pallas kernels, call(): pl.pallas_call(kernel, out_shape=out_shape, in_specs=in_specs, out_specs=...  32.3 us
    ppermute x1, starting transfers between devices, per_device(): units[4] = lax.ppermute(unit, YZ, turned(4))  6.72 us
    ppermute x1, starting transfers between devices, per_device(): mine = lax.ppermute(bundle, Y, turn)  6.21 us
    ppermute x2, waiting for transfers between devices, per_device(): units[-step] = lax.ppermute(units[1 - step], 'z', up)  5.5 us
    ppermute x1, starting transfers between devices, per_device(): received = lax.ppermute(send, 'core', swap)  5.36 us
    ppermute x2, starting transfers between devices, per_device(): units[step] = lax.ppermute(units[step - 1], 'z', down)  4.92 us
    ppermute x1, starting transfers between devices, per_device(): near_part = lax.ppermute(attended, Y, turn)  4.34 us
    ppermute x1, waiting for transfers between devices, per_device(): near_part = lax.ppermute(attended, Y, turn)  4.04 us
  transfers between devices with their start and end apart: 22, of which 10 were waited for; matrix products, arithmetic and copies ran while one was open for 0% of the time, Pallas kernels for 30%

profile of v13, /device:TPU:1, one launch (start us, length us, event | category | flops | bytes accessed | tf_op | source)
XLA Modules:
  0.0 95.5 jit_solution(5154776577062780661)
XLA Ops:
  1.3 6.2 %collective-permute-start.3 = (bf16[17,128,128]{2,1,0:T(8,128)(2,1)S(1)}, bf16[17,128,128]{2,1,0:T(8,128)(2,1)S(1)}, u32[]{:S(2)}, u32[]{:S(2)}) collective-permute-start(bf16[17,128,128]{2,1,0:T(8,128)(2,1)S(1)} %get-tuple-element.31), channel_id=1, source_target_pairs={{0,0},{1,4},{2,2},{3,6},{4,1},{5,5},{6,3},{7,7},{8,8},{9,12},{10,1... | collective-permute-start | bytes 1671176 | tf_op jit(solution)/shard_map/ppermute | solution.py:356
  7.5 6.7 %collective-permute-start.2 = (bf16[4,128,128]{2,1,0:T(8,128)(2,1)S(1)}, bf16[4,128,128]{2,1,0:T(8,128)(2,1)S(1)}, u32[]{:S(2)}, u32[]{:S(2)}) collective-permute-start(bf16[4,128,128]{2,1,0:T(8,128)(2,1)S(1)} %get-tuple-element.30), channel_id=1, source_target_pairs={{0,32},{1,36},{2,34},{3,38},{4,33},{5,37},{6,35},{7,39},{8,40},{9,... | collective-permute-start | bytes 393224 | tf_op jit(solution)/shard_map/ppermute | solution.py:357
  14.3 2.8 %collective-permute-start.1 = (bf16[4,128,128]{2,1,0:T(8,128)(2,1)S(1)}, bf16[4,128,128]{2,1,0:T(8,128)(2,1)S(1)}, u32[]{:S(2)}, u32[]{:S(2)}) collective-permute-start(bf16[4,128,128]{2,1,0:T(8,128)(2,1)S(1)} %get-tuple-element.30), channel_id=1, source_target_pairs={{0,56},{1,60},{2,58},{3,62},{4,57},{5,61},{6,59},{7,63},{8,0},{9,4... | collective-permute-start | bytes 393224 | tf_op jit(solution)/shard_map/ppermute | solution.py:355
  18.4 4.5 %column_half.1 = bf16[768,3072]{1,0:T(8,128)(2,1)} custom-call(s32[1]{0:T(128)} %bitcast.2.half_ref, bf16[768,6144]{1,0:T(8,128)(2,1)} %refs_3_.3), custom_call_target="tpu_custom_call" | custom-call | tf_op jit(solution)/shard_map/column_half/pallas_call | solution.py:43
  25.1 2.6 %collective-permute-start.9 = (bf16[16,128,128]{2,1,0:T(8,128)(2,1)S(1)}, bf16[16,128,128]{2,1,0:T(8,128)(2,1)S(1)}, u32[]{:S(2)}, u32[]{:S(2)}) collective-permute-start(bf16[16,128,128]{2,1,0:T(8,128)(2,1)S(1)} %join.3.refs_3_), channel_id=1, source_target_pairs={{0,192},{64,0},{128,64},{192,128},{1,193},{65,1},{129,65},{193,129... | collective-permute-start | bytes 1572872 | tf_op jit(solution)/shard_map/ppermute | solution.py:367
  28.1 2.2 %collective-permute-start.5 = (bf16[4,128,128]{2,1,0:T(8,128)(2,1)S(1)}, bf16[4,128,128]{2,1,0:T(8,128)(2,1)S(1)}, u32[]{:S(2)}, u32[]{:S(2)}) collective-permute-start(bf16[4,128,128]{2,1,0:T(8,128)(2,1)S(1)} %collective-permute-done.1.refs_1_), channel_id=1, source_target_pairs={{0,56},{8,0},{16,8},{24,16},{32,24},{40,32},{48,40},{56,48},{1,57}... | collective-permute-start | bytes 393224 | tf_op jit(solution)/shard_map/ppermute | solution.py:370
  30.3 2.8 %collective-permute-done.4.refs_0_ = bf16[4,128,128]{2,1,0:T(8,128)(2,1)S(1)} collective-permute-done((bf16[4,128,128]{2,1,0:T(8,128)(2,1)S(1)}, bf16[4,128,128]{2,1,0:T(8,128)(2,1)S(1)}, u32[]{:S(2)}, u32[]{:S(2)}) %collective-permute-start.4) | collective-permute-done | bytes 131104 | tf_op jit(solution)/shard_map/ppermute | solution.py:369
  33.1 2.7 %collective-permute-start.7 = (bf16[4,128,128]{2,1,0:T(8,128)(2,1)S(1)}, bf16[4,128,128]{2,1,0:T(8,128)(2,1)S(1)}, u32[]{:S(2)}, u32[]{:S(2)}) collective-permute-start(bf16[4,128,128]{2,1,0:T(8,128)(2,1)S(1)} %collective-permute-done.5.refs_1_), channel_id=1, source_target_pairs={{0,56},{8,0},{16,8},{24,16},{32,24},{40,32},{48,40},{56,48},{1,57}... | collective-permute-start | bytes 393224 | tf_op jit(solution)/shard_map/ppermute | solution.py:370
  35.8 2.7 %collective-permute-done.6.refs_2_ = bf16[4,128,128]{2,1,0:T(8,128)(2,1)S(1)} collective-permute-done((bf16[4,128,128]{2,1,0:T(8,128)(2,1)S(1)}, bf16[4,128,128]{2,1,0:T(8,128)(2,1)S(1)}, u32[]{:S(2)}, u32[]{:S(2)}) %collective-permute-start.6) | collective-permute-done | bytes 131104 | tf_op jit(solution)/shard_map/ppermute | solution.py:369
  38.6 1.8 %collective-permute-done.8.refs_5_ = bf16[16,128,128]{2,1,0:T(8,128)(2,1)S(1)} collective-permute-done((bf16[16,128,128]{2,1,0:T(8,128)(2,1)S(1)}, bf16[16,128,128]{2,1,0:T(8,128)(2,1)S(1)}, u32[]{:S(2)}, u32[]{:S(2)}) %collective-permute-start.8) | collective-permute-done | bytes 524320 | tf_op jit(solution)/shard_map/ppermute | solution.py:366
  42.0 2.3 %collective-permute-start.16 = (bf16[8,128,128]{2,1,0:T(8,128)(2,1)S(1)}, bf16[8,128,128]{2,1,0:T(8,128)(2,1)S(1)}, u32[]{:S(2)}, u32[]{:S(2)}) collective-permute-start(bf16[8,128,128]{2,1,0:T(8,128)(2,1)S(1)} %slice.23), channel_id=1, source_target_pairs={{0,192},{64,0},{128,64},{192,128},{1,193},{65,1},{129,65},{193,129... | collective-permute-start | bytes 786440 | tf_op jit(solution)/shard_map/ppermute | solution.py:386
  44.3 8.4 %first.1 = (f32[2,152,768]{2,1,0:T(8,128)S(1)}, f32[2,152,768]{2,1,0:T(8,128)S(1)}) custom-call(s32[5,128]{1,0:T(8,128)S(1)} %pad_add_fusion.refs_0_, bf16[17,128,128]{2,1,0:T(8,128)(2,1)S(1)} %collective-permute-done.3.refs_2_.refs_1_, bf16[17,128,128]{2,1,0:T(8,128)(2,1)S(1)} %collective-permute-done.10.refs_2_, bf16[16,128,128]{2,1,0:T(8,128)(2,1)S(1)} %join.3.refs_3_, ...), custom_call_target="tpu_custom_call" | custom-call | tf_op jit(solution)/shard_map/first/pallas_call | solution.py:43
  53.5 1.9 %collective-permute-done.11.refs_3_ = bf16[16,128,128]{2,1,0:T(8,128)(2,1)S(1)} collective-permute-done((bf16[16,128,128]{2,1,0:T(8,128)(2,1)S(1)}, bf16[16,128,128]{2,1,0:T(8,128)(2,1)S(1)}, u32[]{:S(2)}, u32[]{:S(2)}) %collective-permute-start.11) | collective-permute-done | bytes 524320 | tf_op jit(solution)/shard_map/ppermute | solution.py:374
  55.6 2.7 %collective-permute-start.14 = (bf16[8,128,128]{2,1,0:T(8,128)(2,1)S(1)}, bf16[8,128,128]{2,1,0:T(8,128)(2,1)S(1)}, u32[]{:S(2)}, u32[]{:S(2)}) collective-permute-start(bf16[8,128,128]{2,1,0:T(8,128)(2,1)S(1)} %slice.21), channel_id=1, source_target_pairs={{0,192},{64,0},{128,64},{192,128},{1,193},{65,1},{129,65},{193,129... | collective-permute-start | bytes 786440 | tf_op jit(solution)/shard_map/ppermute | solution.py:394
  58.3 5.1 %late.1 = (f32[2,152,768]{2,1,0:T(8,128)S(1)}, f32[2,152,768]{2,1,0:T(8,128)S(1)}) custom-call(s32[5,128]{1,0:T(8,128)S(1)} %pad_add_fusion.refs_0_, bf16[17,128,128]{2,1,0:T(8,128)(2,1)S(1)} %collective-permute-done.3.refs_2_.refs_1_, bf16[17,128,128]{2,1,0:T(8,128)(2,1)S(1)} %collective-permute-done.10.refs_2_, ...), custom_call_target="tpu_custom_call", output_to_operand_aliasing={{0}: (5, {}), {1}: (6, {})} | custom-call | tf_op jit(solution)/shard_map/late/pallas_call | solution.py:43
  63.4 2.6 %opposite.1 = (f32[2,152,768]{2,1,0:T(8,128)S(1)}, f32[2,152,768]{2,1,0:T(8,128)S(1)}) custom-call(s32[5,128]{1,0:T(8,128)S(1)} %pad_add_fusion.refs_0_, bf16[17,128,128]{2,1,0:T(8,128)(2,1)S(1)} %collective-permute-done.3.refs_2_.refs_1_, bf16[17,128,128]{2,1,0:T(8,128)(2,1)S(1)} %collective-permute-done.10.refs_2_, ...), custom_call_target="tpu_custom_call", output_to_operand_aliasing={{0}: (5, {}), {1}: (6, {})} | custom-call | tf_op jit(solution)/shard_map/opposite/pallas_call | solution.py:43
  68.0 5.4 %collective-permute-start.17 = (f32[2,152,768]{2,1,0:T(8,128)S(1)}, f32[2,152,768]{2,1,0:T(8,128)S(1)}, u32[]{:S(2)}, u32[]{:S(2)}) collective-permute-start(f32[2,152,768]{2,1,0:T(8,128)S(1)} %last_send.1), channel_id=1, source_target_pairs={{0,1},{1,0},{2,3},{3,2},{4,5},{5,4},{6,7},{7,6},{8,9},{9,8},{10,11... | collective-permute-start | bytes 2801672 | tf_op jit(solution)/shard_map/ppermute | solution.py:403
  73.3 2.5 %last_keep.1.own_ref = f32[2,152,768]{2,1,0:T(8,128)S(1)} custom-call(s32[5,128]{1,0:T(8,128)S(1)} %pad_add_fusion.refs_0_, bf16[17,128,128]{2,1,0:T(8,128)(2,1)S(1)} %collective-permute-done.3.refs_2_.refs_1_, bf16[17,128,128]{2,1,0:T(8,128)(2,1)S(1)} %collective-permute-done.10.refs_2_, ...), custom_call_target="tpu_custom_call", output_to_operand_aliasing={{}: (5, {})} | custom-call | tf_op jit(solution)/shard_map/last_keep/pallas_call | solution.py:43
  76.0 3.1 %collective-permute-start.19 = (bf16[256,768]{1,0:T(8,128)(2,1)S(1)}, bf16[256,768]{1,0:T(8,128)(2,1)S(1)}, u32[]{:S(2)}, u32[]{:S(2)}) collective-permute-start(bf16[256,768]{1,0:T(8,128)(2,1)S(1)} %merge.1), channel_id=1, source_target_pairs={{0,2},{1,6},{2,0},{3,4},{4,3},{5,7},{6,1},{7,5},{8,10},{9,14},{10,... | collective-permute-start | bytes 1179656 | tf_op jit(solution)/shard_map/ppermute | solution.py:409
  79.1 4.3 %collective-permute-start.18 = (bf16[256,768]{1,0:T(8,128)(2,1)S(1)}, bf16[256,768]{1,0:T(8,128)(2,1)S(1)}, u32[]{:S(2)}, u32[]{:S(2)}) collective-permute-start(bf16[256,768]{1,0:T(8,128)(2,1)S(1)} %merge.1), channel_id=1, source_target_pairs={{0,0},{1,4},{2,2},{3,6},{4,1},{5,5},{6,3},{7,7},{8,8},{9,12},{10,1... | collective-permute-start | bytes 1179656 | tf_op jit(solution)/shard_map/ppermute | solution.py:408
  83.5 2.5 %fetch.1.refs_4_ = bf16[768,3072]{1,0:T(8,128)(2,1)S(1)} custom-call(bf16[768,3072]{1,0:T(8,128)(2,1)} %collective-permute-done.20.source_ref), custom_call_target="tpu_custom_call" | custom-call | tf_op jit(solution)/shard_map/fetch/pallas_call | solution.py:43
  86.0 4.0 %collective-permute-done.18.refs_1_ = bf16[256,768]{1,0:T(8,128)(2,1)S(1)} collective-permute-done((bf16[256,768]{1,0:T(8,128)(2,1)S(1)}, bf16[256,768]{1,0:T(8,128)(2,1)S(1)}, u32[]{:S(2)}, u32[]{:S(2)}) %collective-permute-start.18) | collective-permute-done | bytes 393248 | tf_op jit(solution)/shard_map/ppermute | solution.py:408
  90.1 2.0 %project_send.1 = bf16[256,1536]{1,0:T(8,128)(2,1)S(1)} custom-call(s32[2]{0:T(128)S(1)} %pad_add_fusion.1.refs_0_, bf16[256,768]{1,0:T(8,128)(2,1)S(1)} %collective-permute-done.18.refs_1_, bf16[256,768]{1,0:T(8,128)(2,1)S(1)} %collective-permute-done.19.refs_2_, bf16[768,6144]{1,0:T(8,128)(2,1)S(1)} %bitcast.12, bf16[768,3072]{1,0:T(8,128)(2,1)S(1)} %fetch.1.refs_4_), custom_call_target="tpu_custom_call" | custom-call | tf_op jit(solution)/shard_map/project_send/pallas_call | solution.py:43
  92.2 2.0 %project_keep.1 = f32[256,1536]{1,0:T(8,128)S(1)} custom-call(s32[2]{0:T(128)S(1)} %pad_add_fusion.1.refs_0_, bf16[256,768]{1,0:T(8,128)(2,1)S(1)} %collective-permute-done.18.refs_1_, bf16[256,768]{1,0:T(8,128)(2,1)S(1)} %collective-permute-done.19.refs_2_, bf16[768,6144]{1,0:T(8,128)(2,1)S(1)} %bitcast.12, bf16[768,3072]{1,0:T(8,128)(2,1)S(1)} %fetch.1.refs_4_), custom_call_target="tpu_custom_call" | custom-call | tf_op jit(solution)/shard_map/project_keep/pallas_call | solution.py:43
  (52 shorter events, 11.6 us)
Async XLA Ops:
  1.3 23.7 %collective-permute-start.3 = (bf16[17,128,128]{2,1,0:T(8,128)(2,1)S(1)}, bf16[17,128,128]{2,1,0:T(8,128)(2,1)S(1)}, u32[]{:S(2)}, u32[]{:S(2)}) collective-permute-start(bf16[17,128,128]{2,1,0:T(8,128)(2,1)S(1)} %get-tuple-element.31), channel_id=1, source_target_pairs={{0,0},{1,4},{2,2},{3,6},{4,1},{5,5},{6,3},{7,7},{8,8},{9,12},{10,1... | collective-permute-start | bytes 1671176 | tf_op jit(solution)/shard_map/ppermute | solution.py:356
  7.5 15.4 %collective-permute-start.2 = (bf16[4,128,128]{2,1,0:T(8,128)(2,1)S(1)}, bf16[4,128,128]{2,1,0:T(8,128)(2,1)S(1)}, u32[]{:S(2)}, u32[]{:S(2)}) collective-permute-start(bf16[4,128,128]{2,1,0:T(8,128)(2,1)S(1)} %get-tuple-element.30), channel_id=1, source_target_pairs={{0,32},{1,36},{2,34},{3,38},{4,33},{5,37},{6,35},{7,39},{8,40},{9,... | collective-permute-start | bytes 393224 | tf_op jit(solution)/shard_map/ppermute | solution.py:357
  14.3 9.2 %collective-permute-start.1 = (bf16[4,128,128]{2,1,0:T(8,128)(2,1)S(1)}, bf16[4,128,128]{2,1,0:T(8,128)(2,1)S(1)}, u32[]{:S(2)}, u32[]{:S(2)}) collective-permute-start(bf16[4,128,128]{2,1,0:T(8,128)(2,1)S(1)} %get-tuple-element.30), channel_id=1, source_target_pairs={{0,56},{1,60},{2,58},{3,62},{4,57},{5,61},{6,59},{7,63},{8,0},{9,4... | collective-permute-start | bytes 393224 | tf_op jit(solution)/shard_map/ppermute | solution.py:355
  17.0 8.0 %collective-permute-start = (bf16[4,128,128]{2,1,0:T(8,128)(2,1)S(1)}, bf16[4,128,128]{2,1,0:T(8,128)(2,1)S(1)}, u32[]{:S(2)}, u32[]{:S(2)}) collective-permute-start(bf16[4,128,128]{2,1,0:T(8,128)(2,1)S(1)} %get-tuple-element.30), channel_id=1, source_target_pairs={{0,8},{1,12},{2,10},{3,14},{4,9},{5,13},{6,11},{7,15},{8,16},{9,20... | collective-permute-start | bytes 393224 | tf_op jit(solution)/shard_map/ppermute | solution.py:355
  25.0 58.5 %collective-permute-start.20 = (bf16[768,3072]{1,0:T(8,128)(2,1)}, bf16[768,3072]{1,0:T(8,128)(2,1)}, u32[]{:S(2)}, u32[]{:S(2)}) collective-permute-start(bf16[768,3072]{1,0:T(8,128)(2,1)} %column_half.1), channel_id=1, source_target_pairs={{0,2},{1,7},{2,4},{3,1},{4,6},{5,3},{6,0},{7,5},{8,10},{9,15},{10,... | collective-permute-start | bytes 14155784 | tf_op jit(solution)/shard_map/ppermute | solution.py:363
  25.1 13.5 %collective-permute-start.9 = (bf16[16,128,128]{2,1,0:T(8,128)(2,1)S(1)}, bf16[16,128,128]{2,1,0:T(8,128)(2,1)S(1)}, u32[]{:S(2)}, u32[]{:S(2)}) collective-permute-start(bf16[16,128,128]{2,1,0:T(8,128)(2,1)S(1)} %join.3.refs_3_), channel_id=1, source_target_pairs={{0,192},{64,0},{128,64},{192,128},{1,193},{65,1},{129,65},{193,129... | collective-permute-start | bytes 1572872 | tf_op jit(solution)/shard_map/ppermute | solution.py:367
  27.6 12.7 %collective-permute-start.8 = (bf16[16,128,128]{2,1,0:T(8,128)(2,1)S(1)}, bf16[16,128,128]{2,1,0:T(8,128)(2,1)S(1)}, u32[]{:S(2)}, u32[]{:S(2)}) collective-permute-start(bf16[16,128,128]{2,1,0:T(8,128)(2,1)S(1)} %join.3.refs_3_), channel_id=1, source_target_pairs={{0,64},{64,128},{128,192},{192,0},{1,65},{65,129},{129,193},{193,1... | collective-permute-start | bytes 1572872 | tf_op jit(solution)/shard_map/ppermute | solution.py:366
  27.7 5.4 %collective-permute-start.4 = (bf16[4,128,128]{2,1,0:T(8,128)(2,1)S(1)}, bf16[4,128,128]{2,1,0:T(8,128)(2,1)S(1)}, u32[]{:S(2)}, u32[]{:S(2)}) collective-permute-start(bf16[4,128,128]{2,1,0:T(8,128)(2,1)S(1)} %collective-permute-done.refs_0_), channel_id=1, source_target_pairs={{0,8},{8,16},{16,24},{24,32},{32,40},{40,48},{48,56},{56,0},{1,9},... | collective-permute-start | bytes 393224 | tf_op jit(solution)/shard_map/ppermute | solution.py:369
  28.1 5.0 %collective-permute-start.5 = (bf16[4,128,128]{2,1,0:T(8,128)(2,1)S(1)}, bf16[4,128,128]{2,1,0:T(8,128)(2,1)S(1)}, u32[]{:S(2)}, u32[]{:S(2)}) collective-permute-start(bf16[4,128,128]{2,1,0:T(8,128)(2,1)S(1)} %collective-permute-done.1.refs_1_), channel_id=1, source_target_pairs={{0,56},{8,0},{16,8},{24,16},{32,24},{40,32},{48,40},{56,48},{1,57}... | collective-permute-start | bytes 393224 | tf_op jit(solution)/shard_map/ppermute | solution.py:370
  33.1 5.4 %collective-permute-start.6 = (bf16[4,128,128]{2,1,0:T(8,128)(2,1)S(1)}, bf16[4,128,128]{2,1,0:T(8,128)(2,1)S(1)}, u32[]{:S(2)}, u32[]{:S(2)}) collective-permute-start(bf16[4,128,128]{2,1,0:T(8,128)(2,1)S(1)} %collective-permute-done.4.refs_0_), channel_id=1, source_target_pairs={{0,8},{8,16},{16,24},{24,32},{32,40},{40,48},{48,56},{56,0},{1,9},... | collective-permute-start | bytes 393224 | tf_op jit(solution)/shard_map/ppermute | solution.py:369
  33.1 5.4 %collective-permute-start.7 = (bf16[4,128,128]{2,1,0:T(8,128)(2,1)S(1)}, bf16[4,128,128]{2,1,0:T(8,128)(2,1)S(1)}, u32[]{:S(2)}, u32[]{:S(2)}) collective-permute-start(bf16[4,128,128]{2,1,0:T(8,128)(2,1)S(1)} %collective-permute-done.5.refs_1_), channel_id=1, source_target_pairs={{0,56},{8,0},{16,8},{24,16},{32,24},{40,32},{48,40},{56,48},{1,57}... | collective-permute-start | bytes 393224 | tf_op jit(solution)/shard_map/ppermute | solution.py:370
  40.3 3.9 %collective-permute-start.10 = (bf16[17,128,128]{2,1,0:T(8,128)(2,1)S(1)}, bf16[17,128,128]{2,1,0:T(8,128)(2,1)S(1)}, u32[]{:S(2)}, u32[]{:S(2)}) collective-permute-start(bf16[17,128,128]{2,1,0:T(8,128)(2,1)S(1)} %collective-permute-done.3.refs_2_.refs_1_), channel_id=1, source_target_pairs={{0,1},{1,0},{2,3},{3,2},{4,5},{5,4},{6,7},{7,6},{8,9},{9,8},{10,11... | collective-permute-start | bytes 1671176 | tf_op jit(solution)/shard_map/ppermute | solution.py:376
  40.4 13.1 %collective-permute-start.12 = (bf16[16,128,128]{2,1,0:T(8,128)(2,1)S(1)}, bf16[16,128,128]{2,1,0:T(8,128)(2,1)S(1)}, u32[]{:S(2)}, u32[]{:S(2)}) collective-permute-start(bf16[16,128,128]{2,1,0:T(8,128)(2,1)S(1)} %join.2.refs_4_), channel_id=1, source_target_pairs={{0,192},{64,0},{128,64},{192,128},{1,193},{65,1},{129,65},{193,129... | collective-permute-start | bytes 1572872 | tf_op jit(solution)/shard_map/ppermute | solution.py:375
  41.5 14.0 %collective-permute-start.11 = (bf16[16,128,128]{2,1,0:T(8,128)(2,1)S(1)}, bf16[16,128,128]{2,1,0:T(8,128)(2,1)S(1)}, u32[]{:S(2)}, u32[]{:S(2)}) collective-permute-start(bf16[16,128,128]{2,1,0:T(8,128)(2,1)S(1)} %join.2.refs_4_), channel_id=1, source_target_pairs={{0,64},{64,128},{128,192},{192,0},{1,65},{65,129},{129,193},{193,1... | collective-permute-start | bytes 1572872 | tf_op jit(solution)/shard_map/ppermute | solution.py:374
  42.0 21.4 %collective-permute-start.16 = (bf16[8,128,128]{2,1,0:T(8,128)(2,1)S(1)}, bf16[8,128,128]{2,1,0:T(8,128)(2,1)S(1)}, u32[]{:S(2)}, u32[]{:S(2)}) collective-permute-start(bf16[8,128,128]{2,1,0:T(8,128)(2,1)S(1)} %slice.23), channel_id=1, source_target_pairs={{0,192},{64,0},{128,64},{192,128},{1,193},{65,1},{129,65},{193,129... | collective-permute-start | bytes 786440 | tf_op jit(solution)/shard_map/ppermute | solution.py:386
  44.3 19.1 %collective-permute-start.15 = (bf16[8,128,128]{2,1,0:T(8,128)(2,1)S(1)}, bf16[8,128,128]{2,1,0:T(8,128)(2,1)S(1)}, u32[]{:S(2)}, u32[]{:S(2)}) collective-permute-start(bf16[8,128,128]{2,1,0:T(8,128)(2,1)S(1)} %slice.22), channel_id=1, source_target_pairs={{0,64},{64,128},{128,192},{192,0},{1,65},{65,129},{129,193},{193,1... | collective-permute-start | bytes 786440 | tf_op jit(solution)/shard_map/ppermute | solution.py:385
  55.5 11.2 %collective-permute-start.13 = (bf16[8,128,128]{2,1,0:T(8,128)(2,1)S(1)}, bf16[8,128,128]{2,1,0:T(8,128)(2,1)S(1)}, u32[]{:S(2)}, u32[]{:S(2)}) collective-permute-start(bf16[8,128,128]{2,1,0:T(8,128)(2,1)S(1)} %slice.20), channel_id=1, source_target_pairs={{0,64},{64,128},{128,192},{192,0},{1,65},{65,129},{129,193},{193,1... | collective-permute-start | bytes 786440 | tf_op jit(solution)/shard_map/ppermute | solution.py:393
  55.6 11.1 %collective-permute-start.14 = (bf16[8,128,128]{2,1,0:T(8,128)(2,1)S(1)}, bf16[8,128,128]{2,1,0:T(8,128)(2,1)S(1)}, u32[]{:S(2)}, u32[]{:S(2)}) collective-permute-start(bf16[8,128,128]{2,1,0:T(8,128)(2,1)S(1)} %slice.21), channel_id=1, source_target_pairs={{0,192},{64,0},{128,64},{192,128},{1,193},{65,1},{129,65},{193,129... | collective-permute-start | bytes 786440 | tf_op jit(solution)/shard_map/ppermute | solution.py:394
  66.7 23.3 %slice-start = ((s8[9437184]{0:T(1024)(128)(4,1)}), s8[4194304]{0:T(1024)(128)(4,1)S(1)}, s32[]{:S(2)}) async-start(s8[9437184]{0:T(1024)(128)(4,1)} %bitcast.11), calls=%async_computation | async-start | bytes 8388608
  67.9 22.1 %slice-start.1 = ((s8[9437184]{0:T(1024)(128)(4,1)}), s8[4194304]{0:T(1024)(128)(4,1)S(1)}, s32[]{:S(2)}) async-start(s8[9437184]{0:T(1024)(128)(4,1)} %bitcast.11), calls=%async_computation.1 | async-start | bytes 8388608
  68.0 7.8 %collective-permute-start.17 = (f32[2,152,768]{2,1,0:T(8,128)S(1)}, f32[2,152,768]{2,1,0:T(8,128)S(1)}, u32[]{:S(2)}, u32[]{:S(2)}) collective-permute-start(f32[2,152,768]{2,1,0:T(8,128)S(1)} %last_send.1), channel_id=1, source_target_pairs={{0,1},{1,0},{2,3},{3,2},{4,5},{5,4},{6,7},{7,6},{8,9},{9,8},{10,11... | collective-permute-start | bytes 2801672 | tf_op jit(solution)/shard_map/ppermute | solution.py:403
  76.0 10.0 %collective-permute-start.19 = (bf16[256,768]{1,0:T(8,128)(2,1)S(1)}, bf16[256,768]{1,0:T(8,128)(2,1)S(1)}, u32[]{:S(2)}, u32[]{:S(2)}) collective-permute-start(bf16[256,768]{1,0:T(8,128)(2,1)S(1)} %merge.1), channel_id=1, source_target_pairs={{0,2},{1,6},{2,0},{3,4},{4,3},{5,7},{6,1},{7,5},{8,10},{9,14},{10,... | collective-permute-start | bytes 1179656 | tf_op jit(solution)/shard_map/ppermute | solution.py:409
  79.1 11.0 %collective-permute-start.18 = (bf16[256,768]{1,0:T(8,128)(2,1)S(1)}, bf16[256,768]{1,0:T(8,128)(2,1)S(1)}, u32[]{:S(2)}, u32[]{:S(2)}) collective-permute-start(bf16[256,768]{1,0:T(8,128)(2,1)S(1)} %merge.1), channel_id=1, source_target_pairs={{0,0},{1,4},{2,2},{3,6},{4,1},{5,5},{6,3},{7,7},{8,8},{9,12},{10,1... | collective-permute-start | bytes 1179656 | tf_op jit(solution)/shard_map/ppermute | solution.py:408
  92.1 2.4 %collective-permute-start.21 = (bf16[256,1536]{1,0:T(8,128)(2,1)S(1)}, bf16[256,1536]{1,0:T(8,128)(2,1)S(1)}, u32[]{:S(2)}, u32[]{:S(2)}) collective-permute-start(bf16[256,1536]{1,0:T(8,128)(2,1)S(1)} %project_send.1), channel_id=1, source_target_pairs={{0,1},{1,0},{2,3},{3,2},{4,5},{5,4},{6,7},{7,6},{8,9},{9,8},{10,11... | collective-permute-start | bytes 2359304 | tf_op jit(solution)/shard_map/ppermute | solution.py:413
  (1 other events, 6.5 us)
